TPU v7x, 32 devices: a whole 2x2x4 slice. The times are simulated.
32 devices in a mesh: shard: 4 (over y, x), ctx: 4 (over z), tensor: 2 (over core).
Axes of the slice: x: 2, y: 2, z: 4, core: 2. Of those that a mesh axis runs over, the one named last changes fastest.
Arguments:
- tokens: bfloat16 [8, 1024, 2304], P('shard', 'ctx'), may hold values from -6 to 6
- lengths: int32 [8], P('shard'), may hold values from 256 to 1024, as said below
- span_order: int32 [8], replicated, may hold values from 0 to 7, each once
- attn_gain: bfloat16 [2304], P('shard'), may hold values from 0.5 to 1.5
- w_query: bfloat16 [2304, 2304], P('shard', 'tensor'), may hold values from -0.125 to 0.125
- w_key: bfloat16 [2304, 2304], P('shard', 'tensor'), may hold values from -0.125 to 0.125
- w_value: bfloat16 [2304, 2304], P('shard', 'tensor'), may hold values from -0.125 to 0.125
- w_out: bfloat16 [2304, 2304], P('tensor', 'shard'), may hold values from -4 to 4
- mlp_gain: bfloat16 [2304], P('shard'), may hold values from 0.5 to 1.5
- w_gate: bfloat16 [2304, 5760], P('shard', 'tensor'), may hold values from -0.125 to 0.125
- w_up: bfloat16 [2304, 5760], P('shard', 'tensor'), may hold values from -0.125 to 0.125
- w_down: bfloat16 [5760, 2304], P('tensor', 'shard'), may hold values from -0.4375 to 0.4375
- cotangent: bfloat16 [8, 1024, 2304], P('shard', 'ctx'), may hold values from -6 to 6
Outputs:
- layer_out: bfloat16 [8, 1024, 2304], P('shard', 'ctx')
- grad_tokens: float32 [8, 1024, 2304], P('shard', 'ctx')
- grad_attn_gain: float32 [2304], P('shard')
- grad_query: float32 [2304, 2304], P('shard', 'tensor')
- grad_key: float32 [2304, 2304], P('shard', 'tensor')
- grad_value: float32 [2304, 2304], P('shard', 'tensor')
- grad_out: float32 [2304, 2304], P('tensor', 'shard')
- grad_mlp_gain: float32 [2304], P('shard')
- grad_gate: float32 [2304, 5760], P('shard', 'tensor')
- grad_up: float32 [2304, 5760], P('shard', 'tensor')
- grad_down: float32 [5760, 2304], P('tensor', 'shard')
Inputs may be any that keep to these rules, and one draw needn't show every extreme that they name: `lengths`: rows of a slot whose position is its length or more are padding; some slot is full and some slot holds exactly 256 tokens. `span_order`: each block place of a slot appears once.
All inputs are finite; a program needn't handle non-finite values.
Results may differ from a plain program's by a relative error of at most 0.015.
Values may be sent and summed in bfloat16 or wider, within the bound.
A program may use at most 272 MiB of HBM per device.

v0:
```python
import math

import jax
import jax.numpy as jnp
from jax import lax
from jax.sharding import PartitionSpec as P

HD = 64


NORM_EPS = 1e-05
ROPE_BASE = 10000.0
BRANCH_SCALE = 1.4 / math.sqrt(40.0)
CONTRACT_ROWS = (((0,), (0,)), ((), ()))
CONTRACT_COLS = (((1,), (1,)), ((), ()))


def row_product(left_mat, right_mat):
    return lax.dot_general(left_mat, right_mat, CONTRACT_ROWS, preferred_element_type=jnp.float32)


def col_product(left_mat, right_mat):
    return lax.dot_general(left_mat, right_mat, CONTRACT_COLS, preferred_element_type=jnp.float32)


def plain_product(left_mat, right_mat):
    return jnp.dot(left_mat, right_mat, preferred_element_type=jnp.float32)


def rope_tables(positions, head_dim):
    frequency = ROPE_BASE ** (-(jnp.arange(head_dim // 2) * 2).astype(jnp.float32) / head_dim)
    angles = positions.astype(jnp.float32)[:, None] * frequency[None, :]
    return (jnp.cos(angles)[:, None, :], jnp.sin(angles)[:, None, :])


def rotate(values_in, cos_table, sin_table, sign_dir):
    half_dim = values_in.shape[-1] // 2
    lead_part = values_in[..., :half_dim]
    tail_part = values_in[..., half_dim:]
    turned = sin_table * sign_dir
    return jnp.concatenate(
        [lead_part * cos_table - tail_part * turned, tail_part * cos_table + lead_part * turned],
        axis=-1,
    )


def norm_parts(values_in):
    inverse = lax.rsqrt(jnp.mean(values_in * values_in, axis=-1, keepdims=True) + NORM_EPS)
    return (values_in * inverse, inverse)


def norm_back(grad_in, normed, inverse, gain_vec):
    scaled = grad_in * gain_vec
    return inverse * (scaled - normed * jnp.mean(scaled * normed, axis=-1, keepdims=True))


def local(
    tokens,
    lengths,
    span_order,
    attn_gain,
    w_query,
    w_key,
    w_value,
    w_out,
    mlp_gain,
    w_gate,
    w_up,
    w_down,
    cotangent,
):
    slot_count, row_count, width = tokens.shape
    local_heads = w_query.shape[1] // HD
    span_rows = row_count // 2
    offsets = jnp.arange(span_rows, dtype=jnp.int32)
    all_pos = (span_order[:, None] * span_rows + offsets[None, :]).reshape(-1)
    own_pos = lax.dynamic_slice_in_dim(all_pos, lax.axis_index("ctx") * row_count, row_count)
    cos_own, sin_own = rope_tables(own_pos, HD)
    causal = all_pos[None, :] <= own_pos[:, None]
    score_scale = HD ** (-0.5)

    def masked_scores(query_b, key_all, allowed):
        raw_scores = (
            jnp.einsum("qhd,khd->hqk", query_b, key_all, preferred_element_type=jnp.float32)
            * score_scale
        )
        return jnp.where(allowed[None], raw_scores, -1e30)

    out_blocks = []
    grad_blocks = []
    totals = None
    for slot_index in range(slot_count):
        length = lengths[slot_index]
        gain_one = lax.all_gather(attn_gain, "shard", axis=0, tiled=True)
        query_w = lax.all_gather(w_query, "shard", axis=0, tiled=True)
        key_w = lax.all_gather(w_key, "shard", axis=0, tiled=True)
        value_w = lax.all_gather(w_value, "shard", axis=0, tiled=True)
        out_w = lax.all_gather(w_out, "shard", axis=1, tiled=True)
        gain_two = lax.all_gather(mlp_gain, "shard", axis=0, tiled=True)
        gate_w = lax.all_gather(w_gate, "shard", axis=0, tiled=True)
        up_w = lax.all_gather(w_up, "shard", axis=0, tiled=True)
        down_w = lax.all_gather(w_down, "shard", axis=1, tiled=True)
        live_mask = (own_pos < length).astype(jnp.float32)[:, None]
        run_allowed = causal & (all_pos < length)[None, :]
        gain_a = gain_one.astype(jnp.float32)
        gain_b = gain_two.astype(jnp.float32)
        residual_in = tokens[slot_index].astype(jnp.float32)
        normed_one, inverse_one = norm_parts(residual_in)
        first_in = (normed_one * gain_a).astype(jnp.bfloat16)
        query_f = plain_product(first_in, query_w).reshape(row_count, local_heads, HD)
        key_f = plain_product(first_in, key_w).reshape(row_count, local_heads, HD)
        value_b = plain_product(first_in, value_w).astype(jnp.bfloat16)
        run_query_b = rotate(query_f, cos_own, sin_own, 1.0).astype(jnp.bfloat16)
        key_b = rotate(key_f, cos_own, sin_own, 1.0).astype(jnp.bfloat16).reshape(row_count, -1)
        run_key_all = lax.all_gather(key_b, "ctx", axis=0, tiled=True)
        value_all = lax.all_gather(value_b, "ctx", axis=0, tiled=True)
        run_key_all = run_key_all.reshape(-1, local_heads, HD)
        value_all = value_all.reshape(-1, local_heads, HD)
        scores = masked_scores(run_query_b, run_key_all, run_allowed)
        row_top = jnp.max(scores, axis=-1, keepdims=True)
        weights = jnp.exp(scores - row_top)
        row_total = jnp.sum(weights, axis=-1, keepdims=True)
        log_total = row_top + jnp.log(row_total)
        probs_low = (weights / row_total).astype(jnp.bfloat16)
        attend = (
            jnp.einsum("hqk,khd->qhd", probs_low, value_all, preferred_element_type=jnp.float32)
            .astype(jnp.bfloat16)
            .reshape(row_count, -1)
        )
        attn_out = lax.psum(plain_product(attend, out_w), "tensor")
        middle = residual_in + BRANCH_SCALE * attn_out
        normed_two, inverse_two = norm_parts(middle)
        second_in = (normed_two * gain_b).astype(jnp.bfloat16)
        gate_proj = plain_product(second_in, gate_w)
        up_proj = plain_product(second_in, up_w)
        gate_sig = jax.nn.sigmoid(gate_proj)
        gate_act = gate_proj * gate_sig
        hidden = (gate_act * up_proj).astype(jnp.bfloat16)
        mlp_out = lax.psum(plain_product(hidden, down_w).astype(jnp.bfloat16), "tensor").astype(
            jnp.float32
        )
        layer_rows = ((middle + BRANCH_SCALE * mlp_out) * live_mask).astype(jnp.bfloat16)
        grad_y = cotangent[slot_index].astype(jnp.float32) * live_mask
        grad_mlp = (BRANCH_SCALE * grad_y).astype(jnp.bfloat16)
        grad_down_w = row_product(hidden, grad_mlp)
        grad_hidden = col_product(grad_mlp, down_w)
        grad_gate_b = (
            grad_hidden * up_proj * gate_sig * (1.0 + gate_proj * (1.0 - gate_sig))
        ).astype(jnp.bfloat16)
        grad_up_b = (grad_hidden * gate_act).astype(jnp.bfloat16)
        grad_gate_w = row_product(second_in, grad_gate_b)
        grad_up_w = row_product(second_in, grad_up_b)
        grad_second = lax.psum(
            col_product(grad_gate_b, gate_w) + col_product(grad_up_b, up_w), "tensor"
        )
        grad_gain_two = jnp.sum(grad_second * normed_two, axis=0)
        grad_middle = grad_y + norm_back(grad_second, normed_two, inverse_two, gain_b)
        grad_attn = (BRANCH_SCALE * grad_middle).astype(jnp.bfloat16)
        grad_out_w = row_product(attend, grad_attn)
        grad_attend = (
            col_product(grad_attn, out_w).astype(jnp.bfloat16).reshape(row_count, local_heads, HD)
        )
        probs_new = jnp.exp(masked_scores(run_query_b, run_key_all, run_allowed) - log_total)
        grad_probs = jnp.einsum(
            "qhd,khd->hqk", grad_attend, value_all, preferred_element_type=jnp.float32
        )
        grad_scores = (
            probs_new * (grad_probs - jnp.sum(probs_new * grad_probs, axis=-1, keepdims=True))
        ).astype(jnp.bfloat16)
        grad_query_f = (
            jnp.einsum("hqk,khd->qhd", grad_scores, run_key_all, preferred_element_type=jnp.float32)
            * score_scale
        )
        grad_key_all = (
            jnp.einsum("hqk,qhd->khd", grad_scores, run_query_b, preferred_element_type=jnp.float32)
            * score_scale
        )
        grad_value_all = jnp.einsum(
            "hqk,qhd->khd",
            probs_new.astype(jnp.bfloat16),
            grad_attend,
            preferred_element_type=jnp.float32,
        )
        grad_key_own = lax.psum_scatter(
            grad_key_all.reshape(grad_key_all.shape[0], -1), "ctx", scatter_dimension=0, tiled=True
        )
        grad_value_own = lax.psum_scatter(
            grad_value_all.reshape(grad_value_all.shape[0], -1),
            "ctx",
            scatter_dimension=0,
            tiled=True,
        )
        grad_query_b = (
            rotate(grad_query_f, cos_own, sin_own, -1.0).astype(jnp.bfloat16).reshape(row_count, -1)
        )
        grad_key_b = (
            rotate(grad_key_own.reshape(row_count, local_heads, HD), cos_own, sin_own, -1.0)
            .astype(jnp.bfloat16)
            .reshape(row_count, -1)
        )
        grad_value_b = grad_value_own.astype(jnp.bfloat16)
        grad_query_w = row_product(first_in, grad_query_b)
        grad_key_w = row_product(first_in, grad_key_b)
        grad_value_w = row_product(first_in, grad_value_b)
        grad_first = lax.psum(
            (
                col_product(grad_query_b, query_w)
                + col_product(grad_key_b, key_w)
                + col_product(grad_value_b, value_w)
            ).astype(jnp.bfloat16),
            "tensor",
        ).astype(jnp.float32)
        grad_gain_one = jnp.sum(grad_first * normed_one, axis=0)
        grad_rows = grad_middle + norm_back(grad_first, normed_one, inverse_one, gain_a)
        slot_grads = (
            grad_gain_one,
            grad_query_w,
            grad_key_w,
            grad_value_w,
            grad_out_w,
            grad_gain_two,
            grad_gate_w,
            grad_up_w,
            grad_down_w,
        )
        layer_rows, grad_rows, slot_grads = (layer_rows, grad_rows, slot_grads)
        out_blocks.append(layer_rows)
        grad_blocks.append(grad_rows)
        if totals is None:
            totals = slot_grads
        else:
            totals = tuple(
                (left_val + right_val for left_val, right_val in zip(totals, slot_grads))
            )
    (
        sum_gain_one,
        sum_query,
        sum_key,
        sum_value,
        sum_out,
        sum_gain_two,
        sum_gate,
        sum_up,
        sum_down,
    ) = totals
    spread = (
        lax.psum_scatter(sum_gain_one, ("shard", "ctx"), scatter_dimension=0, tiled=True),
        lax.psum_scatter(sum_query, ("shard", "ctx"), scatter_dimension=0, tiled=True),
        lax.psum_scatter(sum_key, ("shard", "ctx"), scatter_dimension=0, tiled=True),
        lax.psum_scatter(sum_value, ("shard", "ctx"), scatter_dimension=0, tiled=True),
        lax.psum_scatter(sum_out, ("shard", "ctx"), scatter_dimension=1, tiled=True),
        lax.psum_scatter(sum_gain_two, ("shard", "ctx"), scatter_dimension=0, tiled=True),
        lax.psum_scatter(sum_gate, ("shard", "ctx"), scatter_dimension=0, tiled=True),
        lax.psum_scatter(sum_up, ("shard", "ctx"), scatter_dimension=0, tiled=True),
        lax.psum_scatter(sum_down, ("shard", "ctx"), scatter_dimension=1, tiled=True),
    )
    (
        part_gain_one,
        part_query,
        part_key,
        part_value,
        part_out,
        part_gain_two,
        part_gate,
        part_up,
        part_down,
    ) = spread
    final = (
        lax.all_gather(part_gain_one.astype(jnp.bfloat16), "ctx", axis=0, tiled=True).astype(
            part_gain_one.dtype
        ),
        lax.all_gather(part_query.astype(jnp.bfloat16), "ctx", axis=0, tiled=True).astype(
            part_query.dtype
        ),
        lax.all_gather(part_key.astype(jnp.bfloat16), "ctx", axis=0, tiled=True).astype(
            part_key.dtype
        ),
        lax.all_gather(part_value.astype(jnp.bfloat16), "ctx", axis=0, tiled=True).astype(
            part_value.dtype
        ),
        lax.all_gather(part_out.astype(jnp.bfloat16), "ctx", axis=1, tiled=True).astype(
            part_out.dtype
        ),
        lax.all_gather(part_gain_two.astype(jnp.bfloat16), "ctx", axis=0, tiled=True).astype(
            part_gain_two.dtype
        ),
        lax.all_gather(part_gate.astype(jnp.bfloat16), "ctx", axis=0, tiled=True).astype(
            part_gate.dtype
        ),
        lax.all_gather(part_up.astype(jnp.bfloat16), "ctx", axis=0, tiled=True).astype(
            part_up.dtype
        ),
        lax.all_gather(part_down.astype(jnp.bfloat16), "ctx", axis=1, tiled=True).astype(
            part_down.dtype
        ),
    )
    layer_out = jnp.stack(out_blocks, axis=0)
    grad_tokens = jnp.stack(grad_blocks, axis=0)
    return (
        layer_out,
        grad_tokens,
        final[0],
        final[1],
        final[2],
        final[3],
        final[4],
        final[5],
        final[6],
        final[7],
        final[8],
    )


def solution(mesh):
    placed = (
        P("shard", "ctx", None),
        P("shard"),
        P(),
        P("shard"),
        P("shard", "tensor"),
        P("shard", "tensor"),
        P("shard", "tensor"),
        P("tensor", "shard"),
        P("shard"),
        P("shard", "tensor"),
        P("shard", "tensor"),
        P("tensor", "shard"),
        P("shard", "ctx", None),
    )
    return jax.shard_map(
        local,
        mesh=mesh,
        in_specs=placed,
        out_specs=(
            P("shard", "ctx", None),
            P("shard", "ctx", None),
            P("shard"),
            P("shard", "tensor"),
            P("shard", "tensor"),
            P("shard", "tensor"),
            P("tensor", "shard"),
            P("shard"),
            P("shard", "tensor"),
            P("shard", "tensor"),
            P("tensor", "shard"),
        ),
        check_vma=False,
    )
```

profile of v0, /device:TPU:0, one launch (start us, length us, event | category | flops | bytes accessed | tf_op | source)
XLA Modules:
  0.0 3702.8 jit_solution(14417276845363161581)
XLA Ops:
  11.3 18.6 all-reduce.10
  33.7 40.8 %all-gather.23.cloned.1.call-done = bf16[2304,1152]{1,0:T(8,128)(2,1)} async-done(((bf16[576,1152]{1,0:T(8,128)(2,1)}), bf16[2304,1152]{1,0:T(8,128)(2,1)}) %all-gather.23.cloned.1.call-update) | async-done | bytes 5308432 | tf_op jit(solution)/shard_map/all_gather | solution.py:95
  74.5 8.5 copy.41
  83.1 55.2 %all-gather.25.cloned.1.call-done = bf16[2304,1152]{1,0:T(8,128)(2,1)} async-done(((bf16[576,1152]{1,0:T(8,128)(2,1)}), bf16[2304,1152]{1,0:T(8,128)(2,1)}) %all-gather.25.cloned.1.call-update) | async-done | bytes 5308432 | tf_op jit(solution)/shard_map/all_gather | solution.py:96
  138.2 8.5 copy.42
  159.7 42.3 %all-gather.19.cloned.1.call-done = bf16[2304,1152]{1,0:T(8,128)(2,1)} async-done(((bf16[576,1152]{1,0:T(8,128)(2,1)}), bf16[2304,1152]{1,0:T(8,128)(2,1)}) %all-gather.19.cloned.1.call-update) | async-done | bytes 5308432 | tf_op jit(solution)/shard_map/all_gather | solution.py:97
  216.9 37.7 %all-gather.39.cloned.1.call-done = bf16[1024,1152]{0,1:T(8,128)(2,1)} async-done(((bf16[256,1152]{0,1:T(8,128)(2,1)}), bf16[1024,1152]{0,1:T(8,128)(2,1)}) %all-gather.39.cloned.1.call-update) | async-done | bytes 2359312 | tf_op jit(solution)/shard_map/all_gather | solution.py:115
  254.5 10.1 fusion.118
  264.7 40.1 %all-gather.37.cloned.1.call-done = bf16[1024,1152]{1,0:T(8,128)(2,1)} async-done(((bf16[256,1152]{1,0:T(8,128)(2,1)}), bf16[1024,1152]{1,0:T(8,128)(2,1)}) %all-gather.37.cloned.1.call-update) | async-done | bytes 2359312 | tf_op jit(solution)/shard_map/all_gather | solution.py:116
  309.0 46.5 %all-gather.21.cloned.1.call-done = bf16[1024,1152]{1,0:T(8,128)(2,1)} async-done(((bf16[256,1152]{1,0:T(8,128)(2,1)}), bf16[1024,1152]{1,0:T(8,128)(2,1)}) %all-gather.21.cloned.1.call-update) | async-done | bytes 2359312 | tf_op jit(solution)/shard_map/all_gather | solution.py:116
  359.8 47.2 %all-gather.27.cloned.1.call-done = bf16[1024,1152]{0,1:T(8,128)(2,1)} async-done(((bf16[256,1152]{0,1:T(8,128)(2,1)}), bf16[1024,1152]{0,1:T(8,128)(2,1)}) %all-gather.27.cloned.1.call-update) | async-done | bytes 2359312 | tf_op jit(solution)/shard_map/all_gather | solution.py:115
  407.0 10.8 fusion.119
  417.8 9.4 fusion.1
  427.2 9.6 fusion
  436.9 10.9 fusion.58
  456.2 12.7 all-gather.29.cloned.1.call-done
  481.1 26.1 all-reduce.18.cloned.1.call-done
  513.1 127.5 %all-gather.31.cloned.1.call-done = bf16[2304,2880]{1,0:T(8,128)(2,1)} async-done(((bf16[576,2880]{1,0:T(8,128)(2,1)}), bf16[2304,2880]{1,0:T(8,128)(2,1)}) %all-gather.31.cloned.1.call-update) | async-done | bytes 13271056 | tf_op jit(solution)/shard_map/all_gather | solution.py:100
  640.6 11.8 fusion.124
  652.4 120.6 %all-gather.33.cloned.1.call-done = bf16[2304,2880]{1,0:T(8,128)(2,1)} async-done(((bf16[576,2880]{1,0:T(8,128)(2,1)}), bf16[2304,2880]{1,0:T(8,128)(2,1)}) %all-gather.33.cloned.1.call-update) | async-done | bytes 13271056 | tf_op jit(solution)/shard_map/all_gather | solution.py:101
  773.1 12.0 fusion.125
  785.0 13.3 fusion.121
  798.3 11.8 fusion.122
  810.1 95.2 %all-gather.35.cloned.1.call-done = bf16[2880,2304]{0,1:T(8,128)(2,1)} async-done(((bf16[2880,576]{0,1:T(8,128)(2,1)}), bf16[2880,2304]{0,1:T(8,128)(2,1)}) %all-gather.35.cloned.1.call-update) | async-done | bytes 13271056 | tf_op jit(solution)/shard_map/all_gather | solution.py:102
  905.4 15.7 multiply_convert_fusion.2
  921.0 10.7 fusion.128
  931.8 15.1 multiply_convert_fusion.4
  946.9 8.0 fusion.126
  954.9 10.4 convolution_add_fusion.7
  965.3 10.3 convolution_add_fusion.8
  976.3 28.4 all-reduce.16.cloned.1.call-done
  1017.0 17.0 multiply_reduce_fusion.1
  1034.0 13.0 multiply_convert_fusion.1
  1060.3 13.5 multiply_reduce_fusion
  1073.8 13.2 multiply_convert_fusion
  1092.2 10.5 fusion.6
  1103.5 10.6 fusion.4
  1139.5 87.9 %reduce-scatter.16.cloned.1.call-done = f32[256,1152]{0,1:T(8,128)} async-done(((f32[1024,1152]{0,1:T(8,128)}), f32[256,1152]{0,1:T(8,128)}) %reduce-scatter.16.cloned.1.call-update) | async-done | bytes 1179664 | tf_op jit(solution)/shard_map/reduce_scatter | solution.py:184
  1249.6 66.3 %reduce-scatter.14.cloned.1.call-done = f32[256,1152]{0,1:T(8,128)} async-done(((f32[1024,1152]{0,1:T(8,128)}), f32[256,1152]{0,1:T(8,128)}) %reduce-scatter.14.cloned.1.call-update) | async-done | bytes 1179664 | tf_op jit(solution)/shard_map/reduce_scatter | solution.py:187
  1315.9 7.0 fusion.79
  1323.0 81.5 %reduce-scatter.18.cloned.1.call-done = f32[256,1152]{0,1:T(8,128)} async-done(((f32[1024,1152]{0,1:T(8,128)}), f32[256,1152]{0,1:T(8,128)}) %reduce-scatter.18.cloned.1.call-update) | async-done | bytes 1179664 | tf_op jit(solution)/shard_map/reduce_scatter | solution.py:187
  1404.5 10.2 convolution_add_fusion.4
  1415.9 12.4 fusion.130
  1428.3 19.4 convolution_add_fusion.2
  1448.3 12.7 fusion.131
  1460.9 19.3 convolution_add_fusion.1
  1482.0 12.7 fusion.82
  1494.7 19.1 convolution_add_fusion
  1515.1 8.5 convolution_convert_fusion
  1523.7 9.3 convolution_convert_fusion.1
  1546.0 47.4 %reduce-scatter.26.cloned.1.call-done = f32[1152,144]{0,1:T(8,128)} async-done(((f32[1152,2304]{0,1:T(8,128)}), f32[1152,144]{0,1:T(8,128)}) %reduce-scatter.26.cloned.1.call-update) | async-done | bytes 663568 | tf_op jit(solution)/shard_map/reduce_scatter | solution.py:251
  1595.3 186.0 %reduce-scatter.20.cloned.1.call-done = f32[144,1152]{1,0:T(8,128)} async-done(((f32[2304,1152]{1,0:T(8,128)}), f32[144,1152]{1,0:T(8,128)}) %reduce-scatter.20.cloned.1.call-update) | async-done | bytes 663568 | tf_op jit(solution)/shard_map/reduce_scatter | solution.py:248
  1783.3 185.6 %reduce-scatter.22.cloned.1.call-done = f32[144,1152]{1,0:T(8,128)} async-done(((f32[2304,1152]{1,0:T(8,128)}), f32[144,1152]{1,0:T(8,128)}) %reduce-scatter.22.cloned.1.call-update) | async-done | bytes 663568 | tf_op jit(solution)/shard_map/reduce_scatter | solution.py:249
  1970.7 185.7 %reduce-scatter.24.cloned.1.call-done = f32[144,1152]{1,0:T(8,128)} async-done(((f32[2304,1152]{1,0:T(8,128)}), f32[144,1152]{1,0:T(8,128)}) %reduce-scatter.24.cloned.1.call-update) | async-done | bytes 663568 | tf_op jit(solution)/shard_map/reduce_scatter | solution.py:250
  2158.4 384.9 %reduce-scatter.28.cloned.1.call-done = f32[144,2880]{1,0:T(8,128)} async-done(((f32[2304,2880]{1,0:T(8,128)}), f32[144,2880]{1,0:T(8,128)}) %reduce-scatter.28.cloned.1.call-update) | async-done | bytes 1658896 | tf_op jit(solution)/shard_map/reduce_scatter | solution.py:253
  2545.8 384.0 %reduce-scatter.30.cloned.1.call-done = f32[144,2880]{1,0:T(8,128)} async-done(((f32[2304,2880]{1,0:T(8,128)}), f32[144,2880]{1,0:T(8,128)}) %reduce-scatter.30.cloned.1.call-update) | async-done | bytes 1658896 | tf_op jit(solution)/shard_map/reduce_scatter | solution.py:254
  2932.6 383.6 %reduce-scatter.32.cloned.1.call-done = f32[2880,144]{0,1:T(8,128)} async-done(((f32[2880,2304]{0,1:T(8,128)}), f32[2880,144]{0,1:T(8,128)}) %reduce-scatter.32.cloned.1.call-update) | async-done | bytes 1658896 | tf_op jit(solution)/shard_map/reduce_scatter | solution.py:255
  3321.9 26.6 all-reduce.20.cloned.1.call-done
  3352.9 80.1 %all-reduce.6 = (bf16[2304]{0:T(1024)(128)(2,1)}, bf16[2304]{0:T(1024)(128)(2,1)}) all-reduce(f32[2304]{0:T(1024)} %add.262, f32[2304]{0:T(1024)} %add.267), channel_id=6, replica_groups=mesh['shard'=4,'ctx'=4,'tensor'=2] {'shard','ctx'}, use_global_device_ids=true, to_apply=%region_28.29.clone | all-reduce | flops 4608 | bytes 27648
  3439.4 9.7 all-reduce.9
  3472.3 14.4 all-gather.45.cloned.1.call-done
  3489.7 65.6 %all-gather.49.cloned.1.call-done = bf16[576,2880]{1,0:T(8,128)(2,1)} async-done(((bf16[144,2880]{1,0:T(8,128)(2,1)}), bf16[576,2880]{1,0:T(8,128)(2,1)}) %all-gather.49.cloned.1.call-update) | async-done | bytes 3317776 | tf_op jit(solution)/shard_map/all_gather | solution.py:287
  3560.6 62.4 %all-gather.51.cloned.1.call-done = bf16[576,2880]{1,0:T(8,128)(2,1)} async-done(((bf16[144,2880]{1,0:T(8,128)(2,1)}), bf16[576,2880]{1,0:T(8,128)(2,1)}) %all-gather.51.cloned.1.call-update) | async-done | bytes 3317776 | tf_op jit(solution)/shard_map/all_gather | solution.py:290
  3628.4 62.4 %all-gather.53.cloned.1.call-done = bf16[2880,576]{0,1:T(8,128)(2,1)} async-done(((bf16[2880,144]{0,1:T(8,128)(2,1)}), bf16[2880,576]{0,1:T(8,128)(2,1)}) %all-gather.53.cloned.1.call-update) | async-done | bytes 3317776 | tf_op jit(solution)/shard_map/all_gather | solution.py:293
  (415 shorter events, 236.8 us)
Async XLA Ops:
  7.2 22.6 copy-start.98
  7.2 23.3 copy-start.100
  7.2 25.1 copy-start
  7.2 67.3 %all-gather.23.cloned.1.call-start = ((), (), s32[]{:S(2)}) async-start(), calls=%async_computation.13 | async-start | bytes 6635520 | tf_op jit(solution)/shard_map/all_gather | solution.py:95
  8.0 130.3 %all-gather.25.cloned.1.call-start = ((), (), s32[]{:S(2)}) async-start(), calls=%async_computation.14 | async-start | bytes 6635520 | tf_op jit(solution)/shard_map/all_gather | solution.py:96
  8.7 193.2 %all-gather.19.cloned.1.call-start = ((), (), s32[]{:S(2)}) async-start(), calls=%async_computation.11 | async-start | bytes 6635520 | tf_op jit(solution)/shard_map/all_gather | solution.py:97
  9.5 245.1 %all-gather.39.cloned.1.call-start = ((), (), s32[]{:S(2)}) async-start(), calls=%async_computation.21 | async-start | bytes 2949120 | tf_op jit(solution)/shard_map/all_gather | solution.py:115
  29.8 177.3 %copy-start.47 = (f32[2304]{0:T(1024)}, f32[2304]{0:T(1024)S(1)}, u32[]{:S(2)}) copy-start(f32[2304]{0:T(1024)S(1)} %convert_element_type.320) | copy-start | bytes 27652
  32.3 50.8 %copy-start.91 = (s32[256]{0:T(256)}, s32[256]{0:T(256)S(1)}, u32[]{:S(2)}) copy-start(s32[256]{0:T(256)S(1)} %get-tuple-element.38) | copy-start | bytes 3076
  32.9 122.4 %copy-start.81 = (f32[256]{0:T(256)}, f32[256]{0:T(256)S(1)}, u32[]{:S(2)}) copy-start(f32[256]{0:T(256)S(1)} %add_rsqrt_fusion.1) | copy-start | bytes 3076
  32.9 174.2 %copy-start.76 = (f32[256]{0:T(256)}, f32[256]{0:T(256)S(1)}, u32[]{:S(2)}) copy-start(f32[256]{0:T(256)S(1)} %add_rsqrt_fusion.3) | copy-start | bytes 3076
  158.6 95.9 %copy-start.33 = (bf16[256,18,32]{0,2,1:T(8,128)(2,1)}, bf16[256,18,32]{0,2,1:T(8,128)(2,1)S(1)}, u32[]{:S(2)}) copy-start(bf16[256,18,32]{0,2,1:T(8,128)(2,1)S(1)} %get-tuple-element.79) | copy-start | bytes 884740
  158.6 95.9 %copy-start.35 = (bf16[256,18,32]{0,2,1:T(8,128)(2,1)}, bf16[256,18,32]{0,2,1:T(8,128)(2,1)S(1)}, u32[]{:S(2)}) copy-start(bf16[256,18,32]{0,2,1:T(8,128)(2,1)S(1)} %get-tuple-element.80) | copy-start | bytes 884740
  158.6 248.3 %copy-start.37 = (bf16[256,18,32]{0,2,1:T(8,128)(2,1)}, bf16[256,18,32]{0,2,1:T(8,128)(2,1)S(1)}, u32[]{:S(2)}) copy-start(bf16[256,18,32]{0,2,1:T(8,128)(2,1)S(1)} %get-tuple-element.63) | copy-start | bytes 884740
  158.6 248.3 %copy-start.39 = (bf16[256,18,32]{0,2,1:T(8,128)(2,1)}, bf16[256,18,32]{0,2,1:T(8,128)(2,1)S(1)}, u32[]{:S(2)}) copy-start(bf16[256,18,32]{0,2,1:T(8,128)(2,1)S(1)} %get-tuple-element.64) | copy-start | bytes 884740
  159.6 145.1 %all-gather.37.cloned.1.call-start = ((), (), s32[]{:S(2)}) async-start(), calls=%async_computation.20 | async-start | bytes 2949120 | tf_op jit(solution)/shard_map/all_gather | solution.py:116
  207.1 148.4 %all-gather.21.cloned.1.call-start = ((), (), s32[]{:S(2)}) async-start(), calls=%async_computation.12 | async-start | bytes 2949120 | tf_op jit(solution)/shard_map/all_gather | solution.py:116
  212.2 194.7 %all-gather.27.cloned.1.call-start = ((), (), s32[]{:S(2)}) async-start(), calls=%async_computation.15 | async-start | bytes 2949120 | tf_op jit(solution)/shard_map/all_gather | solution.py:115
  214.2 254.6 %all-gather.29.cloned.1.call-start = ((), (), s32[]{:S(2)}) async-start(), calls=%async_computation.16 | async-start | bytes 6635520 | tf_op jit(solution)/shard_map/all_gather | solution.py:98
  215.0 292.2 %all-reduce.18.cloned.1.call-start = ((), (), s32[]{:S(2)}) async-start(), calls=%async_computation.41 | async-start | bytes 9437184 | tf_op jit(solution)/shard_map/psum | solution.py:130
  264.7 153.1 %copy-start.67 = (f32[18,256]{1,0:T(8,128)}, f32[18,256]{1,0:T(8,128)S(1)}, u32[]{:S(2)}) copy-start(f32[18,256]{1,0:T(8,128)S(1)} %get-tuple-element.96) | copy-start | bytes 55300
  427.2 20.5 slice-start
  478.0 162.6 %all-gather.31.cloned.1.call-start = ((), (), s32[]{:S(2)}) async-start(), calls=%async_computation.17 | async-start | bytes 16957440 | tf_op jit(solution)/shard_map/all_gather | solution.py:100
  478.6 294.4 %all-gather.33.cloned.1.call-start = ((), (), s32[]{:S(2)}) async-start(), calls=%async_computation.18 | async-start | bytes 16957440 | tf_op jit(solution)/shard_map/all_gather | solution.py:101
  479.4 27.8 copy-start.1
  479.4 426.0 %all-gather.35.cloned.1.call-start = ((), (), s32[]{:S(2)}) async-start(), calls=%async_computation.19 | async-start | bytes 16957440 | tf_op jit(solution)/shard_map/all_gather | solution.py:102
  480.0 524.7 %all-reduce.16.cloned.1.call-start = ((), (), s32[]{:S(2)}) async-start(), calls=%async_computation.40 | async-start | bytes 9437184 | tf_op jit(solution)/shard_map/psum | solution.py:153
  481.1 528.6 %copy-start.87 = (f32[256]{0:T(256)}, f32[256]{0:T(256)S(1)}, u32[]{:S(2)}) copy-start(f32[256]{0:T(256)S(1)} %compare_convert_fusion) | copy-start | bytes 3076
  513.1 260.0 %copy-start.14 = (bf16[256,2304]{1,0:T(8,128)(2,1)}, bf16[256,2304]{1,0:T(8,128)(2,1)S(1)}, u32[]{:S(2)}) copy-start(bf16[256,2304]{1,0:T(8,128)(2,1)S(1)} %get-tuple-element.86) | copy-start | bytes 3538948
  513.1 285.2 %copy-start.16 = (bf16[256,2304]{1,0:T(8,128)(2,1)}, bf16[256,2304]{1,0:T(8,128)(2,1)S(1)}, u32[]{:S(2)}) copy-start(bf16[256,2304]{1,0:T(8,128)(2,1)S(1)} %get-tuple-element.85) | copy-start | bytes 3538948
  975.6 29.1 copy-start.7
  975.6 163.9 %reduce-scatter.12.cloned.1.call-start = ((), (), s32[]{:S(2)}) async-start(), calls=%async_computation.22 | async-start | bytes 5898240 | tf_op jit(solution)/shard_map/reduce_scatter | solution.py:184
  1017.0 17.1 copy-start.62
  1052.1 175.2 %reduce-scatter.16.cloned.1.call-start = ((), (), s32[]{:S(2)}) async-start(), calls=%async_computation.24 | async-start | bytes 5898240 | tf_op jit(solution)/shard_map/reduce_scatter | solution.py:184
  1060.3 13.5 copy-start.63
  1092.2 223.7 %reduce-scatter.14.cloned.1.call-start = ((), (), s32[]{:S(2)}) async-start(), calls=%async_computation.23 | async-start | bytes 5898240 | tf_op jit(solution)/shard_map/reduce_scatter | solution.py:187
  1102.8 301.7 %reduce-scatter.18.cloned.1.call-start = ((), (), s32[]{:S(2)}) async-start(), calls=%async_computation.25 | async-start | bytes 5898240 | tf_op jit(solution)/shard_map/reduce_scatter | solution.py:187
  1114.1 479.3 %reduce-scatter.26.cloned.1.call-start = ((), (), s32[]{:S(2)}) async-start(), calls=%async_computation.32 | async-start | bytes 11280384 | tf_op jit(solution)/shard_map/reduce_scatter | solution.py:251
  1124.3 657.0 %reduce-scatter.20.cloned.1.call-start = ((), (), s32[]{:S(2)}) async-start(), calls=%async_computation.26 | async-start | bytes 11280384 | tf_op jit(solution)/shard_map/reduce_scatter | solution.py:248
  1132.8 94.6 %copy-start.66 = (f32[256,32]{0,1:T(8,128)S(1)}, f32[256,32]{0,1:T(8,128)}, u32[]{:S(2)}) copy-start(f32[256,32]{0,1:T(8,128)} %get-tuple-element.91) | copy-start | bytes 98308
  1132.8 94.6 %copy-start.72 = (f32[256,32]{0,1:T(8,128)S(1)}, f32[256,32]{0,1:T(8,128)}, u32[]{:S(2)}) copy-start(f32[256,32]{0,1:T(8,128)} %get-tuple-element.89) | copy-start | bytes 98308
  1240.6 728.3 %reduce-scatter.22.cloned.1.call-start = ((), (), s32[]{:S(2)}) async-start(), calls=%async_computation.28 | async-start | bytes 11280384 | tf_op jit(solution)/shard_map/reduce_scatter | solution.py:249
  1249.6 906.9 %reduce-scatter.24.cloned.1.call-start = ((), (), s32[]{:S(2)}) async-start(), calls=%async_computation.30 | async-start | bytes 11280384 | tf_op jit(solution)/shard_map/reduce_scatter | solution.py:250
  1414.7 13.7 copy-start.15
  1414.7 1128.6 %reduce-scatter.28.cloned.1.call-start = ((), (), s32[]{:S(2)}) async-start(), calls=%async_computation.34 | async-start | bytes 28827648 | tf_op jit(solution)/shard_map/reduce_scatter | solution.py:253
  1447.8 1482.0 %reduce-scatter.30.cloned.1.call-start = ((), (), s32[]{:S(2)}) async-start(), calls=%async_computation.36 | async-start | bytes 28827648 | tf_op jit(solution)/shard_map/reduce_scatter | solution.py:254
  1480.3 1836.0 %reduce-scatter.32.cloned.1.call-start = ((), (), s32[]{:S(2)}) async-start(), calls=%async_computation.38 | async-start | bytes 28827648 | tf_op jit(solution)/shard_map/reduce_scatter | solution.py:255
  1513.8 1834.7 %all-reduce.20.cloned.1.call-start = ((), (), s32[]{:S(2)}) async-start(), calls=%async_computation.42 | async-start | bytes 9437184 | tf_op jit(solution)/shard_map/psum | solution.py:139
  1515.1 17.8 slice-start.7
  1545.9 1917.3 %all-gather.47.cloned.1.call-start = ((), (), s32[]{:S(2)}) async-start(), calls=%async_computation.33 | async-start | bytes 1658880 | tf_op jit(solution)/shard_map/all_gather | solution.py:281
  1595.3 1871.0 %all-gather.41.cloned.1.call-start = ((), (), s32[]{:S(2)}) async-start(), calls=%async_computation.27 | async-start | bytes 1658880 | tf_op jit(solution)/shard_map/all_gather | solution.py:272
  1783.2 1686.1 %all-gather.43.cloned.1.call-start = ((), (), s32[]{:S(2)}) async-start(), calls=%async_computation.29 | async-start | bytes 1658880 | tf_op jit(solution)/shard_map/all_gather | solution.py:275
  1970.7 1516.0 %all-gather.45.cloned.1.call-start = ((), (), s32[]{:S(2)}) async-start(), calls=%async_computation.31 | async-start | bytes 1658880 | tf_op jit(solution)/shard_map/all_gather | solution.py:278
  2158.3 1397.0 %all-gather.49.cloned.1.call-start = ((), (), s32[]{:S(2)}) async-start(), calls=%async_computation.35 | async-start | bytes 4239360 | tf_op jit(solution)/shard_map/all_gather | solution.py:287
  2545.8 1077.3 %all-gather.51.cloned.1.call-start = ((), (), s32[]{:S(2)}) async-start(), calls=%async_computation.37 | async-start | bytes 4239360 | tf_op jit(solution)/shard_map/all_gather | solution.py:290
  2932.3 386.5 %copy-start.102 = (u32[32]{0:T(128)S(1)}, u32[32]{0:T(128)}, u32[]{:S(2)}) copy-start(u32[32]{0:T(128)} %constant.64) | copy-start | bytes 388
  2932.3 387.1 %copy-start.101 = (u32[32]{0:T(128)S(1)}, u32[32]{0:T(128)}, u32[]{:S(2)}) copy-start(u32[32]{0:T(128)} %constant.78) | copy-start | bytes 388
  2932.3 389.0 %copy-start.79 = (f32[2304]{0:T(1024)S(1)}, f32[2304]{0:T(1024)}, u32[]{:S(2)}) copy-start(f32[2304]{0:T(1024)} %get-tuple-element.13) | copy-start | bytes 27652
  2932.3 389.0 %copy-start.80 = (f32[2304]{0:T(1024)S(1)}, f32[2304]{0:T(1024)}, u32[]{:S(2)}) copy-start(f32[2304]{0:T(1024)} %get-tuple-element.84) | copy-start | bytes 27652
  2932.3 416.2 %copy-start.3 = (bf16[2,256,2304]{2,1,0:T(8,128)(2,1)S(1)}, bf16[2,256,2304]{2,1,0:T(8,128)(2,1)}, u32[]{:S(2)}) copy-start(bf16[2,256,2304]{2,1,0:T(8,128)(2,1)} %param.13) | copy-start | bytes 7077892
  2932.3 416.2 %copy-start.49 = (f32[2304]{0:T(1024)S(1)}, f32[2304]{0:T(1024)}, u32[]{:S(2)}) copy-start(f32[2304]{0:T(1024)} %copy-done.47) | copy-start | bytes 27652
  2932.3 416.2 %copy-start.78 = (f32[256]{0:T(256)S(1)}, f32[256]{0:T(256)}, u32[]{:S(2)}) copy-start(f32[256]{0:T(256)} %copy-done.76) | copy-start | bytes 3076
  2932.3 758.4 %all-gather.53.cloned.1.call-start = ((), (), s32[]{:S(2)}) async-start(), calls=%async_computation.39 | async-start | bytes 4239360 | tf_op jit(solution)/shard_map/all_gather | solution.py:293
  3348.5 103.8 %copy-start.57 = (bf16[256,2304]{1,0:T(8,128)(2,1)S(1)}, bf16[256,2304]{1,0:T(8,128)(2,1)}, u32[]{:S(2)}) copy-start(bf16[256,2304]{1,0:T(8,128)(2,1)} %get-tuple-element.33) | copy-start | bytes 3538948
  (88 other events, 429.2 us)
Sparse Core Ops, SparseCore 0:
  9.9 64.6 all-gather.22
  76.4 61.8 all-gather.24
  140.1 61.8 all-gather.18
  204.0 50.5 all-gather.38
  256.5 48.1 all-gather.36
  306.7 48.7 all-gather.20
  357.6 49.2 all-gather.26
  408.8 60.0 all-gather.28
  478.2 28.9 all-reduce.17
  508.8 131.7 all-gather.30
  642.5 130.5 all-gather.32
  774.8 130.5 all-gather.34
  975.7 28.9 all-reduce.15
  1052.3 86.4 reduce-scatter.11
  1141.5 85.7 reduce-scatter.15
  1230.1 85.7 reduce-scatter.13
  1318.6 85.7 reduce-scatter.17
  1410.2 183.1 reduce-scatter.25
  1599.2 182.0 reduce-scatter.19
  1787.0 181.7 reduce-scatter.21
  1974.6 181.7 reduce-scatter.23
  2162.4 380.8 reduce-scatter.27
  2549.3 380.5 reduce-scatter.29
  2935.7 380.5 reduce-scatter.31
  3320.2 28.3 all-reduce.19
  3350.0 34.8 all-gather.46
  3386.8 32.8 all-gather.40
  3421.3 32.0 all-gather.42
  3454.9 31.7 all-gather.44
  3488.7 66.5 all-gather.48
  3556.9 66.0 all-gather.50
  3624.6 66.0 all-gather.52
where the time goes:
time: 3710 us; the launch traced here: 3700 us
  waiting for transfers between devices  2950 us (80%)
  matrix products  435 us (12%)
  other arithmetic  131 us (4%)
  blocking collectives  108 us (3%)
  local copies, waits for them, and re-layouts  58 us (2%)
    reduce_scatter x1, waiting for transfers between devices, local(): lax.psum_scatter(sum_gate, ('shard', 'ctx'), scatter_dimension=0, tiled=T...  385 us
    reduce_scatter x1, waiting for transfers between devices, local(): lax.psum_scatter(sum_up, ('shard', 'ctx'), scatter_dimension=0, tiled=True)  384 us
    reduce_scatter x1, waiting for transfers between devices, local(): lax.psum_scatter(sum_down, ('shard', 'ctx'), scatter_dimension=1, tiled=T...  384 us
    reduce_scatter x1, waiting for transfers between devices, local(): lax.psum_scatter(sum_query, ('shard', 'ctx'), scatter_dimension=0, tiled=...  186 us
    reduce_scatter x1, waiting for transfers between devices, local(): lax.psum_scatter(sum_value, ('shard', 'ctx'), scatter_dimension=0, tiled=...  186 us
    reduce_scatter x1, waiting for transfers between devices, local(): lax.psum_scatter(sum_key, ('shard', 'ctx'), scatter_dimension=0, tiled=True)  186 us
    reduce_scatter x2, waiting for transfers between devices, local(): lax.psum_scatter(grad_value_all.reshape(grad_value_all.shape[0], -1), 'ct...  148 us
    dot_general x14, matrix products, row_product(): lax.dot_general(left_mat, right_mat, CONTRACT_ROWS, preferred_element_typ...  137 us
  transfers between devices with their start and end apart: 32, of which 28 were waited for; matrix products, arithmetic and copies ran while one was open for 13% of the time, Pallas kernels for 0%

commit v1 on v0

--- a/solution.py
+++ b/solution.py
@@ -1,3 +1,4 @@
+import functools
 import math
 
 import jax
@@ -54,7 +55,7 @@
     return inverse * (scaled - normed * jnp.mean(scaled * normed, axis=-1, keepdims=True))
 
 
-def local(
+def gather_all(
     tokens,
     lengths,
     span_order,
@@ -311,6 +312,287 @@
     )
 
 
+def swap_pairs():
+    return [(0, 1), (1, 0)]
+
+
+def line_gather(block, axis, size):
+    place = lax.axis_index(axis)
+    ups = [block]
+    downs = [block]
+    for step in range(1, size):
+        ups.append(lax.ppermute(ups[-1], axis, [(i, i + 1) for i in range(step - 1, size - 1)]))
+        downs.append(lax.ppermute(downs[-1], axis, [(i, i - 1) for i in range(1, size - step + 1)]))
+    return [block] + [
+        jnp.where(place >= step, ups[step], downs[size - step]) for step in range(1, size)
+    ]
+
+
+def line_scatter(parts, axis, size):
+    up = None
+    down = None
+    for step in range(1, size):
+        up_part = parts[step]
+        down_part = parts[size - step]
+        if up is not None:
+            up_part = (up_part.astype(jnp.float32) + up.astype(jnp.float32)).astype(jnp.bfloat16)
+            down_part = (down_part.astype(jnp.float32) + down.astype(jnp.float32)).astype(
+                jnp.bfloat16
+            )
+        up = lax.ppermute(up_part, axis, [(i, i + 1) for i in range(min(step, size - 1))])
+        down = lax.ppermute(down_part, axis, [(i, i - 1) for i in range(max(size - step, 1), size)])
+    return parts[0].astype(jnp.float32) + up.astype(jnp.float32) + down.astype(jnp.float32)
+
+
+def column_split(
+    shape,
+    tokens,
+    lengths,
+    span_order,
+    attn_gain,
+    w_query,
+    w_key,
+    w_value,
+    w_out,
+    mlp_gain,
+    w_gate,
+    w_up,
+    w_down,
+    cotangent,
+):
+    shards, lines, cores = shape["shard"], shape["ctx"], shape["tensor"]
+    line = lax.axis_index("ctx")
+    core = lax.axis_index("tensor")
+    per_half = lines // cores
+    owner = core == line // per_half
+    sub = line % per_half
+    slot_count, row_count, width = tokens.shape
+    all_rows = row_count * lines
+    heads = w_query.shape[1] * cores // lines // HD
+    head_cols = heads * HD
+    unit_cols = w_gate.shape[1] * cores // lines
+
+    def column_piece(weights):
+        cut = [
+            lax.dynamic_slice_in_dim(w, sub * (w.shape[1] // per_half), w.shape[1] // per_half, 1)
+            for w in weights
+        ]
+        return jnp.concatenate(cut, axis=1) if len(cut) > 1 else cut[0]
+
+    def row_piece(w):
+        return lax.dynamic_slice_in_dim(w, sub * (w.shape[0] // per_half), w.shape[0] // per_half, 0)
+
+    def to_pair(piece):
+        rows = piece.shape[0] // cores
+        keep = lax.dynamic_slice_in_dim(piece, core * rows, rows, 0)
+        give = lax.dynamic_slice_in_dim(piece, (1 - core) * rows, rows, 0)
+        got = lax.ppermute(give, "tensor", swap_pairs())
+        return jnp.where(owner, keep, got)
+
+    def gather_columns(weights):
+        return lax.all_gather(to_pair(column_piece(weights)), ("shard", "tensor"), axis=0, tiled=True)
+
+    def gather_rows(w):
+        mine = to_pair(row_piece(w))
+        got = lax.all_gather(mine, ("shard", "tensor"), axis=0, tiled=True)
+        got = got.reshape(shards, cores * mine.shape[0], mine.shape[1])
+        return jnp.transpose(got, (1, 0, 2)).reshape(cores * mine.shape[0], -1)
+
+    def spread(piece):
+        got = lax.all_gather(piece, ("ctx", "tensor"), axis=0, tiled=True)
+        got = got.reshape(lines, cores, piece.shape[0], piece.shape[1])
+        return lax.dynamic_slice_in_dim(got, core * per_half, per_half, 0)
+
+    def reduce_columns(grad, count):
+        piece = lax.psum_scatter(
+            grad.astype(jnp.bfloat16), ("shard", "tensor"), scatter_dimension=0, tiled=True
+        )
+        got = spread(piece).astype(jnp.float32)
+        each = grad.shape[1] // count
+        return [
+            jnp.transpose(got[..., k * each : (k + 1) * each], (1, 2, 0, 3)).reshape(
+                width // shards, per_half * each
+            )
+            for k in range(count)
+        ]
+
+    def reduce_rows(grad):
+        rows = grad.shape[0]
+        grad = grad.astype(jnp.bfloat16).reshape(rows, shards, width // shards)
+        grad = jnp.transpose(grad, (1, 0, 2)).reshape(shards * rows, width // shards)
+        piece = lax.psum_scatter(grad, ("shard", "tensor"), scatter_dimension=0, tiled=True)
+        return spread(piece).astype(jnp.float32).reshape(per_half * rows, width // shards)
+
+    def line_all(block):
+        return jnp.concatenate(line_gather(block, "ctx", lines), axis=0)
+
+    def line_sum(partial):
+        partial = partial.astype(jnp.bfloat16)
+        parts = [partial[k * row_count : (k + 1) * row_count] for k in range(lines)]
+        return line_scatter(parts, "ctx", lines)
+
+    length = lengths[core]
+    offsets = jnp.arange(row_count // 2, dtype=jnp.int32)
+    stored_pos = (span_order[:, None] * (row_count // 2) + offsets[None, :]).reshape(lines, row_count)
+    ring_pos = stored_pos[(line - jnp.arange(lines)) % lines].reshape(-1)
+    own_pos = ring_pos[:row_count]
+    cos_all, sin_all = rope_tables(ring_pos, HD)
+    live_all = (ring_pos < length).astype(jnp.float32)[:, None]
+    live_own = live_all[:row_count]
+    allowed = (ring_pos[None, :] <= ring_pos[:, None]) & (ring_pos < length)[None, :]
+    score_scale = HD ** (-0.5)
+
+    gains = lax.all_gather(jnp.stack([attn_gain, mlp_gain]), "shard", axis=1, tiled=True)
+    gain_a = gains[0].astype(jnp.float32)
+    gain_b = gains[1].astype(jnp.float32)
+    own_tokens = lax.dynamic_index_in_dim(tokens, core, 0, keepdims=False)
+    own_cot = lax.dynamic_index_in_dim(cotangent, core, 0, keepdims=False)
+
+    all_tokens = line_all(own_tokens)
+    qkv_w = gather_columns([w_query, w_key, w_value])
+    out_w = gather_rows(w_out)
+    gate_up_w = gather_columns([w_gate, w_up])
+    down_w = gather_rows(w_down)
+
+    first_in = (norm_parts(all_tokens.astype(jnp.float32))[0] * gain_a).astype(jnp.bfloat16)
+    qkv = plain_product(first_in, qkv_w)
+    as_heads = lambda v: v.reshape(all_rows, heads, HD)
+    query_b = rotate(as_heads(qkv[:, :head_cols]), cos_all, sin_all, 1.0).astype(jnp.bfloat16)
+    key_b = rotate(as_heads(qkv[:, head_cols : 2 * head_cols]), cos_all, sin_all, 1.0).astype(
+        jnp.bfloat16
+    )
+    value_b = as_heads(qkv[:, 2 * head_cols :]).astype(jnp.bfloat16)
+
+    def masked_scores():
+        raw_scores = (
+            jnp.einsum("qhd,khd->hqk", query_b, key_b, preferred_element_type=jnp.float32)
+            * score_scale
+        )
+        return jnp.where(allowed[None], raw_scores, -1e30)
+
+    scores = masked_scores()
+    row_top = jnp.max(scores, axis=-1, keepdims=True)
+    weights = jnp.exp(scores - row_top)
+    row_total = jnp.sum(weights, axis=-1, keepdims=True)
+    log_total = row_top + jnp.log(row_total)
+    probs_low = (weights / row_total).astype(jnp.bfloat16)
+    attend = (
+        jnp.einsum("hqk,khd->qhd", probs_low, value_b, preferred_element_type=jnp.float32)
+        .astype(jnp.bfloat16)
+        .reshape(all_rows, head_cols)
+    )
+    own_x = own_tokens.astype(jnp.float32)
+    middle = own_x + BRANCH_SCALE * line_sum(plain_product(attend, out_w))
+    normed_two, inverse_two = norm_parts(middle)
+    second_in = line_all((normed_two * gain_b).astype(jnp.bfloat16))
+    all_cot = line_all(own_cot).astype(jnp.float32) * live_all
+    grad_mlp = (BRANCH_SCALE * all_cot).astype(jnp.bfloat16)
+
+    gate_up = plain_product(second_in, gate_up_w)
+    gate_proj = gate_up[:, :unit_cols]
+    up_proj = gate_up[:, unit_cols:]
+    gate_sig = jax.nn.sigmoid(gate_proj)
+    gate_act = gate_proj * gate_sig
+    hidden = (gate_act * up_proj).astype(jnp.bfloat16)
+    grad_hidden = col_product(grad_mlp, down_w)
+    grad_gate_b = (
+        grad_hidden * up_proj * gate_sig * (1.0 + gate_proj * (1.0 - gate_sig))
+    ).astype(jnp.bfloat16)
+    grad_up_b = (grad_hidden * gate_act).astype(jnp.bfloat16)
+    grad_gate_up = jnp.concatenate([grad_gate_b, grad_up_b], axis=1)
+    grad_second = line_sum(col_product(grad_gate_up, gate_up_w))
+    mlp_out = line_sum(plain_product(hidden, down_w))
+    layer_rows = ((middle + BRANCH_SCALE * mlp_out) * live_own).astype(jnp.bfloat16)
+    own_dy = own_cot.astype(jnp.float32) * live_own
+    grad_gain_two = jnp.sum(grad_second * normed_two, axis=0)
+    grad_middle = own_dy + norm_back(grad_second, normed_two, inverse_two, gain_b)
+    grad_attn = line_all((BRANCH_SCALE * grad_middle).astype(jnp.bfloat16))
+
+    final_down = reduce_rows(row_product(hidden, grad_mlp))
+    final_gate, final_up = reduce_columns(row_product(second_in, grad_gate_up), 2)
+
+    grad_attend = col_product(grad_attn, out_w).astype(jnp.bfloat16).reshape(all_rows, heads, HD)
+    final_out = reduce_rows(row_product(attend, grad_attn))
+    probs_new = jnp.exp(masked_scores() - log_total)
+    grad_probs = jnp.einsum("qhd,khd->hqk", grad_attend, value_b, preferred_element_type=jnp.float32)
+    grad_scores = (
+        probs_new * (grad_probs - jnp.sum(probs_new * grad_probs, axis=-1, keepdims=True))
+    ).astype(jnp.bfloat16)
+    grad_query_f = (
+        jnp.einsum("hqk,khd->qhd", grad_scores, key_b, preferred_element_type=jnp.float32)
+        * score_scale
+    )
+    grad_key_f = (
+        jnp.einsum("hqk,qhd->khd", grad_scores, query_b, preferred_element_type=jnp.float32)
+        * score_scale
+    )
+    grad_value_f = jnp.einsum(
+        "hqk,qhd->khd",
+        probs_new.astype(jnp.bfloat16),
+        grad_attend,
+        preferred_element_type=jnp.float32,
+    )
+    as_columns = lambda v: v.astype(jnp.bfloat16).reshape(all_rows, head_cols)
+    grad_qkv = jnp.concatenate(
+        [
+            as_columns(rotate(grad_query_f, cos_all, sin_all, -1.0)),
+            as_columns(rotate(grad_key_f, cos_all, sin_all, -1.0)),
+            as_columns(grad_value_f),
+        ],
+        axis=1,
+    )
+    grad_first = line_sum(col_product(grad_qkv, qkv_w))
+    final_query, final_key, final_value = reduce_columns(row_product(first_in, grad_qkv), 3)
+    normed_one, inverse_one = norm_parts(own_x)
+    grad_gain_one = jnp.sum(grad_first * normed_one, axis=0)
+    grad_rows = grad_middle + norm_back(grad_first, normed_one, inverse_one, gain_a)
+
+    gain_sums = lax.psum(
+        jnp.stack([grad_gain_one, grad_gain_two]), ("shard", "ctx", "tensor")
+    )
+    gain_sums = lax.dynamic_slice_in_dim(
+        gain_sums, lax.axis_index("shard") * (width // shards), width // shards, 1
+    )
+
+    def both_slots(own):
+        other = lax.ppermute(own, "tensor", swap_pairs())
+        return jnp.stack(
+            [jnp.where(core == 0, own, other), jnp.where(core == 0, other, own)], axis=0
+        )
+
+    layer_out = both_slots(layer_rows)
+    grad_tokens = both_slots(grad_rows.astype(jnp.bfloat16)).astype(jnp.float32)
+    return (
+        layer_out,
+        grad_tokens,
+        gain_sums[0],
+        final_query,
+        final_key,
+        final_value,
+        final_out,
+        gain_sums[1],
+        final_gate,
+        final_up,
+        final_down,
+    )
+
+
+def local(shape, *arrays):
+    shards, lines, cores = shape["shard"], shape["ctx"], shape["tensor"]
+    tokens, w_query, w_gate = arrays[0], arrays[4], arrays[9]
+    fits = (
+        cores == 2
+        and tokens.shape[0] == cores
+        and lines % cores == 0
+        and (w_query.shape[1] * cores) % (lines * HD) == 0
+        and (w_gate.shape[1] * cores) % (lines * cores) == 0
+        and w_query.shape[0] % cores == 0
+    )
+    if fits:
+        return column_split(shape, *arrays)
+    return gather_all(*arrays)
+
+
 def solution(mesh):
     placed = (
         P("shard", "ctx", None),
@@ -328,7 +610,7 @@
         P("shard", "ctx", None),
     )
     return jax.shard_map(
-        local,
+        functools.partial(local, dict(mesh.shape)),
         mesh=mesh,
         in_specs=placed,
         out_specs=(

time: 3710 us -> 1540 us (0.42)
  waiting for transfers between devices: 2950 us -> 708 us
  matrix products: 435 us -> 269 us
  starting transfers between devices: 2.89 us -> 158 us
  local copies, waits for them, and re-layouts: 58 us -> 205 us
  blocking collectives: 108 us -> 47.2 us
    reduce_scatter x11 -> x3, waiting for transfers between devices: 1990 us -> 151 us  [the longest x2 151 us: reduce_columns(): lax.psum_scatter(grad.astype(jnp.bfloat16), ('shard', 'tensor'), scatter_...]
    all_gather x18 -> x8, waiting for transfers between devices: 871 us -> 25.9 us  [the longest x4 25.9 us: spread(): got = lax.all_gather(piece, ('ctx', 'tensor'), axis=0, tiled=True)]
    ppermute x0 -> x54, waiting for transfers between devices: none -> 530 us  [the longest x12 296 us: line_scatter(): lax.ppermute(up_part, axis, [(i, i + 1) for i in range(min(step, size - 1...]
    ppermute x0 -> x54, starting transfers between devices: none -> 157 us  [the longest x12 88.1 us: line_scatter(): lax.ppermute(up_part, axis, [(i, i + 1) for i in range(min(step, size - 1...]
    unnamed x3 -> x0, blocking collectives: 108 us -> none
    dot_general x14 -> x4, matrix products: 137 us -> 49.5 us  [row_product(): lax.dot_general(left_mat, right_mat, CONTRACT_ROWS, preferred_element_typ...]
    psum x3 -> x0, waiting for transfers between devices: 81.2 us -> none  [the longest x1 28.4 us: local(): lax.psum(col_product(grad_gate_b, gate_w) + col_product(grad_up_b, up_w),...]
    reshape x0 -> x10, local copies, waits for them, and re-layouts: none -> 72.9 us  [the longest x5 35.2 us: reduce_columns(): jnp.transpose(got[..., k * each:(k + 1) * each], (1, 2, 0, 3))]
  transfers between devices with their start and end apart: 32 -> 66, of which waited for: 28 -> 28; matrix products, arithmetic and copies ran while one was open for 13% -> 29% of each run, Pallas kernels for 0% -> 0%
where the time goes in v1:
time: 1540 us; the launch traced here: 1530 us
  waiting for transfers between devices  708 us (46%)
  matrix products  269 us (17%)
  local copies, waits for them, and re-layouts  205 us (13%)
  starting transfers between devices  158 us (10%)
  other arithmetic  126 us (8%)
  blocking collectives  47.2 us (3%)
  between operations  16.4 us (1%)
    ppermute x12, waiting for transfers between devices, line_scatter(): lax.ppermute(up_part, axis, [(i, i + 1) for i in range(min(step, size - 1...  296 us
    ppermute x12, waiting for transfers between devices, line_gather(): lax.ppermute(downs[-1], axis, [(i, i - 1) for i in range(1, size - step +...  183 us
    reduce_scatter x2, waiting for transfers between devices, reduce_columns(): lax.psum_scatter(grad.astype(jnp.bfloat16), ('shard', 'tensor'), scatter_...  151 us
    ppermute x12, starting transfers between devices, line_scatter(): lax.ppermute(up_part, axis, [(i, i + 1) for i in range(min(step, size - 1...  88.1 us
    dot_general x4, matrix products, plain_product(): return jnp.dot(left_mat, right_mat, preferred_element_type=jnp.float32)  63.8 us
    dot_general x4, matrix products, col_product(): lax.dot_general(left_mat, right_mat, CONTRACT_COLS, preferred_element_typ...  57.5 us
    transpose x7, local copies, waits for them, and re-layouts, reduce_columns(): jnp.transpose(got[..., k * each:(k + 1) * each], (1, 2, 0, 3))  53.7 us
    dot_general x4, matrix products, row_product(): lax.dot_general(left_mat, right_mat, CONTRACT_ROWS, preferred_element_typ...  49.5 us
  transfers between devices with their start and end apart: 66, of which 28 were waited for; matrix products, arithmetic and copies ran while one was open for 29% of the time, Pallas kernels for 0%

profile of v1, /device:TPU:0, one launch (start us, length us, event | category | flops | bytes accessed | tf_op | source)
XLA Modules:
  0.0 1528.8 jit_solution(12920696174153049118)
XLA Ops:
  36.3 6.2 collective-permute-start
  48.9 8.7 all-gather
  57.9 8.2 collective-permute-done.1
  74.3 21.5 %collective-permute-done.2 = bf16[256,2304]{1,0:T(8,128)(2,1)} collective-permute-done((bf16[256,2304]{1,0:T(8,128)(2,1)S(1)}, bf16[256,2304]{1,0:T(8,128)(2,1)}, u32[]{:S(2)}, u32[]{:S(2)}) %collective-permute-start.2) | collective-permute-done | bytes 1179680 | tf_op jit(solution)/shard_map/ppermute | solution.py:325
  103.3 21.6 %collective-permute-done.3 = bf16[256,2304]{1,0:T(8,128)(2,1)} collective-permute-done((bf16[256,2304]{1,0:T(8,128)(2,1)}, bf16[256,2304]{1,0:T(8,128)(2,1)}, u32[]{:S(2)}, u32[]{:S(2)}) %collective-permute-start.3) | collective-permute-done | bytes 1179680 | tf_op jit(solution)/shard_map/ppermute | solution.py:325
  133.0 16.0 %fusion.37 = f32[1024,1728]{0,1:T(8,128)} fusion(bf16[2304,1728]{1,0:T(8,128)(2,1)} %all-gather.12.cloned.1.call-done, f32[2304]{0:T(1024)S(1)} %get-tuple-element.51, f32[1024]{0:T(1024)S(1)} %copy-done.65, bf16[256,2304]{1,0:T(8,128)(2,1)} %copy-done.19, bf16[256,2304]{1,0:T(8,128)(2,1)S(1)} %broadcast_select_fusion.7, bf16[256,2304]{1,0:T(8,128)(2,1)} %copy-done.17, ...), kind=kOutput, calls=%fused_computation.108 | convolution fusion | flops 8179679232 | bytes 19772416 | tf_op jit(solution)/shard_map/dot_general | solution.py:28
  153.0 16.1 %fusion.6 = (f32[9,1024]{1,0:T(8,128)S(1)}, f32[9,1024,1024]{1,2,0:T(8,128)}) fusion(pred[1024,1024]{0,1:T(8,128)(4,1)S(1)} %compare_and_fusion, bf16[1024,9,32]{0,2,1:T(8,128)(2,1)S(1)} %get-tuple-element.111, bf16[1024,9,32]{0,2,1:T(8,128)(2,1)S(1)} %get-tuple-element.112, bf16[1024,9,32]{0,2,1:T(8,128)(2,1)S(1)} %get-tuple-element.99, ...), kind=kOutput, calls=%fused_computation.13 | convolution fusion | flops 1240980480 | bytes 41193472 | tf_op jit(solution)/shard_map/qhd,khd->hqk/dot_general | solution.py:468
  169.1 16.6 %fusion = f32[9,1024]{1,0:T(8,128)S(1)} fusion(f32[9,1024]{1,0:T(8,128)S(1)} %get-tuple-element.116, f32[9,1024,1024]{1,2,0:T(8,128)} %get-tuple-element.117, pred[1024,1024]{0,1:T(8,128)(4,1)S(1)} %compare_and_fusion), kind=kLoop, calls=%fused_computation.7 | loop fusion | flops 37739520 | bytes 38871040 | tf_op jit(solution)/shard_map/reduce_sum | solution.py:476
  187.6 18.5 %fusion.32 = bf16[9,64,1024]{2,1,0:T(8,128)(2,1)} fusion(bf16[1024,9,64]{0,2,1:T(8,128)(2,1)S(1)} %bitcast.113, f32[9,1024]{1,0:T(8,128)S(1)} %fusion, f32[9,1024]{1,0:T(8,128)S(1)} %get-tuple-element.116, f32[9,1024,1024]{1,2,0:T(8,128)} %get-tuple-element.117, pred[1024,1024]{0,1:T(8,128)(4,1)S(1)} %compare_and_fusion), kind=kOutput, calls=%fused_computation.105 | convolution fusion | flops 1255735296 | bytes 41230336 | tf_op jit(solution)/shard_map/hqk,khd->qhd/dot_general | solution.py:480
  206.1 6.1 convolution_convert_fusion.4
  216.2 23.6 %collective-permute-done.8 = bf16[256,2304]{1,0:T(8,128)(2,1)S(1)} collective-permute-done((bf16[256,2304]{1,0:T(8,128)(2,1)S(1)}, bf16[256,2304]{1,0:T(8,128)(2,1)S(1)}, u32[]{:S(2)}, u32[]{:S(2)}) %collective-permute-start.8) | collective-permute-done | bytes 1179680 | tf_op jit(solution)/shard_map/ppermute | solution.py:342
  247.4 7.6 collective-permute-start.29
  255.0 17.2 %collective-permute-done.9 = bf16[256,2304]{1,0:T(8,128)(2,1)S(1)} collective-permute-done((bf16[256,2304]{1,0:T(8,128)(2,1)S(1)}, bf16[256,2304]{1,0:T(8,128)(2,1)S(1)}, u32[]{:S(2)}, u32[]{:S(2)}) %collective-permute-start.9) | collective-permute-done | bytes 1179680 | tf_op jit(solution)/shard_map/ppermute | solution.py:342
  272.9 7.0 collective-permute-start.10
  282.6 15.0 collective-permute-done.29
  298.3 21.0 %collective-permute-done.10 = bf16[256,2304]{1,0:T(8,128)(2,1)S(1)} collective-permute-done((bf16[256,2304]{1,0:T(8,128)(2,1)S(1)}, bf16[256,2304]{1,0:T(8,128)(2,1)S(1)}, u32[]{:S(2)}, u32[]{:S(2)}) %collective-permute-start.10) | collective-permute-done | bytes 1179680 | tf_op jit(solution)/shard_map/ppermute | solution.py:342
  321.8 12.2 collective-permute-start.14
  336.1 21.1 %collective-permute-done.15 = bf16[256,2304]{1,0:T(8,128)(2,1)S(1)} collective-permute-done((bf16[256,2304]{1,0:T(8,128)(2,1)S(1)}, bf16[256,2304]{1,0:T(8,128)(2,1)S(1)}, u32[]{:S(2)}, u32[]{:S(2)}) %collective-permute-start.15) | collective-permute-done | bytes 1179680 | tf_op jit(solution)/shard_map/ppermute | solution.py:325
  362.8 40.5 %collective-permute-done.16 = bf16[256,2304]{1,0:T(8,128)(2,1)} collective-permute-done((bf16[256,2304]{1,0:T(8,128)(2,1)S(1)}, bf16[256,2304]{1,0:T(8,128)(2,1)}, u32[]{:S(2)}, u32[]{:S(2)}) %collective-permute-start.16) | collective-permute-done | bytes 1179680 | tf_op jit(solution)/shard_map/ppermute | solution.py:325
  405.7 9.9 copy.73
  415.6 10.1 copy.74
  432.6 30.8 %fusion.39 = f32[1024,2880]{0,1:T(8,128)} fusion(bf16[2304,2880]{1,0:T(8,128)(2,1)} %all-gather.16.cloned.1.call-done, bf16[256,2304]{1,0:T(8,128)(2,1)} %broadcast_select_fusion.2, bf16[256,2304]{1,0:T(8,128)(2,1)} %broadcast_select_fusion.6, bf16[256,2304]{1,0:T(8,128)(2,1)} %broadcast_select_fusion.10, bf16[256,2304]{1,0:T(8,128)(2,1)S(1)} %multiply_convert_fusion.7), kind=kOutput, calls=%fused_computation.141 | convolution fusion | flops 13608419328 | bytes 29786112 | tf_op jit(solution)/shard_map/dot_general | solution.py:28
  463.4 18.9 %multiply_convert_fusion.3 = (bf16[1024,1440]{0,1:T(8,128)(2,1)}, bf16[1024,1440]{0,1:T(8,128)(2,1)}, bf16[1024,1440]{0,1:T(8,128)(2,1)}) fusion(f32[1024,2880]{0,1:T(8,128)} %fusion.39, bf16[1440,2304]{0,1:T(8,128)(2,1)} %bitcast.111, bf16[256,2304]{1,0:T(8,128)(2,1)} %broadcast_select_fusion.1, bf16[256,2304]{1,0:T(8,128)(2,1)} %broadcast_select_fusion.5, ...), kind=kOutput, calls=%fused_computation.27 | convolution fusion | flops 6842843136 | bytes 32002048 | tf_op jit(solution)/shard_map/dot_general | solution.py:24
  482.3 19.4 %convolution_convert_fusion.5 = bf16[1024,2304]{1,0:T(8,128)(2,1)S(1)} fusion(bf16[2304,2880]{1,0:T(8,128)(2,1)} %all-gather.16.cloned.1.call-done, bf16[1024,1440]{0,1:T(8,128)(2,1)} %get-tuple-element.61, bf16[1024,1440]{0,1:T(8,128)(2,1)} %get-tuple-element.60), kind=kOutput, calls=%fused_computation.33 | convolution fusion | flops 13603700736 | bytes 23887872 | tf_op jit(solution)/shard_map/dot_general | solution.py:24
  508.4 10.9 convolution_convert_fusion.6
  521.7 12.3 collective-permute-done.35
  539.7 19.5 %collective-permute-done.22 = bf16[256,2304]{1,0:T(8,128)(2,1)S(1)} collective-permute-done((bf16[256,2304]{1,0:T(8,128)(2,1)S(1)}, bf16[256,2304]{1,0:T(8,128)(2,1)S(1)}, u32[]{:S(2)}, u32[]{:S(2)}) %collective-permute-start.22) | collective-permute-done | bytes 1179680 | tf_op jit(solution)/shard_map/ppermute | solution.py:342
  565.0 19.5 %collective-permute-done.36 = bf16[256,2304]{1,0:T(8,128)(2,1)S(1)} collective-permute-done((bf16[256,2304]{1,0:T(8,128)(2,1)S(1)}, bf16[256,2304]{1,0:T(8,128)(2,1)S(1)}, u32[]{:S(2)}, u32[]{:S(2)}) %collective-permute-start.36) | collective-permute-done | bytes 1179680 | tf_op jit(solution)/shard_map/ppermute | solution.py:342
  591.0 18.7 %collective-permute-done.23 = bf16[256,2304]{1,0:T(8,128)(2,1)S(1)} collective-permute-done((bf16[256,2304]{1,0:T(8,128)(2,1)S(1)}, bf16[256,2304]{1,0:T(8,128)(2,1)S(1)}, u32[]{:S(2)}, u32[]{:S(2)}) %collective-permute-start.23) | collective-permute-done | bytes 1179680 | tf_op jit(solution)/shard_map/ppermute | solution.py:342
  616.2 18.9 %collective-permute-done.37 = bf16[256,2304]{1,0:T(8,128)(2,1)S(1)} collective-permute-done((bf16[256,2304]{1,0:T(8,128)(2,1)S(1)}, bf16[256,2304]{1,0:T(8,128)(2,1)S(1)}, u32[]{:S(2)}, u32[]{:S(2)}) %collective-permute-start.37) | collective-permute-done | bytes 1179680 | tf_op jit(solution)/shard_map/ppermute | solution.py:342
  636.7 17.9 %collective-permute-done.24 = bf16[256,2304]{1,0:T(8,128)(2,1)S(1)} collective-permute-done((bf16[256,2304]{1,0:T(8,128)(2,1)S(1)}, bf16[256,2304]{1,0:T(8,128)(2,1)S(1)}, u32[]{:S(2)}, u32[]{:S(2)}) %collective-permute-start.24) | collective-permute-done | bytes 1179680 | tf_op jit(solution)/shard_map/ppermute | solution.py:342
  664.2 18.5 %collective-permute-done.42 = bf16[256,2304]{1,0:T(8,128)(2,1)S(1)} collective-permute-done((bf16[256,2304]{1,0:T(8,128)(2,1)S(1)}, bf16[256,2304]{1,0:T(8,128)(2,1)S(1)}, u32[]{:S(2)}, u32[]{:S(2)}) %collective-permute-start.42) | collective-permute-done | bytes 1179680 | tf_op jit(solution)/shard_map/ppermute | solution.py:325
  684.7 30.3 %collective-permute-done.43 = bf16[256,2304]{1,0:T(8,128)(2,1)S(1)} collective-permute-done((bf16[256,2304]{1,0:T(8,128)(2,1)S(1)}, bf16[256,2304]{1,0:T(8,128)(2,1)S(1)}, u32[]{:S(2)}, u32[]{:S(2)}) %collective-permute-start.43) | collective-permute-done | bytes 1179680 | tf_op jit(solution)/shard_map/ppermute | solution.py:325
  717.4 21.4 %collective-permute-done.44 = bf16[256,2304]{1,0:T(8,128)(2,1)S(1)} collective-permute-done((bf16[256,2304]{1,0:T(8,128)(2,1)S(1)}, bf16[256,2304]{1,0:T(8,128)(2,1)S(1)}, u32[]{:S(2)}, u32[]{:S(2)}) %collective-permute-start.44) | collective-permute-done | bytes 1179680 | tf_op jit(solution)/shard_map/ppermute | solution.py:325
  745.5 7.1 reshape.366
  757.8 12.4 convolution_convert_fusion.1
  770.2 10.3 copy.84
  780.5 10.0 copy.94
  790.6 6.1 convolution_convert_fusion.8
  796.7 29.0 %multiply_reduce_fusion = (f32[9,1024]{1,0:T(8,128)S(1)}, f32[9,1024,1024]{1,2,0:T(8,128)}) fusion(f32[9,1024]{1,0:T(8,128)S(1)} %log_add_fusion, f32[9,1024,1024]{1,2,0:T(8,128)} %get-tuple-element.117, pred[1024,1024]{0,1:T(8,128)(4,1)S(1)} %copy-done.7, bf16[1024,9,64]{0,2,1:T(8,128)(2,1)S(1)} %bitcast.122, bf16[1024,9,64]{0,2,1:T(8,128)(2,1)S(1)} %bitcast.114), kind=kOutput, calls=%fused_computation.2 | convolution fusion | flops 1255136256 | bytes 78979072 | tf_op jit(solution)/shard_map/qhd,khd->hqk/dot_general | solution.py:517
  825.8 31.9 %multiply_convert_fusion = bf16[9,1024,1024]{1,2,0:T(8,128)(2,1)} fusion(f32[9,1024,1024]{1,2,0:T(8,128)} %get-tuple-element.119, f32[9,1024]{1,0:T(8,128)S(1)} %get-tuple-element.118, f32[9,1024]{1,0:T(8,128)S(1)} %log_add_fusion, f32[9,1024,1024]{1,2,0:T(8,128)} %get-tuple-element.117, pred[1024,1024]{0,1:T(8,128)(4,1)S(1)} %copy-done.7), kind=kLoop, calls=%fused_computation.1 | loop fusion | flops 56623104 | bytes 95494144 | tf_op jit(solution)/shard_map/convert_element_type | solution.py:520
  857.7 10.1 multiply_bitcast_fusion
  867.8 8.3 multiply_bitcast_fusion.1
  878.8 16.5 %fusion.33 = bf16[9,64,1024]{2,1,0:T(8,128)(2,1)S(1)} fusion(bf16[1024,9,64]{0,2,1:T(8,128)(2,1)S(1)} %bitcast.123, f32[9,1024]{1,0:T(8,128)S(1)} %copy-done.51, f32[9,1024,1024]{1,2,0:T(8,128)} %get-tuple-element.117, pred[1024,1024]{0,1:T(8,128)(4,1)S(1)} %copy-done.7), kind=kOutput, calls=%fused_computation.106 | convolution fusion | flops 1246298112 | bytes 41193472 | tf_op jit(solution)/shard_map/hqk,qhd->khd/dot_general | solution.py:529
  895.4 12.0 convolution_convert_fusion.2
  908.6 20.6 %convolution_convert_fusion = bf16[2304,2880]{1,0:T(8,128)(2,1)} fusion(bf16[1024,1440]{0,1:T(8,128)(2,1)} %get-tuple-element.61, bf16[1024,1440]{0,1:T(8,128)(2,1)} %get-tuple-element.60, bf16[256,2304]{1,0:T(8,128)(2,1)} %broadcast_select_fusion.2, bf16[256,2304]{1,0:T(8,128)(2,1)} %broadcast_select_fusion.6, ...), kind=kOutput, calls=%fused_computation.12 | convolution fusion | flops 13626851328 | bytes 23887872 | tf_op jit(solution)/shard_map/dot_general | solution.py:20
  932.4 50.6 %reduce-scatter.7.cloned.1.call-done = bf16[288,1728]{1,0:T(8,128)(2,1)} async-done(((bf16[2304,1728]{1,0:T(8,128)(2,1)}), bf16[288,1728]{1,0:T(8,128)(2,1)}) %reduce-scatter.7.cloned.1.call-update) | async-done | bytes 995344 | tf_op jit(solution)/shard_map/reduce_scatter | solution.py:407
  983.1 100.6 %reduce-scatter.11.cloned.1.call-done = bf16[288,2880]{1,0:T(8,128)(2,1)} async-done(((bf16[2304,2880]{1,0:T(8,128)(2,1)}), bf16[288,2880]{1,0:T(8,128)(2,1)}) %reduce-scatter.11.cloned.1.call-update) | async-done | bytes 1658896 | tf_op jit(solution)/shard_map/reduce_scatter | solution.py:407
  1083.7 13.0 convolution_convert_fusion.3
  1101.1 41.4 %collective-permute-done.47 = bf16[256,2304]{1,0:T(8,128)(2,1)S(1)} collective-permute-done((bf16[256,2304]{1,0:T(8,128)(2,1)S(1)}, bf16[256,2304]{1,0:T(8,128)(2,1)S(1)}, u32[]{:S(2)}, u32[]{:S(2)}) %collective-permute-start.47) | collective-permute-done | bytes 1179680 | tf_op jit(solution)/shard_map/ppermute | solution.py:342
  1148.4 48.0 %collective-permute-done.48 = bf16[256,2304]{1,0:T(8,128)(2,1)S(1)} collective-permute-done((bf16[256,2304]{1,0:T(8,128)(2,1)S(1)}, bf16[256,2304]{1,0:T(8,128)(2,1)S(1)}, u32[]{:S(2)}, u32[]{:S(2)}) %collective-permute-start.48) | collective-permute-done | bytes 1179680 | tf_op jit(solution)/shard_map/ppermute | solution.py:342
  1198.3 40.2 %collective-permute-start.49 = (bf16[256,2304]{1,0:T(8,128)(2,1)}, bf16[256,2304]{1,0:T(8,128)(2,1)}, u32[]{:S(2)}, u32[]{:S(2)}) collective-permute-start(bf16[256,2304]{1,0:T(8,128)(2,1)} %get-tuple-element.70), channel_id=1, source_target_pairs={{0,2},{2,4},{4,6},{1,3},{3,5},{5,7},{8,10},{10,12},{12,14},{9,11},... | collective-permute-start | bytes 3538952 | tf_op jit(solution)/shard_map/ppermute | solution.py:342
  1239.9 38.2 %collective-permute-done.49 = bf16[256,2304]{1,0:T(8,128)(2,1)} collective-permute-done((bf16[256,2304]{1,0:T(8,128)(2,1)}, bf16[256,2304]{1,0:T(8,128)(2,1)}, u32[]{:S(2)}, u32[]{:S(2)}) %collective-permute-start.49) | collective-permute-done | bytes 1179680 | tf_op jit(solution)/shard_map/ppermute | solution.py:342
  1278.1 29.6 %collective-permute-done.52 = bf16[256,2304]{1,0:T(8,128)(2,1)} collective-permute-done((bf16[256,2304]{1,0:T(8,128)(2,1)}, bf16[256,2304]{1,0:T(8,128)(2,1)}, u32[]{:S(2)}, u32[]{:S(2)}) %collective-permute-start.52) | collective-permute-done | bytes 1179680 | tf_op jit(solution)/shard_map/ppermute | solution.py:343
  1316.7 38.6 %psum.7 = f32[2,2304]{1,0:T(2,128)S(1)} all-reduce(f32[2,2304]{1,0:T(2,128)S(1)} %pad_maximum_fusion.22), channel_id=1, replica_groups=mesh['shard'=4,'ctx'=4,'tensor'=2] {'shard','ctx','tensor'}, use_global_device_ids=true, to_apply=%region_10.11 | all-reduce | flops 4608 | bytes 36864 | tf_op jit(solution)/shard_map/psum | solution.py:550
  1372.9 11.5 copy.86
  1384.4 10.7 reshape.384
  1431.7 25.9 %all-gather.22.cloned.1.call-done = bf16[2304,2880]{1,0:T(8,128)(2,1)} async-done(((bf16[288,2880]{1,0:T(8,128)(2,1)}), bf16[2304,2880]{1,0:T(8,128)(2,1)}) %all-gather.22.cloned.1.call-update) | async-done | bytes 13271056 | tf_op jit(solution)/shard_map/all_gather | solution.py:402
  1457.6 8.6 dynamic-slice_convert_fusion
  1466.2 12.0 slice_bitcast_fusion
  1478.2 11.3 copy.82
  1489.5 10.4 reshape.372
  1499.9 11.3 copy.83
  1511.2 10.3 reshape.373
  (367 shorter events, 244.2 us)
Async XLA Ops:
  7.2 121.2 %all-gather.14.cloned.1.call-start = ((), (), s32[]{:S(2)}) async-start(), calls=%async_computation.5 | async-start | bytes 3317760 | tf_op jit(solution)/shard_map/all_gather | solution.py:397
  12.9 120.1 %all-gather.12.cloned.1.call-start = ((), (), s32[]{:S(2)}) async-start(), calls=%async_computation.4 | async-start | bytes 9289728 | tf_op jit(solution)/shard_map/all_gather | solution.py:393
  21.1 3.7 collective-permute-start.6
  26.0 379.7 %all-gather.24.cloned.1.call-start = ((), (), s32[]{:S(2)}) async-start(), calls=%async_computation.13 | async-start | bytes 7962624 | tf_op jit(solution)/shard_map/all_gather | solution.py:397
  32.8 399.7 %all-gather.16.cloned.1.call-start = ((), (), s32[]{:S(2)}) async-start(), calls=%async_computation.6 | async-start | bytes 15261696 | tf_op jit(solution)/shard_map/all_gather | solution.py:393
  35.0 31.0 %collective-permute-start.1 = (bf16[256,2304]{1,0:T(8,128)(2,1)S(1)}, bf16[256,2304]{1,0:T(8,128)(2,1)S(1)}, u32[]{:S(2)}, u32[]{:S(2)}) collective-permute-start(bf16[256,2304]{1,0:T(8,128)(2,1)S(1)} %get-tuple-element.55), channel_id=1, source_target_pairs={{2,0},{4,2},{6,4},{3,1},{5,3},{7,5},{10,8},{12,10},{14,12},{11,9},... | collective-permute-start | bytes 3538952 | tf_op jit(solution)/shard_map/ppermute | solution.py:325
  36.3 34.7 %collective-permute-start = (bf16[256,2304]{1,0:T(8,128)(2,1)S(1)}, bf16[256,2304]{1,0:T(8,128)(2,1)}, u32[]{:S(2)}, u32[]{:S(2)}) collective-permute-start(bf16[256,2304]{1,0:T(8,128)(2,1)S(1)} %get-tuple-element.55), channel_id=1, source_target_pairs={{0,2},{2,4},{4,6},{1,3},{3,5},{5,7},{8,10},{10,12},{12,14},{9,11},... | collective-permute-start | bytes 3538952 | tf_op jit(solution)/shard_map/ppermute | solution.py:324
  48.8 48.4 %collective-permute-start.20 = (bf16[288,2880]{1,0:T(8,128)(2,1)}, bf16[288,2880]{1,0:T(8,128)(2,1)}, u32[]{:S(2)}, u32[]{:S(2)}) collective-permute-start(bf16[288,2880]{1,0:T(8,128)(2,1)} %fusion.29), channel_id=1, source_target_pairs={{0,1},{1,0},{2,3},{3,2},{4,5},{5,4},{6,7},{7,6},{8,9},{9,8},{10,11... | collective-permute-start | bytes 4976648 | tf_op jit(solution)/shard_map/ppermute | solution.py:389
  66.1 29.8 %collective-permute-start.2 = (bf16[256,2304]{1,0:T(8,128)(2,1)S(1)}, bf16[256,2304]{1,0:T(8,128)(2,1)}, u32[]{:S(2)}, u32[]{:S(2)}) collective-permute-start(bf16[256,2304]{1,0:T(8,128)(2,1)S(1)} %collective-permute-done.1), channel_id=1, source_target_pairs={{2,0},{4,2},{3,1},{5,3},{10,8},{12,10},{11,9},{13,11},{18,16},{20,... | collective-permute-start | bytes 3538952 | tf_op jit(solution)/shard_map/ppermute | solution.py:325
  71.0 29.6 %collective-permute-start.4 = (bf16[256,2304]{1,0:T(8,128)(2,1)}, bf16[256,2304]{1,0:T(8,128)(2,1)}, u32[]{:S(2)}, u32[]{:S(2)}) collective-permute-start(bf16[256,2304]{1,0:T(8,128)(2,1)} %collective-permute-done), channel_id=1, source_target_pairs={{2,4},{4,6},{3,5},{5,7},{10,12},{12,14},{11,13},{13,15},{18,20},{2... | collective-permute-start | bytes 3538952 | tf_op jit(solution)/shard_map/ppermute | solution.py:324
  95.8 29.1 %collective-permute-start.3 = (bf16[256,2304]{1,0:T(8,128)(2,1)}, bf16[256,2304]{1,0:T(8,128)(2,1)}, u32[]{:S(2)}, u32[]{:S(2)}) collective-permute-start(bf16[256,2304]{1,0:T(8,128)(2,1)} %collective-permute-done.2), channel_id=1, source_target_pairs={{2,0},{3,1},{10,8},{11,9},{18,16},{19,17},{26,24},{27,25}} | collective-permute-start | bytes 3538952 | tf_op jit(solution)/shard_map/ppermute | solution.py:325
  100.6 828.7 %reduce-scatter.9.cloned.1.call-start = ((), (), s32[]{:S(2)}) async-start(), calls=%async_computation.9 | async-start | bytes 3317760 | tf_op jit(solution)/shard_map/reduce_scatter | solution.py:423
  100.7 25.7 %collective-permute-start.5 = (bf16[256,2304]{1,0:T(8,128)(2,1)}, bf16[256,2304]{1,0:T(8,128)(2,1)S(1)}, u32[]{:S(2)}, u32[]{:S(2)}) collective-permute-start(bf16[256,2304]{1,0:T(8,128)(2,1)} %collective-permute-done.4), channel_id=1, source_target_pairs={{4,6},{5,7},{12,14},{13,15},{20,22},{21,23},{28,30},{29,31}} | collective-permute-start | bytes 3538952 | tf_op jit(solution)/shard_map/ppermute | solution.py:324
  212.4 3.7 collective-permute-start.11
  213.2 26.5 %collective-permute-start.8 = (bf16[256,2304]{1,0:T(8,128)(2,1)S(1)}, bf16[256,2304]{1,0:T(8,128)(2,1)S(1)}, u32[]{:S(2)}, u32[]{:S(2)}) collective-permute-start(bf16[256,2304]{1,0:T(8,128)(2,1)S(1)} %get-tuple-element.92), channel_id=1, source_target_pairs={{0,2},{1,3},{8,10},{9,11},{16,18},{17,19},{24,26},{25,27}} | collective-permute-start | bytes 3538952 | tf_op jit(solution)/shard_map/ppermute | solution.py:342
  240.2 14.8 collective-permute-start.12
  241.0 31.3 %collective-permute-start.9 = (bf16[256,2304]{1,0:T(8,128)(2,1)S(1)}, bf16[256,2304]{1,0:T(8,128)(2,1)S(1)}, u32[]{:S(2)}, u32[]{:S(2)}) collective-permute-start(bf16[256,2304]{1,0:T(8,128)(2,1)S(1)} %get-tuple-element.90), channel_id=1, source_target_pairs={{0,2},{2,4},{1,3},{3,5},{8,10},{10,12},{9,11},{11,13},{16,18},{18,... | collective-permute-start | bytes 3538952 | tf_op jit(solution)/shard_map/ppermute | solution.py:342
  246.1 35.1 %collective-permute-start.30 = (bf16[256,2304]{1,0:T(8,128)(2,1)S(1)}, bf16[256,2304]{1,0:T(8,128)(2,1)S(1)}, u32[]{:S(2)}, u32[]{:S(2)}) collective-permute-start(bf16[256,2304]{1,0:T(8,128)(2,1)S(1)} %dynamic-slice_bitcast_fusion), channel_id=1, source_target_pairs={{2,0},{4,2},{6,4},{3,1},{5,3},{7,5},{10,8},{12,10},{14,12},{11,9},... | collective-permute-start | bytes 3538952 | tf_op jit(solution)/shard_map/ppermute | solution.py:325
  247.4 50.1 %collective-permute-start.29 = (bf16[256,2304]{1,0:T(8,128)(2,1)S(1)}, bf16[256,2304]{1,0:T(8,128)(2,1)S(1)}, u32[]{:S(2)}, u32[]{:S(2)}) collective-permute-start(bf16[256,2304]{1,0:T(8,128)(2,1)S(1)} %dynamic-slice_bitcast_fusion), channel_id=1, source_target_pairs={{0,2},{2,4},{4,6},{1,3},{3,5},{5,7},{8,10},{10,12},{12,14},{9,11},... | collective-permute-start | bytes 3538952 | tf_op jit(solution)/shard_map/ppermute | solution.py:324
  272.9 46.4 %collective-permute-start.10 = (bf16[256,2304]{1,0:T(8,128)(2,1)S(1)}, bf16[256,2304]{1,0:T(8,128)(2,1)S(1)}, u32[]{:S(2)}, u32[]{:S(2)}) collective-permute-start(bf16[256,2304]{1,0:T(8,128)(2,1)S(1)} %get-tuple-element.88), channel_id=1, source_target_pairs={{0,2},{2,4},{4,6},{1,3},{3,5},{5,7},{8,10},{10,12},{12,14},{9,11},... | collective-permute-start | bytes 3538952 | tf_op jit(solution)/shard_map/ppermute | solution.py:342
  279.9 39.3 %collective-permute-start.13 = (bf16[256,2304]{1,0:T(8,128)(2,1)S(1)}, bf16[256,2304]{1,0:T(8,128)(2,1)S(1)}, u32[]{:S(2)}, u32[]{:S(2)}) collective-permute-start(bf16[256,2304]{1,0:T(8,128)(2,1)S(1)} %get-tuple-element.89), channel_id=1, source_target_pairs={{2,0},{4,2},{6,4},{3,1},{5,3},{7,5},{10,8},{12,10},{14,12},{11,9},... | collective-permute-start | bytes 3538952 | tf_op jit(solution)/shard_map/ppermute | solution.py:343
  281.3 53.5 %collective-permute-start.31 = (bf16[256,2304]{1,0:T(8,128)(2,1)S(1)}, bf16[256,2304]{1,0:T(8,128)(2,1)S(1)}, u32[]{:S(2)}, u32[]{:S(2)}) collective-permute-start(bf16[256,2304]{1,0:T(8,128)(2,1)S(1)} %collective-permute-done.30), channel_id=1, source_target_pairs={{2,0},{4,2},{3,1},{5,3},{10,8},{12,10},{11,9},{13,11},{18,16},{20,... | collective-permute-start | bytes 3538952 | tf_op jit(solution)/shard_map/ppermute | solution.py:325
  297.5 36.5 %collective-permute-start.33 = (bf16[256,2304]{1,0:T(8,128)(2,1)S(1)}, bf16[256,2304]{1,0:T(8,128)(2,1)S(1)}, u32[]{:S(2)}, u32[]{:S(2)}) collective-permute-start(bf16[256,2304]{1,0:T(8,128)(2,1)S(1)} %collective-permute-done.29), channel_id=1, source_target_pairs={{2,4},{4,6},{3,5},{5,7},{10,12},{12,14},{11,13},{13,15},{18,20},{2... | collective-permute-start | bytes 3538952 | tf_op jit(solution)/shard_map/ppermute | solution.py:324
  320.5 36.7 %collective-permute-start.15 = (bf16[256,2304]{1,0:T(8,128)(2,1)S(1)}, bf16[256,2304]{1,0:T(8,128)(2,1)S(1)}, u32[]{:S(2)}, u32[]{:S(2)}) collective-permute-start(bf16[256,2304]{1,0:T(8,128)(2,1)S(1)} %multiply_convert_fusion.7), channel_id=1, source_target_pairs={{2,0},{4,2},{6,4},{3,1},{5,3},{7,5},{10,8},{12,10},{14,12},{11,9},... | collective-permute-start | bytes 3538952 | tf_op jit(solution)/shard_map/ppermute | solution.py:325
  321.8 37.8 %collective-permute-start.14 = (bf16[256,2304]{1,0:T(8,128)(2,1)S(1)}, bf16[256,2304]{1,0:T(8,128)(2,1)}, u32[]{:S(2)}, u32[]{:S(2)}) collective-permute-start(bf16[256,2304]{1,0:T(8,128)(2,1)S(1)} %multiply_convert_fusion.7), channel_id=1, source_target_pairs={{0,2},{2,4},{4,6},{1,3},{3,5},{5,7},{8,10},{10,12},{12,14},{9,11},... | collective-permute-start | bytes 3538952 | tf_op jit(solution)/shard_map/ppermute | solution.py:324
  334.0 27.5 %collective-permute-start.34 = (bf16[256,2304]{1,0:T(8,128)(2,1)S(1)}, bf16[256,2304]{1,0:T(8,128)(2,1)S(1)}, u32[]{:S(2)}, u32[]{:S(2)}) collective-permute-start(bf16[256,2304]{1,0:T(8,128)(2,1)S(1)} %collective-permute-done.33), channel_id=1, source_target_pairs={{4,6},{5,7},{12,14},{13,15},{20,22},{21,23},{28,30},{29,31}} | collective-permute-start | bytes 3538952 | tf_op jit(solution)/shard_map/ppermute | solution.py:324
  334.8 69.8 %collective-permute-start.32 = (bf16[256,2304]{1,0:T(8,128)(2,1)S(1)}, bf16[256,2304]{1,0:T(8,128)(2,1)S(1)}, u32[]{:S(2)}, u32[]{:S(2)}) collective-permute-start(bf16[256,2304]{1,0:T(8,128)(2,1)S(1)} %collective-permute-done.31), channel_id=1, source_target_pairs={{2,0},{3,1},{10,8},{11,9},{18,16},{19,17},{26,24},{27,25}} | collective-permute-start | bytes 3538952 | tf_op jit(solution)/shard_map/ppermute | solution.py:325
  357.2 46.0 %collective-permute-start.16 = (bf16[256,2304]{1,0:T(8,128)(2,1)S(1)}, bf16[256,2304]{1,0:T(8,128)(2,1)}, u32[]{:S(2)}, u32[]{:S(2)}) collective-permute-start(bf16[256,2304]{1,0:T(8,128)(2,1)S(1)} %collective-permute-done.15), channel_id=1, source_target_pairs={{2,0},{4,2},{3,1},{5,3},{10,8},{12,10},{11,9},{13,11},{18,16},{20,... | collective-permute-start | bytes 3538952 | tf_op jit(solution)/shard_map/ppermute | solution.py:325
  359.7 66.1 %collective-permute-start.18 = (bf16[256,2304]{1,0:T(8,128)(2,1)}, bf16[256,2304]{1,0:T(8,128)(2,1)}, u32[]{:S(2)}, u32[]{:S(2)}) collective-permute-start(bf16[256,2304]{1,0:T(8,128)(2,1)} %collective-permute-done.14), channel_id=1, source_target_pairs={{2,4},{4,6},{3,5},{5,7},{10,12},{12,14},{11,13},{13,15},{18,20},{2... | collective-permute-start | bytes 3538952 | tf_op jit(solution)/shard_map/ppermute | solution.py:324
  403.3 25.7 %collective-permute-start.17 = (bf16[256,2304]{1,0:T(8,128)(2,1)}, bf16[256,2304]{1,0:T(8,128)(2,1)}, u32[]{:S(2)}, u32[]{:S(2)}) collective-permute-start(bf16[256,2304]{1,0:T(8,128)(2,1)} %collective-permute-done.16), channel_id=1, source_target_pairs={{2,0},{3,1},{10,8},{11,9},{18,16},{19,17},{26,24},{27,25}} | collective-permute-start | bytes 3538952 | tf_op jit(solution)/shard_map/ppermute | solution.py:325
  425.8 5.7 collective-permute-start.19
  501.9 32.0 %collective-permute-start.35 = (bf16[256,2304]{1,0:T(8,128)(2,1)S(1)}, bf16[256,2304]{1,0:T(8,128)(2,1)S(1)}, u32[]{:S(2)}, u32[]{:S(2)}) collective-permute-start(bf16[256,2304]{1,0:T(8,128)(2,1)S(1)} %get-tuple-element.80), channel_id=1, source_target_pairs={{0,2},{1,3},{8,10},{9,11},{16,18},{17,19},{24,26},{25,27}} | collective-permute-start | bytes 3538952 | tf_op jit(solution)/shard_map/ppermute | solution.py:342
  507.7 26.3 %collective-permute-start.38 = (bf16[256,2304]{1,0:T(8,128)(2,1)S(1)}, bf16[256,2304]{1,0:T(8,128)(2,1)S(1)}, u32[]{:S(2)}, u32[]{:S(2)}) collective-permute-start(bf16[256,2304]{1,0:T(8,128)(2,1)S(1)} %get-tuple-element.81), channel_id=1, source_target_pairs={{6,4},{7,5},{14,12},{15,13},{22,20},{23,21},{30,28},{31,29}} | collective-permute-start | bytes 3538952 | tf_op jit(solution)/shard_map/ppermute | solution.py:343
  519.5 39.7 %collective-permute-start.22 = (bf16[256,2304]{1,0:T(8,128)(2,1)S(1)}, bf16[256,2304]{1,0:T(8,128)(2,1)S(1)}, u32[]{:S(2)}, u32[]{:S(2)}) collective-permute-start(bf16[256,2304]{1,0:T(8,128)(2,1)S(1)} %get-tuple-element.86), channel_id=1, source_target_pairs={{0,2},{1,3},{8,10},{9,11},{16,18},{17,19},{24,26},{25,27}} | collective-permute-start | bytes 3538952 | tf_op jit(solution)/shard_map/ppermute | solution.py:342
  520.9 38.3 %collective-permute-start.25 = (bf16[256,2304]{1,0:T(8,128)(2,1)S(1)}, bf16[256,2304]{1,0:T(8,128)(2,1)S(1)}, u32[]{:S(2)}, u32[]{:S(2)}) collective-permute-start(bf16[256,2304]{1,0:T(8,128)(2,1)S(1)} %get-tuple-element.87), channel_id=1, source_target_pairs={{6,4},{7,5},{14,12},{15,13},{22,20},{23,21},{30,28},{31,29}} | collective-permute-start | bytes 3538952 | tf_op jit(solution)/shard_map/ppermute | solution.py:343
  534.5 50.0 %collective-permute-start.36 = (bf16[256,2304]{1,0:T(8,128)(2,1)S(1)}, bf16[256,2304]{1,0:T(8,128)(2,1)S(1)}, u32[]{:S(2)}, u32[]{:S(2)}) collective-permute-start(bf16[256,2304]{1,0:T(8,128)(2,1)S(1)} %get-tuple-element.78), channel_id=1, source_target_pairs={{0,2},{2,4},{1,3},{3,5},{8,10},{10,12},{9,11},{11,13},{16,18},{18,... | collective-permute-start | bytes 3538952 | tf_op jit(solution)/shard_map/ppermute | solution.py:342
  538.9 45.6 %collective-permute-start.39 = (bf16[256,2304]{1,0:T(8,128)(2,1)S(1)}, bf16[256,2304]{1,0:T(8,128)(2,1)S(1)}, u32[]{:S(2)}, u32[]{:S(2)}) collective-permute-start(bf16[256,2304]{1,0:T(8,128)(2,1)S(1)} %get-tuple-element.79), channel_id=1, source_target_pairs={{4,2},{6,4},{5,3},{7,5},{12,10},{14,12},{13,11},{15,13},{20,18},{2... | collective-permute-start | bytes 3538952 | tf_op jit(solution)/shard_map/ppermute | solution.py:343
  559.8 50.0 %collective-permute-start.23 = (bf16[256,2304]{1,0:T(8,128)(2,1)S(1)}, bf16[256,2304]{1,0:T(8,128)(2,1)S(1)}, u32[]{:S(2)}, u32[]{:S(2)}) collective-permute-start(bf16[256,2304]{1,0:T(8,128)(2,1)S(1)} %get-tuple-element.84), channel_id=1, source_target_pairs={{0,2},{2,4},{1,3},{3,5},{8,10},{10,12},{9,11},{11,13},{16,18},{18,... | collective-permute-start | bytes 3538952 | tf_op jit(solution)/shard_map/ppermute | solution.py:342
  564.3 45.5 %collective-permute-start.26 = (bf16[256,2304]{1,0:T(8,128)(2,1)S(1)}, bf16[256,2304]{1,0:T(8,128)(2,1)S(1)}, u32[]{:S(2)}, u32[]{:S(2)}) collective-permute-start(bf16[256,2304]{1,0:T(8,128)(2,1)S(1)} %get-tuple-element.85), channel_id=1, source_target_pairs={{4,2},{6,4},{5,3},{7,5},{12,10},{14,12},{13,11},{15,13},{20,18},{2... | collective-permute-start | bytes 3538952 | tf_op jit(solution)/shard_map/ppermute | solution.py:343
  585.1 49.9 %collective-permute-start.37 = (bf16[256,2304]{1,0:T(8,128)(2,1)S(1)}, bf16[256,2304]{1,0:T(8,128)(2,1)S(1)}, u32[]{:S(2)}, u32[]{:S(2)}) collective-permute-start(bf16[256,2304]{1,0:T(8,128)(2,1)S(1)} %get-tuple-element.76), channel_id=1, source_target_pairs={{0,2},{2,4},{4,6},{1,3},{3,5},{5,7},{8,10},{10,12},{12,14},{9,11},... | collective-permute-start | bytes 3538952 | tf_op jit(solution)/shard_map/ppermute | solution.py:342
  589.6 45.5 %collective-permute-start.40 = (bf16[256,2304]{1,0:T(8,128)(2,1)S(1)}, bf16[256,2304]{1,0:T(8,128)(2,1)S(1)}, u32[]{:S(2)}, u32[]{:S(2)}) collective-permute-start(bf16[256,2304]{1,0:T(8,128)(2,1)S(1)} %get-tuple-element.77), channel_id=1, source_target_pairs={{2,0},{4,2},{6,4},{3,1},{5,3},{7,5},{10,8},{12,10},{14,12},{11,9},... | collective-permute-start | bytes 3538952 | tf_op jit(solution)/shard_map/ppermute | solution.py:343
  610.4 44.2 %collective-permute-start.24 = (bf16[256,2304]{1,0:T(8,128)(2,1)S(1)}, bf16[256,2304]{1,0:T(8,128)(2,1)S(1)}, u32[]{:S(2)}, u32[]{:S(2)}) collective-permute-start(bf16[256,2304]{1,0:T(8,128)(2,1)S(1)} %get-tuple-element.82), channel_id=1, source_target_pairs={{0,2},{2,4},{4,6},{1,3},{3,5},{5,7},{8,10},{10,12},{12,14},{9,11},... | collective-permute-start | bytes 3538952 | tf_op jit(solution)/shard_map/ppermute | solution.py:342
  614.9 39.7 %collective-permute-start.27 = (bf16[256,2304]{1,0:T(8,128)(2,1)S(1)}, bf16[256,2304]{1,0:T(8,128)(2,1)S(1)}, u32[]{:S(2)}, u32[]{:S(2)}) collective-permute-start(bf16[256,2304]{1,0:T(8,128)(2,1)S(1)} %get-tuple-element.83), channel_id=1, source_target_pairs={{2,0},{4,2},{6,4},{3,1},{5,3},{7,5},{10,8},{12,10},{14,12},{11,9},... | collective-permute-start | bytes 3538952 | tf_op jit(solution)/shard_map/ppermute | solution.py:343
  657.8 24.9 %collective-permute-start.42 = (bf16[256,2304]{1,0:T(8,128)(2,1)S(1)}, bf16[256,2304]{1,0:T(8,128)(2,1)S(1)}, u32[]{:S(2)}, u32[]{:S(2)}) collective-permute-start(bf16[256,2304]{1,0:T(8,128)(2,1)S(1)} %get-tuple-element.52), channel_id=1, source_target_pairs={{2,0},{4,2},{6,4},{3,1},{5,3},{7,5},{10,8},{12,10},{14,12},{11,9},... | collective-permute-start | bytes 3538952 | tf_op jit(solution)/shard_map/ppermute | solution.py:325
  659.1 24.9 %collective-permute-start.41 = (bf16[256,2304]{1,0:T(8,128)(2,1)S(1)}, bf16[256,2304]{1,0:T(8,128)(2,1)S(1)}, u32[]{:S(2)}, u32[]{:S(2)}) collective-permute-start(bf16[256,2304]{1,0:T(8,128)(2,1)S(1)} %get-tuple-element.52), channel_id=1, source_target_pairs={{0,2},{2,4},{4,6},{1,3},{3,5},{5,7},{8,10},{10,12},{12,14},{9,11},... | collective-permute-start | bytes 3538952 | tf_op jit(solution)/shard_map/ppermute | solution.py:324
  682.7 32.3 %collective-permute-start.43 = (bf16[256,2304]{1,0:T(8,128)(2,1)S(1)}, bf16[256,2304]{1,0:T(8,128)(2,1)S(1)}, u32[]{:S(2)}, u32[]{:S(2)}) collective-permute-start(bf16[256,2304]{1,0:T(8,128)(2,1)S(1)} %collective-permute-done.42), channel_id=1, source_target_pairs={{2,0},{4,2},{3,1},{5,3},{10,8},{12,10},{11,9},{13,11},{18,16},{20,... | collective-permute-start | bytes 3538952 | tf_op jit(solution)/shard_map/ppermute | solution.py:325
  684.0 32.3 %collective-permute-start.45 = (bf16[256,2304]{1,0:T(8,128)(2,1)S(1)}, bf16[256,2304]{1,0:T(8,128)(2,1)S(1)}, u32[]{:S(2)}, u32[]{:S(2)}) collective-permute-start(bf16[256,2304]{1,0:T(8,128)(2,1)S(1)} %collective-permute-done.41), channel_id=1, source_target_pairs={{2,4},{4,6},{3,5},{5,7},{10,12},{12,14},{11,13},{13,15},{18,20},{2... | collective-permute-start | bytes 3538952 | tf_op jit(solution)/shard_map/ppermute | solution.py:324
  715.0 23.8 %collective-permute-start.44 = (bf16[256,2304]{1,0:T(8,128)(2,1)S(1)}, bf16[256,2304]{1,0:T(8,128)(2,1)S(1)}, u32[]{:S(2)}, u32[]{:S(2)}) collective-permute-start(bf16[256,2304]{1,0:T(8,128)(2,1)S(1)} %collective-permute-done.43), channel_id=1, source_target_pairs={{2,0},{3,1},{10,8},{11,9},{18,16},{19,17},{26,24},{27,25}} | collective-permute-start | bytes 3538952 | tf_op jit(solution)/shard_map/ppermute | solution.py:325
  716.3 22.7 %collective-permute-start.46 = (bf16[256,2304]{1,0:T(8,128)(2,1)S(1)}, bf16[256,2304]{1,0:T(8,128)(2,1)S(1)}, u32[]{:S(2)}, u32[]{:S(2)}) collective-permute-start(bf16[256,2304]{1,0:T(8,128)(2,1)S(1)} %collective-permute-done.45), channel_id=1, source_target_pairs={{4,6},{5,7},{12,14},{13,15},{20,22},{21,23},{28,30},{29,31}} | collective-permute-start | bytes 3538952 | tf_op jit(solution)/shard_map/ppermute | solution.py:324
  756.5 173.6 %reduce-scatter.13.cloned.1.call-start = ((), (), s32[]{:S(2)}) async-start(), calls=%async_computation.15 | async-start | bytes 8294400
  790.5 192.5 %reduce-scatter.7.cloned.1.call-start = ((), (), s32[]{:S(2)}) async-start(), calls=%async_computation.7 | async-start | bytes 9289728 | tf_op jit(solution)/shard_map/reduce_scatter | solution.py:407
  907.4 176.3 %reduce-scatter.11.cloned.1.call-start = ((), (), s32[]{:S(2)}) async-start(), calls=%async_computation.11 | async-start | bytes 15261696 | tf_op jit(solution)/shard_map/reduce_scatter | solution.py:407
  929.2 431.2 %all-gather.20.cloned.1.call-start = ((), (), s32[]{:S(2)}) async-start(), calls=%async_computation.10 | async-start | bytes 3317760 | tf_op jit(solution)/shard_map/all_gather | solution.py:402
  930.0 437.3 %all-gather.26.cloned.1.call-start = ((), (), s32[]{:S(2)}) async-start(), calls=%async_computation.14 | async-start | bytes 7962624 | tf_op jit(solution)/shard_map/all_gather | solution.py:402
  932.3 462.8 %all-gather.18.cloned.1.call-start = ((), (), s32[]{:S(2)}) async-start(), calls=%async_computation.8 | async-start | bytes 9289728 | tf_op jit(solution)/shard_map/all_gather | solution.py:402
  983.0 474.5 %all-gather.22.cloned.1.call-start = ((), (), s32[]{:S(2)}) async-start(), calls=%async_computation.12 | async-start | bytes 15261696 | tf_op jit(solution)/shard_map/all_gather | solution.py:402
  1096.9 45.5 %collective-permute-start.47 = (bf16[256,2304]{1,0:T(8,128)(2,1)S(1)}, bf16[256,2304]{1,0:T(8,128)(2,1)S(1)}, u32[]{:S(2)}, u32[]{:S(2)}) collective-permute-start(bf16[256,2304]{1,0:T(8,128)(2,1)S(1)} %get-tuple-element.74), channel_id=1, source_target_pairs={{0,2},{1,3},{8,10},{9,11},{16,18},{17,19},{24,26},{25,27}} | collective-permute-start | bytes 3538952 | tf_op jit(solution)/shard_map/ppermute | solution.py:342
  1100.4 42.1 %collective-permute-start.50 = (bf16[256,2304]{1,0:T(8,128)(2,1)S(1)}, bf16[256,2304]{1,0:T(8,128)(2,1)S(1)}, u32[]{:S(2)}, u32[]{:S(2)}) collective-permute-start(bf16[256,2304]{1,0:T(8,128)(2,1)S(1)} %get-tuple-element.75), channel_id=1, source_target_pairs={{6,4},{7,5},{14,12},{15,13},{22,20},{23,21},{30,28},{31,29}} | collective-permute-start | bytes 3538952 | tf_op jit(solution)/shard_map/ppermute | solution.py:343
  1143.0 53.4 %collective-permute-start.48 = (bf16[256,2304]{1,0:T(8,128)(2,1)S(1)}, bf16[256,2304]{1,0:T(8,128)(2,1)S(1)}, u32[]{:S(2)}, u32[]{:S(2)}) collective-permute-start(bf16[256,2304]{1,0:T(8,128)(2,1)S(1)} %get-tuple-element.72), channel_id=1, source_target_pairs={{0,2},{2,4},{1,3},{3,5},{8,10},{10,12},{9,11},{11,13},{16,18},{18,... | collective-permute-start | bytes 3538952 | tf_op jit(solution)/shard_map/ppermute | solution.py:342
  1147.5 48.9 %collective-permute-start.51 = (bf16[256,2304]{1,0:T(8,128)(2,1)S(1)}, bf16[256,2304]{1,0:T(8,128)(2,1)S(1)}, u32[]{:S(2)}, u32[]{:S(2)}) collective-permute-start(bf16[256,2304]{1,0:T(8,128)(2,1)S(1)} %get-tuple-element.73), channel_id=1, source_target_pairs={{4,2},{6,4},{5,3},{7,5},{12,10},{14,12},{13,11},{15,13},{20,18},{2... | collective-permute-start | bytes 3538952 | tf_op jit(solution)/shard_map/ppermute | solution.py:343
  1198.3 79.8 %collective-permute-start.49 = (bf16[256,2304]{1,0:T(8,128)(2,1)}, bf16[256,2304]{1,0:T(8,128)(2,1)}, u32[]{:S(2)}, u32[]{:S(2)}) collective-permute-start(bf16[256,2304]{1,0:T(8,128)(2,1)} %get-tuple-element.70), channel_id=1, source_target_pairs={{0,2},{2,4},{4,6},{1,3},{3,5},{5,7},{8,10},{10,12},{12,14},{9,11},... | collective-permute-start | bytes 3538952 | tf_op jit(solution)/shard_map/ppermute | solution.py:342
  1238.5 69.2 %collective-permute-start.52 = (bf16[256,2304]{1,0:T(8,128)(2,1)}, bf16[256,2304]{1,0:T(8,128)(2,1)}, u32[]{:S(2)}, u32[]{:S(2)}) collective-permute-start(bf16[256,2304]{1,0:T(8,128)(2,1)} %get-tuple-element.71), channel_id=1, source_target_pairs={{2,0},{4,2},{6,4},{3,1},{5,3},{7,5},{10,8},{12,10},{14,12},{11,9},... | collective-permute-start | bytes 3538952 | tf_op jit(solution)/shard_map/ppermute | solution.py:343
  1239.9 75.1 %collective-permute-start.28 = (bf16[256,2304]{1,0:T(8,128)(2,1)S(1)}, bf16[256,2304]{1,0:T(8,128)(2,1)S(1)}, u32[]{:S(2)}, u32[]{:S(2)}) collective-permute-start(bf16[256,2304]{1,0:T(8,128)(2,1)S(1)} %copy-done.14), channel_id=1, source_target_pairs={{0,1},{1,0},{2,3},{3,2},{4,5},{5,4},{6,7},{7,6},{8,9},{9,8},{10,11... | collective-permute-start | bytes 3538952 | tf_op jit(solution)/shard_map/ppermute | solution.py:558
  1314.9 41.1 %collective-permute-start.53 = (bf16[256,2304]{1,0:T(8,128)(2,1)}, bf16[256,2304]{1,0:T(8,128)(2,1)}, u32[]{:S(2)}, u32[]{:S(2)}) collective-permute-start(bf16[256,2304]{1,0:T(8,128)(2,1)} %fusion.26), channel_id=1, source_target_pairs={{0,1},{1,0},{2,3},{3,2},{4,5},{5,4},{6,7},{7,6},{8,9},{9,8},{10,11... | collective-permute-start | bytes 3538952 | tf_op jit(solution)/shard_map/ppermute | solution.py:558
  (76 other events, 2382.4 us)
Sparse Core Ops, SparseCore 0:
  13.0 34.8 all-gather.13
  50.4 53.8 all-gather.11
  106.8 48.7 all-gather.23
  157.8 76.1 all-gather.15
  756.6 48.9 reduce-scatter.8
  809.0 66.6 reduce-scatter.12
  907.5 75.4 reduce-scatter.6
  986.5 97.1 reduce-scatter.10
  1085.3 48.6 all-gather.19
  1136.1 101.0 all-gather.25
  1238.9 94.1 all-gather.17
  1334.5 122.9 all-gather.21

commit v2 on v0

--- a/solution.py
+++ b/solution.py
@@ -1,8 +1,11 @@
+import functools
 import math
 
 import jax
 import jax.numpy as jnp
 from jax import lax
+from jax.experimental import pallas as pl
+from jax.experimental.pallas import tpu as pltpu
 from jax.sharding import PartitionSpec as P
 
 HD = 64
@@ -54,7 +57,7 @@
     return inverse * (scaled - normed * jnp.mean(scaled * normed, axis=-1, keepdims=True))
 
 
-def local(
+def gather_all(
     tokens,
     lengths,
     span_order,
@@ -311,6 +314,601 @@
     )
 
 
+LANES = 128
+QUERY_TILE = 256
+
+
+def lane_partner(values_in):
+    lane = lax.broadcasted_iota(jnp.int32, values_in.shape, 1) % HD
+    return jnp.where(
+        lane < HD // 2,
+        -pltpu.roll(values_in, LANES - HD // 2, 1),
+        pltpu.roll(values_in, HD // 2, 1),
+    )
+
+
+def head_lanes(values_in, head):
+    lane = lax.broadcasted_iota(jnp.int32, values_in.shape, 1)
+    return jnp.where(lane // HD == head, values_in, jnp.zeros_like(values_in))
+
+
+def tile_allowed(rows, start, length):
+    key = lax.broadcasted_iota(jnp.int32, (rows, QUERY_TILE), 0)
+    query = lax.broadcasted_iota(jnp.int32, (rows, QUERY_TILE), 1) + start
+    return (key <= query) & (key < length)
+
+
+def attend_kernel(
+    heads, span, order, length, q_in, k_in, v_in, cos, sin, out, q_out, k_out, v_out, log_out,
+    q_sort, k_sort, v_sort, turned,
+):
+    rows = q_in.shape[0]
+    pair = pl.program_id(0)
+    for block in range(rows // span):
+        place = pl.ds(pl.multiple_of(order[block] * span, span), span)
+        stored = slice(block * span, (block + 1) * span)
+        q_sort[place, :] = q_in[stored, :]
+        k_sort[place, :] = k_in[stored, :]
+        v_sort[place, :] = v_in[stored, :]
+    queries = q_sort[...]
+    keys = k_sort[...]
+    q_out[...] = (queries * cos[...] + lane_partner(queries) * sin[...]).astype(jnp.bfloat16)
+    k_out[...] = (keys * cos[...] + lane_partner(keys) * sin[...]).astype(jnp.bfloat16)
+    v_out[...] = v_sort[...].astype(jnp.bfloat16)
+    values_t = jnp.transpose(v_out[...])
+    turned[...] = jnp.zeros_like(turned)
+    log_out[...] = jnp.zeros_like(log_out)
+    for head in range(LANES // HD):
+
+        @pl.when(pair * (LANES // HD) + head < heads)
+        def _():
+            for start in range(0, rows, QUERY_TILE):
+                used = start + QUERY_TILE
+                query = head_lanes(q_out[start:used, :] * (HD**-0.5), head).astype(jnp.bfloat16)
+                scores = col_product(k_out[:used, :], query)
+                scores = jnp.where(tile_allowed(used, start, length[0]), scores, -1e30)
+                top = jnp.max(scores, axis=0, keepdims=True)
+                weights = jnp.exp(scores - top)
+                total = jnp.sum(weights, axis=0, keepdims=True)
+                probs = (weights * (1.0 / total)).astype(jnp.bfloat16)
+                turned[head * HD : (head + 1) * HD, start:used] = plain_product(
+                    values_t[head * HD : (head + 1) * HD, :used], probs
+                )
+                log_out[0, head : head + 1, start:used] = top + jnp.log(total)
+
+    q_sort[...] = jnp.transpose(turned[...])
+    for block in range(rows // span):
+        place = pl.ds(pl.multiple_of(order[block] * span, span), span)
+        out[block * span : (block + 1) * span, :] = q_sort[place, :].astype(jnp.bfloat16)
+
+
+def attend_back_kernel(
+    heads, span, order, length, q_in, k_in, v_in, log_in, o_in, do_in, cos, sin, grads,
+    o_sort, do_sort, dq_turned, dq_sum, dk_sum, dv_sum, piece, sems,
+):
+    rows = q_in.shape[0]
+    pair = pl.program_id(0)
+    pairs = pl.num_programs(0)
+    for block in range(rows // span):
+        place = pl.ds(pl.multiple_of(order[block] * span, span), span)
+        stored = slice(block * span, (block + 1) * span)
+        o_sort[place, :] = o_in[stored, :].astype(jnp.float32)
+        do_sort[place, :] = do_in[stored, :].astype(jnp.float32)
+    means_t = jnp.transpose(o_sort[...] * do_sort[...])
+    keys_t = jnp.transpose(k_in[...])
+    dq_turned[...] = jnp.zeros_like(dq_turned)
+    dk_sum[...] = jnp.zeros_like(dk_sum)
+    dv_sum[...] = jnp.zeros_like(dv_sum)
+    for head in range(LANES // HD):
+
+        @pl.when(pair * (LANES // HD) + head < heads)
+        def _():
+            inner = jnp.sum(means_t[head * HD : (head + 1) * HD, :], axis=0, keepdims=True)
+            for start in range(0, rows, QUERY_TILE):
+                used = start + QUERY_TILE
+                query = head_lanes(q_in[start:used, :] * (HD**-0.5), head).astype(jnp.bfloat16)
+                grad_o = head_lanes(do_sort[start:used, :], head).astype(jnp.bfloat16)
+                scores = col_product(k_in[:used, :], query)
+                probs = jnp.where(
+                    tile_allowed(used, start, length[0]),
+                    jnp.exp(scores - log_in[0, head : head + 1, start:used]),
+                    0.0,
+                )
+                grad_p = col_product(v_in[:used, :], grad_o)
+                grad_s = (probs * (grad_p - inner[:, start:used])).astype(jnp.bfloat16)
+                dv_sum[:used, :] += plain_product(probs.astype(jnp.bfloat16), grad_o)
+                dk_sum[:used, :] += plain_product(grad_s, query)
+                dq_turned[head * HD : (head + 1) * HD, start:used] = plain_product(
+                    keys_t[head * HD : (head + 1) * HD, :used], grad_s
+                )
+
+    grad_q = jnp.transpose(dq_turned[...]) * (HD**-0.5)
+    grad_k = dk_sum[...]
+    dq_sum[...] = grad_q * cos[...] - lane_partner(grad_q) * sin[...]
+    dk_sum[...] = grad_k * cos[...] - lane_partner(grad_k) * sin[...]
+    copies = []
+    for which, total in enumerate((dq_sum, dk_sum, dv_sum)):
+        for block in range(rows // span):
+            place = pl.ds(pl.multiple_of(order[block] * span, span), span)
+            piece[which, block * span : (block + 1) * span, :] = total[place, :].astype(jnp.bfloat16)
+        column = pl.multiple_of((which * pairs + pair) * LANES, LANES)
+        copies.append(
+            pltpu.make_async_copy(
+                piece.at[which], grads.at[:, pl.ds(column, LANES)], sems.at[which]
+            )
+        )
+        copies[-1].start()
+    for copy in copies:
+        copy.wait()
+
+
+def attend_forward(heads, span, order, length, qkv, cos, sin):
+    rows = qkv.shape[0]
+    pairs = qkv.shape[1] // (3 * LANES)
+    column = lambda offset: pl.BlockSpec((rows, LANES), lambda i, *_: (0, offset + i))
+    fixed = pl.BlockSpec((rows, LANES), lambda i, *_: (0, 0))
+    flat = jax.ShapeDtypeStruct((rows, pairs * LANES), jnp.bfloat16)
+    return pl.pallas_call(
+        functools.partial(attend_kernel, heads, span),
+        grid_spec=pltpu.PrefetchScalarGridSpec(
+            num_scalar_prefetch=2,
+            grid=(pairs,),
+            in_specs=[column(0), column(pairs), column(2 * pairs), fixed, fixed],
+            out_specs=[column(0)] * 4 + [pl.BlockSpec((1, 8, rows), lambda i, *_: (i, 0, 0))],
+            scratch_shapes=[pltpu.VMEM((rows, LANES), jnp.float32)] * 3
+            + [pltpu.VMEM((LANES, rows), jnp.float32)],
+        ),
+        out_shape=[flat] * 4 + [jax.ShapeDtypeStruct((pairs, 8, rows), jnp.float32)],
+        compiler_params=pltpu.CompilerParams(vmem_limit_bytes=40 << 20),
+        cost_estimate=pl.CostEstimate(
+            flops=4 * heads * rows * rows * HD,
+            bytes_accessed=rows * pairs * LANES * 24,
+            transcendentals=heads * rows * rows,
+        ),
+        name="attend",
+    )(order, length, qkv, qkv, qkv, cos, sin)
+
+
+def attend_backward(heads, span, order, length, kept, attend, grad_attend, cos, sin):
+    queries, keys, values, logs = kept
+    rows = queries.shape[0]
+    pairs = queries.shape[1] // LANES
+    column = pl.BlockSpec((rows, LANES), lambda i, *_: (0, i))
+    fixed = pl.BlockSpec((rows, LANES), lambda i, *_: (0, 0))
+    return pl.pallas_call(
+        functools.partial(attend_back_kernel, heads, span),
+        grid_spec=pltpu.PrefetchScalarGridSpec(
+            num_scalar_prefetch=2,
+            grid=(pairs,),
+            in_specs=[column] * 3
+            + [pl.BlockSpec((1, 8, rows), lambda i, *_: (i, 0, 0)), column, column, fixed, fixed],
+            out_specs=pl.BlockSpec(memory_space=pl.ANY),
+            scratch_shapes=[pltpu.VMEM((rows, LANES), jnp.float32)] * 2
+            + [pltpu.VMEM((LANES, rows), jnp.float32)]
+            + [pltpu.VMEM((rows, LANES), jnp.float32)] * 3
+            + [pltpu.VMEM((3, rows, LANES), jnp.bfloat16), pltpu.SemaphoreType.DMA((3,))],
+        ),
+        out_shape=jax.ShapeDtypeStruct((rows, 3 * pairs * LANES), jnp.bfloat16),
+        compiler_params=pltpu.CompilerParams(vmem_limit_bytes=40 << 20),
+        cost_estimate=pl.CostEstimate(
+            flops=10 * heads * rows * rows * HD,
+            bytes_accessed=rows * pairs * LANES * 16,
+            transcendentals=heads * rows * rows,
+        ),
+        name="attend_back",
+    )(order, length, queries, keys, values, logs, attend, grad_attend, cos, sin)
+
+
+def swap_pairs():
+    return [(0, 1), (1, 0)]
+
+
+class LineGather:
+    def __init__(self, block, axis, size):
+        self.axis, self.size = axis, size
+        self.ups, self.downs = [block], [block]
+
+    def step(self):
+        done = len(self.ups)
+        up_pairs = [(i, i + 1) for i in range(done - 1, self.size - 1)]
+        down_pairs = [(i, i - 1) for i in range(1, self.size - done + 1)]
+        self.ups.append(lax.ppermute(self.ups[-1], self.axis, up_pairs))
+        self.downs.append(lax.ppermute(self.downs[-1], self.axis, down_pairs))
+
+    def held(self):
+        return (self.ups[-1], self.downs[-1])
+
+    def hold(self, values):
+        self.ups[-1], self.downs[-1] = values
+
+    def near(self, mask):
+        place = lax.axis_index(self.axis)
+        found = None
+        for here in range(self.size):
+            there = here ^ mask
+            block = self.ups[here - there] if there < here else self.downs[there - here]
+            found = block if found is None else jnp.where(place == here, block, found)
+        return found
+
+    def before(self, count):
+        if count == 0:
+            return self.ups[0]
+        place = lax.axis_index(self.axis)
+        return jnp.where(place >= count, self.ups[count], self.downs[self.size - count])
+
+
+class LineScatter:
+    def __init__(self, parts, axis, size):
+        self.axis, self.size, self.parts = axis, size, parts
+        self.done = 0
+        self.up = self.down = None
+
+    def part(self, offsets):
+        place = lax.axis_index(self.axis)
+        masks = {}
+        for here, there in offsets:
+            masks.setdefault(here ^ there, []).append(here)
+        found = None
+        for mask, places in sorted(masks.items()):
+            if found is None:
+                found = self.parts[mask]
+                continue
+            chosen = functools.reduce(jnp.logical_or, [place == here for here in places])
+            found = jnp.where(chosen, self.parts[mask], found)
+        return found
+
+    def step(self):
+        self.done += 1
+        gap = self.size - self.done
+        ups = [(i, i + gap) for i in range(self.done)]
+        downs = [(i, i - gap) for i in range(gap, self.size)]
+        up, down = self.part(ups), self.part(downs)
+        if self.done > 1:
+            up = (up.astype(jnp.float32) + self.up.astype(jnp.float32)).astype(jnp.bfloat16)
+            down = (down.astype(jnp.float32) + self.down.astype(jnp.float32)).astype(jnp.bfloat16)
+        self.up = lax.ppermute(up, self.axis, [(i, i + 1) for i, _ in ups])
+        self.down = lax.ppermute(down, self.axis, [(i, i - 1) for i, _ in downs])
+
+    def held(self):
+        return (self.up, self.down)
+
+    def hold(self, values):
+        self.up, self.down = values
+
+    def total(self):
+        return (
+            self.parts[0].astype(jnp.float32)
+            + self.up.astype(jnp.float32)
+            + self.down.astype(jnp.float32)
+        )
+
+
+def stage(chains, *arrays):
+    held = [chain.held() for chain in chains]
+    held, arrays = lax.optimization_barrier((held, arrays))
+    for chain, values in zip(chains, held):
+        chain.hold(values)
+    return arrays
+
+
+def column_split(
+    shape,
+    tokens,
+    lengths,
+    span_order,
+    attn_gain,
+    w_query,
+    w_key,
+    w_value,
+    w_out,
+    mlp_gain,
+    w_gate,
+    w_up,
+    w_down,
+    cotangent,
+):
+    shards, lines, cores = shape["shard"], shape["ctx"], shape["tensor"]
+    line = lax.axis_index("ctx")
+    core = lax.axis_index("tensor")
+    per_half = lines // cores
+    owner = core == line // per_half
+    sub = line % per_half
+    slot_count, row_count, width = tokens.shape
+    all_rows = row_count * lines
+    heads = w_query.shape[1] * cores // lines // HD
+    head_cols = heads * HD
+    pad_cols = -(-head_cols // LANES) * LANES
+    widen = lambda v, dim: jnp.pad(v, [(0, pad_cols - head_cols if d == dim else 0) for d in (0, 1)])
+    unit_cols = w_gate.shape[1] * cores // lines
+
+    def column_piece(weights, shape_up=lambda v: v):
+        cut = [
+            shape_up(
+                lax.dynamic_slice_in_dim(w, sub * (w.shape[1] // per_half), w.shape[1] // per_half, 1)
+            )
+            for w in weights
+        ]
+        return jnp.concatenate(cut, axis=1) if len(cut) > 1 else cut[0]
+
+    def row_piece(w):
+        return lax.dynamic_slice_in_dim(w, sub * (w.shape[0] // per_half), w.shape[0] // per_half, 0)
+
+    def to_pair(piece):
+        rows = piece.shape[0] // cores
+        keep = lax.dynamic_slice_in_dim(piece, core * rows, rows, 0)
+        give = lax.dynamic_slice_in_dim(piece, (1 - core) * rows, rows, 0)
+        got = lax.ppermute(give, "tensor", swap_pairs())
+        return jnp.where(owner, keep, got)
+
+    def gather_columns(piece):
+        return lax.all_gather(to_pair(piece), ("shard", "tensor"), axis=0, tiled=True)
+
+    def gather_rows(w):
+        mine = to_pair(row_piece(w))
+        got = lax.all_gather(mine, ("shard", "tensor"), axis=0, tiled=True)
+        rows = cores * mine.shape[0]
+        return jnp.concatenate([got[k * rows : (k + 1) * rows] for k in range(shards)], axis=1)
+
+    def reduce_pair(grad):
+        return lax.psum_scatter(grad, ("shard", "tensor"), scatter_dimension=0, tiled=True)
+
+    def by_shard(grad):
+        cols = width // shards
+        return jnp.concatenate([grad[:, k * cols : (k + 1) * cols] for k in range(shards)], axis=0)
+
+    def gathered_halves(chain):
+        rows, cols = chain.ups[0].shape
+        ring = jnp.stack([chain.before(k) for k in range(lines)])
+        take = lambda half: jnp.stack(
+            [
+                lax.dynamic_index_in_dim(ring, (line - half * per_half - k) % lines, 0, False)
+                for k in range(per_half)
+            ]
+        )
+        other = lax.ppermute(take(1 - core), "tensor", swap_pairs())
+        own = take(core)
+        first = jnp.where(core == 0, own, other)
+        second = jnp.where(core == 0, other, own)
+        return [[first[k], second[k]] for k in range(per_half)]
+
+    def spread_columns(chain, count, used):
+        pieces = gathered_halves(chain)
+        each = pieces[0][0].shape[1] // count
+        cut = lambda k: jnp.concatenate(
+            [
+                jnp.concatenate([piece[:, k * each : k * each + used] for piece in row], axis=1)
+                for row in zip(*pieces)
+            ],
+            axis=0,
+        )
+        return [cut(k).astype(jnp.float32) for k in range(count)]
+
+    def spread_rows(chain):
+        pieces = gathered_halves(chain)
+        return jnp.concatenate([p for quarter in pieces for p in quarter], axis=0).astype(
+            jnp.float32
+        )
+
+    def walk(block):
+        return LineGather(block, "ctx", lines)
+
+    def add_up(parts):
+        return LineScatter(parts, "ctx", lines)
+
+    def blocks_of(v):
+        v = v.astype(jnp.bfloat16)
+        return [v[k * row_count : (k + 1) * row_count] for k in range(v.shape[0] // row_count)]
+
+    length = lengths[core]
+    offsets = jnp.arange(row_count // 2, dtype=jnp.int32)
+    stored_pos = (span_order[:, None] * (row_count // 2) + offsets[None, :]).reshape(lines, row_count)
+    ring_pos = stored_pos[line ^ jnp.arange(lines)].reshape(-1)
+    own_pos = ring_pos[:row_count]
+    span = row_count // 2
+    order = ring_pos[::span] // span
+    frequency = ROPE_BASE ** (-(jnp.arange(HD // 2) * 2).astype(jnp.float32) / HD)
+    angles = jnp.arange(all_rows, dtype=jnp.float32)[:, None] * jnp.tile(frequency, 2 * LANES // HD)
+    cos_all, sin_all = jnp.cos(angles), jnp.sin(angles)
+    live_all = (ring_pos < length).astype(jnp.float32)[:, None]
+    live_own = live_all[:row_count]
+    gains = lax.all_gather(jnp.stack([attn_gain, mlp_gain]), "shard", axis=1, tiled=True)
+    gain_a = gains[0].astype(jnp.float32)
+    gain_b = gains[1].astype(jnp.float32)
+    own_tokens = lax.dynamic_index_in_dim(tokens, core, 0, keepdims=False)
+    own_cot = lax.dynamic_index_in_dim(cotangent, core, 0, keepdims=False)
+
+    qkv_w = gather_columns(column_piece([w_query, w_key, w_value], lambda v: widen(v, 1)))
+    out_w = widen(gather_rows(w_out), 0)
+    gate_up_w = gather_columns(column_piece([w_gate, w_up]))
+    down_w = gather_rows(w_down)
+
+    tokens_line = walk(own_tokens)
+    for _ in range(lines - 1):
+        tokens_line.step()
+    all_tokens = jnp.concatenate([tokens_line.near(k) for k in range(lines)], axis=0)
+    first_in = (norm_parts(all_tokens.astype(jnp.float32))[0] * gain_a).astype(jnp.bfloat16)
+    first_in, own_cot = stage([], first_in, own_cot)
+
+    cot_line = walk(own_cot)
+    cot_line.step()
+    qkv = plain_product(first_in, qkv_w)
+    attend, *kept = attend_forward(heads, span, order, length.reshape(1), qkv, cos_all, sin_all)
+    attn_part = plain_product(attend, out_w).astype(jnp.bfloat16)
+    (attn_part,) = stage([cot_line], attn_part)
+
+    attn_line = add_up(blocks_of(attn_part))
+    attn_line.step()
+    cot_line.step()
+    stage([attn_line, cot_line])
+    attn_line.step()
+    cot_line.step()
+    stage([attn_line, cot_line])
+    attn_line.step()
+    all_cot = jnp.concatenate([cot_line.near(k) for k in range(lines)], axis=0)
+    grad_mlp = (BRANCH_SCALE * (all_cot.astype(jnp.float32) * live_all)).astype(jnp.bfloat16)
+    half_rows = all_rows // 2
+    grad_hidden = [
+        col_product(grad_mlp[k * half_rows : (k + 1) * half_rows], down_w).astype(jnp.float32)
+        for k in range(2)
+    ]
+    grad_hidden = stage([attn_line], *grad_hidden)
+    own_x = own_tokens.astype(jnp.float32)
+    middle = own_x + BRANCH_SCALE * attn_line.total()
+    normed_two, inverse_two = norm_parts(middle)
+
+    second_line = walk((normed_two * gain_b).astype(jnp.bfloat16))
+    second_line.step()
+    stage([second_line])
+
+    def units(second_half, grad_half):
+        gate_up = plain_product(second_half, gate_up_w)
+        gate_proj = gate_up[:, :unit_cols]
+        up_proj = gate_up[:, unit_cols:]
+        gate_sig = jax.nn.sigmoid(gate_proj)
+        gate_act = gate_proj * gate_sig
+        hidden_half = (gate_act * up_proj).astype(jnp.bfloat16)
+        grad_gate_b = (
+            grad_half * up_proj * gate_sig * (1.0 + gate_proj * (1.0 - gate_sig))
+        ).astype(jnp.bfloat16)
+        grad_up_b = (grad_half * gate_act).astype(jnp.bfloat16)
+        return hidden_half, jnp.concatenate([grad_gate_b, grad_up_b], axis=1)
+
+    near_half = jnp.concatenate([second_line.near(k) for k in range(lines // 2)], axis=0)
+    second_line.step()
+    hidden_near, grad_near = units(near_half, grad_hidden[0])
+    hidden_near, grad_near = stage([second_line], hidden_near, grad_near)
+    second_line.step()
+    part_near = col_product(grad_near, gate_up_w).astype(jnp.bfloat16)
+    (part_near,) = stage([second_line], part_near)
+    far_half = jnp.concatenate([second_line.near(k) for k in range(lines // 2, lines)], axis=0)
+    hidden_far, grad_far = units(far_half, grad_hidden[1])
+    part_far = col_product(grad_far, gate_up_w).astype(jnp.bfloat16)
+
+    grad_line = add_up(blocks_of(part_near) + blocks_of(part_far))
+    grad_line.step()
+    hidden = jnp.concatenate([hidden_near, hidden_far], axis=0)
+    second_in = jnp.concatenate([near_half, far_half], axis=0)
+    grad_gate_up = jnp.concatenate([grad_near, grad_far], axis=0)
+    down_grad = by_shard(row_product(hidden, grad_mlp).astype(jnp.bfloat16))
+    (down_grad,) = stage([grad_line], down_grad)
+    grad_line.step()
+    down_piece = reduce_pair(down_grad)
+    gate_up_grad = row_product(second_in, grad_gate_up).astype(jnp.bfloat16)
+    (gate_up_grad,) = stage([grad_line], gate_up_grad)
+    gate_up_piece = reduce_pair(gate_up_grad)
+    grad_line.step()
+    mlp_part = plain_product(hidden, down_w).astype(jnp.bfloat16)
+    (mlp_part,) = stage([grad_line], mlp_part)
+    grad_second = grad_line.total()
+
+    own_dy = own_cot.astype(jnp.float32) * live_own
+    grad_gain_two = jnp.sum(grad_second * normed_two, axis=0)
+    grad_middle = own_dy + norm_back(grad_second, normed_two, inverse_two, gain_b)
+    attn_grad_line = walk((BRANCH_SCALE * grad_middle).astype(jnp.bfloat16))
+    attn_grad_line.step()
+    stage([attn_grad_line])
+    attn_grad_line.step()
+    (down_piece,) = stage([attn_grad_line], down_piece)
+    attn_grad_line.step()
+    gate_up_piece, down_piece = stage([attn_grad_line], gate_up_piece, down_piece)
+    grad_attn = jnp.concatenate([attn_grad_line.near(k) for k in range(lines)], axis=0)
+
+    down_line = walk(down_piece)
+    gate_up_line = walk(gate_up_piece)
+    mlp_line = add_up(blocks_of(mlp_part))
+    mlp_line.step()
+    down_line.step()
+    gate_up_line.step()
+    out_grad = by_shard(row_product(attend, grad_attn)[:head_cols].astype(jnp.bfloat16))
+    out_piece = reduce_pair(out_grad)
+    grad_attend = col_product(grad_attn, out_w).astype(jnp.bfloat16)
+    grad_qkv = attend_backward(
+        heads, span, order, length.reshape(1), kept, attend, grad_attend, cos_all, sin_all
+    )
+    moving = [mlp_line, down_line, gate_up_line]
+    (grad_qkv,) = stage(moving, grad_qkv)
+    for chain in moving:
+        chain.step()
+    first_part = col_product(grad_qkv, qkv_w).astype(jnp.bfloat16)
+    qkv_grad = row_product(first_in, grad_qkv).astype(jnp.bfloat16)
+    first_part, qkv_grad, out_piece = stage(moving, first_part, qkv_grad, out_piece)
+    qkv_piece = reduce_pair(qkv_grad)
+    for chain in moving:
+        chain.step()
+    first_line = add_up(blocks_of(first_part))
+    first_line.step()
+    stage(moving + [first_line])
+    first_line.step()
+    layer_rows = ((middle + BRANCH_SCALE * mlp_line.total()) * live_own).astype(jnp.bfloat16)
+    final_down = spread_rows(down_line)
+    out_line = walk(out_piece)
+    out_line.step()
+    layer_rows, final_down, qkv_piece = stage(
+        [first_line, out_line], layer_rows, final_down, qkv_piece
+    )
+    first_line.step()
+    out_line.step()
+    qkv_line = walk(qkv_piece)
+    qkv_line.step()
+    final_gate, final_up = spread_columns(gate_up_line, 2, unit_cols)
+    final_gate, final_up = stage([first_line, out_line, qkv_line], final_gate, final_up)
+    qkv_line.step()
+    out_line.step()
+    grad_first = first_line.total()
+    normed_one, inverse_one = norm_parts(own_x)
+    grad_gain_one = jnp.sum(grad_first * normed_one, axis=0)
+    grad_rows = grad_middle + norm_back(grad_first, normed_one, inverse_one, gain_a)
+
+    gain_sums = lax.psum(jnp.stack([grad_gain_one, grad_gain_two]), ("shard", "ctx", "tensor"))
+    gain_sums, grad_rows = stage([qkv_line, out_line], gain_sums, grad_rows)
+    qkv_line.step()
+    final_out = spread_rows(out_line)
+    stage([qkv_line])
+    final_query, final_key, final_value = spread_columns(qkv_line, 3, head_cols)
+    gain_sums = lax.dynamic_slice_in_dim(
+        gain_sums, lax.axis_index("shard") * (width // shards), width // shards, 1
+    )
+
+    def both_slots(own):
+        other = lax.ppermute(own, "tensor", swap_pairs())
+        return jnp.stack(
+            [jnp.where(core == 0, own, other), jnp.where(core == 0, other, own)], axis=0
+        )
+
+    layer_out = both_slots(layer_rows)
+    grad_tokens = both_slots(grad_rows.astype(jnp.bfloat16)).astype(jnp.float32)
+    return (
+        layer_out,
+        grad_tokens,
+        gain_sums[0],
+        final_query,
+        final_key,
+        final_value,
+        final_out,
+        gain_sums[1],
+        final_gate,
+        final_up,
+        final_down,
+    )
+
+
+def local(shape, *arrays):
+    shards, lines, cores = shape["shard"], shape["ctx"], shape["tensor"]
+    tokens, w_query, w_gate = arrays[0], arrays[4], arrays[9]
+    fits = (
+        cores == 2
+        and tokens.shape[0] == cores
+        and lines % cores == 0
+        and lines == 4
+        and (w_query.shape[1] * cores) % (lines * HD) == 0
+        and (w_gate.shape[1] * cores) % (lines * cores) == 0
+        and w_query.shape[0] % cores == 0
+    )
+    if fits:
+        return column_split(shape, *arrays)
+    return gather_all(*arrays)
+
+
 def solution(mesh):
     placed = (
         P("shard", "ctx", None),
@@ -328,7 +926,7 @@
         P("shard", "ctx", None),
     )
     return jax.shard_map(
-        local,
+        functools.partial(local, dict(mesh.shape)),
         mesh=mesh,
         in_specs=placed,
         out_specs=(

time: 3710 us -> 1240 us (0.33)
  waiting for transfers between devices: 2950 us -> 279 us
  matrix products: 435 us -> 163 us
  starting transfers between devices: 2.89 us -> 203 us
  local copies, waits for them, and re-layouts: 58 us -> 212 us
  other arithmetic: 131 us -> 225 us
  Pallas kernels: 0 us -> 57.3 us
    reduce_scatter x11 -> x3, waiting for transfers between devices: 1990 us -> 0.02 us  [reduce_pair(): lax.psum_scatter(grad, ('shard', 'tensor'), scatter_dimension=0, tiled=True)]
    all_gather x18 -> x4, waiting for transfers between devices: 871 us -> 0.03 us  [the longest x2 0.02 us: gather_rows(): got = lax.all_gather(mine, ('shard', 'tensor'), axis=0, tiled=True)]
    ppermute x0 -> x82, waiting for transfers between devices: none -> 274 us  [the longest x24 215 us: step(): self.downs.append(lax.ppermute(self.downs[-1], self.axis, down_pairs))]
    ppermute x0 -> x82, starting transfers between devices: none -> 203 us  [the longest x12 86.2 us: step(): self.up = lax.ppermute(up, self.axis, [(i, i + 1) for i, _ in ups])]
    dot_general x12 -> x0, matrix products: 112 us -> none  [the longest x2 30.5 us: local(): jnp.einsum('qhd,khd->hqk', grad_attend, value_all, preferred_element_type...]
    unnamed x3 -> x0, blocking collectives: 108 us -> none
    dot_general x14 -> x4, matrix products: 137 us -> 52.7 us  [row_product(): lax.dot_general(left_mat, right_mat, CONTRACT_ROWS, preferred_element_typ...]
    psum x3 -> x0, waiting for transfers between devices: 81.2 us -> none  [the longest x1 28.4 us: local(): lax.psum(col_product(grad_gate_b, gate_w) + col_product(grad_up_b, up_w),...]
  transfers between devices with their start and end apart: 32 -> 90, of which waited for: 28 -> 25; matrix products, arithmetic and copies ran while one was open for 13% -> 44% of each run, Pallas kernels for 0% -> 5%
where the time goes in v2:
time: 1240 us; the launch traced here: 1230 us
  waiting for transfers between devices  279 us (22%)
  other arithmetic  225 us (18%)
  local copies, waits for them, and re-layouts  212 us (17%)
  starting transfers between devices  203 us (16%)
  matrix products  163 us (13%)
  blocking collectives  73.6 us (6%)
  Pallas kernels  57.3 us (5%)
  between operations  16.2 us (1%)
    ppermute x24, waiting for transfers between devices, step(): self.downs.append(lax.ppermute(self.downs[-1], self.axis, down_pairs))  215 us
    ppermute x12, starting transfers between devices, step(): self.up = lax.ppermute(up, self.axis, [(i, i + 1) for i, _ in ups])  86.2 us
    ppermute x24, starting transfers between devices, step(): self.ups.append(lax.ppermute(self.ups[-1], self.axis, up_pairs))  65.3 us
    psum x1, blocking collectives, column_split(): lax.psum(jnp.stack([grad_gain_one, grad_gain_two]), ('shard', 'ctx', 'ten...  64.5 us
    unnamed x162, local copies, waits for them, and re-layouts  63 us
    dot_general x5, matrix products, plain_product(): return jnp.dot(left_mat, right_mat, preferred_element_type=jnp.float32)  56 us
    dot_general x6, matrix products, col_product(): lax.dot_general(left_mat, right_mat, CONTRACT_COLS, preferred_element_typ...  54.3 us
    dot_general x4, matrix products, row_product(): lax.dot_general(left_mat, right_mat, CONTRACT_ROWS, preferred_element_typ...  52.7 us
  transfers between devices with their start and end apart: 90, of which 25 were waited for; matrix products, arithmetic and copies ran while one was open for 44% of the time, Pallas kernels for 5%

profile of v2, /device:TPU:0, one launch (start us, length us, event | category | flops | bytes accessed | tf_op | source)
XLA Modules:
  0.0 1228.5 jit_solution(1328473764002353799)
XLA Ops:
  43.5 6.2 collective-permute-start
  49.7 23.4 %collective-permute-done.1 = bf16[256,2304]{1,0:T(8,128)(2,1)} collective-permute-done((bf16[256,2304]{1,0:T(8,128)(2,1)S(1)}, bf16[256,2304]{1,0:T(8,128)(2,1)}, u32[]{:S(2)}, u32[]{:S(2)}) %collective-permute-start.1) | collective-permute-done | bytes 1179680 | tf_op jit(solution)/shard_map/ppermute | solution.py:516
  77.1 9.1 all-gather
  88.2 14.6 %collective-permute-done.3 = bf16[256,2304]{1,0:T(8,128)(2,1)} collective-permute-done((bf16[256,2304]{1,0:T(8,128)(2,1)}, bf16[256,2304]{1,0:T(8,128)(2,1)}, u32[]{:S(2)}, u32[]{:S(2)}) %collective-permute-start.3) | collective-permute-done | bytes 1179680 | tf_op jit(solution)/shard_map/ppermute | solution.py:516
  109.7 22.0 %collective-permute-done.5 = bf16[256,2304]{1,0:T(8,128)(2,1)} collective-permute-done((bf16[256,2304]{1,0:T(8,128)(2,1)}, bf16[256,2304]{1,0:T(8,128)(2,1)}, u32[]{:S(2)}, u32[]{:S(2)}) %collective-permute-start.5) | collective-permute-done | bytes 1179680 | tf_op jit(solution)/shard_map/ppermute | solution.py:516
  135.0 8.8 fusion.2
  145.1 5.6 collective-permute-start.6
  154.0 5.6 concatenate.102
  159.6 13.9 %fusion.102.q_in.k_in.v_in = f32[1024,1920]{1,0:T(8,128)S(1)} fusion(bf16[1024,2304]{1,0:T(8,128)(2,1)} %fusion.2, bf16[2304,1920]{1,0:T(8,128)(2,1)} %all-gather.7.cloned.1.call-done), kind=kOutput, calls=%fused_computation.293 | convolution fusion | flops 9059696640 | bytes 21430272 | tf_op jit(solution)/shard_map/dot_general | solution.py:30
  173.5 30.3 %attend.1 = (bf16[1024,640]{1,0:T(8,128)(2,1)S(1)}, bf16[1024,640]{1,0:T(8,128)(2,1)S(1)}, bf16[1024,640]{1,0:T(8,128)(2,1)S(1)}, bf16[1024,640]{1,0:T(8,128)(2,1)S(1)}, f32[5,8,1024]{2,1,0:T(8,128)S(1)}) custom-call(s32[8]{0:T(128)S(1)} %and_select_fusion.order, s32[1]{0:T(128)} %dynamic_slice.120.length, f32[1024,1920]{1,0:T(8,128)S(1)} %fusion.102.q_in.k_in.v_in, ...), custom_call_target="tpu_custom_call" | custom-call | flops 2415919104 | bytes 15728640 | tf_op jit(solution)/shard_map/attend/pallas_call | solution.py:451
  216.9 17.2 %collective-permute-done.10 = bf16[256,2304]{1,0:T(8,128)(2,1)S(1)} collective-permute-done((bf16[256,2304]{1,0:T(8,128)(2,1)S(1)}, bf16[256,2304]{1,0:T(8,128)(2,1)S(1)}, u32[]{:S(2)}, u32[]{:S(2)}) %collective-permute-start.10) | collective-permute-done | bytes 1179680 | tf_op jit(solution)/shard_map/ppermute | solution.py:569
  234.0 9.0 collective-permute-done.13
  246.6 12.2 collective-permute-start.14
  261.8 6.1 fusion.90
  283.4 11.6 concatenate.104
  301.2 6.2 collective-permute-start.18
  312.9 5.2 fusion.44
  318.2 5.2 fusion.46
  332.5 6.1 collective-permute-start.21
  338.6 17.1 %collective-permute-done.22 = bf16[256,2304]{1,0:T(8,128)(2,1)} collective-permute-done((bf16[256,2304]{1,0:T(8,128)(2,1)S(1)}, bf16[256,2304]{1,0:T(8,128)(2,1)}, u32[]{:S(2)}, u32[]{:S(2)}) %collective-permute-start.22) | collective-permute-done | bytes 1179680 | tf_op jit(solution)/shard_map/ppermute | solution.py:516
  362.9 12.7 %fusion.48 = f32[512,2880]{0,1:T(8,128)} fusion(bf16[2304,2880]{1,0:T(8,128)(2,1)} %all-gather.11.cloned.1.call-done, bf16[256,2304]{1,0:T(8,128)(2,1)} %fusion.59, bf16[256,2304]{1,0:T(8,128)(2,1)S(1)} %multiply_convert_fusion.9), kind=kOutput, calls=%fused_computation.104 | convolution fusion | flops 6799491072 | bytes 21528576 | tf_op jit(solution)/shard_map/dot_general | solution.py:30
  375.6 5.4 multiply_convert_fusion.5
  381.2 5.3 collective-permute-done.24
  388.5 12.5 %convolution_convert_fusion.8 = bf16[512,2304]{1,0:T(8,128)(2,1)} fusion(bf16[512,2880]{0,1:T(8,128)(2,1)S(1)} %pad_maximum_fusion.8, bf16[2304,2880]{1,0:T(8,128)(2,1)} %all-gather.11.cloned.1.call-done), kind=kOutput, calls=%fused_computation.33 | convolution fusion | flops 6795952128 | bytes 18579456 | tf_op jit(solution)/shard_map/dot_general | solution.py:26
  403.8 6.1 collective-permute-done.27
  411.3 12.6 %fusion.52 = f32[512,2880]{0,1:T(8,128)} fusion(bf16[2304,2880]{1,0:T(8,128)(2,1)} %all-gather.11.cloned.1.call-done, bf16[256,2304]{1,0:T(8,128)(2,1)S(1)} %select_select_fusion.9, bf16[256,2304]{1,0:T(8,128)(2,1)} %select_select_fusion.2), kind=kOutput, calls=%fused_computation.108 | convolution fusion | flops 6799491072 | bytes 21528576 | tf_op jit(solution)/shard_map/dot_general | solution.py:30
  423.8 5.4 multiply_convert_fusion.3
  430.3 13.1 %convolution_convert_fusion.7 = bf16[512,2304]{1,0:T(8,128)(2,1)} fusion(bf16[2304,2880]{1,0:T(8,128)(2,1)} %all-gather.11.cloned.1.call-done, bf16[512,1440]{0,1:T(8,128)(2,1)} %get-tuple-element.268, bf16[512,1440]{0,1:T(8,128)(2,1)S(1)} %get-tuple-element.267), kind=kOutput, calls=%fused_computation.32 | convolution fusion | flops 6801850368 | bytes 18579456 | tf_op jit(solution)/shard_map/dot_general | solution.py:26
  451.5 9.7 convolution_convert_fusion.2
  463.5 24.4 %pad_maximum_fusion.1 = bf16[5760,576]{1,0:T(8,128)(2,1)} fusion(bf16[1440,576]{1,0:T(8,128)(2,1)S(1)} %get-tuple-element.276, bf16[1440,576]{1,0:T(8,128)(2,1)S(1)} %get-tuple-element.277, bf16[1440,576]{1,0:T(8,128)(2,1)S(1)} %get-tuple-element.278, bf16[1440,576]{1,0:T(8,128)(2,1)S(1)} %get-tuple-element.275), kind=kLoop, calls=%fused_computation.11 | loop fusion | flops 26542080 | bytes 13271040 | tf_op jit(solution)/shard_map/concatenate | solution.py:657
  496.1 25.7 %convolution_convert_fusion = bf16[2304,2880]{0,1:T(8,128)(2,1)} fusion(bf16[512,1440]{0,1:T(8,128)(2,1)} %get-tuple-element.268, bf16[512,1440]{0,1:T(8,128)(2,1)S(1)} %copy-done.49, bf16[512,2880]{0,1:T(8,128)(2,1)} %copy-done.41, bf16[256,2304]{1,0:T(8,128)(2,1)} %copy-done.53, bf16[256,2304]{1,0:T(8,128)(2,1)} %select_select_fusion.2, ...), kind=kOutput, calls=%fused_computation.1 | convolution fusion | flops 13632749568 | bytes 23887872 | tf_op jit(solution)/shard_map/dot_general | solution.py:22
  521.8 18.3 %copy.78 = bf16[2304,2880]{1,0:T(8,128)(2,1)} copy(bf16[2304,2880]{0,1:T(8,128)(2,1)} %convolution_convert_fusion) | data formatting | bytes 26542080
  550.7 12.8 %convolution_convert_fusion.5 = bf16[1024,2304]{1,0:T(8,128)(2,1)} fusion(bf16[1440,2304]{1,0:T(8,128)(2,1)} %concatenate.104, bf16[512,1440]{0,1:T(8,128)(2,1)S(1)} %copy-done.47, bf16[512,1440]{0,1:T(8,128)(2,1)S(1)} %copy-done.45), kind=kOutput, calls=%fused_computation.21 | convolution fusion | flops 6803030016 | bytes 14303232 | tf_op jit(solution)/shard_map/dot_general | solution.py:30
  572.0 5.1 collective-permute-start.36
  577.2 16.0 %collective-permute-done.37 = bf16[256,2304]{1,0:T(8,128)(2,1)S(1)} collective-permute-done((bf16[256,2304]{1,0:T(8,128)(2,1)S(1)}, bf16[256,2304]{1,0:T(8,128)(2,1)S(1)}, u32[]{:S(2)}, u32[]{:S(2)}) %collective-permute-start.37) | collective-permute-done | bytes 1179680 | tf_op jit(solution)/shard_map/ppermute | solution.py:516
  595.2 39.8 %collective-permute-done.39 = bf16[256,2304]{1,0:T(8,128)(2,1)} collective-permute-done((bf16[256,2304]{1,0:T(8,128)(2,1)S(1)}, bf16[256,2304]{1,0:T(8,128)(2,1)}, u32[]{:S(2)}, u32[]{:S(2)}) %collective-permute-start.39) | collective-permute-done | bytes 1179680 | tf_op jit(solution)/shard_map/ppermute | solution.py:516
  642.1 6.6 collective-permute-start.34
  665.1 5.9 collective-permute-start.44
  673.2 5.1 convolution_convert_fusion.6
  678.3 4.9 fusion.65.do_in
  689.4 5.5 collective-permute-start.42
  694.8 8.0 pad_maximum_fusion.10
  708.2 27.0 %attend_back.1 = bf16[1024,1920]{1,0:T(8,128)(2,1)S(1)} custom-call(s32[8]{0:T(128)S(1)} %and_select_fusion.order, s32[1]{0:T(128)} %dynamic_slice.120.length, bf16[1024,640]{1,0:T(8,128)(2,1)S(1)} %copy-done.5, bf16[1024,640]{1,0:T(8,128)(2,1)S(1)} %copy-done.7, bf16[1024,640]{1,0:T(8,128)(2,1)S(1)} %copy-done.9, ...), custom_call_target="tpu_custom_call" | custom-call | flops 6039797760 | bytes 10485760 | tf_op jit(solution)/shard_map/attend_back/pallas_call | solution.py:478
  741.5 8.6 collective-permute-start.46
  751.9 13.4 %convolution_convert_fusion.3 = bf16[1024,2304]{1,0:T(8,128)(2,1)} fusion(bf16[1024,1920]{1,0:T(8,128)(2,1)S(1)} %attend_back.1, bf16[2304,1920]{1,0:T(8,128)(2,1)} %all-gather.7.cloned.1.call-done), kind=kOutput, calls=%fused_computation.19 | convolution fusion | flops 9062055936 | bytes 17498112 | tf_op jit(solution)/shard_map/dot_general | solution.py:26
  766.7 12.2 convolution_convert_fusion.1
  778.9 26.5 %collective-permute-done.51 = bf16[288,2880]{1,0:T(8,128)(2,1)} collective-permute-done((bf16[288,2880]{1,0:T(8,128)(2,1)}, bf16[288,2880]{1,0:T(8,128)(2,1)}, u32[]{:S(2)}, u32[]{:S(2)}) %collective-permute-start.51) | collective-permute-done | bytes 1658912 | tf_op jit(solution)/shard_map/ppermute | solution.py:516
  818.3 23.6 %collective-permute-start.58 = (bf16[256,2304]{1,0:T(8,128)(2,1)}, bf16[256,2304]{1,0:T(8,128)(2,1)}, u32[]{:S(2)}, u32[]{:S(2)}) collective-permute-start(bf16[256,2304]{1,0:T(8,128)(2,1)} %slice.285), channel_id=1, source_target_pairs={{0,2},{1,3},{8,10},{9,11},{16,18},{17,19},{24,26},{25,27}} | collective-permute-start | bytes 3538952 | tf_op jit(solution)/shard_map/ppermute | solution.py:569
  841.9 8.7 collective-permute-done.55
  851.9 5.6 collective-permute-start.52
  888.3 24.0 %collective-permute-done.53 = bf16[256,2304]{1,0:T(8,128)(2,1)} collective-permute-done((bf16[256,2304]{1,0:T(8,128)(2,1)}, bf16[256,2304]{1,0:T(8,128)(2,1)}, u32[]{:S(2)}, u32[]{:S(2)}) %collective-permute-start.53) | collective-permute-done | bytes 1179680 | tf_op jit(solution)/shard_map/ppermute | solution.py:570
  940.3 6.3 copy.71
  971.7 9.5 maximum_convert_fusion
  981.2 6.2 copy.72
  998.0 5.6 collective-permute-start.70
  1009.6 5.6 collective-permute-start.66
  1017.1 18.5 %maximum_convert_fusion.2 = f32[576,2880]{0,1:T(8,128)} fusion(bf16[288,1440]{0,1:T(8,128)(2,1)S(1)} %get-tuple-element.341, bf16[288,1440]{0,1:T(8,128)(2,1)S(1)} %copy-done.35, bf16[288,1440]{0,1:T(8,128)(2,1)S(1)} %copy-done.34, bf16[288,1440]{0,1:T(8,128)(2,1)S(1)} %copy-done.33), kind=kLoop, calls=%fused_computation.52 | loop fusion | flops 13271040 | bytes 9953280 | tf_op jit(solution)/shard_map/convert_element_type | solution.py:684
  1037.3 18.6 %maximum_convert_fusion.1 = f32[576,2880]{0,1:T(8,128)} fusion(bf16[288,1440]{0,1:T(8,128)(2,1)S(1)} %get-tuple-element.342, bf16[288,1440]{0,1:T(8,128)(2,1)S(1)} %copy-done.32, bf16[288,1440]{0,1:T(8,128)(2,1)S(1)} %copy-done.31, bf16[288,1440]{0,1:T(8,128)(2,1)S(1)} %copy-done.30), kind=kLoop, calls=%fused_computation.51 | loop fusion | flops 13271040 | bytes 9953280 | tf_op jit(solution)/shard_map/convert_element_type | solution.py:684
  1055.9 8.7 copy.77
  1064.6 6.0 collective-permute-done.69
  1084.7 8.6 copy.75
  1093.3 8.6 copy.76
  1101.9 64.5 %psum.7 = f32[2,2304]{1,0:T(2,128)S(1)} all-reduce(f32[2,2304]{1,0:T(2,128)S(1)} %pad_maximum_fusion.29), channel_id=1, replica_groups=mesh['shard'=4,'ctx'=4,'tensor'=2] {'shard','ctx','tensor'}, use_global_device_ids=true, to_apply=%region_10.11 | all-reduce | flops 4608 | bytes 36864 | tf_op jit(solution)/shard_map/psum | solution.py:862
  1175.8 20.9 %collective-permute-done.79 = bf16[288,1920]{1,0:T(8,128)(2,1)S(1)} collective-permute-done((bf16[288,1920]{1,0:T(8,128)(2,1)}, bf16[288,1920]{1,0:T(8,128)(2,1)S(1)}, u32[]{:S(2)}, u32[]{:S(2)}) %collective-permute-start.79) | collective-permute-done | bytes 1105952 | tf_op jit(solution)/shard_map/ppermute | solution.py:516
  (471 shorter events, 379.1 us)
Async XLA Ops:
  7.2 143.5 %all-gather.9.cloned.1.call-start = ((), (), s32[]{:S(2)}) async-start(), calls=%async_computation.5 | async-start | bytes 3317760 | tf_op jit(solution)/shard_map/all_gather | solution.py:648
  12.8 146.7 %all-gather.7.cloned.1.call-start = ((), (), s32[]{:S(2)}) async-start(), calls=%async_computation.4 | async-start | bytes 9953280 | tf_op jit(solution)/shard_map/all_gather | solution.py:644
  20.9 240.9 %all-gather.13.cloned.1.call-start = ((), (), s32[]{:S(2)}) async-start(), calls=%async_computation.10 | async-start | bytes 7962624 | tf_op jit(solution)/shard_map/all_gather | solution.py:648
  28.9 334.0 %all-gather.11.cloned.1.call-start = ((), (), s32[]{:S(2)}) async-start(), calls=%async_computation.6 | async-start | bytes 15261696 | tf_op jit(solution)/shard_map/all_gather | solution.py:644
  39.9 595.1 %reduce-scatter.7.cloned.1.call-start = ((), (), s32[]{:S(2)}) async-start(), calls=%async_computation.7 | async-start | bytes 8294400 | tf_op jit(solution)/shard_map/reduce_scatter | solution.py:653
  42.2 30.9 %collective-permute-start.1 = (bf16[256,2304]{1,0:T(8,128)(2,1)S(1)}, bf16[256,2304]{1,0:T(8,128)(2,1)}, u32[]{:S(2)}, u32[]{:S(2)}) collective-permute-start(bf16[256,2304]{1,0:T(8,128)(2,1)S(1)} %get-tuple-element.256), channel_id=1, source_target_pairs={{2,0},{4,2},{6,4},{3,1},{5,3},{7,5},{10,8},{12,10},{14,12},{11,9},... | collective-permute-start | bytes 3538952 | tf_op jit(solution)/shard_map/ppermute | solution.py:516
  43.5 30.9 %collective-permute-start = (bf16[256,2304]{1,0:T(8,128)(2,1)S(1)}, bf16[256,2304]{1,0:T(8,128)(2,1)}, u32[]{:S(2)}, u32[]{:S(2)}) collective-permute-start(bf16[256,2304]{1,0:T(8,128)(2,1)S(1)} %get-tuple-element.256), channel_id=1, source_target_pairs={{0,2},{2,4},{4,6},{1,3},{3,5},{5,7},{8,10},{10,12},{12,14},{9,11},... | collective-permute-start | bytes 3538952 | tf_op jit(solution)/shard_map/ppermute | solution.py:515
  73.1 29.7 %collective-permute-start.3 = (bf16[256,2304]{1,0:T(8,128)(2,1)}, bf16[256,2304]{1,0:T(8,128)(2,1)}, u32[]{:S(2)}, u32[]{:S(2)}) collective-permute-start(bf16[256,2304]{1,0:T(8,128)(2,1)} %collective-permute-done.1), channel_id=1, source_target_pairs={{2,0},{4,2},{3,1},{5,3},{10,8},{12,10},{11,9},{13,11},{18,16},{20,... | collective-permute-start | bytes 3538952 | tf_op jit(solution)/shard_map/ppermute | solution.py:516
  74.4 29.7 %collective-permute-start.2 = (bf16[256,2304]{1,0:T(8,128)(2,1)}, bf16[256,2304]{1,0:T(8,128)(2,1)}, u32[]{:S(2)}, u32[]{:S(2)}) collective-permute-start(bf16[256,2304]{1,0:T(8,128)(2,1)} %collective-permute-done), channel_id=1, source_target_pairs={{2,4},{4,6},{3,5},{5,7},{10,12},{12,14},{11,13},{13,15},{18,20},{2... | collective-permute-start | bytes 3538952 | tf_op jit(solution)/shard_map/ppermute | solution.py:515
  102.8 28.8 %collective-permute-start.5 = (bf16[256,2304]{1,0:T(8,128)(2,1)}, bf16[256,2304]{1,0:T(8,128)(2,1)}, u32[]{:S(2)}, u32[]{:S(2)}) collective-permute-start(bf16[256,2304]{1,0:T(8,128)(2,1)} %collective-permute-done.3), channel_id=1, source_target_pairs={{2,0},{3,1},{10,8},{11,9},{18,16},{19,17},{26,24},{27,25}} | collective-permute-start | bytes 3538952 | tf_op jit(solution)/shard_map/ppermute | solution.py:516
  104.1 27.5 %collective-permute-start.4 = (bf16[256,2304]{1,0:T(8,128)(2,1)}, bf16[256,2304]{1,0:T(8,128)(2,1)}, u32[]{:S(2)}, u32[]{:S(2)}) collective-permute-start(bf16[256,2304]{1,0:T(8,128)(2,1)} %collective-permute-done.2), channel_id=1, source_target_pairs={{4,6},{5,7},{12,14},{13,15},{20,22},{21,23},{28,30},{29,31}} | collective-permute-start | bytes 3538952 | tf_op jit(solution)/shard_map/ppermute | solution.py:515
  143.8 64.2 %collective-permute-start.7 = (bf16[256,2304]{1,0:T(8,128)(2,1)}, bf16[256,2304]{1,0:T(8,128)(2,1)}, u32[]{:S(2)}, u32[]{:S(2)}) collective-permute-start(bf16[256,2304]{1,0:T(8,128)(2,1)} %dynamic-slice_bitcast_fusion), channel_id=1, source_target_pairs={{2,0},{4,2},{6,4},{3,1},{5,3},{7,5},{10,8},{12,10},{14,12},{11,9},... | collective-permute-start | bytes 3538952 | tf_op jit(solution)/shard_map/ppermute | solution.py:516
  145.1 62.9 %collective-permute-start.6 = (bf16[256,2304]{1,0:T(8,128)(2,1)}, bf16[256,2304]{1,0:T(8,128)(2,1)}, u32[]{:S(2)}, u32[]{:S(2)}) collective-permute-start(bf16[256,2304]{1,0:T(8,128)(2,1)} %dynamic-slice_bitcast_fusion), channel_id=1, source_target_pairs={{0,2},{2,4},{4,6},{1,3},{3,5},{5,7},{8,10},{10,12},{12,14},{9,11},... | collective-permute-start | bytes 3538952 | tf_op jit(solution)/shard_map/ppermute | solution.py:515
  214.9 28.2 %collective-permute-start.13 = (bf16[256,2304]{1,0:T(8,128)(2,1)}, bf16[256,2304]{1,0:T(8,128)(2,1)}, u32[]{:S(2)}, u32[]{:S(2)}) collective-permute-start(bf16[256,2304]{1,0:T(8,128)(2,1)} %collective-permute-done.7), channel_id=1, source_target_pairs={{2,0},{4,2},{3,1},{5,3},{10,8},{12,10},{11,9},{13,11},{18,16},{20,... | collective-permute-start | bytes 3538952 | tf_op jit(solution)/shard_map/ppermute | solution.py:516
  244.9 51.9 %collective-permute-start.15 = (bf16[256,2304]{1,0:T(8,128)(2,1)}, bf16[256,2304]{1,0:T(8,128)(2,1)}, u32[]{:S(2)}, u32[]{:S(2)}) collective-permute-start(bf16[256,2304]{1,0:T(8,128)(2,1)} %get-tuple-element.293), channel_id=1, source_target_pairs={{4,2},{6,4},{5,3},{7,5},{12,10},{14,12},{13,11},{15,13},{20,18},{2... | collective-permute-start | bytes 3538952 | tf_op jit(solution)/shard_map/ppermute | solution.py:570
  246.6 50.2 %collective-permute-start.14 = (bf16[256,2304]{1,0:T(8,128)(2,1)}, bf16[256,2304]{1,0:T(8,128)(2,1)}, u32[]{:S(2)}, u32[]{:S(2)}) collective-permute-start(bf16[256,2304]{1,0:T(8,128)(2,1)} %get-tuple-element.294), channel_id=1, source_target_pairs={{0,2},{2,4},{1,3},{3,5},{8,10},{10,12},{9,11},{11,13},{16,18},{18,... | collective-permute-start | bytes 3538952 | tf_op jit(solution)/shard_map/ppermute | solution.py:569
  258.8 38.0 %collective-permute-start.16 = (bf16[256,2304]{1,0:T(8,128)(2,1)}, bf16[256,2304]{1,0:T(8,128)(2,1)}, u32[]{:S(2)}, u32[]{:S(2)}) collective-permute-start(bf16[256,2304]{1,0:T(8,128)(2,1)} %collective-permute-done.12), channel_id=1, source_target_pairs={{4,6},{5,7},{12,14},{13,15},{20,22},{21,23},{28,30},{29,31}} | collective-permute-start | bytes 3538952 | tf_op jit(solution)/shard_map/ppermute | solution.py:515
  260.5 36.3 %collective-permute-start.17 = (bf16[256,2304]{1,0:T(8,128)(2,1)}, bf16[256,2304]{1,0:T(8,128)(2,1)}, u32[]{:S(2)}, u32[]{:S(2)}) collective-permute-start(bf16[256,2304]{1,0:T(8,128)(2,1)} %collective-permute-done.13), channel_id=1, source_target_pairs={{2,0},{3,1},{10,8},{11,9},{18,16},{19,17},{26,24},{27,25}} | collective-permute-start | bytes 3538952 | tf_op jit(solution)/shard_map/ppermute | solution.py:516
  299.9 26.3 %collective-permute-start.19 = (bf16[256,2304]{1,0:T(8,128)(2,1)S(1)}, bf16[256,2304]{1,0:T(8,128)(2,1)S(1)}, u32[]{:S(2)}, u32[]{:S(2)}) collective-permute-start(bf16[256,2304]{1,0:T(8,128)(2,1)S(1)} %get-tuple-element.291), channel_id=1, source_target_pairs={{2,0},{4,2},{6,4},{3,1},{5,3},{7,5},{10,8},{12,10},{14,12},{11,9},... | collective-permute-start | bytes 3538952 | tf_op jit(solution)/shard_map/ppermute | solution.py:570
  358.4 28.1 %collective-permute-start.24 = (bf16[256,2304]{1,0:T(8,128)(2,1)}, bf16[256,2304]{1,0:T(8,128)(2,1)}, u32[]{:S(2)}, u32[]{:S(2)}) collective-permute-start(bf16[256,2304]{1,0:T(8,128)(2,1)} %collective-permute-done.22), channel_id=1, source_target_pairs={{2,0},{4,2},{3,1},{5,3},{10,8},{12,10},{11,9},{13,11},{18,16},{20,... | collective-permute-start | bytes 3538952 | tf_op jit(solution)/shard_map/ppermute | solution.py:516
  445.9 42.0 %collective-permute-start.28 = (bf16[256,2304]{1,0:T(8,128)(2,1)}, bf16[256,2304]{1,0:T(8,128)(2,1)}, u32[]{:S(2)}, u32[]{:S(2)}) collective-permute-start(bf16[256,2304]{1,0:T(8,128)(2,1)} %slice.349), channel_id=1, source_target_pairs={{0,2},{1,3},{8,10},{9,11},{16,18},{17,19},{24,26},{25,27}} | collective-permute-start | bytes 3538952 | tf_op jit(solution)/shard_map/ppermute | solution.py:569
  449.8 38.2 %collective-permute-start.29 = (bf16[256,2304]{1,0:T(8,128)(2,1)}, bf16[256,2304]{1,0:T(8,128)(2,1)}, u32[]{:S(2)}, u32[]{:S(2)}) collective-permute-start(bf16[256,2304]{1,0:T(8,128)(2,1)} %slice.349), channel_id=1, source_target_pairs={{6,4},{7,5},{14,12},{15,13},{22,20},{23,21},{30,28},{31,29}} | collective-permute-start | bytes 3538952 | tf_op jit(solution)/shard_map/ppermute | solution.py:570
  488.0 167.7 %reduce-scatter.13.cloned.1.call-start = ((), (), s32[]{:S(2)}) async-start(), calls=%async_computation.11 | async-start | bytes 15261696
  492.1 29.7 %collective-permute-start.31 = (bf16[256,2304]{1,0:T(8,128)(2,1)}, bf16[256,2304]{1,0:T(8,128)(2,1)}, u32[]{:S(2)}, u32[]{:S(2)}) collective-permute-start(bf16[256,2304]{1,0:T(8,128)(2,1)} %get-tuple-element.325), channel_id=1, source_target_pairs={{4,2},{6,4},{5,3},{7,5},{12,10},{14,12},{13,11},{15,13},{20,18},{2... | collective-permute-start | bytes 3538952 | tf_op jit(solution)/shard_map/ppermute | solution.py:570
  493.8 28.0 %collective-permute-start.30 = (bf16[256,2304]{1,0:T(8,128)(2,1)}, bf16[256,2304]{1,0:T(8,128)(2,1)}, u32[]{:S(2)}, u32[]{:S(2)}) collective-permute-start(bf16[256,2304]{1,0:T(8,128)(2,1)} %get-tuple-element.326), channel_id=1, source_target_pairs={{0,2},{2,4},{1,3},{3,5},{8,10},{10,12},{9,11},{11,13},{16,18},{18,... | collective-permute-start | bytes 3538952 | tf_op jit(solution)/shard_map/ppermute | solution.py:569
  540.1 265.3 %reduce-scatter.9.cloned.1.call-start = ((), (), s32[]{:S(2)}) async-start(), calls=%async_computation.8 | async-start | bytes 3317760 | tf_op jit(solution)/shard_map/reduce_scatter | solution.py:653
  593.9 41.1 %collective-permute-start.39 = (bf16[256,2304]{1,0:T(8,128)(2,1)S(1)}, bf16[256,2304]{1,0:T(8,128)(2,1)}, u32[]{:S(2)}, u32[]{:S(2)}) collective-permute-start(bf16[256,2304]{1,0:T(8,128)(2,1)S(1)} %collective-permute-done.37), channel_id=1, source_target_pairs={{2,0},{4,2},{3,1},{5,3},{10,8},{12,10},{11,9},{13,11},{18,16},{20,... | collective-permute-start | bytes 3538952 | tf_op jit(solution)/shard_map/ppermute | solution.py:516
  640.4 49.0 %collective-permute-start.35 = (bf16[256,2304]{1,0:T(8,128)(2,1)}, bf16[256,2304]{1,0:T(8,128)(2,1)}, u32[]{:S(2)}, u32[]{:S(2)}) collective-permute-start(bf16[256,2304]{1,0:T(8,128)(2,1)} %slice.276), channel_id=1, source_target_pairs={{6,4},{7,5},{14,12},{15,13},{22,20},{23,21},{30,28},{31,29}} | collective-permute-start | bytes 3538952 | tf_op jit(solution)/shard_map/ppermute | solution.py:570
  642.1 93.2 %collective-permute-start.34 = (bf16[256,2304]{1,0:T(8,128)(2,1)}, bf16[256,2304]{1,0:T(8,128)(2,1)}, u32[]{:S(2)}, u32[]{:S(2)}) collective-permute-start(bf16[256,2304]{1,0:T(8,128)(2,1)} %slice.276), channel_id=1, source_target_pairs={{0,2},{1,3},{8,10},{9,11},{16,18},{17,19},{24,26},{25,27}} | collective-permute-start | bytes 3538952 | tf_op jit(solution)/shard_map/ppermute | solution.py:569
  663.5 71.8 %collective-permute-start.45 = (bf16[288,2880]{1,0:T(8,128)(2,1)}, bf16[288,2880]{1,0:T(8,128)(2,1)}, u32[]{:S(2)}, u32[]{:S(2)}) collective-permute-start(bf16[288,2880]{1,0:T(8,128)(2,1)} %copy.54), channel_id=1, source_target_pairs={{2,0},{4,2},{6,4},{3,1},{5,3},{7,5},{10,8},{12,10},{14,12},{11,9},... | collective-permute-start | bytes 4976648 | tf_op jit(solution)/shard_map/ppermute | solution.py:516
  665.1 70.2 %collective-permute-start.44 = (bf16[288,2880]{1,0:T(8,128)(2,1)}, bf16[288,2880]{1,0:T(8,128)(2,1)}, u32[]{:S(2)}, u32[]{:S(2)}) collective-permute-start(bf16[288,2880]{1,0:T(8,128)(2,1)} %copy.54), channel_id=1, source_target_pairs={{0,2},{2,4},{4,6},{1,3},{3,5},{5,7},{8,10},{10,12},{12,14},{9,11},... | collective-permute-start | bytes 4976648 | tf_op jit(solution)/shard_map/ppermute | solution.py:515
  685.5 49.8 %collective-permute-start.43 = (bf16[720,576]{0,1:T(8,128)(2,1)}, bf16[720,576]{0,1:T(8,128)(2,1)}, u32[]{:S(2)}, u32[]{:S(2)}) collective-permute-start(bf16[720,576]{0,1:T(8,128)(2,1)} %copy.52), channel_id=1, source_target_pairs={{2,0},{4,2},{6,4},{3,1},{5,3},{7,5},{10,8},{12,10},{14,12},{11,9},... | collective-permute-start | bytes 2488328 | tf_op jit(solution)/shard_map/ppermute | solution.py:516
  689.4 45.9 %collective-permute-start.42 = (bf16[720,576]{0,1:T(8,128)(2,1)}, bf16[720,576]{0,1:T(8,128)(2,1)}, u32[]{:S(2)}, u32[]{:S(2)}) collective-permute-start(bf16[720,576]{0,1:T(8,128)(2,1)} %copy.52), channel_id=1, source_target_pairs={{0,2},{2,4},{4,6},{1,3},{3,5},{5,7},{8,10},{10,12},{12,14},{9,11},... | collective-permute-start | bytes 2488328 | tf_op jit(solution)/shard_map/ppermute | solution.py:515
  702.8 293.9 %reduce-scatter.11.cloned.1.call-start = ((), (), s32[]{:S(2)}) async-start(), calls=%async_computation.9 | async-start | bytes 9953280 | tf_op jit(solution)/shard_map/reduce_scatter | solution.py:653
  735.3 30.0 %collective-permute-start.48 = (bf16[720,576]{0,1:T(8,128)(2,1)}, bf16[720,576]{0,1:T(8,128)(2,1)}, u32[]{:S(2)}, u32[]{:S(2)}) collective-permute-start(bf16[720,576]{0,1:T(8,128)(2,1)} %collective-permute-done.42), channel_id=1, source_target_pairs={{2,4},{4,6},{3,5},{5,7},{10,12},{12,14},{11,13},{13,15},{18,20},{2... | collective-permute-start | bytes 2488328 | tf_op jit(solution)/shard_map/ppermute | solution.py:515
  736.9 42.0 %collective-permute-start.49 = (bf16[720,576]{0,1:T(8,128)(2,1)}, bf16[720,576]{0,1:T(8,128)(2,1)}, u32[]{:S(2)}, u32[]{:S(2)}) collective-permute-start(bf16[720,576]{0,1:T(8,128)(2,1)} %collective-permute-done.43), channel_id=1, source_target_pairs={{2,0},{4,2},{3,1},{5,3},{10,8},{12,10},{11,9},{13,11},{18,16},{20,... | collective-permute-start | bytes 2488328 | tf_op jit(solution)/shard_map/ppermute | solution.py:516
  740.8 38.1 %collective-permute-start.47 = (bf16[256,2304]{1,0:T(8,128)(2,1)S(1)}, bf16[256,2304]{1,0:T(8,128)(2,1)S(1)}, u32[]{:S(2)}, u32[]{:S(2)}) collective-permute-start(bf16[256,2304]{1,0:T(8,128)(2,1)S(1)} %get-tuple-element.287), channel_id=1, source_target_pairs={{4,2},{6,4},{5,3},{7,5},{12,10},{14,12},{13,11},{15,13},{20,18},{2... | collective-permute-start | bytes 3538952 | tf_op jit(solution)/shard_map/ppermute | solution.py:570
  741.5 37.3 %collective-permute-start.46 = (bf16[256,2304]{1,0:T(8,128)(2,1)S(1)}, bf16[256,2304]{1,0:T(8,128)(2,1)}, u32[]{:S(2)}, u32[]{:S(2)}) collective-permute-start(bf16[256,2304]{1,0:T(8,128)(2,1)S(1)} %get-tuple-element.288), channel_id=1, source_target_pairs={{0,2},{2,4},{1,3},{3,5},{8,10},{10,12},{9,11},{11,13},{16,18},{18,... | collective-permute-start | bytes 3538952 | tf_op jit(solution)/shard_map/ppermute | solution.py:569
  750.1 28.8 %collective-permute-start.50 = (bf16[288,2880]{1,0:T(8,128)(2,1)}, bf16[288,2880]{1,0:T(8,128)(2,1)}, u32[]{:S(2)}, u32[]{:S(2)}) collective-permute-start(bf16[288,2880]{1,0:T(8,128)(2,1)} %collective-permute-done.44), channel_id=1, source_target_pairs={{2,4},{4,6},{3,5},{5,7},{10,12},{12,14},{11,13},{13,15},{18,20},{2... | collective-permute-start | bytes 4976648 | tf_op jit(solution)/shard_map/ppermute | solution.py:515
  765.3 40.1 %collective-permute-start.51 = (bf16[288,2880]{1,0:T(8,128)(2,1)}, bf16[288,2880]{1,0:T(8,128)(2,1)}, u32[]{:S(2)}, u32[]{:S(2)}) collective-permute-start(bf16[288,2880]{1,0:T(8,128)(2,1)} %collective-permute-done.45), channel_id=1, source_target_pairs={{2,0},{4,2},{3,1},{5,3},{10,8},{12,10},{11,9},{13,11},{18,16},{20,... | collective-permute-start | bytes 4976648 | tf_op jit(solution)/shard_map/ppermute | solution.py:516
  807.8 44.1 %collective-permute-start.59 = (bf16[256,2304]{1,0:T(8,128)(2,1)}, bf16[256,2304]{1,0:T(8,128)(2,1)S(1)}, u32[]{:S(2)}, u32[]{:S(2)}) collective-permute-start(bf16[256,2304]{1,0:T(8,128)(2,1)} %slice.285), channel_id=1, source_target_pairs={{6,4},{7,5},{14,12},{15,13},{22,20},{23,21},{30,28},{31,29}} | collective-permute-start | bytes 3538952 | tf_op jit(solution)/shard_map/ppermute | solution.py:570
  809.4 41.2 %collective-permute-start.55 = (bf16[720,576]{0,1:T(8,128)(2,1)}, bf16[720,576]{0,1:T(8,128)(2,1)S(1)}, u32[]{:S(2)}, u32[]{:S(2)}) collective-permute-start(bf16[720,576]{0,1:T(8,128)(2,1)} %collective-permute-done.49), channel_id=1, source_target_pairs={{2,0},{3,1},{10,8},{11,9},{18,16},{19,17},{26,24},{27,25}} | collective-permute-start | bytes 2488328 | tf_op jit(solution)/shard_map/ppermute | solution.py:516
  810.7 103.8 %collective-permute-start.56 = (bf16[288,2880]{1,0:T(8,128)(2,1)}, bf16[288,2880]{1,0:T(8,128)(2,1)}, u32[]{:S(2)}, u32[]{:S(2)}) collective-permute-start(bf16[288,2880]{1,0:T(8,128)(2,1)} %collective-permute-done.50), channel_id=1, source_target_pairs={{4,6},{5,7},{12,14},{13,15},{20,22},{21,23},{28,30},{29,31}} | collective-permute-start | bytes 4976648 | tf_op jit(solution)/shard_map/ppermute | solution.py:515
  812.5 102.0 %collective-permute-start.57 = (bf16[288,2880]{1,0:T(8,128)(2,1)}, bf16[288,2880]{1,0:T(8,128)(2,1)}, u32[]{:S(2)}, u32[]{:S(2)}) collective-permute-start(bf16[288,2880]{1,0:T(8,128)(2,1)} %collective-permute-done.51), channel_id=1, source_target_pairs={{2,0},{3,1},{10,8},{11,9},{18,16},{19,17},{26,24},{27,25}} | collective-permute-start | bytes 4976648 | tf_op jit(solution)/shard_map/ppermute | solution.py:516
  818.3 68.7 %collective-permute-start.58 = (bf16[256,2304]{1,0:T(8,128)(2,1)}, bf16[256,2304]{1,0:T(8,128)(2,1)}, u32[]{:S(2)}, u32[]{:S(2)}) collective-permute-start(bf16[256,2304]{1,0:T(8,128)(2,1)} %slice.285), channel_id=1, source_target_pairs={{0,2},{1,3},{8,10},{9,11},{16,18},{17,19},{24,26},{25,27}} | collective-permute-start | bytes 3538952 | tf_op jit(solution)/shard_map/ppermute | solution.py:569
  850.6 61.7 %collective-permute-start.53 = (bf16[256,2304]{1,0:T(8,128)(2,1)}, bf16[256,2304]{1,0:T(8,128)(2,1)}, u32[]{:S(2)}, u32[]{:S(2)}) collective-permute-start(bf16[256,2304]{1,0:T(8,128)(2,1)} %get-tuple-element.285), channel_id=1, source_target_pairs={{2,0},{4,2},{6,4},{3,1},{5,3},{7,5},{10,8},{12,10},{14,12},{11,9},... | collective-permute-start | bytes 3538952 | tf_op jit(solution)/shard_map/ppermute | solution.py:570
  851.9 62.6 %collective-permute-start.52 = (bf16[256,2304]{1,0:T(8,128)(2,1)}, bf16[256,2304]{1,0:T(8,128)(2,1)}, u32[]{:S(2)}, u32[]{:S(2)}) collective-permute-start(bf16[256,2304]{1,0:T(8,128)(2,1)} %get-tuple-element.286), channel_id=1, source_target_pairs={{0,2},{2,4},{4,6},{1,3},{3,5},{5,7},{8,10},{10,12},{12,14},{9,11},... | collective-permute-start | bytes 3538952 | tf_op jit(solution)/shard_map/ppermute | solution.py:569
  887.0 109.6 %collective-permute-start.63 = (bf16[288,576]{1,0:T(8,128)(2,1)}, bf16[288,576]{1,0:T(8,128)(2,1)}, u32[]{:S(2)}, u32[]{:S(2)}) collective-permute-start(bf16[288,576]{1,0:T(8,128)(2,1)} %reduce-scatter.9.cloned.1.call-done), channel_id=1, source_target_pairs={{2,0},{4,2},{6,4},{3,1},{5,3},{7,5},{10,8},{12,10},{14,12},{11,9},... | collective-permute-start | bytes 995336 | tf_op jit(solution)/shard_map/ppermute | solution.py:516
  912.3 84.4 %collective-permute-start.62 = (bf16[288,576]{1,0:T(8,128)(2,1)}, bf16[288,576]{1,0:T(8,128)(2,1)}, u32[]{:S(2)}, u32[]{:S(2)}) collective-permute-start(bf16[288,576]{1,0:T(8,128)(2,1)} %reduce-scatter.9.cloned.1.call-done), channel_id=1, source_target_pairs={{0,2},{2,4},{4,6},{1,3},{3,5},{5,7},{8,10},{10,12},{12,14},{9,11},... | collective-permute-start | bytes 995336 | tf_op jit(solution)/shard_map/ppermute | solution.py:515
  946.5 34.6 %collective-permute-start.72 = (bf16[2,288,2880]{2,1,0:T(8,128)(2,1)}, bf16[2,288,2880]{2,1,0:T(8,128)(2,1)}, u32[]{:S(2)}, u32[]{:S(2)}) collective-permute-start(bf16[2,288,2880]{2,1,0:T(8,128)(2,1)} %copy.71), channel_id=1, source_target_pairs={{0,1},{1,0},{2,3},{3,2},{4,5},{5,4},{6,7},{7,6},{8,9},{9,8},{10,11... | collective-permute-start | bytes 9953288 | tf_op jit(solution)/shard_map/ppermute | solution.py:668
  957.3 39.3 %collective-permute-start.61 = (bf16[256,2304]{1,0:T(8,128)(2,1)}, bf16[256,2304]{1,0:T(8,128)(2,1)}, u32[]{:S(2)}, u32[]{:S(2)}) collective-permute-start(bf16[256,2304]{1,0:T(8,128)(2,1)} %get-tuple-element.283), channel_id=1, source_target_pairs={{4,2},{6,4},{5,3},{7,5},{12,10},{14,12},{13,11},{15,13},{20,18},{2... | collective-permute-start | bytes 3538952 | tf_op jit(solution)/shard_map/ppermute | solution.py:570
  962.8 33.9 %collective-permute-start.60 = (bf16[256,2304]{1,0:T(8,128)(2,1)}, bf16[256,2304]{1,0:T(8,128)(2,1)}, u32[]{:S(2)}, u32[]{:S(2)}) collective-permute-start(bf16[256,2304]{1,0:T(8,128)(2,1)} %get-tuple-element.284), channel_id=1, source_target_pairs={{0,2},{2,4},{1,3},{3,5},{8,10},{10,12},{9,11},{11,13},{16,18},{18,... | collective-permute-start | bytes 3538952 | tf_op jit(solution)/shard_map/ppermute | solution.py:569
  996.7 73.9 %collective-permute-start.71 = (bf16[288,1920]{1,0:T(8,128)(2,1)}, bf16[288,1920]{1,0:T(8,128)(2,1)}, u32[]{:S(2)}, u32[]{:S(2)}) collective-permute-start(bf16[288,1920]{1,0:T(8,128)(2,1)} %reduce-scatter.11.cloned.1.call-done), channel_id=1, source_target_pairs={{2,0},{4,2},{6,4},{3,1},{5,3},{7,5},{10,8},{12,10},{14,12},{11,9},... | collective-permute-start | bytes 3317768 | tf_op jit(solution)/shard_map/ppermute | solution.py:516
  998.0 72.6 %collective-permute-start.70 = (bf16[288,1920]{1,0:T(8,128)(2,1)}, bf16[288,1920]{1,0:T(8,128)(2,1)}, u32[]{:S(2)}, u32[]{:S(2)}) collective-permute-start(bf16[288,1920]{1,0:T(8,128)(2,1)} %reduce-scatter.11.cloned.1.call-done), channel_id=1, source_target_pairs={{0,2},{2,4},{4,6},{1,3},{3,5},{5,7},{8,10},{10,12},{12,14},{9,11},... | collective-permute-start | bytes 3317768 | tf_op jit(solution)/shard_map/ppermute | solution.py:515
  1008.0 62.6 %collective-permute-start.67 = (bf16[256,2304]{1,0:T(8,128)(2,1)}, bf16[256,2304]{1,0:T(8,128)(2,1)S(1)}, u32[]{:S(2)}, u32[]{:S(2)}) collective-permute-start(bf16[256,2304]{1,0:T(8,128)(2,1)} %get-tuple-element.281), channel_id=1, source_target_pairs={{2,0},{4,2},{6,4},{3,1},{5,3},{7,5},{10,8},{12,10},{14,12},{11,9},... | collective-permute-start | bytes 3538952 | tf_op jit(solution)/shard_map/ppermute | solution.py:570
  1009.6 61.1 %collective-permute-start.66 = (bf16[256,2304]{1,0:T(8,128)(2,1)}, bf16[256,2304]{1,0:T(8,128)(2,1)}, u32[]{:S(2)}, u32[]{:S(2)}) collective-permute-start(bf16[256,2304]{1,0:T(8,128)(2,1)} %get-tuple-element.282), channel_id=1, source_target_pairs={{0,2},{2,4},{4,6},{1,3},{3,5},{5,7},{8,10},{10,12},{12,14},{9,11},... | collective-permute-start | bytes 3538952 | tf_op jit(solution)/shard_map/ppermute | solution.py:569
  1035.6 35.0 %collective-permute-start.69 = (bf16[288,576]{1,0:T(8,128)(2,1)}, bf16[288,576]{1,0:T(8,128)(2,1)}, u32[]{:S(2)}, u32[]{:S(2)}) collective-permute-start(bf16[288,576]{1,0:T(8,128)(2,1)} %collective-permute-done.63), channel_id=1, source_target_pairs={{2,0},{4,2},{3,1},{5,3},{10,8},{12,10},{11,9},{13,11},{18,16},{20,... | collective-permute-start | bytes 995336 | tf_op jit(solution)/shard_map/ppermute | solution.py:516
  1073.8 93.7 %collective-permute-start.75 = (bf16[288,576]{1,0:T(8,128)(2,1)}, bf16[288,576]{1,0:T(8,128)(2,1)}, u32[]{:S(2)}, u32[]{:S(2)}) collective-permute-start(bf16[288,576]{1,0:T(8,128)(2,1)} %collective-permute-done.68), channel_id=1, source_target_pairs={{4,6},{5,7},{12,14},{13,15},{20,22},{21,23},{28,30},{29,31}} | collective-permute-start | bytes 995336 | tf_op jit(solution)/shard_map/ppermute | solution.py:515
  1075.2 92.3 %collective-permute-start.76 = (bf16[288,576]{1,0:T(8,128)(2,1)}, bf16[288,576]{1,0:T(8,128)(2,1)}, u32[]{:S(2)}, u32[]{:S(2)}) collective-permute-start(bf16[288,576]{1,0:T(8,128)(2,1)} %collective-permute-done.69), channel_id=1, source_target_pairs={{2,0},{3,1},{10,8},{11,9},{18,16},{19,17},{26,24},{27,25}} | collective-permute-start | bytes 995336 | tf_op jit(solution)/shard_map/ppermute | solution.py:516
  1076.5 91.0 %collective-permute-start.73 = (bf16[288,1920]{1,0:T(8,128)(2,1)}, bf16[288,1920]{1,0:T(8,128)(2,1)}, u32[]{:S(2)}, u32[]{:S(2)}) collective-permute-start(bf16[288,1920]{1,0:T(8,128)(2,1)} %collective-permute-done.70), channel_id=1, source_target_pairs={{2,4},{4,6},{3,5},{5,7},{10,12},{12,14},{11,13},{13,15},{18,20},{2... | collective-permute-start | bytes 3317768 | tf_op jit(solution)/shard_map/ppermute | solution.py:515
  1078.1 89.4 %collective-permute-start.74 = (bf16[288,1920]{1,0:T(8,128)(2,1)}, bf16[288,1920]{1,0:T(8,128)(2,1)}, u32[]{:S(2)}, u32[]{:S(2)}) collective-permute-start(bf16[288,1920]{1,0:T(8,128)(2,1)} %collective-permute-done.71), channel_id=1, source_target_pairs={{2,0},{4,2},{3,1},{5,3},{10,8},{12,10},{11,9},{13,11},{18,16},{20,... | collective-permute-start | bytes 3317768 | tf_op jit(solution)/shard_map/ppermute | solution.py:516
  1169.3 27.5 %collective-permute-start.79 = (bf16[288,1920]{1,0:T(8,128)(2,1)}, bf16[288,1920]{1,0:T(8,128)(2,1)S(1)}, u32[]{:S(2)}, u32[]{:S(2)}) collective-permute-start(bf16[288,1920]{1,0:T(8,128)(2,1)} %collective-permute-done.74), channel_id=1, source_target_pairs={{2,0},{3,1},{10,8},{11,9},{18,16},{19,17},{26,24},{27,25}} | collective-permute-start | bytes 3317768 | tf_op jit(solution)/shard_map/ppermute | solution.py:516
  1173.2 30.1 %collective-permute-start.81 = (bf16[2,288,576]{2,1,0:T(8,128)(2,1)S(1)}, bf16[2,288,576]{2,1,0:T(8,128)(2,1)S(1)}, u32[]{:S(2)}, u32[]{:S(2)}) collective-permute-start(bf16[2,288,576]{2,1,0:T(8,128)(2,1)S(1)} %pad_maximum_fusion.28), channel_id=1, source_target_pairs={{0,1},{1,0},{2,3},{3,2},{4,5},{5,4},{6,7},{7,6},{8,9},{9,8},{10,11... | collective-permute-start | bytes 1990664 | tf_op jit(solution)/shard_map/ppermute | solution.py:668
  1173.3 35.6 %collective-permute-start.77 = (bf16[256,2304]{1,0:T(8,128)(2,1)S(1)}, bf16[256,2304]{1,0:T(8,128)(2,1)}, u32[]{:S(2)}, u32[]{:S(2)}) collective-permute-start(bf16[256,2304]{1,0:T(8,128)(2,1)S(1)} %fusion.42), channel_id=1, source_target_pairs={{0,1},{1,0},{2,3},{3,2},{4,5},{5,4},{6,7},{7,6},{8,9},{9,8},{10,11... | collective-permute-start | bytes 3538952 | tf_op jit(solution)/shard_map/ppermute | solution.py:873
  (102 other events, 1487.3 us)
Sparse Core Ops, SparseCore 0:
  12.9 33.9 all-gather.8
  49.4 56.2 all-gather.6
  108.1 48.7 all-gather.12
  158.6 76.1 all-gather.10
  488.1 66.9 reduce-scatter.6
  558.5 97.1 reduce-scatter.12
  703.0 44.0 reduce-scatter.8
  882.0 74.1 reduce-scatter.10

commit v3 on v2

--- a/solution.py
+++ b/solution.py
@@ -499,6 +499,67 @@
     )(order, length, queries, keys, values, logs, attend, grad_attend, cos, sin)
 
 
+def columns_kernel(count, each, used, core, own, other, *outs):
+    mine = pl.program_id(0) == core[0]
+    for k in range(own.shape[0]):
+        rows = jnp.where(mine, own[k].astype(jnp.float32), other[k].astype(jnp.float32))
+        for j in range(count):
+            outs[j][:, k * used : (k + 1) * used] = rows[:, j * each : j * each + used]
+
+
+def join_columns(core, own, other, count, each, used):
+    pieces, rows, cols = own.shape
+    tile = rows // 3 if rows % 48 == 0 else rows
+    taken = pl.BlockSpec((pieces, tile, cols), lambda c, r, *_: (0, r, 0))
+    given = pl.BlockSpec((tile, pieces * used), lambda c, r, *_: (c * (rows // tile) + r, 0))
+    return pl.pallas_call(
+        functools.partial(columns_kernel, count, each, used),
+        grid_spec=pltpu.PrefetchScalarGridSpec(
+            num_scalar_prefetch=1,
+            grid=(2, rows // tile),
+            in_specs=[taken, taken],
+            out_specs=[given] * count,
+        ),
+        out_shape=[jax.ShapeDtypeStruct((2 * rows, pieces * used), jnp.float32)] * count,
+        compiler_params=pltpu.CompilerParams(vmem_limit_bytes=40 << 20),
+        cost_estimate=pl.CostEstimate(
+            flops=0, bytes_accessed=8 * pieces * rows * (cols + used * count), transcendentals=0
+        ),
+        name="join_columns",
+    )(core, own, other)
+
+
+def turned_kernel(start, used, core, own, other, out, joined):
+    rows = own.shape[1]
+    first = core[0] == 0
+    left = own[0, :, start : start + used].astype(jnp.float32)
+    right = other[0, :, start : start + used].astype(jnp.float32)
+    joined[:rows, :] = jnp.where(first, left, right)
+    joined[rows:, :] = jnp.where(first, right, left)
+    out[...] = jnp.transpose(joined[...])
+
+
+def join_turned(core, own, other, start, used):
+    pieces, rows, cols = own.shape
+    taken = pl.BlockSpec((1, rows, cols), lambda k, *_: (k, 0, 0))
+    return pl.pallas_call(
+        functools.partial(turned_kernel, start, used),
+        grid_spec=pltpu.PrefetchScalarGridSpec(
+            num_scalar_prefetch=1,
+            grid=(pieces,),
+            in_specs=[taken, taken],
+            out_specs=pl.BlockSpec((used, 2 * rows), lambda k, *_: (k, 0)),
+            scratch_shapes=[pltpu.VMEM((2 * rows, used), jnp.float32)],
+        ),
+        out_shape=jax.ShapeDtypeStruct((pieces * used, 2 * rows), jnp.float32),
+        compiler_params=pltpu.CompilerParams(vmem_limit_bytes=40 << 20),
+        cost_estimate=pl.CostEstimate(
+            flops=0, bytes_accessed=8 * pieces * rows * (cols + used), transcendentals=0
+        ),
+        name="join_turned",
+    )(core, own, other)
+
+
 def swap_pairs():
     return [(0, 1), (1, 0)]
 
@@ -530,11 +591,14 @@
             found = block if found is None else jnp.where(place == here, block, found)
         return found
 
-    def before(self, count):
-        if count == 0:
-            return self.ups[0]
+    def at(self, target):
         place = lax.axis_index(self.axis)
-        return jnp.where(place >= count, self.ups[count], self.downs[self.size - count])
+        found = self.ups[0]
+        for here in range(self.size):
+            if here != target:
+                block = self.ups[here - target] if target < here else self.downs[target - here]
+                found = jnp.where(place == here, block, found)
+        return found
 
 
 class LineScatter:
@@ -630,8 +694,9 @@
         ]
         return jnp.concatenate(cut, axis=1) if len(cut) > 1 else cut[0]
 
-    def row_piece(w):
-        return lax.dynamic_slice_in_dim(w, sub * (w.shape[0] // per_half), w.shape[0] // per_half, 0)
+    def turned_piece(w):
+        rows = w.shape[0] // per_half
+        return jnp.transpose(lax.dynamic_slice_in_dim(w, sub * rows, rows, 0))
 
     def to_pair(piece):
         rows = piece.shape[0] // cores
@@ -640,54 +705,36 @@
         got = lax.ppermute(give, "tensor", swap_pairs())
         return jnp.where(owner, keep, got)
 
-    def gather_columns(piece):
-        return lax.all_gather(to_pair(piece), ("shard", "tensor"), axis=0, tiled=True)
-
-    def gather_rows(w):
-        mine = to_pair(row_piece(w))
-        got = lax.all_gather(mine, ("shard", "tensor"), axis=0, tiled=True)
-        rows = cores * mine.shape[0]
-        return jnp.concatenate([got[k * rows : (k + 1) * rows] for k in range(shards)], axis=1)
+    def gather_pair(mine):
+        return lax.all_gather(mine, ("shard", "tensor"), axis=0, tiled=True)
 
     def reduce_pair(grad):
         return lax.psum_scatter(grad, ("shard", "tensor"), scatter_dimension=0, tiled=True)
 
-    def by_shard(grad):
-        cols = width // shards
-        return jnp.concatenate([grad[:, k * cols : (k + 1) * cols] for k in range(shards)], axis=0)
-
-    def gathered_halves(chain):
-        rows, cols = chain.ups[0].shape
-        ring = jnp.stack([chain.before(k) for k in range(lines)])
-        take = lambda half: jnp.stack(
-            [
-                lax.dynamic_index_in_dim(ring, (line - half * per_half - k) % lines, 0, False)
-                for k in range(per_half)
-            ]
-        )
-        other = lax.ppermute(take(1 - core), "tensor", swap_pairs())
-        own = take(core)
-        first = jnp.where(core == 0, own, other)
-        second = jnp.where(core == 0, other, own)
-        return [[first[k], second[k]] for k in range(per_half)]
-
-    def spread_columns(chain, count, used):
-        pieces = gathered_halves(chain)
-        each = pieces[0][0].shape[1] // count
-        cut = lambda k: jnp.concatenate(
-            [
-                jnp.concatenate([piece[:, k * each : k * each + used] for piece in row], axis=1)
-                for row in zip(*pieces)
-            ],
-            axis=0,
-        )
-        return [cut(k).astype(jnp.float32) for k in range(count)]
-
-    def spread_rows(chain):
-        pieces = gathered_halves(chain)
-        return jnp.concatenate([p for quarter in pieces for p in quarter], axis=0).astype(
-            jnp.float32
-        )
+    def gain_marks(weights, piece):
+        used = weights.shape[1]
+        total = jnp.sum(
+            weights.astype(jnp.float32) * piece[:, :used].astype(jnp.float32), axis=1, keepdims=True
+        )
+        high = total.astype(jnp.bfloat16)
+        low = (total - high.astype(jnp.float32)).astype(jnp.bfloat16)
+        return jnp.concatenate([high, low], axis=1)
+
+    def line_pieces(chain):
+        found = [chain.at(q) for q in range(lines)]
+        halves = [jnp.stack(found[h * per_half : (h + 1) * per_half]) for h in range(cores)]
+        own = jnp.where(core == 0, halves[0], halves[1])
+        give = jnp.where(core == 0, halves[1], halves[0])
+        return own, lax.ppermute(give, "tensor", swap_pairs()), found
+
+    def gain_total(found, column, gain):
+        marks = sum(piece[:, column : column + 2].astype(jnp.float32) for piece in found)
+        own = jnp.sum(marks, axis=1)
+        other = lax.ppermute(own, "tensor", swap_pairs())
+        total = jnp.concatenate(
+            [jnp.where(core == 0, own, other), jnp.where(core == 0, other, own)]
+        )
+        return total / gain.astype(jnp.float32)
 
     def walk(block):
         return LineGather(block, "ctx", lines)
@@ -711,45 +758,56 @@
     cos_all, sin_all = jnp.cos(angles), jnp.sin(angles)
     live_all = (ring_pos < length).astype(jnp.float32)[:, None]
     live_own = live_all[:row_count]
-    gains = lax.all_gather(jnp.stack([attn_gain, mlp_gain]), "shard", axis=1, tiled=True)
+    core_index = core.astype(jnp.int32).reshape(1)
+    own_tokens = lax.dynamic_index_in_dim(tokens, core, 0, keepdims=False)
+    own_cot = lax.dynamic_index_in_dim(cotangent, core, 0, keepdims=False)
+
+    tokens_line = walk(own_tokens)
+    tokens_line.step()
+    qkv_mine = to_pair(column_piece([w_query, w_key, w_value], lambda v: widen(v, 1)))
+    qkv_w = gather_pair(qkv_mine)
+    w_out, w_gate, w_up, w_down, gain_pair = stage(
+        [tokens_line], w_out, w_gate, w_up, w_down, jnp.stack([attn_gain, mlp_gain])
+    )
+    tokens_line.step()
+    gains = lax.all_gather(gain_pair, "shard", axis=1, tiled=True)
     gain_a = gains[0].astype(jnp.float32)
     gain_b = gains[1].astype(jnp.float32)
-    own_tokens = lax.dynamic_index_in_dim(tokens, core, 0, keepdims=False)
-    own_cot = lax.dynamic_index_in_dim(cotangent, core, 0, keepdims=False)
-
-    qkv_w = gather_columns(column_piece([w_query, w_key, w_value], lambda v: widen(v, 1)))
-    out_w = widen(gather_rows(w_out), 0)
-    gate_up_w = gather_columns(column_piece([w_gate, w_up]))
-    down_w = gather_rows(w_down)
-
-    tokens_line = walk(own_tokens)
-    for _ in range(lines - 1):
-        tokens_line.step()
+    out_mine = to_pair(widen(turned_piece(w_out), 1))
+    down_mine = to_pair(turned_piece(w_down))
+    gate_up_mine = to_pair(column_piece([w_gate, w_up]))
+    stage([tokens_line])
+    tokens_line.step()
+    out_mine, qkv_w = lax.optimization_barrier((out_mine, qkv_w))
+    out_w = gather_pair(out_mine)
+    own_cot, down_mine = stage([tokens_line], own_cot, down_mine)
+    down_w = gather_pair(down_mine)
+
+    cot_line = walk(own_cot)
+    cot_line.step()
     all_tokens = jnp.concatenate([tokens_line.near(k) for k in range(lines)], axis=0)
     first_in = (norm_parts(all_tokens.astype(jnp.float32))[0] * gain_a).astype(jnp.bfloat16)
-    first_in, own_cot = stage([], first_in, own_cot)
-
-    cot_line = walk(own_cot)
+    qkv = plain_product(first_in, qkv_w)
+    qkv, gate_up_mine = stage([cot_line], qkv, gate_up_mine)
+    gate_up_w = gather_pair(gate_up_mine)
+
     cot_line.step()
-    qkv = plain_product(first_in, qkv_w)
     attend, *kept = attend_forward(heads, span, order, length.reshape(1), qkv, cos_all, sin_all)
-    attn_part = plain_product(attend, out_w).astype(jnp.bfloat16)
-    (attn_part,) = stage([cot_line], attn_part)
-
+    (attend,) = stage([cot_line], attend)
+
+    cot_line.step()
+    attn_part = col_product(attend, out_w).astype(jnp.bfloat16)
     attn_line = add_up(blocks_of(attn_part))
     attn_line.step()
-    cot_line.step()
-    stage([attn_line, cot_line])
-    attn_line.step()
-    cot_line.step()
     stage([attn_line, cot_line])
     attn_line.step()
     all_cot = jnp.concatenate([cot_line.near(k) for k in range(lines)], axis=0)
     grad_mlp = (BRANCH_SCALE * (all_cot.astype(jnp.float32) * live_all)).astype(jnp.bfloat16)
+    (grad_mlp,) = stage([attn_line], grad_mlp)
+    attn_line.step()
     half_rows = all_rows // 2
     grad_hidden = [
-        col_product(grad_mlp[k * half_rows : (k + 1) * half_rows], down_w).astype(jnp.float32)
-        for k in range(2)
+        plain_product(grad_mlp[k * half_rows : (k + 1) * half_rows], down_w) for k in range(2)
     ]
     grad_hidden = stage([attn_line], *grad_hidden)
     own_x = own_tokens.astype(jnp.float32)
@@ -789,85 +847,82 @@
     hidden = jnp.concatenate([hidden_near, hidden_far], axis=0)
     second_in = jnp.concatenate([near_half, far_half], axis=0)
     grad_gate_up = jnp.concatenate([grad_near, grad_far], axis=0)
-    down_grad = by_shard(row_product(hidden, grad_mlp).astype(jnp.bfloat16))
-    (down_grad,) = stage([grad_line], down_grad)
+    down_grad = row_product(grad_mlp, hidden).astype(jnp.bfloat16)
+    down_piece = reduce_pair(down_grad)
+    mlp_part = col_product(hidden, down_w).astype(jnp.bfloat16)
+    second_in, mlp_part = stage([grad_line], second_in, mlp_part)
     grad_line.step()
-    down_piece = reduce_pair(down_grad)
     gate_up_grad = row_product(second_in, grad_gate_up).astype(jnp.bfloat16)
     (gate_up_grad,) = stage([grad_line], gate_up_grad)
     gate_up_piece = reduce_pair(gate_up_grad)
     grad_line.step()
-    mlp_part = plain_product(hidden, down_w).astype(jnp.bfloat16)
-    (mlp_part,) = stage([grad_line], mlp_part)
+    stage([grad_line])
     grad_second = grad_line.total()
 
     own_dy = own_cot.astype(jnp.float32) * live_own
-    grad_gain_two = jnp.sum(grad_second * normed_two, axis=0)
     grad_middle = own_dy + norm_back(grad_second, normed_two, inverse_two, gain_b)
     attn_grad_line = walk((BRANCH_SCALE * grad_middle).astype(jnp.bfloat16))
     attn_grad_line.step()
-    stage([attn_grad_line])
-    attn_grad_line.step()
-    (down_piece,) = stage([attn_grad_line], down_piece)
-    attn_grad_line.step()
-    gate_up_piece, down_piece = stage([attn_grad_line], gate_up_piece, down_piece)
-    grad_attn = jnp.concatenate([attn_grad_line.near(k) for k in range(lines)], axis=0)
-
-    down_line = walk(down_piece)
-    gate_up_line = walk(gate_up_piece)
+    (mlp_part,) = stage([attn_grad_line], mlp_part)
     mlp_line = add_up(blocks_of(mlp_part))
     mlp_line.step()
-    down_line.step()
-    gate_up_line.step()
-    out_grad = by_shard(row_product(attend, grad_attn)[:head_cols].astype(jnp.bfloat16))
+    attn_grad_line.step()
+    stage([attn_grad_line, mlp_line])
+    attn_grad_line.step()
+    mlp_line.step()
+    stage([attn_grad_line, mlp_line])
+    mlp_line.step()
+    grad_attn = jnp.concatenate([attn_grad_line.near(k) for k in range(lines)], axis=0)
+
+    out_grad = row_product(grad_attn, attend).astype(jnp.bfloat16)
     out_piece = reduce_pair(out_grad)
-    grad_attend = col_product(grad_attn, out_w).astype(jnp.bfloat16)
+    grad_attend = plain_product(grad_attn, out_w).astype(jnp.bfloat16)
+    grad_attend, gate_up_piece, down_piece = lax.optimization_barrier(
+        (grad_attend, gate_up_piece, down_piece)
+    )
+    unit_marks = gain_marks(gate_up_mine, gate_up_piece)
+    unit_line = walk(
+        jnp.pad(
+            jnp.concatenate([gate_up_piece, down_piece, unit_marks], axis=1),
+            [(0, 0), (0, -(3 * unit_cols + 2) % LANES)],
+        )
+    )
+    unit_line.step()
     grad_qkv = attend_backward(
         heads, span, order, length.reshape(1), kept, attend, grad_attend, cos_all, sin_all
     )
-    moving = [mlp_line, down_line, gate_up_line]
-    (grad_qkv,) = stage(moving, grad_qkv)
-    for chain in moving:
-        chain.step()
+    qkv_grad = row_product(first_in, grad_qkv).astype(jnp.bfloat16)
+    qkv_piece = reduce_pair(qkv_grad)
     first_part = col_product(grad_qkv, qkv_w).astype(jnp.bfloat16)
-    qkv_grad = row_product(first_in, grad_qkv).astype(jnp.bfloat16)
-    first_part, qkv_grad, out_piece = stage(moving, first_part, qkv_grad, out_piece)
-    qkv_piece = reduce_pair(qkv_grad)
-    for chain in moving:
-        chain.step()
+    (first_part,) = stage([unit_line, mlp_line], first_part)
+
     first_line = add_up(blocks_of(first_part))
     first_line.step()
-    stage(moving + [first_line])
+    unit_line.step()
+    layer_rows = ((middle + BRANCH_SCALE * mlp_line.total()) * live_own).astype(jnp.bfloat16)
+    (layer_rows,) = stage([unit_line, first_line], layer_rows)
     first_line.step()
-    layer_rows = ((middle + BRANCH_SCALE * mlp_line.total()) * live_own).astype(jnp.bfloat16)
-    final_down = spread_rows(down_line)
-    out_line = walk(out_piece)
-    out_line.step()
-    layer_rows, final_down, qkv_piece = stage(
-        [first_line, out_line], layer_rows, final_down, qkv_piece
-    )
+    unit_line.step()
+    stage([unit_line, first_line])
     first_line.step()
-    out_line.step()
-    qkv_line = walk(qkv_piece)
-    qkv_line.step()
-    final_gate, final_up = spread_columns(gate_up_line, 2, unit_cols)
-    final_gate, final_up = stage([first_line, out_line, qkv_line], final_gate, final_up)
-    qkv_line.step()
-    out_line.step()
+    qkv_marks = gain_marks(qkv_mine, qkv_piece)
+    head_line = walk(
+        jnp.concatenate(
+            [qkv_piece[:, :head_cols], qkv_marks, qkv_piece[:, head_cols + 2 :], out_piece], axis=1
+        )
+    )
+    head_line.step()
+    own, other, found = line_pieces(unit_line)
+    final_gate, final_up = join_columns(core_index, own, other, 2, unit_cols, unit_cols)
+    final_down = join_turned(core_index, own, other, 2 * unit_cols, unit_cols)
+    final_gain_two = gain_total(found, 3 * unit_cols, mlp_gain)
+    final_gate, final_up, final_down = stage([first_line, head_line], final_gate, final_up, final_down)
+    head_line.step()
     grad_first = first_line.total()
     normed_one, inverse_one = norm_parts(own_x)
-    grad_gain_one = jnp.sum(grad_first * normed_one, axis=0)
     grad_rows = grad_middle + norm_back(grad_first, normed_one, inverse_one, gain_a)
-
-    gain_sums = lax.psum(jnp.stack([grad_gain_one, grad_gain_two]), ("shard", "ctx", "tensor"))
-    gain_sums, grad_rows = stage([qkv_line, out_line], gain_sums, grad_rows)
-    qkv_line.step()
-    final_out = spread_rows(out_line)
-    stage([qkv_line])
-    final_query, final_key, final_value = spread_columns(qkv_line, 3, head_cols)
-    gain_sums = lax.dynamic_slice_in_dim(
-        gain_sums, lax.axis_index("shard") * (width // shards), width // shards, 1
-    )
+    (grad_rows,) = stage([head_line], grad_rows)
+    head_line.step()
 
     def both_slots(own):
         other = lax.ppermute(own, "tensor", swap_pairs())
@@ -877,19 +932,30 @@
 
     layer_out = both_slots(layer_rows)
     grad_tokens = both_slots(grad_rows.astype(jnp.bfloat16)).astype(jnp.float32)
+    layer_out, grad_tokens = stage([head_line], layer_out, grad_tokens)
+    own, other, found = line_pieces(head_line)
+    final_query, final_key, final_value = join_columns(
+        core_index, own, other, 3, pad_cols, head_cols
+    )
+    final_out = join_turned(core_index, own, other, 3 * pad_cols, head_cols)
+    final_gain_one = gain_total(found, head_cols, attn_gain)
     return (
         layer_out,
         grad_tokens,
-        gain_sums[0],
+        final_gain_one,
         final_query,
         final_key,
         final_value,
         final_out,
-        gain_sums[1],
+        final_gain_two,
         final_gate,
         final_up,
         final_down,
     )
+
+
+def heads_of(w_query, cores, lines):
+    return w_query.shape[1] * cores // lines
 
 
 def local(shape, *arrays):
@@ -903,6 +969,7 @@
         and (w_query.shape[1] * cores) % (lines * HD) == 0
         and (w_gate.shape[1] * cores) % (lines * cores) == 0
         and w_query.shape[0] % cores == 0
+        and -(-heads_of(w_query, cores, lines) // LANES) * LANES >= heads_of(w_query, cores, lines) + 2
     )
     if fits:
         return column_split(shape, *arrays)

time: 1240 us -> 1120 us (0.903)
  waiting for transfers between devices: 279 us -> 462 us
  local copies, waits for them, and re-layouts: 212 us -> 71.4 us
  other arithmetic: 225 us -> 112 us
  blocking collectives: 73.6 us -> 8.53 us
  starting transfers between devices: 203 us -> 168 us
  Pallas kernels: 57.3 us -> 84.3 us
  matrix products: 163 us -> 189 us
    psum x1 -> x0, blocking collectives: 64.5 us -> none  [column_split(): lax.psum(jnp.stack([grad_gain_one, grad_gain_two]), ('shard', 'ctx', 'ten...]
    ppermute x12, waiting for transfers between devices: 27 us -> 90.8 us  [step(): self.down = lax.ppermute(down, self.axis, [(i, i - 1) for i, _ in downs])]
    convert_element_type x8 -> x4, other arithmetic: 62.8 us -> 0.05 us  [gain_marks(): low = (total - high.astype(jnp.float32)).astype(jnp.bfloat16)]
    ppermute x12, waiting for transfers between devices: 20.1 us -> 72.6 us  [step(): self.up = lax.ppermute(up, self.axis, [(i, i + 1) for i, _ in ups])]
    optimization_barrier x15 -> x0, local copies, waits for them, and re-layouts: 46.2 us -> none  [stage(): held, arrays = lax.optimization_barrier((held, arrays))]
    ppermute x24 -> x18, waiting for transfers between devices: 215 us -> 254 us  [step(): self.downs.append(lax.ppermute(self.downs[-1], self.axis, down_pairs))]
    slice x17 -> x3, local copies, waits for them, and re-layouts: 35.9 us -> 1.21 us  [the longest x1 1.21 us: column_split(): qkv_piece[:, head_cols + 2:]]
    concatenate x2 -> x1, other arithmetic: 32.4 us -> 1.47 us  [column_split(): second_in = jnp.concatenate([near_half, far_half], axis=0)]
  transfers between devices with their start and end apart: 90 -> 78, of which waited for: 25 -> 37; matrix products, arithmetic and copies ran while one was open for 44% -> 25% of each run, Pallas kernels for 5% -> 4%
where the time goes in v3:
time: 1120 us; the launch traced here: 1110 us
  waiting for transfers between devices  462 us (41%)
  matrix products  189 us (17%)
  starting transfers between devices  168 us (15%)
  other arithmetic  112 us (10%)
  Pallas kernels  84.3 us (8%)
  local copies, waits for them, and re-layouts  71.4 us (6%)
  between operations  16.1 us (1%)
    ppermute x18, waiting for transfers between devices, step(): self.downs.append(lax.ppermute(self.downs[-1], self.axis, down_pairs))  254 us
    ppermute x12, waiting for transfers between devices, step(): self.down = lax.ppermute(down, self.axis, [(i, i - 1) for i, _ in downs])  90.8 us
    dot_general x6, matrix products, plain_product(): return jnp.dot(left_mat, right_mat, preferred_element_type=jnp.float32)  78.6 us
    ppermute x12, starting transfers between devices, step(): self.up = lax.ppermute(up, self.axis, [(i, i + 1) for i, _ in ups])  78.2 us
    ppermute x12, waiting for transfers between devices, step(): self.up = lax.ppermute(up, self.axis, [(i, i + 1) for i, _ in ups])  72.6 us
    dot_general x5, matrix products, col_product(): lax.dot_general(left_mat, right_mat, CONTRACT_COLS, preferred_element_typ...  58.2 us
    dot_general x4, matrix products, row_product(): lax.dot_general(left_mat, right_mat, CONTRACT_ROWS, preferred_element_typ...  51.9 us
    ppermute x18, starting transfers between devices, step(): self.ups.append(lax.ppermute(self.ups[-1], self.axis, up_pairs))  49.8 us
  transfers between devices with their start and end apart: 78, of which 37 were waited for; matrix products, arithmetic and copies ran while one was open for 25% of the time, Pallas kernels for 4%

profile of v3, /device:TPU:0, one launch (start us, length us, event | category | flops | bytes accessed | tf_op | source)
XLA Modules:
  0.0 1110.3 jit_solution(1141273110388599917)
XLA Ops:
  22.9 6.3 collective-permute-start
  29.3 23.3 %collective-permute-done.1 = bf16[256,2304]{1,0:T(8,128)(2,1)S(1)} collective-permute-done((bf16[256,2304]{1,0:T(8,128)(2,1)S(1)}, bf16[256,2304]{1,0:T(8,128)(2,1)S(1)}, u32[]{:S(2)}, u32[]{:S(2)}) %collective-permute-start.1) | collective-permute-done | bytes 1179680 | tf_op jit(solution)/shard_map/ppermute | solution.py:577
  56.7 21.4 %all-gather.6.cloned.1.call-done = bf16[2304,1920]{1,0:T(8,128)(2,1)} async-done(((bf16[288,1920]{1,0:T(8,128)(2,1)}), bf16[2304,1920]{1,0:T(8,128)(2,1)}) %all-gather.6.cloned.1.call-update) | async-done | bytes 8847376 | tf_op jit(solution)/shard_map/all_gather | solution.py:709
  84.0 28.4 %collective-permute-done.3 = bf16[256,2304]{1,0:T(8,128)(2,1)} collective-permute-done((bf16[256,2304]{1,0:T(8,128)(2,1)}, bf16[256,2304]{1,0:T(8,128)(2,1)}, u32[]{:S(2)}, u32[]{:S(2)}) %collective-permute-start.3) | collective-permute-done | bytes 1179680 | tf_op jit(solution)/shard_map/ppermute | solution.py:577
  119.1 24.4 %collective-permute-done.5 = bf16[256,2304]{1,0:T(8,128)(2,1)} collective-permute-done((bf16[256,2304]{1,0:T(8,128)(2,1)}, bf16[256,2304]{1,0:T(8,128)(2,1)}, u32[]{:S(2)}, u32[]{:S(2)}) %collective-permute-start.5) | collective-permute-done | bytes 1179680 | tf_op jit(solution)/shard_map/ppermute | solution.py:577
  149.2 8.5 all-gather
  164.2 5.9 collective-permute-start.7
  173.7 18.6 %fusion.54.q_in.k_in.v_in = f32[1024,1920]{1,0:T(8,128)} fusion(bf16[2304,1920]{1,0:T(8,128)(2,1)} %all-gather.6.cloned.1.call-done, f32[2304]{0:T(1024)S(1)} %get-tuple-element.273, f32[1024]{0:T(1024)S(1)} %add_rsqrt_fusion, bf16[256,2304]{1,0:T(8,128)(2,1)S(1)} %get-tuple-element.323, bf16[256,2304]{1,0:T(8,128)(2,1)S(1)} %copy-done.51, ...), kind=kOutput, calls=%fused_computation.143 | convolution fusion | flops 9085648896 | bytes 21443584 | tf_op jit(solution)/shard_map/dot_general | solution.py:30
  206.3 30.2 %attend.1 = (bf16[1024,640]{1,0:T(8,128)(2,1)S(1)}, bf16[1024,640]{1,0:T(8,128)(2,1)S(1)}, bf16[1024,640]{1,0:T(8,128)(2,1)S(1)}, bf16[1024,640]{1,0:T(8,128)(2,1)S(1)}, f32[5,8,1024]{2,1,0:T(8,128)S(1)}) custom-call(s32[8]{0:T(128)S(1)} %and_select_fusion.order, s32[1]{0:T(128)} %dynamic_slice.57.length, f32[1024,1920]{1,0:T(8,128)S(1)} %copy-done.2, ...), custom_call_target="tpu_custom_call" | custom-call | flops 2415919104 | bytes 15728640 | tf_op jit(solution)/shard_map/attend/pallas_call | solution.py:451
  242.8 5.9 convolution_convert_fusion.4
  248.9 6.8 collective-permute-start.14
  259.0 13.7 %collective-permute-done.17 = bf16[256,2304]{1,0:T(8,128)(2,1)} collective-permute-done((bf16[256,2304]{1,0:T(8,128)(2,1)}, bf16[256,2304]{1,0:T(8,128)(2,1)}, u32[]{:S(2)}, u32[]{:S(2)}) %collective-permute-start.17) | collective-permute-done | bytes 1179680 | tf_op jit(solution)/shard_map/ppermute | solution.py:577
  272.7 8.0 collective-permute-done.14
  281.9 5.3 collective-permute-start.18
  289.5 9.1 multiply_convert_fusion
  298.6 12.5 %collective-permute-done.18 = bf16[256,2304]{1,0:T(8,128)(2,1)S(1)} collective-permute-done((bf16[256,2304]{1,0:T(8,128)(2,1)S(1)}, bf16[256,2304]{1,0:T(8,128)(2,1)S(1)}, u32[]{:S(2)}, u32[]{:S(2)}) %collective-permute-start.18) | collective-permute-done | bytes 1179680 | tf_op jit(solution)/shard_map/ppermute | solution.py:633
  314.1 7.2 collective-permute-start.20
  321.3 9.1 fusion.40
  330.4 7.1 fusion.42
  347.5 6.1 collective-permute-start.22
  353.6 20.2 %collective-permute-done.23 = bf16[256,2304]{1,0:T(8,128)(2,1)} collective-permute-done((bf16[256,2304]{1,0:T(8,128)(2,1)S(1)}, bf16[256,2304]{1,0:T(8,128)(2,1)}, u32[]{:S(2)}, u32[]{:S(2)}) %collective-permute-start.23) | collective-permute-done | bytes 1179680 | tf_op jit(solution)/shard_map/ppermute | solution.py:577
  380.9 17.9 %fusion.32 = f32[512,2880]{0,1:T(8,128)} fusion(bf16[2304,2880]{1,0:T(8,128)(2,1)} %all-gather.12.cloned.1.call-done, bf16[256,2304]{1,0:T(8,128)(2,1)} %fusion.47, bf16[256,2304]{1,0:T(8,128)(2,1)} %copy-done.47), kind=kOutput, calls=%fused_computation.90 | convolution fusion | flops 6799491072 | bytes 21528576 | tf_op jit(solution)/shard_map/dot_general | solution.py:30
  398.8 5.4 multiply_convert_fusion.5
  408.8 12.5 %convolution_convert_fusion.8 = bf16[512,2304]{1,0:T(8,128)(2,1)} fusion(bf16[512,2880]{0,1:T(8,128)(2,1)S(1)} %pad_maximum_fusion.5, bf16[2304,2880]{1,0:T(8,128)(2,1)} %all-gather.12.cloned.1.call-done), kind=kOutput, calls=%fused_computation.29 | convolution fusion | flops 6795952128 | bytes 18579456 | tf_op jit(solution)/shard_map/dot_general | solution.py:26
  424.0 10.8 collective-permute-done.27
  436.2 17.9 %fusion.36 = f32[512,2880]{0,1:T(8,128)} fusion(bf16[2304,2880]{1,0:T(8,128)(2,1)} %all-gather.12.cloned.1.call-done, bf16[256,2304]{1,0:T(8,128)(2,1)} %select_select_fusion.17, bf16[256,2304]{1,0:T(8,128)(2,1)} %select_select_fusion.6), kind=kOutput, calls=%fused_computation.94 | convolution fusion | flops 6799491072 | bytes 21528576 | tf_op jit(solution)/shard_map/dot_general | solution.py:30
  454.1 5.7 multiply_convert_fusion.3
  460.9 12.3 %convolution_convert_fusion.2 = bf16[2304,1440]{1,0:T(8,128)(2,1)} fusion(bf16[1024,2304]{1,0:T(8,128)(2,1)} %multiply_convert_fusion, bf16[512,1440]{0,1:T(8,128)(2,1)S(1)} %get-tuple-element.292, bf16[512,1440]{0,1:T(8,128)(2,1)S(1)} %copy-done.62), kind=kOutput, calls=%fused_computation.5 | convolution fusion | flops 6803988480 | bytes 14303232 | tf_op jit(solution)/shard_map/dot_general | solution.py:22
  473.3 14.2 %convolution_convert_fusion.7 = bf16[512,2304]{1,0:T(8,128)(2,1)} fusion(bf16[2304,2880]{1,0:T(8,128)(2,1)} %all-gather.12.cloned.1.call-done, bf16[512,1440]{0,1:T(8,128)(2,1)} %get-tuple-element.283, bf16[512,1440]{0,1:T(8,128)(2,1)} %get-tuple-element.282), kind=kOutput, calls=%fused_computation.28 | convolution fusion | flops 6801850368 | bytes 18579456 | tf_op jit(solution)/shard_map/dot_general | solution.py:26
  494.7 13.0 %convolution_convert_fusion.5 = bf16[1024,2304]{1,0:T(8,128)(2,1)} fusion(bf16[2304,1440]{1,0:T(8,128)(2,1)} %all-gather.10.cloned.1.call-done, bf16[512,1440]{0,1:T(8,128)(2,1)S(1)} %copy-done.65, bf16[512,1440]{0,1:T(8,128)(2,1)S(1)} %copy-done.63), kind=kOutput, calls=%fused_computation.19 | convolution fusion | flops 6803030016 | bytes 14303232 | tf_op jit(solution)/shard_map/dot_general | solution.py:26
  507.7 4.7 collective-permute-done.28
  516.1 5.0 collective-permute-start.30
  521.1 19.3 %convolution_convert_fusion = bf16[2304,2880]{1,0:T(8,128)(2,1)} fusion(bf16[1024,2304]{1,0:T(8,128)(2,1)S(1)} %pad_maximum_fusion.3, bf16[512,1440]{0,1:T(8,128)(2,1)} %get-tuple-element.283, bf16[512,1440]{0,1:T(8,128)(2,1)} %get-tuple-element.282, bf16[512,2880]{0,1:T(8,128)(2,1)S(1)} %copy-done.59), kind=kOutput, calls=%fused_computation.1 | convolution fusion | flops 13613875200 | bytes 23887872 | tf_op jit(solution)/shard_map/dot_general | solution.py:22
  545.0 4.8 collective-permute-start.32
  550.5 16.9 %collective-permute-done.33 = bf16[256,2304]{1,0:T(8,128)(2,1)S(1)} collective-permute-done((bf16[256,2304]{1,0:T(8,128)(2,1)S(1)}, bf16[256,2304]{1,0:T(8,128)(2,1)S(1)}, u32[]{:S(2)}, u32[]{:S(2)}) %collective-permute-start.33) | collective-permute-done | bytes 1179680 | tf_op jit(solution)/shard_map/ppermute | solution.py:634
  573.7 5.0 collective-permute-start.34
  578.7 16.8 %collective-permute-done.35 = bf16[256,2304]{1,0:T(8,128)(2,1)S(1)} collective-permute-done((bf16[256,2304]{1,0:T(8,128)(2,1)S(1)}, bf16[256,2304]{1,0:T(8,128)(2,1)S(1)}, u32[]{:S(2)}, u32[]{:S(2)}) %collective-permute-start.35) | collective-permute-done | bytes 1179680 | tf_op jit(solution)/shard_map/ppermute | solution.py:577
  606.8 17.8 %collective-permute-done.38 = bf16[256,2304]{1,0:T(8,128)(2,1)S(1)} collective-permute-done((bf16[256,2304]{1,0:T(8,128)(2,1)S(1)}, bf16[256,2304]{1,0:T(8,128)(2,1)S(1)}, u32[]{:S(2)}, u32[]{:S(2)}) %collective-permute-start.38) | collective-permute-done | bytes 1179680 | tf_op jit(solution)/shard_map/ppermute | solution.py:633
  625.8 9.7 collective-permute-start.42
  637.7 11.4 %collective-permute-done.42 = bf16[256,2304]{1,0:T(8,128)(2,1)S(1)} collective-permute-done((bf16[256,2304]{1,0:T(8,128)(2,1)S(1)}, bf16[256,2304]{1,0:T(8,128)(2,1)S(1)}, u32[]{:S(2)}, u32[]{:S(2)}) %collective-permute-start.42) | collective-permute-done | bytes 1179680 | tf_op jit(solution)/shard_map/ppermute | solution.py:633
  656.0 7.9 convolution_convert_fusion.9.do_in
  669.3 26.7 %attend_back.1 = bf16[1024,1920]{1,0:T(8,128)(2,1)S(1)} custom-call(s32[8]{0:T(128)S(1)} %copy-done.12, s32[1]{0:T(128)} %dynamic_slice.57.length, bf16[1024,640]{1,0:T(8,128)(2,1)S(1)} %copy-done.16, bf16[1024,640]{1,0:T(8,128)(2,1)S(1)} %copy-done.18, bf16[1024,640]{1,0:T(8,128)(2,1)S(1)} %copy-done.20, f32[5,8,1024]{2,1,0:T(8,128)S(1)} %get-tuple-element.182.log_in, ...), custom_call_target="tpu_custom_call" | custom-call | flops 6039797760 | bytes 10485760 | tf_op jit(solution)/shard_map/attend_back/pallas_call | solution.py:478
  697.9 12.8 %convolution_convert_fusion.1 = bf16[2304,1920]{1,0:T(8,128)(2,1)} fusion(bf16[1024,1920]{1,0:T(8,128)(2,1)S(1)} %attend_back.1, f32[2304]{0:T(1024)S(1)} %copy-done.80, f32[1024]{0:T(1024)S(1)} %copy-done.90, bf16[256,2304]{1,0:T(8,128)(2,1)S(1)} %copy-done.57, bf16[256,2304]{1,0:T(8,128)(2,1)S(1)} %copy-done.52, bf16[256,2304]{1,0:T(8,128)(2,1)S(1)} %copy-done.55, ...), kind=kOutput, calls=%fused_computation.4 | convolution fusion | flops 9090072576 | bytes 17511424 | tf_op jit(solution)/shard_map/dot_general | solution.py:22
  713.8 5.2 concatenate.61
  724.6 4.7 collective-permute-start.44
  734.4 5.6 collective-permute-start.46
  740.0 12.5 %convolution_convert_fusion.3 = bf16[1024,2304]{1,0:T(8,128)(2,1)S(1)} fusion(bf16[1024,1920]{1,0:T(8,128)(2,1)S(1)} %copy-done.22, bf16[2304,1920]{1,0:T(8,128)(2,1)} %all-gather.6.cloned.1.call-done), kind=kOutput, calls=%fused_computation.17 | convolution fusion | flops 9062055936 | bytes 17498112 | tf_op jit(solution)/shard_map/dot_general | solution.py:26
  752.5 42.4 %collective-permute-done.47 = bf16[256,2304]{1,0:T(8,128)(2,1)S(1)} collective-permute-done((bf16[256,2304]{1,0:T(8,128)(2,1)}, bf16[256,2304]{1,0:T(8,128)(2,1)S(1)}, u32[]{:S(2)}, u32[]{:S(2)}) %collective-permute-start.47) | collective-permute-done | bytes 1179680 | tf_op jit(solution)/shard_map/ppermute | solution.py:634
  800.2 14.5 %collective-permute-start.50 = (bf16[256,2304]{1,0:T(8,128)(2,1)S(1)}, bf16[256,2304]{1,0:T(8,128)(2,1)S(1)}, u32[]{:S(2)}, u32[]{:S(2)}) collective-permute-start(bf16[256,2304]{1,0:T(8,128)(2,1)S(1)} %slice.130), channel_id=1, source_target_pairs={{0,2},{1,3},{8,10},{9,11},{16,18},{17,19},{24,26},{25,27}} | collective-permute-start | bytes 3538952 | tf_op jit(solution)/shard_map/ppermute | solution.py:633
  818.9 9.5 collective-permute-done.50
  828.4 25.3 %collective-permute-done.49 = bf16[288,4352]{1,0:T(8,128)(2,1)} collective-permute-done((bf16[288,4352]{1,0:T(8,128)(2,1)S(1)}, bf16[288,4352]{1,0:T(8,128)(2,1)}, u32[]{:S(2)}, u32[]{:S(2)}) %collective-permute-start.49) | collective-permute-done | bytes 2506784 | tf_op jit(solution)/shard_map/ppermute | solution.py:577
  860.7 6.9 collective-permute-start.54
  867.7 7.5 convolution_convert_fusion.6
  875.2 5.1 collective-permute-done.54
  880.3 18.5 %collective-permute-done.53 = bf16[288,4352]{1,0:T(8,128)(2,1)} collective-permute-done((bf16[288,4352]{1,0:T(8,128)(2,1)}, bf16[288,4352]{1,0:T(8,128)(2,1)}, u32[]{:S(2)}, u32[]{:S(2)}) %collective-permute-start.53) | collective-permute-done | bytes 2506784 | tf_op jit(solution)/shard_map/ppermute | solution.py:577
  898.8 6.8 select_select_fusion.3
  916.0 8.7 reduce-scatter.11.cloned.1.call-done
  944.3 7.1 join_turned.2
  951.4 10.5 join_columns.2
  961.9 26.9 %collective-permute-done.57 = bf16[256,2304]{1,0:T(8,128)(2,1)S(1)} collective-permute-done((bf16[256,2304]{1,0:T(8,128)(2,1)}, bf16[256,2304]{1,0:T(8,128)(2,1)S(1)}, u32[]{:S(2)}, u32[]{:S(2)}) %collective-permute-start.57) | collective-permute-done | bytes 1179680 | tf_op jit(solution)/shard_map/ppermute | solution.py:634
  994.6 34.1 %collective-permute-done.62 = bf16[288,2560]{1,0:T(8,128)(2,1)S(1)} collective-permute-done((bf16[288,2560]{1,0:T(8,128)(2,1)S(1)}, bf16[288,2560]{1,0:T(8,128)(2,1)S(1)}, u32[]{:S(2)}, u32[]{:S(2)}) %collective-permute-start.62) | collective-permute-done | bytes 1474592 | tf_op jit(solution)/shard_map/ppermute | solution.py:577
  1036.6 30.9 %collective-permute-done.64 = bf16[288,2560]{1,0:T(8,128)(2,1)S(1)} collective-permute-done((bf16[288,2560]{1,0:T(8,128)(2,1)S(1)}, bf16[288,2560]{1,0:T(8,128)(2,1)S(1)}, u32[]{:S(2)}, u32[]{:S(2)}) %collective-permute-start.64) | collective-permute-done | bytes 1474592 | tf_op jit(solution)/shard_map/ppermute | solution.py:577
  1077.1 8.6 copy.59
  1095.8 7.4 join_columns.3
  (436 shorter events, 248.9 us)
Async XLA Ops:
  7.2 70.9 %all-gather.6.cloned.1.call-start = ((), (), s32[]{:S(2)}) async-start(), calls=%async_computation.4 | async-start | bytes 9953280 | tf_op jit(solution)/shard_map/all_gather | solution.py:709
  19.3 223.6 %all-gather.8.cloned.1.call-start = ((), (), s32[]{:S(2)}) async-start(), calls=%async_computation.5 | async-start | bytes 3317760 | tf_op jit(solution)/shard_map/all_gather | solution.py:709
  21.6 30.9 %collective-permute-start.1 = (bf16[256,2304]{1,0:T(8,128)(2,1)S(1)}, bf16[256,2304]{1,0:T(8,128)(2,1)S(1)}, u32[]{:S(2)}, u32[]{:S(2)}) collective-permute-start(bf16[256,2304]{1,0:T(8,128)(2,1)S(1)} %get-tuple-element.275), channel_id=1, source_target_pairs={{2,0},{4,2},{6,4},{3,1},{5,3},{7,5},{10,8},{12,10},{14,12},{11,9},... | collective-permute-start | bytes 3538952 | tf_op jit(solution)/shard_map/ppermute | solution.py:577
  22.9 30.8 %collective-permute-start = (bf16[256,2304]{1,0:T(8,128)(2,1)S(1)}, bf16[256,2304]{1,0:T(8,128)(2,1)}, u32[]{:S(2)}, u32[]{:S(2)}) collective-permute-start(bf16[256,2304]{1,0:T(8,128)(2,1)S(1)} %get-tuple-element.275), channel_id=1, source_target_pairs={{0,2},{2,4},{4,6},{1,3},{3,5},{5,7},{8,10},{10,12},{12,14},{9,11},... | collective-permute-start | bytes 3538952 | tf_op jit(solution)/shard_map/ppermute | solution.py:576
  78.1 243.2 %all-gather.10.cloned.1.call-start = ((), (), s32[]{:S(2)}) async-start(), calls=%async_computation.6 | async-start | bytes 7962624 | tf_op jit(solution)/shard_map/all_gather | solution.py:709
  79.8 32.5 %collective-permute-start.3 = (bf16[256,2304]{1,0:T(8,128)(2,1)}, bf16[256,2304]{1,0:T(8,128)(2,1)}, u32[]{:S(2)}, u32[]{:S(2)}) collective-permute-start(bf16[256,2304]{1,0:T(8,128)(2,1)} %copy-done.71), channel_id=1, source_target_pairs={{2,0},{4,2},{3,1},{5,3},{10,8},{12,10},{11,9},{13,11},{18,16},{20,... | collective-permute-start | bytes 3538952 | tf_op jit(solution)/shard_map/ppermute | solution.py:577
  83.7 32.7 %collective-permute-start.6 = (bf16[288,1440]{1,0:T(8,128)(2,1)}, bf16[288,1440]{1,0:T(8,128)(2,1)}, u32[]{:S(2)}, u32[]{:S(2)}) collective-permute-start(bf16[288,1440]{1,0:T(8,128)(2,1)} %dynamic-slice_bitcast_fusion.2), channel_id=1, source_target_pairs={{0,1},{1,0},{2,3},{3,2},{4,5},{5,4},{6,7},{7,6},{8,9},{9,8},{10,11... | collective-permute-start | bytes 2488328 | tf_op jit(solution)/shard_map/ppermute | solution.py:705
  114.0 29.5 %collective-permute-start.5 = (bf16[256,2304]{1,0:T(8,128)(2,1)}, bf16[256,2304]{1,0:T(8,128)(2,1)}, u32[]{:S(2)}, u32[]{:S(2)}) collective-permute-start(bf16[256,2304]{1,0:T(8,128)(2,1)} %collective-permute-done.3), channel_id=1, source_target_pairs={{2,0},{3,1},{10,8},{11,9},{18,16},{19,17},{26,24},{27,25}} | collective-permute-start | bytes 3538952 | tf_op jit(solution)/shard_map/ppermute | solution.py:577
  143.5 237.3 %all-gather.12.cloned.1.call-start = ((), (), s32[]{:S(2)}) async-start(), calls=%async_computation.7 | async-start | bytes 15261696 | tf_op jit(solution)/shard_map/all_gather | solution.py:709
  162.7 30.8 %collective-permute-start.8 = (bf16[256,2304]{1,0:T(8,128)(2,1)}, bf16[256,2304]{1,0:T(8,128)(2,1)}, u32[]{:S(2)}, u32[]{:S(2)}) collective-permute-start(bf16[256,2304]{1,0:T(8,128)(2,1)} %dynamic-slice_bitcast_fusion), channel_id=1, source_target_pairs={{2,0},{4,2},{6,4},{3,1},{5,3},{7,5},{10,8},{12,10},{14,12},{11,9},... | collective-permute-start | bytes 3538952 | tf_op jit(solution)/shard_map/ppermute | solution.py:577
  164.2 30.5 %collective-permute-start.7 = (bf16[256,2304]{1,0:T(8,128)(2,1)}, bf16[256,2304]{1,0:T(8,128)(2,1)}, u32[]{:S(2)}, u32[]{:S(2)}) collective-permute-start(bf16[256,2304]{1,0:T(8,128)(2,1)} %dynamic-slice_bitcast_fusion), channel_id=1, source_target_pairs={{0,2},{2,4},{4,6},{1,3},{3,5},{5,7},{8,10},{10,12},{12,14},{9,11},... | collective-permute-start | bytes 3538952 | tf_op jit(solution)/shard_map/ppermute | solution.py:576
  194.7 469.2 %reduce-scatter.7.cloned.1.call-start = ((), (), s32[]{:S(2)}) async-start(), calls=%async_computation.9 | async-start | bytes 7962624 | tf_op jit(solution)/shard_map/reduce_scatter | solution.py:712
  194.8 44.9 %collective-permute-start.12 = (bf16[256,2304]{1,0:T(8,128)(2,1)}, bf16[256,2304]{1,0:T(8,128)(2,1)}, u32[]{:S(2)}, u32[]{:S(2)}) collective-permute-start(bf16[256,2304]{1,0:T(8,128)(2,1)} %collective-permute-done.7), channel_id=1, source_target_pairs={{2,4},{4,6},{3,5},{5,7},{10,12},{12,14},{11,13},{13,15},{18,20},{2... | collective-permute-start | bytes 3538952 | tf_op jit(solution)/shard_map/ppermute | solution.py:576
  196.6 43.2 %collective-permute-start.13 = (bf16[256,2304]{1,0:T(8,128)(2,1)}, bf16[256,2304]{1,0:T(8,128)(2,1)}, u32[]{:S(2)}, u32[]{:S(2)}) collective-permute-start(bf16[256,2304]{1,0:T(8,128)(2,1)} %collective-permute-done.8), channel_id=1, source_target_pairs={{2,0},{4,2},{3,1},{5,3},{10,8},{12,10},{11,9},{13,11},{18,16},{20,... | collective-permute-start | bytes 3538952 | tf_op jit(solution)/shard_map/ppermute | solution.py:577
  239.8 19.2 %collective-permute-start.16 = (bf16[256,2304]{1,0:T(8,128)(2,1)}, bf16[256,2304]{1,0:T(8,128)(2,1)}, u32[]{:S(2)}, u32[]{:S(2)}) collective-permute-start(bf16[256,2304]{1,0:T(8,128)(2,1)} %collective-permute-done.12), channel_id=1, source_target_pairs={{4,6},{5,7},{12,14},{13,15},{20,22},{21,23},{28,30},{29,31}} | collective-permute-start | bytes 3538952 | tf_op jit(solution)/shard_map/ppermute | solution.py:576
  241.5 31.1 %collective-permute-start.17 = (bf16[256,2304]{1,0:T(8,128)(2,1)}, bf16[256,2304]{1,0:T(8,128)(2,1)}, u32[]{:S(2)}, u32[]{:S(2)}) collective-permute-start(bf16[256,2304]{1,0:T(8,128)(2,1)} %collective-permute-done.13), channel_id=1, source_target_pairs={{2,0},{3,1},{10,8},{11,9},{18,16},{19,17},{26,24},{27,25}} | collective-permute-start | bytes 3538952 | tf_op jit(solution)/shard_map/ppermute | solution.py:577
  248.9 31.7 %collective-permute-start.14 = (bf16[256,2304]{1,0:T(8,128)(2,1)S(1)}, bf16[256,2304]{1,0:T(8,128)(2,1)S(1)}, u32[]{:S(2)}, u32[]{:S(2)}) collective-permute-start(bf16[256,2304]{1,0:T(8,128)(2,1)S(1)} %slice.149), channel_id=1, source_target_pairs={{0,2},{1,3},{8,10},{9,11},{16,18},{17,19},{24,26},{25,27}} | collective-permute-start | bytes 3538952 | tf_op jit(solution)/shard_map/ppermute | solution.py:633
  255.8 24.9 %collective-permute-start.15 = (bf16[256,2304]{1,0:T(8,128)(2,1)S(1)}, bf16[256,2304]{1,0:T(8,128)(2,1)S(1)}, u32[]{:S(2)}, u32[]{:S(2)}) collective-permute-start(bf16[256,2304]{1,0:T(8,128)(2,1)S(1)} %slice.149), channel_id=1, source_target_pairs={{6,4},{7,5},{14,12},{15,13},{22,20},{23,21},{30,28},{31,29}} | collective-permute-start | bytes 3538952 | tf_op jit(solution)/shard_map/ppermute | solution.py:634
  281.2 17.4 %collective-permute-start.19 = (bf16[256,2304]{1,0:T(8,128)(2,1)S(1)}, bf16[256,2304]{1,0:T(8,128)(2,1)S(1)}, u32[]{:S(2)}, u32[]{:S(2)}) collective-permute-start(bf16[256,2304]{1,0:T(8,128)(2,1)S(1)} %get-tuple-element.306), channel_id=1, source_target_pairs={{4,2},{6,4},{5,3},{7,5},{12,10},{14,12},{13,11},{15,13},{20,18},{2... | collective-permute-start | bytes 3538952 | tf_op jit(solution)/shard_map/ppermute | solution.py:634
  281.9 29.2 %collective-permute-start.18 = (bf16[256,2304]{1,0:T(8,128)(2,1)S(1)}, bf16[256,2304]{1,0:T(8,128)(2,1)S(1)}, u32[]{:S(2)}, u32[]{:S(2)}) collective-permute-start(bf16[256,2304]{1,0:T(8,128)(2,1)S(1)} %get-tuple-element.307), channel_id=1, source_target_pairs={{0,2},{2,4},{1,3},{3,5},{8,10},{10,12},{9,11},{11,13},{16,18},{18,... | collective-permute-start | bytes 3538952 | tf_op jit(solution)/shard_map/ppermute | solution.py:633
  312.8 29.2 %collective-permute-start.21 = (bf16[256,2304]{1,0:T(8,128)(2,1)}, bf16[256,2304]{1,0:T(8,128)(2,1)S(1)}, u32[]{:S(2)}, u32[]{:S(2)}) collective-permute-start(bf16[256,2304]{1,0:T(8,128)(2,1)} %get-tuple-element.304), channel_id=1, source_target_pairs={{2,0},{4,2},{6,4},{3,1},{5,3},{7,5},{10,8},{12,10},{14,12},{11,9},... | collective-permute-start | bytes 3538952 | tf_op jit(solution)/shard_map/ppermute | solution.py:634
  314.1 29.0 %collective-permute-start.20 = (bf16[256,2304]{1,0:T(8,128)(2,1)S(1)}, bf16[256,2304]{1,0:T(8,128)(2,1)}, u32[]{:S(2)}, u32[]{:S(2)}) collective-permute-start(bf16[256,2304]{1,0:T(8,128)(2,1)S(1)} %get-tuple-element.305), channel_id=1, source_target_pairs={{0,2},{2,4},{4,6},{1,3},{3,5},{5,7},{8,10},{10,12},{12,14},{9,11},... | collective-permute-start | bytes 3538952 | tf_op jit(solution)/shard_map/ppermute | solution.py:633
  346.2 27.6 %collective-permute-start.23 = (bf16[256,2304]{1,0:T(8,128)(2,1)S(1)}, bf16[256,2304]{1,0:T(8,128)(2,1)}, u32[]{:S(2)}, u32[]{:S(2)}) collective-permute-start(bf16[256,2304]{1,0:T(8,128)(2,1)S(1)} %multiply_convert_fusion.9), channel_id=1, source_target_pairs={{2,0},{4,2},{6,4},{3,1},{5,3},{7,5},{10,8},{12,10},{14,12},{11,9},... | collective-permute-start | bytes 3538952 | tf_op jit(solution)/shard_map/ppermute | solution.py:577
  347.5 27.4 %collective-permute-start.22 = (bf16[256,2304]{1,0:T(8,128)(2,1)S(1)}, bf16[256,2304]{1,0:T(8,128)(2,1)}, u32[]{:S(2)}, u32[]{:S(2)}) collective-permute-start(bf16[256,2304]{1,0:T(8,128)(2,1)S(1)} %multiply_convert_fusion.9), channel_id=1, source_target_pairs={{0,2},{2,4},{4,6},{1,3},{3,5},{5,7},{8,10},{10,12},{12,14},{9,11},... | collective-permute-start | bytes 3538952 | tf_op jit(solution)/shard_map/ppermute | solution.py:576
  374.9 29.5 %collective-permute-start.24 = (bf16[256,2304]{1,0:T(8,128)(2,1)}, bf16[256,2304]{1,0:T(8,128)(2,1)}, u32[]{:S(2)}, u32[]{:S(2)}) collective-permute-start(bf16[256,2304]{1,0:T(8,128)(2,1)} %collective-permute-done.22), channel_id=1, source_target_pairs={{2,4},{4,6},{3,5},{5,7},{10,12},{12,14},{11,13},{13,15},{18,20},{2... | collective-permute-start | bytes 3538952 | tf_op jit(solution)/shard_map/ppermute | solution.py:576
  376.6 29.8 %collective-permute-start.25 = (bf16[256,2304]{1,0:T(8,128)(2,1)}, bf16[256,2304]{1,0:T(8,128)(2,1)}, u32[]{:S(2)}, u32[]{:S(2)}) collective-permute-start(bf16[256,2304]{1,0:T(8,128)(2,1)} %collective-permute-done.23), channel_id=1, source_target_pairs={{2,0},{4,2},{3,1},{5,3},{10,8},{12,10},{11,9},{13,11},{18,16},{20,... | collective-permute-start | bytes 3538952 | tf_op jit(solution)/shard_map/ppermute | solution.py:577
  406.3 17.7 %collective-permute-start.26 = (bf16[256,2304]{1,0:T(8,128)(2,1)}, bf16[256,2304]{1,0:T(8,128)(2,1)S(1)}, u32[]{:S(2)}, u32[]{:S(2)}) collective-permute-start(bf16[256,2304]{1,0:T(8,128)(2,1)} %collective-permute-done.24), channel_id=1, source_target_pairs={{4,6},{5,7},{12,14},{13,15},{20,22},{21,23},{28,30},{29,31}} | collective-permute-start | bytes 3538952 | tf_op jit(solution)/shard_map/ppermute | solution.py:576
  407.1 27.7 %collective-permute-start.27 = (bf16[256,2304]{1,0:T(8,128)(2,1)}, bf16[256,2304]{1,0:T(8,128)(2,1)S(1)}, u32[]{:S(2)}, u32[]{:S(2)}) collective-permute-start(bf16[256,2304]{1,0:T(8,128)(2,1)} %collective-permute-done.25), channel_id=1, source_target_pairs={{2,0},{3,1},{10,8},{11,9},{18,16},{19,17},{26,24},{27,25}} | collective-permute-start | bytes 3538952 | tf_op jit(solution)/shard_map/ppermute | solution.py:577
  473.3 190.7 %reduce-scatter.5.cloned.1.call-start = ((), (), s32[]{:S(2)}) async-start(), calls=%async_computation.8 | async-start | bytes 15261696 | tf_op jit(solution)/shard_map/reduce_scatter | solution.py:712
  489.2 23.3 %collective-permute-start.28 = (bf16[256,2304]{1,0:T(8,128)(2,1)S(1)}, bf16[256,2304]{1,0:T(8,128)(2,1)S(1)}, u32[]{:S(2)}, u32[]{:S(2)}) collective-permute-start(bf16[256,2304]{1,0:T(8,128)(2,1)S(1)} %slice.157), channel_id=1, source_target_pairs={{0,2},{1,3},{8,10},{9,11},{16,18},{17,19},{24,26},{25,27}} | collective-permute-start | bytes 3538952 | tf_op jit(solution)/shard_map/ppermute | solution.py:633
  492.4 20.0 %collective-permute-start.29 = (bf16[256,2304]{1,0:T(8,128)(2,1)S(1)}, bf16[256,2304]{1,0:T(8,128)(2,1)S(1)}, u32[]{:S(2)}, u32[]{:S(2)}) collective-permute-start(bf16[256,2304]{1,0:T(8,128)(2,1)S(1)} %slice.157), channel_id=1, source_target_pairs={{6,4},{7,5},{14,12},{15,13},{22,20},{23,21},{30,28},{31,29}} | collective-permute-start | bytes 3538952 | tf_op jit(solution)/shard_map/ppermute | solution.py:634
  514.4 26.0 %collective-permute-start.31 = (bf16[256,2304]{1,0:T(8,128)(2,1)}, bf16[256,2304]{1,0:T(8,128)(2,1)}, u32[]{:S(2)}, u32[]{:S(2)}) collective-permute-start(bf16[256,2304]{1,0:T(8,128)(2,1)} %get-tuple-element.318), channel_id=1, source_target_pairs={{4,2},{6,4},{5,3},{7,5},{12,10},{14,12},{13,11},{15,13},{20,18},{2... | collective-permute-start | bytes 3538952 | tf_op jit(solution)/shard_map/ppermute | solution.py:634
  516.1 24.3 %collective-permute-start.30 = (bf16[256,2304]{1,0:T(8,128)(2,1)}, bf16[256,2304]{1,0:T(8,128)(2,1)}, u32[]{:S(2)}, u32[]{:S(2)}) collective-permute-start(bf16[256,2304]{1,0:T(8,128)(2,1)} %get-tuple-element.319), channel_id=1, source_target_pairs={{0,2},{2,4},{1,3},{3,5},{8,10},{10,12},{9,11},{11,13},{16,18},{18,... | collective-permute-start | bytes 3538952 | tf_op jit(solution)/shard_map/ppermute | solution.py:633
  540.4 372.1 %reduce-scatter.9.cloned.1.call-start = ((), (), s32[]{:S(2)}) async-start(), calls=%async_computation.10 | async-start | bytes 9953280 | tf_op jit(solution)/shard_map/reduce_scatter | solution.py:712
  543.7 23.8 %collective-permute-start.33 = (bf16[256,2304]{1,0:T(8,128)(2,1)S(1)}, bf16[256,2304]{1,0:T(8,128)(2,1)S(1)}, u32[]{:S(2)}, u32[]{:S(2)}) collective-permute-start(bf16[256,2304]{1,0:T(8,128)(2,1)S(1)} %get-tuple-element.302), channel_id=1, source_target_pairs={{2,0},{4,2},{6,4},{3,1},{5,3},{7,5},{10,8},{12,10},{14,12},{11,9},... | collective-permute-start | bytes 3538952 | tf_op jit(solution)/shard_map/ppermute | solution.py:634
  545.0 23.6 %collective-permute-start.32 = (bf16[256,2304]{1,0:T(8,128)(2,1)S(1)}, bf16[256,2304]{1,0:T(8,128)(2,1)S(1)}, u32[]{:S(2)}, u32[]{:S(2)}) collective-permute-start(bf16[256,2304]{1,0:T(8,128)(2,1)S(1)} %get-tuple-element.303), channel_id=1, source_target_pairs={{0,2},{2,4},{4,6},{1,3},{3,5},{5,7},{8,10},{10,12},{12,14},{9,11},... | collective-permute-start | bytes 3538952 | tf_op jit(solution)/shard_map/ppermute | solution.py:633
  572.4 23.0 %collective-permute-start.35 = (bf16[256,2304]{1,0:T(8,128)(2,1)S(1)}, bf16[256,2304]{1,0:T(8,128)(2,1)S(1)}, u32[]{:S(2)}, u32[]{:S(2)}) collective-permute-start(bf16[256,2304]{1,0:T(8,128)(2,1)S(1)} %get-tuple-element.276), channel_id=1, source_target_pairs={{2,0},{4,2},{6,4},{3,1},{5,3},{7,5},{10,8},{12,10},{14,12},{11,9},... | collective-permute-start | bytes 3538952 | tf_op jit(solution)/shard_map/ppermute | solution.py:577
  573.7 25.7 %collective-permute-start.34 = (bf16[256,2304]{1,0:T(8,128)(2,1)S(1)}, bf16[256,2304]{1,0:T(8,128)(2,1)S(1)}, u32[]{:S(2)}, u32[]{:S(2)}) collective-permute-start(bf16[256,2304]{1,0:T(8,128)(2,1)S(1)} %get-tuple-element.276), channel_id=1, source_target_pairs={{0,2},{2,4},{4,6},{1,3},{3,5},{5,7},{8,10},{10,12},{12,14},{9,11},... | collective-permute-start | bytes 3538952 | tf_op jit(solution)/shard_map/ppermute | solution.py:576
  600.2 24.3 %collective-permute-start.38 = (bf16[256,2304]{1,0:T(8,128)(2,1)S(1)}, bf16[256,2304]{1,0:T(8,128)(2,1)S(1)}, u32[]{:S(2)}, u32[]{:S(2)}) collective-permute-start(bf16[256,2304]{1,0:T(8,128)(2,1)S(1)} %slice.127), channel_id=1, source_target_pairs={{0,2},{1,3},{8,10},{9,11},{16,18},{17,19},{24,26},{25,27}} | collective-permute-start | bytes 3538952 | tf_op jit(solution)/shard_map/ppermute | solution.py:633
  604.7 19.8 %collective-permute-start.36 = (bf16[256,2304]{1,0:T(8,128)(2,1)S(1)}, bf16[256,2304]{1,0:T(8,128)(2,1)S(1)}, u32[]{:S(2)}, u32[]{:S(2)}) collective-permute-start(bf16[256,2304]{1,0:T(8,128)(2,1)S(1)} %collective-permute-done.34), channel_id=1, source_target_pairs={{2,4},{4,6},{3,5},{5,7},{10,12},{12,14},{11,13},{13,15},{18,20},{2... | collective-permute-start | bytes 3538952 | tf_op jit(solution)/shard_map/ppermute | solution.py:576
  605.5 19.1 %collective-permute-start.37 = (bf16[256,2304]{1,0:T(8,128)(2,1)S(1)}, bf16[256,2304]{1,0:T(8,128)(2,1)S(1)}, u32[]{:S(2)}, u32[]{:S(2)}) collective-permute-start(bf16[256,2304]{1,0:T(8,128)(2,1)S(1)} %collective-permute-done.35), channel_id=1, source_target_pairs={{2,0},{4,2},{3,1},{5,3},{10,8},{12,10},{11,9},{13,11},{18,16},{20,... | collective-permute-start | bytes 3538952 | tf_op jit(solution)/shard_map/ppermute | solution.py:577
  625.8 23.3 %collective-permute-start.42 = (bf16[256,2304]{1,0:T(8,128)(2,1)S(1)}, bf16[256,2304]{1,0:T(8,128)(2,1)S(1)}, u32[]{:S(2)}, u32[]{:S(2)}) collective-permute-start(bf16[256,2304]{1,0:T(8,128)(2,1)S(1)} %get-tuple-element.301), channel_id=1, source_target_pairs={{0,2},{2,4},{1,3},{3,5},{8,10},{10,12},{9,11},{11,13},{16,18},{18,... | collective-permute-start | bytes 3538952 | tf_op jit(solution)/shard_map/ppermute | solution.py:633
  636.3 18.1 %collective-permute-start.41 = (bf16[256,2304]{1,0:T(8,128)(2,1)S(1)}, bf16[256,2304]{1,0:T(8,128)(2,1)S(1)}, u32[]{:S(2)}, u32[]{:S(2)}) collective-permute-start(bf16[256,2304]{1,0:T(8,128)(2,1)S(1)} %collective-permute-done.37), channel_id=1, source_target_pairs={{2,0},{3,1},{10,8},{11,9},{18,16},{19,17},{26,24},{27,25}} | collective-permute-start | bytes 3538952 | tf_op jit(solution)/shard_map/ppermute | solution.py:577
  710.7 214.0 %reduce-scatter.11.cloned.1.call-start = ((), (), s32[]{:S(2)}) async-start(), calls=%async_computation.11 | async-start | bytes 3317760 | tf_op jit(solution)/shard_map/reduce_scatter | solution.py:712
  723.0 73.1 %collective-permute-start.45 = (bf16[288,4352]{1,0:T(8,128)(2,1)}, bf16[288,4352]{1,0:T(8,128)(2,1)S(1)}, u32[]{:S(2)}, u32[]{:S(2)}) collective-permute-start(bf16[288,4352]{1,0:T(8,128)(2,1)} %pad.21), channel_id=1, source_target_pairs={{2,0},{4,2},{6,4},{3,1},{5,3},{7,5},{10,8},{12,10},{14,12},{11,9},... | collective-permute-start | bytes 7520264 | tf_op jit(solution)/shard_map/ppermute | solution.py:577
  724.6 71.6 %collective-permute-start.44 = (bf16[288,4352]{1,0:T(8,128)(2,1)}, bf16[288,4352]{1,0:T(8,128)(2,1)S(1)}, u32[]{:S(2)}, u32[]{:S(2)}) collective-permute-start(bf16[288,4352]{1,0:T(8,128)(2,1)} %pad.21), channel_id=1, source_target_pairs={{0,2},{2,4},{4,6},{1,3},{3,5},{5,7},{8,10},{10,12},{12,14},{9,11},... | collective-permute-start | bytes 7520264 | tf_op jit(solution)/shard_map/ppermute | solution.py:576
  733.1 61.8 %collective-permute-start.47 = (bf16[256,2304]{1,0:T(8,128)(2,1)}, bf16[256,2304]{1,0:T(8,128)(2,1)S(1)}, u32[]{:S(2)}, u32[]{:S(2)}) collective-permute-start(bf16[256,2304]{1,0:T(8,128)(2,1)} %get-tuple-element.298), channel_id=1, source_target_pairs={{2,0},{4,2},{6,4},{3,1},{5,3},{7,5},{10,8},{12,10},{14,12},{11,9},... | collective-permute-start | bytes 3538952 | tf_op jit(solution)/shard_map/ppermute | solution.py:634
  734.4 61.8 %collective-permute-start.46 = (bf16[256,2304]{1,0:T(8,128)(2,1)}, bf16[256,2304]{1,0:T(8,128)(2,1)}, u32[]{:S(2)}, u32[]{:S(2)}) collective-permute-start(bf16[256,2304]{1,0:T(8,128)(2,1)} %get-tuple-element.299), channel_id=1, source_target_pairs={{0,2},{2,4},{4,6},{1,3},{3,5},{5,7},{8,10},{10,12},{12,14},{9,11},... | collective-permute-start | bytes 3538952 | tf_op jit(solution)/shard_map/ppermute | solution.py:633
  796.1 32.3 %collective-permute-start.48 = (bf16[288,4352]{1,0:T(8,128)(2,1)S(1)}, bf16[288,4352]{1,0:T(8,128)(2,1)}, u32[]{:S(2)}, u32[]{:S(2)}) collective-permute-start(bf16[288,4352]{1,0:T(8,128)(2,1)S(1)} %collective-permute-done.44), channel_id=1, source_target_pairs={{2,4},{4,6},{3,5},{5,7},{10,12},{12,14},{11,13},{13,15},{18,20},{2... | collective-permute-start | bytes 7520264 | tf_op jit(solution)/shard_map/ppermute | solution.py:576
  798.9 54.9 %collective-permute-start.49 = (bf16[288,4352]{1,0:T(8,128)(2,1)S(1)}, bf16[288,4352]{1,0:T(8,128)(2,1)}, u32[]{:S(2)}, u32[]{:S(2)}) collective-permute-start(bf16[288,4352]{1,0:T(8,128)(2,1)S(1)} %collective-permute-done.45), channel_id=1, source_target_pairs={{2,0},{4,2},{3,1},{5,3},{10,8},{12,10},{11,9},{13,11},{18,16},{20,... | collective-permute-start | bytes 7520264 | tf_op jit(solution)/shard_map/ppermute | solution.py:577
  800.2 28.2 %collective-permute-start.50 = (bf16[256,2304]{1,0:T(8,128)(2,1)S(1)}, bf16[256,2304]{1,0:T(8,128)(2,1)S(1)}, u32[]{:S(2)}, u32[]{:S(2)}) collective-permute-start(bf16[256,2304]{1,0:T(8,128)(2,1)S(1)} %slice.130), channel_id=1, source_target_pairs={{0,2},{1,3},{8,10},{9,11},{16,18},{17,19},{24,26},{25,27}} | collective-permute-start | bytes 3538952 | tf_op jit(solution)/shard_map/ppermute | solution.py:633
  853.7 26.6 %collective-permute-start.52 = (bf16[288,4352]{1,0:T(8,128)(2,1)}, bf16[288,4352]{1,0:T(8,128)(2,1)}, u32[]{:S(2)}, u32[]{:S(2)}) collective-permute-start(bf16[288,4352]{1,0:T(8,128)(2,1)} %collective-permute-done.48), channel_id=1, source_target_pairs={{4,6},{5,7},{12,14},{13,15},{20,22},{21,23},{28,30},{29,31}} | collective-permute-start | bytes 7520264 | tf_op jit(solution)/shard_map/ppermute | solution.py:576
  855.8 43.0 %collective-permute-start.53 = (bf16[288,4352]{1,0:T(8,128)(2,1)}, bf16[288,4352]{1,0:T(8,128)(2,1)}, u32[]{:S(2)}, u32[]{:S(2)}) collective-permute-start(bf16[288,4352]{1,0:T(8,128)(2,1)} %collective-permute-done.49), channel_id=1, source_target_pairs={{2,0},{3,1},{10,8},{11,9},{18,16},{19,17},{26,24},{27,25}} | collective-permute-start | bytes 7520264 | tf_op jit(solution)/shard_map/ppermute | solution.py:577
  859.0 16.2 %collective-permute-start.55 = (bf16[256,2304]{1,0:T(8,128)(2,1)}, bf16[256,2304]{1,0:T(8,128)(2,1)}, u32[]{:S(2)}, u32[]{:S(2)}) collective-permute-start(bf16[256,2304]{1,0:T(8,128)(2,1)} %get-tuple-element.296), channel_id=1, source_target_pairs={{4,2},{6,4},{5,3},{7,5},{12,10},{14,12},{13,11},{15,13},{20,18},{2... | collective-permute-start | bytes 3538952 | tf_op jit(solution)/shard_map/ppermute | solution.py:634
  860.7 19.6 %collective-permute-start.54 = (bf16[256,2304]{1,0:T(8,128)(2,1)}, bf16[256,2304]{1,0:T(8,128)(2,1)}, u32[]{:S(2)}, u32[]{:S(2)}) collective-permute-start(bf16[256,2304]{1,0:T(8,128)(2,1)} %get-tuple-element.297), channel_id=1, source_target_pairs={{0,2},{2,4},{1,3},{3,5},{8,10},{10,12},{9,11},{11,13},{16,18},{18,... | collective-permute-start | bytes 3538952 | tf_op jit(solution)/shard_map/ppermute | solution.py:633
  912.5 31.7 %collective-permute-start.60 = (bf16[2,288,4352]{2,1,0:T(8,128)(2,1)}, bf16[2,288,4352]{2,1,0:T(8,128)(2,1)}, u32[]{:S(2)}, u32[]{:S(2)}) collective-permute-start(bf16[2,288,4352]{2,1,0:T(8,128)(2,1)} %get-tuple-element.280), channel_id=1, source_target_pairs={{0,1},{1,0},{2,3},{3,2},{4,5},{5,4},{6,7},{7,6},{8,9},{9,8},{10,11... | collective-permute-start | bytes 15040520 | tf_op jit(solution)/shard_map/ppermute | solution.py:728
  927.5 62.6 %collective-permute-start.59 = (bf16[288,2560]{1,0:T(8,128)(2,1)S(1)}, bf16[288,2560]{1,0:T(8,128)(2,1)S(1)}, u32[]{:S(2)}, u32[]{:S(2)}) collective-permute-start(bf16[288,2560]{1,0:T(8,128)(2,1)S(1)} %concatenate.62), channel_id=1, source_target_pairs={{2,0},{4,2},{6,4},{3,1},{5,3},{7,5},{10,8},{12,10},{14,12},{11,9},... | collective-permute-start | bytes 4423688 | tf_op jit(solution)/shard_map/ppermute | solution.py:577
  929.0 61.0 %collective-permute-start.58 = (bf16[288,2560]{1,0:T(8,128)(2,1)S(1)}, bf16[288,2560]{1,0:T(8,128)(2,1)S(1)}, u32[]{:S(2)}, u32[]{:S(2)}) collective-permute-start(bf16[288,2560]{1,0:T(8,128)(2,1)S(1)} %concatenate.62), channel_id=1, source_target_pairs={{0,2},{2,4},{4,6},{1,3},{3,5},{5,7},{8,10},{10,12},{12,14},{9,11},... | collective-permute-start | bytes 4423688 | tf_op jit(solution)/shard_map/ppermute | solution.py:576
  938.2 50.5 %collective-permute-start.57 = (bf16[256,2304]{1,0:T(8,128)(2,1)}, bf16[256,2304]{1,0:T(8,128)(2,1)S(1)}, u32[]{:S(2)}, u32[]{:S(2)}) collective-permute-start(bf16[256,2304]{1,0:T(8,128)(2,1)} %get-tuple-element.294), channel_id=1, source_target_pairs={{2,0},{4,2},{6,4},{3,1},{5,3},{7,5},{10,8},{12,10},{14,12},{11,9},... | collective-permute-start | bytes 3538952 | tf_op jit(solution)/shard_map/ppermute | solution.py:634
  939.5 50.5 %collective-permute-start.56 = (bf16[256,2304]{1,0:T(8,128)(2,1)}, bf16[256,2304]{1,0:T(8,128)(2,1)S(1)}, u32[]{:S(2)}, u32[]{:S(2)}) collective-permute-start(bf16[256,2304]{1,0:T(8,128)(2,1)} %get-tuple-element.295), channel_id=1, source_target_pairs={{0,2},{2,4},{4,6},{1,3},{3,5},{5,7},{8,10},{10,12},{12,14},{9,11},... | collective-permute-start | bytes 3538952 | tf_op jit(solution)/shard_map/ppermute | solution.py:633
  944.2 84.5 %collective-permute-start.65 = (bf16[256,2304]{1,0:T(8,128)(2,1)S(1)}, bf16[256,2304]{1,0:T(8,128)(2,1)}, u32[]{:S(2)}, u32[]{:S(2)}) collective-permute-start(bf16[256,2304]{1,0:T(8,128)(2,1)S(1)} %copy-done.53), channel_id=1, source_target_pairs={{0,1},{1,0},{2,3},{3,2},{4,5},{5,4},{6,7},{7,6},{8,9},{9,8},{10,11... | collective-permute-start | bytes 3538952 | tf_op jit(solution)/shard_map/ppermute | solution.py:928
  990.9 37.7 %collective-permute-start.62 = (bf16[288,2560]{1,0:T(8,128)(2,1)S(1)}, bf16[288,2560]{1,0:T(8,128)(2,1)S(1)}, u32[]{:S(2)}, u32[]{:S(2)}) collective-permute-start(bf16[288,2560]{1,0:T(8,128)(2,1)S(1)} %collective-permute-done.59), channel_id=1, source_target_pairs={{2,0},{4,2},{3,1},{5,3},{10,8},{12,10},{11,9},{13,11},{18,16},{20,... | collective-permute-start | bytes 4423688 | tf_op jit(solution)/shard_map/ppermute | solution.py:577
  1030.9 36.6 %collective-permute-start.64 = (bf16[288,2560]{1,0:T(8,128)(2,1)S(1)}, bf16[288,2560]{1,0:T(8,128)(2,1)S(1)}, u32[]{:S(2)}, u32[]{:S(2)}) collective-permute-start(bf16[288,2560]{1,0:T(8,128)(2,1)S(1)} %collective-permute-done.62), channel_id=1, source_target_pairs={{2,0},{3,1},{10,8},{11,9},{18,16},{19,17},{26,24},{27,25}} | collective-permute-start | bytes 4423688 | tf_op jit(solution)/shard_map/ppermute | solution.py:577
  1070.2 16.1 %collective-permute-start.68 = (bf16[2,288,2560]{2,1,0:T(8,128)(2,1)}, bf16[2,288,2560]{2,1,0:T(8,128)(2,1)}, u32[]{:S(2)}, u32[]{:S(2)}) collective-permute-start(bf16[2,288,2560]{2,1,0:T(8,128)(2,1)} %get-tuple-element.290), channel_id=1, source_target_pairs={{0,1},{1,0},{2,3},{3,2},{4,5},{5,4},{6,7},{7,6},{8,9},{9,8},{10,11... | collective-permute-start | bytes 8847368 | tf_op jit(solution)/shard_map/ppermute | solution.py:728
  (114 other events, 2302.0 us)
Sparse Core Ops, SparseCore 0:
  19.4 58.6 all-gather.5
  80.5 31.3 all-gather.7
  143.7 45.9 all-gather.9
  194.9 75.3 all-gather.11
  473.4 65.3 reduce-scatter.6
  542.2 97.1 reduce-scatter.4
  710.8 71.1 reduce-scatter.8
  875.3 49.3 reduce-scatter.10

commit v4 on v3

--- a/solution.py
+++ b/solution.py
@@ -529,37 +529,6 @@
     )(core, own, other)
 
 
-def turned_kernel(start, used, core, own, other, out, joined):
-    rows = own.shape[1]
-    first = core[0] == 0
-    left = own[0, :, start : start + used].astype(jnp.float32)
-    right = other[0, :, start : start + used].astype(jnp.float32)
-    joined[:rows, :] = jnp.where(first, left, right)
-    joined[rows:, :] = jnp.where(first, right, left)
-    out[...] = jnp.transpose(joined[...])
-
-
-def join_turned(core, own, other, start, used):
-    pieces, rows, cols = own.shape
-    taken = pl.BlockSpec((1, rows, cols), lambda k, *_: (k, 0, 0))
-    return pl.pallas_call(
-        functools.partial(turned_kernel, start, used),
-        grid_spec=pltpu.PrefetchScalarGridSpec(
-            num_scalar_prefetch=1,
-            grid=(pieces,),
-            in_specs=[taken, taken],
-            out_specs=pl.BlockSpec((used, 2 * rows), lambda k, *_: (k, 0)),
-            scratch_shapes=[pltpu.VMEM((2 * rows, used), jnp.float32)],
-        ),
-        out_shape=jax.ShapeDtypeStruct((pieces * used, 2 * rows), jnp.float32),
-        compiler_params=pltpu.CompilerParams(vmem_limit_bytes=40 << 20),
-        cost_estimate=pl.CostEstimate(
-            flops=0, bytes_accessed=8 * pieces * rows * (cols + used), transcendentals=0
-        ),
-        name="join_turned",
-    )(core, own, other)
-
-
 def swap_pairs():
     return [(0, 1), (1, 0)]
 
@@ -762,6 +731,9 @@
     own_tokens = lax.dynamic_index_in_dim(tokens, core, 0, keepdims=False)
     own_cot = lax.dynamic_index_in_dim(cotangent, core, 0, keepdims=False)
 
+    own_tokens, w_query, w_key, w_value = lax.optimization_barrier(
+        (own_tokens, w_query, w_key, w_value)
+    )
     tokens_line = walk(own_tokens)
     tokens_line.step()
     qkv_mine = to_pair(column_piece([w_query, w_key, w_value], lambda v: widen(v, 1)))
@@ -776,9 +748,8 @@
     out_mine = to_pair(widen(turned_piece(w_out), 1))
     down_mine = to_pair(turned_piece(w_down))
     gate_up_mine = to_pair(column_piece([w_gate, w_up]))
-    stage([tokens_line])
+    gain_a, gain_b, out_mine = stage([tokens_line], gain_a, gain_b, out_mine)
     tokens_line.step()
-    out_mine, qkv_w = lax.optimization_barrier((out_mine, qkv_w))
     out_w = gather_pair(out_mine)
     own_cot, down_mine = stage([tokens_line], own_cot, down_mine)
     down_w = gather_pair(down_mine)
@@ -840,23 +811,24 @@
     (part_near,) = stage([second_line], part_near)
     far_half = jnp.concatenate([second_line.near(k) for k in range(lines // 2, lines)], axis=0)
     hidden_far, grad_far = units(far_half, grad_hidden[1])
+    hidden = jnp.concatenate([hidden_near, hidden_far], axis=0)
+    down_grad = row_product(grad_mlp, hidden).astype(jnp.bfloat16)
+    down_grad, grad_far = lax.optimization_barrier((down_grad, grad_far))
+    down_piece = reduce_pair(down_grad)
     part_far = col_product(grad_far, gate_up_w).astype(jnp.bfloat16)
 
     grad_line = add_up(blocks_of(part_near) + blocks_of(part_far))
     grad_line.step()
-    hidden = jnp.concatenate([hidden_near, hidden_far], axis=0)
     second_in = jnp.concatenate([near_half, far_half], axis=0)
     grad_gate_up = jnp.concatenate([grad_near, grad_far], axis=0)
-    down_grad = row_product(grad_mlp, hidden).astype(jnp.bfloat16)
-    down_piece = reduce_pair(down_grad)
-    mlp_part = col_product(hidden, down_w).astype(jnp.bfloat16)
-    second_in, mlp_part = stage([grad_line], second_in, mlp_part)
+    gate_up_grad = row_product(second_in, grad_gate_up).astype(jnp.bfloat16)
+    (hidden,) = stage([grad_line], hidden)
     grad_line.step()
-    gate_up_grad = row_product(second_in, grad_gate_up).astype(jnp.bfloat16)
-    (gate_up_grad,) = stage([grad_line], gate_up_grad)
+    gate_up_grad, down_piece = stage([grad_line], gate_up_grad, down_piece)
     gate_up_piece = reduce_pair(gate_up_grad)
     grad_line.step()
-    stage([grad_line])
+    mlp_part = col_product(hidden, down_w).astype(jnp.bfloat16)
+    (mlp_part,) = stage([grad_line], mlp_part)
     grad_second = grad_line.total()
 
     own_dy = own_cot.astype(jnp.float32) * live_own
@@ -870,39 +842,32 @@
     stage([attn_grad_line, mlp_line])
     attn_grad_line.step()
     mlp_line.step()
-    stage([attn_grad_line, mlp_line])
+    unit_marks = gain_marks(gate_up_mine, gate_up_piece)
+    rest = jnp.zeros((unit_marks.shape[0], -(3 * unit_cols + 2) % LANES), jnp.bfloat16)
+    unit_block = jnp.concatenate([gate_up_piece, down_piece, unit_marks, rest], axis=1)
+    (unit_block,) = stage([attn_grad_line, mlp_line], unit_block)
     mlp_line.step()
+    unit_line = walk(unit_block)
+    unit_line.step()
     grad_attn = jnp.concatenate([attn_grad_line.near(k) for k in range(lines)], axis=0)
-
     out_grad = row_product(grad_attn, attend).astype(jnp.bfloat16)
     out_piece = reduce_pair(out_grad)
+    grad_attn, out_grad = stage([unit_line, mlp_line], grad_attn, out_grad)
+    unit_line.step()
     grad_attend = plain_product(grad_attn, out_w).astype(jnp.bfloat16)
-    grad_attend, gate_up_piece, down_piece = lax.optimization_barrier(
-        (grad_attend, gate_up_piece, down_piece)
-    )
-    unit_marks = gain_marks(gate_up_mine, gate_up_piece)
-    unit_line = walk(
-        jnp.pad(
-            jnp.concatenate([gate_up_piece, down_piece, unit_marks], axis=1),
-            [(0, 0), (0, -(3 * unit_cols + 2) % LANES)],
-        )
-    )
-    unit_line.step()
     grad_qkv = attend_backward(
         heads, span, order, length.reshape(1), kept, attend, grad_attend, cos_all, sin_all
     )
     qkv_grad = row_product(first_in, grad_qkv).astype(jnp.bfloat16)
+    grad_qkv, qkv_grad, out_piece = stage([unit_line], grad_qkv, qkv_grad, out_piece)
+    unit_line.step()
     qkv_piece = reduce_pair(qkv_grad)
     first_part = col_product(grad_qkv, qkv_w).astype(jnp.bfloat16)
-    (first_part,) = stage([unit_line, mlp_line], first_part)
-
     first_line = add_up(blocks_of(first_part))
     first_line.step()
-    unit_line.step()
     layer_rows = ((middle + BRANCH_SCALE * mlp_line.total()) * live_own).astype(jnp.bfloat16)
-    (layer_rows,) = stage([unit_line, first_line], layer_rows)
+    (layer_rows,) = stage([first_line], layer_rows)
     first_line.step()
-    unit_line.step()
     stage([unit_line, first_line])
     first_line.step()
     qkv_marks = gain_marks(qkv_mine, qkv_piece)
@@ -913,8 +878,7 @@
     )
     head_line.step()
     own, other, found = line_pieces(unit_line)
-    final_gate, final_up = join_columns(core_index, own, other, 2, unit_cols, unit_cols)
-    final_down = join_turned(core_index, own, other, 2 * unit_cols, unit_cols)
+    final_gate, final_up, final_down = join_columns(core_index, own, other, 3, unit_cols, unit_cols)
     final_gain_two = gain_total(found, 3 * unit_cols, mlp_gain)
     final_gate, final_up, final_down = stage([first_line, head_line], final_gate, final_up, final_down)
     head_line.step()
@@ -934,10 +898,9 @@
     grad_tokens = both_slots(grad_rows.astype(jnp.bfloat16)).astype(jnp.float32)
     layer_out, grad_tokens = stage([head_line], layer_out, grad_tokens)
     own, other, found = line_pieces(head_line)
-    final_query, final_key, final_value = join_columns(
-        core_index, own, other, 3, pad_cols, head_cols
-    )
-    final_out = join_turned(core_index, own, other, 3 * pad_cols, head_cols)
+    final_query, final_key, final_value, final_out = join_columns(
+        core_index, own, other, 4, pad_cols, head_cols
+    )
     final_gain_one = gain_total(found, head_cols, attn_gain)
     return (
         layer_out,
@@ -946,11 +909,11 @@
         final_query,
         final_key,
         final_value,
-        final_out,
+        jnp.transpose(final_out),
         final_gain_two,
         final_gate,
         final_up,
-        final_down,
+        jnp.transpose(final_down),
     )
 
 

time: 1120 us -> 1060 us (0.946)
  local copies, waits for them, and re-layouts: 71.4 us -> 50.1 us
  waiting for transfers between devices: 462 us -> 443 us
  starting transfers between devices: 168 us -> 150 us
  other arithmetic: 112 us -> 124 us
    ppermute x12, waiting for transfers between devices: 72.6 us -> 172 us  [step(): self.up = lax.ppermute(up, self.axis, [(i, i + 1) for i, _ in ups])]
    ppermute x18, waiting for transfers between devices: 254 us -> 176 us  [step(): self.downs.append(lax.ppermute(self.downs[-1], self.axis, down_pairs))]
    ppermute x12, waiting for transfers between devices: 90.8 us -> 18.5 us  [step(): self.down = lax.ppermute(down, self.axis, [(i, i - 1) for i, _ in downs])]
    ppermute x18, waiting for transfers between devices: 6.42 us -> 68.5 us  [step(): self.ups.append(lax.ppermute(self.ups[-1], self.axis, up_pairs))]
    unnamed x203 -> x161, local copies, waits for them, and re-layouts: 40.8 us -> 18.4 us
    all_gather x4, waiting for transfers between devices: 21.4 us -> 0.06 us  [gather_pair(): return lax.all_gather(mine, ('shard', 'tensor'), axis=0, tiled=True)]
    ppermute x12, starting transfers between devices: 78.2 us -> 58.2 us  [step(): self.up = lax.ppermute(up, self.axis, [(i, i + 1) for i, _ in ups])]
    ppermute x12, starting transfers between devices: 13 us -> 24.9 us  [step(): self.down = lax.ppermute(down, self.axis, [(i, i - 1) for i, _ in downs])]
  transfers between devices with their start and end apart: 78 -> 78, of which waited for: 37 -> 38; matrix products, arithmetic and copies ran while one was open for 25% -> 27% of each run, Pallas kernels for 4% -> 7%
where the time goes in v4:
time: 1060 us; the launch traced here: 1050 us
  waiting for transfers between devices  443 us (42%)
  matrix products  182 us (17%)
  starting transfers between devices  150 us (14%)
  other arithmetic  124 us (12%)
  Pallas kernels  77.7 us (7%)
  local copies, waits for them, and re-layouts  50.1 us (5%)
  between operations  16.2 us (2%)
    ppermute x18, waiting for transfers between devices, step(): self.downs.append(lax.ppermute(self.downs[-1], self.axis, down_pairs))  176 us
    ppermute x12, waiting for transfers between devices, step(): self.up = lax.ppermute(up, self.axis, [(i, i + 1) for i, _ in ups])  172 us
    dot_general x6, matrix products, plain_product(): return jnp.dot(left_mat, right_mat, preferred_element_type=jnp.float32)  73.9 us
    ppermute x18, waiting for transfers between devices, step(): self.ups.append(lax.ppermute(self.ups[-1], self.axis, up_pairs))  68.5 us
    ppermute x12, starting transfers between devices, step(): self.up = lax.ppermute(up, self.axis, [(i, i + 1) for i, _ in ups])  58.2 us
    dot_general x5, matrix products, col_product(): lax.dot_general(left_mat, right_mat, CONTRACT_COLS, preferred_element_typ...  56.4 us
    dot_general x4, matrix products, row_product(): lax.dot_general(left_mat, right_mat, CONTRACT_ROWS, preferred_element_typ...  51.3 us
    ppermute x18, starting transfers between devices, step(): self.ups.append(lax.ppermute(self.ups[-1], self.axis, up_pairs))  40.5 us
  transfers between devices with their start and end apart: 78, of which 38 were waited for; matrix products, arithmetic and copies ran while one was open for 27% of the time, Pallas kernels for 7%

profile of v4, /device:TPU:0, one launch (start us, length us, event | category | flops | bytes accessed | tf_op | source)
XLA Modules:
  0.0 1051.3 jit_solution(17769011724328332651)
XLA Ops:
  18.9 5.8 collective-permute-start
  26.0 23.5 %collective-permute-done = bf16[256,2304]{1,0:T(8,128)(2,1)} collective-permute-done((bf16[256,2304]{1,0:T(8,128)(2,1)S(1)}, bf16[256,2304]{1,0:T(8,128)(2,1)}, u32[]{:S(2)}, u32[]{:S(2)}) %collective-permute-start) | collective-permute-done | bytes 1179680 | tf_op jit(solution)/shard_map/ppermute | solution.py:545
  49.4 5.8 collective-permute-done.1
  59.9 8.6 all-gather
  70.1 16.3 %collective-permute-done.3 = bf16[256,2304]{1,0:T(8,128)(2,1)} collective-permute-done((bf16[256,2304]{1,0:T(8,128)(2,1)}, bf16[256,2304]{1,0:T(8,128)(2,1)}, u32[]{:S(2)}, u32[]{:S(2)}) %collective-permute-start.3) | collective-permute-done | bytes 1179680 | tf_op jit(solution)/shard_map/ppermute | solution.py:546
  97.1 24.2 %collective-permute-done.6 = bf16[256,2304]{1,0:T(8,128)(2,1)} collective-permute-done((bf16[256,2304]{1,0:T(8,128)(2,1)}, bf16[256,2304]{1,0:T(8,128)(2,1)}, u32[]{:S(2)}, u32[]{:S(2)}) %collective-permute-start.6) | collective-permute-done | bytes 1179680 | tf_op jit(solution)/shard_map/ppermute | solution.py:546
  140.5 18.0 %fusion.56.q_in.k_in.v_in = f32[1024,1920]{1,0:T(8,128)} fusion(bf16[2304,1920]{1,0:T(8,128)(2,1)} %all-gather.6.cloned.1.call-done, f32[2304]{0:T(1024)} %get-tuple-element.136, f32[1024]{0:T(1024)S(1)} %add_rsqrt_fusion, bf16[256,2304]{1,0:T(8,128)(2,1)} %copy-done.51, bf16[256,2304]{1,0:T(8,128)(2,1)S(1)} %copy-done.46, ...), kind=kOutput, calls=%fused_computation.145 | convolution fusion | flops 9085648896 | bytes 21443584 | tf_op jit(solution)/shard_map/dot_general | solution.py:30
  160.1 5.7 collective-permute-done.9
  178.0 30.1 %attend.1 = (bf16[1024,640]{1,0:T(8,128)(2,1)S(1)}, bf16[1024,640]{1,0:T(8,128)(2,1)S(1)}, bf16[1024,640]{1,0:T(8,128)(2,1)S(1)}, bf16[1024,640]{1,0:T(8,128)(2,1)S(1)}, f32[5,8,1024]{2,1,0:T(8,128)S(1)}) custom-call(s32[8]{0:T(128)S(1)} %and_select_fusion.order, s32[1]{0:T(128)} %dynamic_slice.60.length, f32[1024,1920]{1,0:T(8,128)S(1)} %copy-done.2, ...), custom_call_target="tpu_custom_call" | custom-call | flops 2415919104 | bytes 15728640 | tf_op jit(solution)/shard_map/attend/pallas_call | solution.py:451
  210.2 6.4 convolution_convert_fusion.4
  216.7 5.1 collective-permute-start.14
  226.9 20.8 %collective-permute-done.14 = bf16[256,2304]{1,0:T(8,128)(2,1)S(1)} collective-permute-done((bf16[256,2304]{1,0:T(8,128)(2,1)S(1)}, bf16[256,2304]{1,0:T(8,128)(2,1)S(1)}, u32[]{:S(2)}, u32[]{:S(2)}) %collective-permute-start.14) | collective-permute-done | bytes 1179680 | tf_op jit(solution)/shard_map/ppermute | solution.py:602
  247.7 5.9 collective-permute-done.17
  255.7 11.2 %collective-permute-start.19 = (bf16[256,2304]{1,0:T(8,128)(2,1)S(1)}, bf16[256,2304]{1,0:T(8,128)(2,1)S(1)}, u32[]{:S(2)}, u32[]{:S(2)}) collective-permute-start(bf16[256,2304]{1,0:T(8,128)(2,1)S(1)} %get-tuple-element.271), channel_id=1, source_target_pairs={{4,2},{6,4},{5,3},{7,5},{12,10},{14,12},{13,11},{15,13},{20,18},{2... | collective-permute-start | bytes 3538952 | tf_op jit(solution)/shard_map/ppermute | solution.py:603
  268.9 9.1 multiply_convert_fusion
  282.7 6.5 collective-permute-start.20
  290.5 9.2 fusion.44
  299.7 7.0 fusion.42
  306.8 6.5 collective-permute-done.20
  325.8 21.6 %collective-permute-done.22 = bf16[256,2304]{1,0:T(8,128)(2,1)S(1)} collective-permute-done((bf16[256,2304]{1,0:T(8,128)(2,1)S(1)}, bf16[256,2304]{1,0:T(8,128)(2,1)S(1)}, u32[]{:S(2)}, u32[]{:S(2)}) %collective-permute-start.22) | collective-permute-done | bytes 1179680 | tf_op jit(solution)/shard_map/ppermute | solution.py:545
  347.4 4.3 collective-permute-done.23
  357.4 17.9 %fusion.34 = f32[512,2880]{0,1:T(8,128)} fusion(bf16[2304,2880]{1,0:T(8,128)(2,1)} %all-gather.12.cloned.1.call-done, bf16[256,2304]{1,0:T(8,128)(2,1)} %fusion.49, bf16[256,2304]{1,0:T(8,128)(2,1)} %copy-done.62), kind=kOutput, calls=%fused_computation.92 | convolution fusion | flops 6799491072 | bytes 21528576 | tf_op jit(solution)/shard_map/dot_general | solution.py:30
  375.3 5.4 multiply_convert_fusion.5
  383.4 12.5 %convolution_convert_fusion.8 = bf16[512,2304]{1,0:T(8,128)(2,1)} fusion(bf16[512,2880]{0,1:T(8,128)(2,1)S(1)} %pad_maximum_fusion.4, bf16[2304,2880]{1,0:T(8,128)(2,1)} %all-gather.12.cloned.1.call-done), kind=kOutput, calls=%fused_computation.33 | convolution fusion | flops 6795952128 | bytes 18579456 | tf_op jit(solution)/shard_map/dot_general | solution.py:26
  398.7 9.4 collective-permute-done.27
  409.5 17.9 %fusion.38 = f32[512,2880]{0,1:T(8,128)} fusion(bf16[2304,2880]{1,0:T(8,128)(2,1)} %all-gather.12.cloned.1.call-done, bf16[256,2304]{1,0:T(8,128)(2,1)} %select_select_fusion.17, bf16[256,2304]{1,0:T(8,128)(2,1)} %select_select_fusion.6), kind=kOutput, calls=%fused_computation.96 | convolution fusion | flops 6799491072 | bytes 21528576 | tf_op jit(solution)/shard_map/dot_general | solution.py:30
  427.4 5.7 multiply_convert_fusion.2
  434.2 12.4 %convolution_convert_fusion.2 = bf16[2304,1440]{1,0:T(8,128)(2,1)} fusion(bf16[1024,2304]{1,0:T(8,128)(2,1)} %multiply_convert_fusion, bf16[512,1440]{0,1:T(8,128)(2,1)S(1)} %get-tuple-element.257, bf16[512,1440]{0,1:T(8,128)(2,1)S(1)} %copy-done.34), kind=kOutput, calls=%fused_computation.5 | convolution fusion | flops 6803988480 | bytes 14303232 | tf_op jit(solution)/shard_map/dot_general | solution.py:22
  450.3 12.5 %convolution_convert_fusion.7 = bf16[512,2304]{1,0:T(8,128)(2,1)S(1)} fusion(bf16[512,2880]{0,1:T(8,128)(2,1)} %pad_maximum_fusion.6, bf16[2304,2880]{1,0:T(8,128)(2,1)} %all-gather.12.cloned.1.call-done), kind=kOutput, calls=%fused_computation.32 | convolution fusion | flops 6795952128 | bytes 18579456 | tf_op jit(solution)/shard_map/dot_general | solution.py:26
  468.8 18.1 %collective-permute-done.28 = bf16[256,2304]{1,0:T(8,128)(2,1)S(1)} collective-permute-done((bf16[256,2304]{1,0:T(8,128)(2,1)S(1)}, bf16[256,2304]{1,0:T(8,128)(2,1)S(1)}, u32[]{:S(2)}, u32[]{:S(2)}) %collective-permute-start.28) | collective-permute-done | bytes 1179680 | tf_op jit(solution)/shard_map/ppermute | solution.py:602
  488.8 5.4 collective-permute-start.30
  495.9 18.8 %convolution_convert_fusion = bf16[2304,2880]{1,0:T(8,128)(2,1)} fusion(bf16[512,2880]{0,1:T(8,128)(2,1)S(1)} %copy-done.56, bf16[512,2880]{0,1:T(8,128)(2,1)S(1)} %copy-done.54, bf16[256,2304]{1,0:T(8,128)(2,1)} %select_select_fusion.17, bf16[256,2304]{1,0:T(8,128)(2,1)} %select_select_fusion.6, bf16[256,2304]{1,0:T(8,128)(2,1)} %fusion.49, ...), kind=kOutput, calls=%fused_computation.1 | convolution fusion | flops 13626851328 | bytes 23887872 | tf_op jit(solution)/shard_map/dot_general | solution.py:22
  519.0 5.6 collective-permute-start.32
  526.2 11.7 %convolution_convert_fusion.5 = bf16[1024,2304]{1,0:T(8,128)(2,1)S(1)} fusion(bf16[1024,1440]{0,1:T(8,128)(2,1)S(1)} %copy-done.55, bf16[2304,1440]{1,0:T(8,128)(2,1)} %all-gather.10.cloned.1.call-done), kind=kOutput, calls=%fused_computation.17 | convolution fusion | flops 6797131776 | bytes 14303232 | tf_op jit(solution)/shard_map/dot_general | solution.py:26
  537.9 9.5 collective-permute-done.32
  547.5 4.5 collective-permute-done.33
  560.2 21.9 %collective-permute-done.34 = bf16[256,2304]{1,0:T(8,128)(2,1)S(1)} collective-permute-done((bf16[256,2304]{1,0:T(8,128)(2,1)S(1)}, bf16[256,2304]{1,0:T(8,128)(2,1)S(1)}, u32[]{:S(2)}, u32[]{:S(2)}) %collective-permute-start.34) | collective-permute-done | bytes 1179680 | tf_op jit(solution)/shard_map/ppermute | solution.py:545
  582.1 4.5 collective-permute-done.35
  588.7 5.9 collective-permute-start.38
  595.4 20.9 %collective-permute-done.37 = bf16[256,2304]{1,0:T(8,128)(2,1)} collective-permute-done((bf16[256,2304]{1,0:T(8,128)(2,1)S(1)}, bf16[256,2304]{1,0:T(8,128)(2,1)}, u32[]{:S(2)}, u32[]{:S(2)}) %collective-permute-start.37) | collective-permute-done | bytes 1179680 | tf_op jit(solution)/shard_map/ppermute | solution.py:546
  622.4 6.6 collective-permute-start.42
  636.1 5.3 concatenate.60
  641.4 4.7 collective-permute-done.41
  650.2 10.7 %collective-permute-start.44 = (bf16[288,4352]{1,0:T(8,128)(2,1)}, bf16[288,4352]{1,0:T(8,128)(2,1)}, u32[]{:S(2)}, u32[]{:S(2)}) collective-permute-start(bf16[288,4352]{1,0:T(8,128)(2,1)} %concatenate.60), channel_id=1, source_target_pairs={{0,2},{2,4},{4,6},{1,3},{3,5},{5,7},{8,10},{10,12},{12,14},{9,11},... | collective-permute-start | bytes 7520264 | tf_op jit(solution)/shard_map/ppermute | solution.py:545
  662.2 4.4 add_convert_fusion.2
  666.6 5.5 collective-permute-start.46
  676.7 5.4 convolution_convert_fusion.6
  685.6 48.2 %collective-permute-done.46 = bf16[256,2304]{1,0:T(8,128)(2,1)} collective-permute-done((bf16[256,2304]{1,0:T(8,128)(2,1)}, bf16[256,2304]{1,0:T(8,128)(2,1)}, u32[]{:S(2)}, u32[]{:S(2)}) %collective-permute-start.46) | collective-permute-done | bytes 1179680 | tf_op jit(solution)/shard_map/ppermute | solution.py:602
  733.8 5.7 collective-permute-done.47
  746.9 30.2 %attend_back.1 = bf16[1024,1920]{1,0:T(8,128)(2,1)} custom-call(s32[8]{0:T(128)S(1)} %copy-done.9, s32[1]{0:T(128)} %dynamic_slice.60.length, bf16[1024,640]{1,0:T(8,128)(2,1)S(1)} %get-tuple-element.199.q_in, bf16[1024,640]{1,0:T(8,128)(2,1)S(1)} %copy-done.13, bf16[1024,640]{1,0:T(8,128)(2,1)S(1)} %copy-done.15, ...), custom_call_target="tpu_custom_call" | custom-call | flops 6039797760 | bytes 10485760 | tf_op jit(solution)/shard_map/attend_back/pallas_call | solution.py:478
  777.2 14.8 %convolution_convert_fusion.1 = bf16[2304,1920]{1,0:T(8,128)(2,1)} fusion(bf16[1024,1920]{1,0:T(8,128)(2,1)} %attend_back.1, f32[2304]{0:T(1024)S(1)} %copy-done.69, f32[1024]{0:T(1024)S(1)} %copy-done.76, bf16[256,2304]{1,0:T(8,128)(2,1)S(1)} %copy-done.52, bf16[256,2304]{1,0:T(8,128)(2,1)S(1)} %copy-done.47, bf16[256,2304]{1,0:T(8,128)(2,1)S(1)} %copy-done.50, ...), kind=kOutput, calls=%fused_computation.4 | convolution fusion | flops 9090072576 | bytes 17511424 | tf_op jit(solution)/shard_map/dot_general | solution.py:22
  794.1 13.4 %convolution_convert_fusion.3 = bf16[1024,2304]{1,0:T(8,128)(2,1)S(1)} fusion(bf16[1024,1920]{1,0:T(8,128)(2,1)} %attend_back.1, bf16[2304,1920]{1,0:T(8,128)(2,1)} %all-gather.6.cloned.1.call-done), kind=kOutput, calls=%fused_computation.15 | convolution fusion | flops 9062055936 | bytes 17498112 | tf_op jit(solution)/shard_map/dot_general | solution.py:26
  817.3 12.7 %collective-permute-done.52 = bf16[256,2304]{1,0:T(8,128)(2,1)S(1)} collective-permute-done((bf16[256,2304]{1,0:T(8,128)(2,1)S(1)}, bf16[256,2304]{1,0:T(8,128)(2,1)S(1)}, u32[]{:S(2)}, u32[]{:S(2)}) %collective-permute-start.52) | collective-permute-done | bytes 1179680 | tf_op jit(solution)/shard_map/ppermute | solution.py:602
  831.8 5.4 collective-permute-start.54
  839.0 15.9 %collective-permute-done.54 = bf16[256,2304]{1,0:T(8,128)(2,1)} collective-permute-done((bf16[256,2304]{1,0:T(8,128)(2,1)}, bf16[256,2304]{1,0:T(8,128)(2,1)}, u32[]{:S(2)}, u32[]{:S(2)}) %collective-permute-start.54) | collective-permute-done | bytes 1179680 | tf_op jit(solution)/shard_map/ppermute | solution.py:602
  856.3 7.7 collective-permute-done.51
  864.0 6.0 select_select_fusion.3
  870.0 4.9 broadcast_select_fusion
  892.9 4.6 collective-permute-start.56
  901.4 12.1 %join_columns.2 = (f32[576,2880]{1,0:T(8,128)}, f32[576,2880]{1,0:T(8,128)}, f32[576,2880]{1,0:T(8,128)}) custom-call(s32[1]{0:T(128)} %bitcast.11.core, bf16[2,288,4352]{2,1,0:T(8,128)(2,1)S(1)} %copy-done.3, bf16[2,288,4352]{2,1,0:T(8,128)(2,1)} %collective-permute-done.60.other), custom_call_target="tpu_custom_call" | custom-call | bytes 39960576 | tf_op jit(solution)/shard_map/join_columns/pallas_call | solution.py:515
  913.5 32.0 %collective-permute-done.56 = bf16[256,2304]{1,0:T(8,128)(2,1)S(1)} collective-permute-done((bf16[256,2304]{1,0:T(8,128)(2,1)}, bf16[256,2304]{1,0:T(8,128)(2,1)S(1)}, u32[]{:S(2)}, u32[]{:S(2)}) %collective-permute-start.56) | collective-permute-done | bytes 1179680 | tf_op jit(solution)/shard_map/ppermute | solution.py:602
  957.7 33.3 %collective-permute-done.62 = bf16[288,2560]{1,0:T(8,128)(2,1)S(1)} collective-permute-done((bf16[288,2560]{1,0:T(8,128)(2,1)}, bf16[288,2560]{1,0:T(8,128)(2,1)S(1)}, u32[]{:S(2)}, u32[]{:S(2)}) %collective-permute-start.62) | collective-permute-done | bytes 1474592 | tf_op jit(solution)/shard_map/ppermute | solution.py:546
  999.0 30.8 %collective-permute-done.64 = bf16[288,2560]{1,0:T(8,128)(2,1)S(1)} collective-permute-done((bf16[288,2560]{1,0:T(8,128)(2,1)S(1)}, bf16[288,2560]{1,0:T(8,128)(2,1)S(1)}, u32[]{:S(2)}, u32[]{:S(2)}) %collective-permute-start.64) | collective-permute-done | bytes 1474592 | tf_op jit(solution)/shard_map/ppermute | solution.py:546
  1038.8 5.3 join_columns.3
  (392 shorter events, 237.6 us)
Async XLA Ops:
  7.2 133.1 %all-gather.6.cloned.1.call-start = ((), (), s32[]{:S(2)}) async-start(), calls=%async_computation.4 | async-start | bytes 9953280 | tf_op jit(solution)/shard_map/all_gather | solution.py:678
  18.8 191.4 %all-gather.8.cloned.1.call-start = ((), (), s32[]{:S(2)}) async-start(), calls=%async_computation.5 | async-start | bytes 3317760 | tf_op jit(solution)/shard_map/all_gather | solution.py:678
  18.9 30.6 %collective-permute-start = (bf16[256,2304]{1,0:T(8,128)(2,1)S(1)}, bf16[256,2304]{1,0:T(8,128)(2,1)}, u32[]{:S(2)}, u32[]{:S(2)}) collective-permute-start(bf16[256,2304]{1,0:T(8,128)(2,1)S(1)} %dynamic-slice_bitcast_fusion.1), channel_id=1, source_target_pairs={{0,2},{2,4},{4,6},{1,3},{3,5},{5,7},{8,10},{10,12},{12,14},{9,11},... | collective-permute-start | bytes 3538952 | tf_op jit(solution)/shard_map/ppermute | solution.py:545
  24.6 30.7 %collective-permute-start.1 = (bf16[256,2304]{1,0:T(8,128)(2,1)S(1)}, bf16[256,2304]{1,0:T(8,128)(2,1)}, u32[]{:S(2)}, u32[]{:S(2)}) collective-permute-start(bf16[256,2304]{1,0:T(8,128)(2,1)S(1)} %dynamic-slice_bitcast_fusion.1), channel_id=1, source_target_pairs={{2,0},{4,2},{6,4},{3,1},{5,3},{7,5},{10,8},{12,10},{14,12},{11,9},... | collective-permute-start | bytes 3538952 | tf_op jit(solution)/shard_map/ppermute | solution.py:546
  56.0 30.4 %collective-permute-start.3 = (bf16[256,2304]{1,0:T(8,128)(2,1)}, bf16[256,2304]{1,0:T(8,128)(2,1)}, u32[]{:S(2)}, u32[]{:S(2)}) collective-permute-start(bf16[256,2304]{1,0:T(8,128)(2,1)} %collective-permute-done.1), channel_id=1, source_target_pairs={{2,0},{4,2},{3,1},{5,3},{10,8},{12,10},{11,9},{13,11},{18,16},{20,... | collective-permute-start | bytes 3538952 | tf_op jit(solution)/shard_map/ppermute | solution.py:546
  86.4 204.1 %all-gather.10.cloned.1.call-start = ((), (), s32[]{:S(2)}) async-start(), calls=%async_computation.6 | async-start | bytes 7962624 | tf_op jit(solution)/shard_map/all_gather | solution.py:678
  90.7 30.6 %collective-permute-start.6 = (bf16[256,2304]{1,0:T(8,128)(2,1)}, bf16[256,2304]{1,0:T(8,128)(2,1)}, u32[]{:S(2)}, u32[]{:S(2)}) collective-permute-start(bf16[256,2304]{1,0:T(8,128)(2,1)} %collective-permute-done.3), channel_id=1, source_target_pairs={{2,0},{3,1},{10,8},{11,9},{18,16},{19,17},{26,24},{27,25}} | collective-permute-start | bytes 3538952 | tf_op jit(solution)/shard_map/ppermute | solution.py:546
  121.3 236.1 %all-gather.12.cloned.1.call-start = ((), (), s32[]{:S(2)}) async-start(), calls=%async_computation.7 | async-start | bytes 15261696 | tf_op jit(solution)/shard_map/all_gather | solution.py:678
  132.8 27.3 %collective-permute-start.8 = (bf16[256,2304]{1,0:T(8,128)(2,1)}, bf16[256,2304]{1,0:T(8,128)(2,1)}, u32[]{:S(2)}, u32[]{:S(2)}) collective-permute-start(bf16[256,2304]{1,0:T(8,128)(2,1)} %dynamic-slice_bitcast_fusion), channel_id=1, source_target_pairs={{0,2},{2,4},{4,6},{1,3},{3,5},{5,7},{8,10},{10,12},{12,14},{9,11},... | collective-permute-start | bytes 3538952 | tf_op jit(solution)/shard_map/ppermute | solution.py:545
  135.4 30.5 %collective-permute-start.9 = (bf16[256,2304]{1,0:T(8,128)(2,1)}, bf16[256,2304]{1,0:T(8,128)(2,1)}, u32[]{:S(2)}, u32[]{:S(2)}) collective-permute-start(bf16[256,2304]{1,0:T(8,128)(2,1)} %dynamic-slice_bitcast_fusion), channel_id=1, source_target_pairs={{2,0},{4,2},{6,4},{3,1},{5,3},{7,5},{10,8},{12,10},{14,12},{11,9},... | collective-permute-start | bytes 3538952 | tf_op jit(solution)/shard_map/ppermute | solution.py:546
  165.9 349.8 %reduce-scatter.5.cloned.1.call-start = ((), (), s32[]{:S(2)}) async-start(), calls=%async_computation.8 | async-start | bytes 7962624 | tf_op jit(solution)/shard_map/reduce_scatter | solution.py:681
  166.8 43.4 %collective-permute-start.12 = (bf16[256,2304]{1,0:T(8,128)(2,1)}, bf16[256,2304]{1,0:T(8,128)(2,1)}, u32[]{:S(2)}, u32[]{:S(2)}) collective-permute-start(bf16[256,2304]{1,0:T(8,128)(2,1)} %collective-permute-done.8), channel_id=1, source_target_pairs={{2,4},{4,6},{3,5},{5,7},{10,12},{12,14},{11,13},{13,15},{18,20},{2... | collective-permute-start | bytes 3538952 | tf_op jit(solution)/shard_map/ppermute | solution.py:545
  168.5 41.7 %collective-permute-start.13 = (bf16[256,2304]{1,0:T(8,128)(2,1)}, bf16[256,2304]{1,0:T(8,128)(2,1)}, u32[]{:S(2)}, u32[]{:S(2)}) collective-permute-start(bf16[256,2304]{1,0:T(8,128)(2,1)} %collective-permute-done.9), channel_id=1, source_target_pairs={{2,0},{4,2},{3,1},{5,3},{10,8},{12,10},{11,9},{13,11},{18,16},{20,... | collective-permute-start | bytes 3538952 | tf_op jit(solution)/shard_map/ppermute | solution.py:546
  216.7 31.0 %collective-permute-start.14 = (bf16[256,2304]{1,0:T(8,128)(2,1)S(1)}, bf16[256,2304]{1,0:T(8,128)(2,1)S(1)}, u32[]{:S(2)}, u32[]{:S(2)}) collective-permute-start(bf16[256,2304]{1,0:T(8,128)(2,1)S(1)} %slice.150), channel_id=1, source_target_pairs={{0,2},{1,3},{8,10},{9,11},{16,18},{17,19},{24,26},{25,27}} | collective-permute-start | bytes 3538952 | tf_op jit(solution)/shard_map/ppermute | solution.py:602
  221.8 25.9 %collective-permute-start.15 = (bf16[256,2304]{1,0:T(8,128)(2,1)S(1)}, bf16[256,2304]{1,0:T(8,128)(2,1)S(1)}, u32[]{:S(2)}, u32[]{:S(2)}) collective-permute-start(bf16[256,2304]{1,0:T(8,128)(2,1)S(1)} %slice.150), channel_id=1, source_target_pairs={{6,4},{7,5},{14,12},{15,13},{22,20},{23,21},{30,28},{31,29}} | collective-permute-start | bytes 3538952 | tf_op jit(solution)/shard_map/ppermute | solution.py:603
  222.5 25.2 %collective-permute-start.16 = (bf16[256,2304]{1,0:T(8,128)(2,1)}, bf16[256,2304]{1,0:T(8,128)(2,1)S(1)}, u32[]{:S(2)}, u32[]{:S(2)}) collective-permute-start(bf16[256,2304]{1,0:T(8,128)(2,1)} %collective-permute-done.12), channel_id=1, source_target_pairs={{4,6},{5,7},{12,14},{13,15},{20,22},{21,23},{28,30},{29,31}} | collective-permute-start | bytes 3538952 | tf_op jit(solution)/shard_map/ppermute | solution.py:545
  223.3 30.3 %collective-permute-start.17 = (bf16[256,2304]{1,0:T(8,128)(2,1)}, bf16[256,2304]{1,0:T(8,128)(2,1)S(1)}, u32[]{:S(2)}, u32[]{:S(2)}) collective-permute-start(bf16[256,2304]{1,0:T(8,128)(2,1)} %collective-permute-done.13), channel_id=1, source_target_pairs={{2,0},{3,1},{10,8},{11,9},{18,16},{19,17},{26,24},{27,25}} | collective-permute-start | bytes 3538952 | tf_op jit(solution)/shard_map/ppermute | solution.py:546
  254.1 26.4 %collective-permute-start.18 = (bf16[256,2304]{1,0:T(8,128)(2,1)S(1)}, bf16[256,2304]{1,0:T(8,128)(2,1)S(1)}, u32[]{:S(2)}, u32[]{:S(2)}) collective-permute-start(bf16[256,2304]{1,0:T(8,128)(2,1)S(1)} %get-tuple-element.272), channel_id=1, source_target_pairs={{0,2},{2,4},{1,3},{3,5},{8,10},{10,12},{9,11},{11,13},{16,18},{18,... | collective-permute-start | bytes 3538952 | tf_op jit(solution)/shard_map/ppermute | solution.py:602
  255.7 24.8 %collective-permute-start.19 = (bf16[256,2304]{1,0:T(8,128)(2,1)S(1)}, bf16[256,2304]{1,0:T(8,128)(2,1)S(1)}, u32[]{:S(2)}, u32[]{:S(2)}) collective-permute-start(bf16[256,2304]{1,0:T(8,128)(2,1)S(1)} %get-tuple-element.271), channel_id=1, source_target_pairs={{4,2},{6,4},{5,3},{7,5},{12,10},{14,12},{13,11},{15,13},{20,18},{2... | collective-permute-start | bytes 3538952 | tf_op jit(solution)/shard_map/ppermute | solution.py:603
  282.7 30.6 %collective-permute-start.20 = (bf16[256,2304]{1,0:T(8,128)(2,1)}, bf16[256,2304]{1,0:T(8,128)(2,1)S(1)}, u32[]{:S(2)}, u32[]{:S(2)}) collective-permute-start(bf16[256,2304]{1,0:T(8,128)(2,1)} %get-tuple-element.270), channel_id=1, source_target_pairs={{0,2},{2,4},{4,6},{1,3},{3,5},{5,7},{8,10},{10,12},{12,14},{9,11},... | collective-permute-start | bytes 3538952 | tf_op jit(solution)/shard_map/ppermute | solution.py:602
  289.2 28.3 %collective-permute-start.21 = (bf16[256,2304]{1,0:T(8,128)(2,1)}, bf16[256,2304]{1,0:T(8,128)(2,1)}, u32[]{:S(2)}, u32[]{:S(2)}) collective-permute-start(bf16[256,2304]{1,0:T(8,128)(2,1)} %get-tuple-element.269), channel_id=1, source_target_pairs={{2,0},{4,2},{6,4},{3,1},{5,3},{7,5},{10,8},{12,10},{14,12},{11,9},... | collective-permute-start | bytes 3538952 | tf_op jit(solution)/shard_map/ppermute | solution.py:603
  322.3 25.1 %collective-permute-start.22 = (bf16[256,2304]{1,0:T(8,128)(2,1)S(1)}, bf16[256,2304]{1,0:T(8,128)(2,1)S(1)}, u32[]{:S(2)}, u32[]{:S(2)}) collective-permute-start(bf16[256,2304]{1,0:T(8,128)(2,1)S(1)} %multiply_convert_fusion.9), channel_id=1, source_target_pairs={{0,2},{2,4},{4,6},{1,3},{3,5},{5,7},{8,10},{10,12},{12,14},{9,11},... | collective-permute-start | bytes 3538952 | tf_op jit(solution)/shard_map/ppermute | solution.py:545
  324.5 27.2 %collective-permute-start.23 = (bf16[256,2304]{1,0:T(8,128)(2,1)S(1)}, bf16[256,2304]{1,0:T(8,128)(2,1)}, u32[]{:S(2)}, u32[]{:S(2)}) collective-permute-start(bf16[256,2304]{1,0:T(8,128)(2,1)S(1)} %multiply_convert_fusion.9), channel_id=1, source_target_pairs={{2,0},{4,2},{6,4},{3,1},{5,3},{7,5},{10,8},{12,10},{14,12},{11,9},... | collective-permute-start | bytes 3538952 | tf_op jit(solution)/shard_map/ppermute | solution.py:546
  351.7 29.2 %collective-permute-start.24 = (bf16[256,2304]{1,0:T(8,128)(2,1)S(1)}, bf16[256,2304]{1,0:T(8,128)(2,1)}, u32[]{:S(2)}, u32[]{:S(2)}) collective-permute-start(bf16[256,2304]{1,0:T(8,128)(2,1)S(1)} %collective-permute-done.22), channel_id=1, source_target_pairs={{2,4},{4,6},{3,5},{5,7},{10,12},{12,14},{11,13},{13,15},{18,20},{2... | collective-permute-start | bytes 3538952 | tf_op jit(solution)/shard_map/ppermute | solution.py:545
  353.5 27.5 %collective-permute-start.25 = (bf16[256,2304]{1,0:T(8,128)(2,1)}, bf16[256,2304]{1,0:T(8,128)(2,1)}, u32[]{:S(2)}, u32[]{:S(2)}) collective-permute-start(bf16[256,2304]{1,0:T(8,128)(2,1)} %collective-permute-done.23), channel_id=1, source_target_pairs={{2,0},{4,2},{3,1},{5,3},{10,8},{12,10},{11,9},{13,11},{18,16},{20,... | collective-permute-start | bytes 3538952 | tf_op jit(solution)/shard_map/ppermute | solution.py:546
  380.9 17.7 %collective-permute-start.26 = (bf16[256,2304]{1,0:T(8,128)(2,1)}, bf16[256,2304]{1,0:T(8,128)(2,1)S(1)}, u32[]{:S(2)}, u32[]{:S(2)}) collective-permute-start(bf16[256,2304]{1,0:T(8,128)(2,1)} %collective-permute-done.24), channel_id=1, source_target_pairs={{4,6},{5,7},{12,14},{13,15},{20,22},{21,23},{28,30},{29,31}} | collective-permute-start | bytes 3538952 | tf_op jit(solution)/shard_map/ppermute | solution.py:545
  381.7 26.4 %collective-permute-start.27 = (bf16[256,2304]{1,0:T(8,128)(2,1)}, bf16[256,2304]{1,0:T(8,128)(2,1)S(1)}, u32[]{:S(2)}, u32[]{:S(2)}) collective-permute-start(bf16[256,2304]{1,0:T(8,128)(2,1)} %collective-permute-done.25), channel_id=1, source_target_pairs={{2,0},{3,1},{10,8},{11,9},{18,16},{19,17},{26,24},{27,25}} | collective-permute-start | bytes 3538952 | tf_op jit(solution)/shard_map/ppermute | solution.py:546
  450.2 182.8 %reduce-scatter.7.cloned.1.call-start = ((), (), s32[]{:S(2)}) async-start(), calls=%async_computation.9 | async-start | bytes 15261696 | tf_op jit(solution)/shard_map/reduce_scatter | solution.py:681
  462.9 24.1 %collective-permute-start.28 = (bf16[256,2304]{1,0:T(8,128)(2,1)S(1)}, bf16[256,2304]{1,0:T(8,128)(2,1)S(1)}, u32[]{:S(2)}, u32[]{:S(2)}) collective-permute-start(bf16[256,2304]{1,0:T(8,128)(2,1)S(1)} %slice.157), channel_id=1, source_target_pairs={{0,2},{1,3},{8,10},{9,11},{16,18},{17,19},{24,26},{25,27}} | collective-permute-start | bytes 3538952 | tf_op jit(solution)/shard_map/ppermute | solution.py:602
  466.0 20.9 %collective-permute-start.29 = (bf16[256,2304]{1,0:T(8,128)(2,1)S(1)}, bf16[256,2304]{1,0:T(8,128)(2,1)S(1)}, u32[]{:S(2)}, u32[]{:S(2)}) collective-permute-start(bf16[256,2304]{1,0:T(8,128)(2,1)S(1)} %slice.157), channel_id=1, source_target_pairs={{6,4},{7,5},{14,12},{15,13},{22,20},{23,21},{30,28},{31,29}} | collective-permute-start | bytes 3538952 | tf_op jit(solution)/shard_map/ppermute | solution.py:603
  488.8 25.8 %collective-permute-start.30 = (bf16[256,2304]{1,0:T(8,128)(2,1)}, bf16[256,2304]{1,0:T(8,128)(2,1)}, u32[]{:S(2)}, u32[]{:S(2)}) collective-permute-start(bf16[256,2304]{1,0:T(8,128)(2,1)} %get-tuple-element.284), channel_id=1, source_target_pairs={{0,2},{2,4},{1,3},{3,5},{8,10},{10,12},{9,11},{11,13},{16,18},{18,... | collective-permute-start | bytes 3538952 | tf_op jit(solution)/shard_map/ppermute | solution.py:602
  494.2 20.5 %collective-permute-start.31 = (bf16[256,2304]{1,0:T(8,128)(2,1)}, bf16[256,2304]{1,0:T(8,128)(2,1)}, u32[]{:S(2)}, u32[]{:S(2)}) collective-permute-start(bf16[256,2304]{1,0:T(8,128)(2,1)} %get-tuple-element.283), channel_id=1, source_target_pairs={{4,2},{6,4},{5,3},{7,5},{12,10},{14,12},{13,11},{15,13},{20,18},{2... | collective-permute-start | bytes 3538952 | tf_op jit(solution)/shard_map/ppermute | solution.py:603
  515.8 276.1 %reduce-scatter.9.cloned.1.call-start = ((), (), s32[]{:S(2)}) async-start(), calls=%async_computation.10 | async-start | bytes 3317760 | tf_op jit(solution)/shard_map/reduce_scatter | solution.py:681
  519.0 28.5 %collective-permute-start.32 = (bf16[256,2304]{1,0:T(8,128)(2,1)S(1)}, bf16[256,2304]{1,0:T(8,128)(2,1)S(1)}, u32[]{:S(2)}, u32[]{:S(2)}) collective-permute-start(bf16[256,2304]{1,0:T(8,128)(2,1)S(1)} %get-tuple-element.268), channel_id=1, source_target_pairs={{0,2},{2,4},{4,6},{1,3},{3,5},{5,7},{8,10},{10,12},{12,14},{9,11},... | collective-permute-start | bytes 3538952 | tf_op jit(solution)/shard_map/ppermute | solution.py:602
  524.7 27.3 %collective-permute-start.33 = (bf16[256,2304]{1,0:T(8,128)(2,1)S(1)}, bf16[256,2304]{1,0:T(8,128)(2,1)S(1)}, u32[]{:S(2)}, u32[]{:S(2)}) collective-permute-start(bf16[256,2304]{1,0:T(8,128)(2,1)S(1)} %get-tuple-element.267), channel_id=1, source_target_pairs={{2,0},{4,2},{6,4},{3,1},{5,3},{7,5},{10,8},{12,10},{14,12},{11,9},... | collective-permute-start | bytes 3538952 | tf_op jit(solution)/shard_map/ppermute | solution.py:603
  555.5 26.5 %collective-permute-start.34 = (bf16[256,2304]{1,0:T(8,128)(2,1)S(1)}, bf16[256,2304]{1,0:T(8,128)(2,1)S(1)}, u32[]{:S(2)}, u32[]{:S(2)}) collective-permute-start(bf16[256,2304]{1,0:T(8,128)(2,1)S(1)} %get-tuple-element.241), channel_id=1, source_target_pairs={{0,2},{2,4},{4,6},{1,3},{3,5},{5,7},{8,10},{10,12},{12,14},{9,11},... | collective-permute-start | bytes 3538952 | tf_op jit(solution)/shard_map/ppermute | solution.py:545
  558.9 27.7 %collective-permute-start.35 = (bf16[256,2304]{1,0:T(8,128)(2,1)S(1)}, bf16[256,2304]{1,0:T(8,128)(2,1)S(1)}, u32[]{:S(2)}, u32[]{:S(2)}) collective-permute-start(bf16[256,2304]{1,0:T(8,128)(2,1)S(1)} %get-tuple-element.241), channel_id=1, source_target_pairs={{2,0},{4,2},{6,4},{3,1},{5,3},{7,5},{10,8},{12,10},{14,12},{11,9},... | collective-permute-start | bytes 3538952 | tf_op jit(solution)/shard_map/ppermute | solution.py:546
  587.4 28.9 %collective-permute-start.37 = (bf16[256,2304]{1,0:T(8,128)(2,1)S(1)}, bf16[256,2304]{1,0:T(8,128)(2,1)}, u32[]{:S(2)}, u32[]{:S(2)}) collective-permute-start(bf16[256,2304]{1,0:T(8,128)(2,1)S(1)} %collective-permute-done.35), channel_id=1, source_target_pairs={{2,0},{4,2},{3,1},{5,3},{10,8},{12,10},{11,9},{13,11},{18,16},{20,... | collective-permute-start | bytes 3538952 | tf_op jit(solution)/shard_map/ppermute | solution.py:546
  588.7 28.7 %collective-permute-start.38 = (bf16[256,2304]{1,0:T(8,128)(2,1)S(1)}, bf16[256,2304]{1,0:T(8,128)(2,1)S(1)}, u32[]{:S(2)}, u32[]{:S(2)}) collective-permute-start(bf16[256,2304]{1,0:T(8,128)(2,1)S(1)} %slice.127), channel_id=1, source_target_pairs={{0,2},{1,3},{8,10},{9,11},{16,18},{17,19},{24,26},{25,27}} | collective-permute-start | bytes 3538952 | tf_op jit(solution)/shard_map/ppermute | solution.py:602
  594.6 22.8 %collective-permute-start.39 = (bf16[256,2304]{1,0:T(8,128)(2,1)S(1)}, bf16[256,2304]{1,0:T(8,128)(2,1)S(1)}, u32[]{:S(2)}, u32[]{:S(2)}) collective-permute-start(bf16[256,2304]{1,0:T(8,128)(2,1)S(1)} %slice.127), channel_id=1, source_target_pairs={{6,4},{7,5},{14,12},{15,13},{22,20},{23,21},{30,28},{31,29}} | collective-permute-start | bytes 3538952 | tf_op jit(solution)/shard_map/ppermute | solution.py:603
  617.4 23.9 %collective-permute-start.40 = (bf16[256,2304]{1,0:T(8,128)(2,1)S(1)}, bf16[256,2304]{1,0:T(8,128)(2,1)}, u32[]{:S(2)}, u32[]{:S(2)}) collective-permute-start(bf16[256,2304]{1,0:T(8,128)(2,1)S(1)} %collective-permute-done.36), channel_id=1, source_target_pairs={{4,6},{5,7},{12,14},{13,15},{20,22},{21,23},{28,30},{29,31}} | collective-permute-start | bytes 3538952 | tf_op jit(solution)/shard_map/ppermute | solution.py:545
  619.2 27.0 %collective-permute-start.41 = (bf16[256,2304]{1,0:T(8,128)(2,1)}, bf16[256,2304]{1,0:T(8,128)(2,1)}, u32[]{:S(2)}, u32[]{:S(2)}) collective-permute-start(bf16[256,2304]{1,0:T(8,128)(2,1)} %collective-permute-done.37), channel_id=1, source_target_pairs={{2,0},{3,1},{10,8},{11,9},{18,16},{19,17},{26,24},{27,25}} | collective-permute-start | bytes 3538952 | tf_op jit(solution)/shard_map/ppermute | solution.py:546
  622.4 27.8 %collective-permute-start.42 = (bf16[256,2304]{1,0:T(8,128)(2,1)}, bf16[256,2304]{1,0:T(8,128)(2,1)}, u32[]{:S(2)}, u32[]{:S(2)}) collective-permute-start(bf16[256,2304]{1,0:T(8,128)(2,1)} %get-tuple-element.266), channel_id=1, source_target_pairs={{0,2},{2,4},{1,3},{3,5},{8,10},{10,12},{9,11},{11,13},{16,18},{18,... | collective-permute-start | bytes 3538952 | tf_op jit(solution)/shard_map/ppermute | solution.py:602
  628.9 21.3 %collective-permute-start.43 = (bf16[256,2304]{1,0:T(8,128)(2,1)}, bf16[256,2304]{1,0:T(8,128)(2,1)}, u32[]{:S(2)}, u32[]{:S(2)}) collective-permute-start(bf16[256,2304]{1,0:T(8,128)(2,1)} %get-tuple-element.265), channel_id=1, source_target_pairs={{4,2},{6,4},{5,3},{7,5},{12,10},{14,12},{13,11},{15,13},{20,18},{2... | collective-permute-start | bytes 3538952 | tf_op jit(solution)/shard_map/ppermute | solution.py:603
  650.2 89.3 %collective-permute-start.44 = (bf16[288,4352]{1,0:T(8,128)(2,1)}, bf16[288,4352]{1,0:T(8,128)(2,1)}, u32[]{:S(2)}, u32[]{:S(2)}) collective-permute-start(bf16[288,4352]{1,0:T(8,128)(2,1)} %concatenate.60), channel_id=1, source_target_pairs={{0,2},{2,4},{4,6},{1,3},{3,5},{5,7},{8,10},{10,12},{12,14},{9,11},... | collective-permute-start | bytes 7520264 | tf_op jit(solution)/shard_map/ppermute | solution.py:545
  660.9 78.6 %collective-permute-start.45 = (bf16[288,4352]{1,0:T(8,128)(2,1)}, bf16[288,4352]{1,0:T(8,128)(2,1)}, u32[]{:S(2)}, u32[]{:S(2)}) collective-permute-start(bf16[288,4352]{1,0:T(8,128)(2,1)} %concatenate.60), channel_id=1, source_target_pairs={{2,0},{4,2},{6,4},{3,1},{5,3},{7,5},{10,8},{12,10},{14,12},{11,9},... | collective-permute-start | bytes 7520264 | tf_op jit(solution)/shard_map/ppermute | solution.py:546
  666.6 67.2 %collective-permute-start.46 = (bf16[256,2304]{1,0:T(8,128)(2,1)}, bf16[256,2304]{1,0:T(8,128)(2,1)}, u32[]{:S(2)}, u32[]{:S(2)}) collective-permute-start(bf16[256,2304]{1,0:T(8,128)(2,1)} %get-tuple-element.264), channel_id=1, source_target_pairs={{0,2},{2,4},{4,6},{1,3},{3,5},{5,7},{8,10},{10,12},{12,14},{9,11},... | collective-permute-start | bytes 3538952 | tf_op jit(solution)/shard_map/ppermute | solution.py:602
  672.1 67.3 %collective-permute-start.47 = (bf16[256,2304]{1,0:T(8,128)(2,1)}, bf16[256,2304]{1,0:T(8,128)(2,1)}, u32[]{:S(2)}, u32[]{:S(2)}) collective-permute-start(bf16[256,2304]{1,0:T(8,128)(2,1)} %get-tuple-element.263), channel_id=1, source_target_pairs={{2,0},{4,2},{6,4},{3,1},{5,3},{7,5},{10,8},{12,10},{14,12},{11,9},... | collective-permute-start | bytes 3538952 | tf_op jit(solution)/shard_map/ppermute | solution.py:603
  682.1 193.9 %reduce-scatter.11.cloned.1.call-start = ((), (), s32[]{:S(2)}) async-start(), calls=%async_computation.11 | async-start | bytes 9953280 | tf_op jit(solution)/shard_map/reduce_scatter | solution.py:681
  739.5 52.4 %collective-permute-start.48 = (bf16[288,4352]{1,0:T(8,128)(2,1)}, bf16[288,4352]{1,0:T(8,128)(2,1)}, u32[]{:S(2)}, u32[]{:S(2)}) collective-permute-start(bf16[288,4352]{1,0:T(8,128)(2,1)} %collective-permute-done.44), channel_id=1, source_target_pairs={{2,4},{4,6},{3,5},{5,7},{10,12},{12,14},{11,13},{13,15},{18,20},{2... | collective-permute-start | bytes 7520264 | tf_op jit(solution)/shard_map/ppermute | solution.py:545
  741.6 52.5 %collective-permute-start.49 = (bf16[288,4352]{1,0:T(8,128)(2,1)}, bf16[288,4352]{1,0:T(8,128)(2,1)}, u32[]{:S(2)}, u32[]{:S(2)}) collective-permute-start(bf16[288,4352]{1,0:T(8,128)(2,1)} %collective-permute-done.45), channel_id=1, source_target_pairs={{2,0},{4,2},{3,1},{5,3},{10,8},{12,10},{11,9},{13,11},{18,16},{20,... | collective-permute-start | bytes 7520264 | tf_op jit(solution)/shard_map/ppermute | solution.py:546
  807.6 22.3 %collective-permute-start.52 = (bf16[256,2304]{1,0:T(8,128)(2,1)S(1)}, bf16[256,2304]{1,0:T(8,128)(2,1)S(1)}, u32[]{:S(2)}, u32[]{:S(2)}) collective-permute-start(bf16[256,2304]{1,0:T(8,128)(2,1)S(1)} %slice.159), channel_id=1, source_target_pairs={{0,2},{1,3},{8,10},{9,11},{16,18},{17,19},{24,26},{25,27}} | collective-permute-start | bytes 3538952 | tf_op jit(solution)/shard_map/ppermute | solution.py:602
  810.5 19.5 %collective-permute-start.53 = (bf16[256,2304]{1,0:T(8,128)(2,1)S(1)}, bf16[256,2304]{1,0:T(8,128)(2,1)S(1)}, u32[]{:S(2)}, u32[]{:S(2)}) collective-permute-start(bf16[256,2304]{1,0:T(8,128)(2,1)S(1)} %slice.159), channel_id=1, source_target_pairs={{6,4},{7,5},{14,12},{15,13},{22,20},{23,21},{30,28},{31,29}} | collective-permute-start | bytes 3538952 | tf_op jit(solution)/shard_map/ppermute | solution.py:603
  811.2 43.6 %collective-permute-start.50 = (bf16[288,4352]{1,0:T(8,128)(2,1)}, bf16[288,4352]{1,0:T(8,128)(2,1)S(1)}, u32[]{:S(2)}, u32[]{:S(2)}) collective-permute-start(bf16[288,4352]{1,0:T(8,128)(2,1)} %collective-permute-done.48), channel_id=1, source_target_pairs={{4,6},{5,7},{12,14},{13,15},{20,22},{21,23},{28,30},{29,31}} | collective-permute-start | bytes 7520264 | tf_op jit(solution)/shard_map/ppermute | solution.py:545
  812.1 51.9 %collective-permute-start.51 = (bf16[288,4352]{1,0:T(8,128)(2,1)}, bf16[288,4352]{1,0:T(8,128)(2,1)}, u32[]{:S(2)}, u32[]{:S(2)}) collective-permute-start(bf16[288,4352]{1,0:T(8,128)(2,1)} %collective-permute-done.49), channel_id=1, source_target_pairs={{2,0},{3,1},{10,8},{11,9},{18,16},{19,17},{26,24},{27,25}} | collective-permute-start | bytes 7520264 | tf_op jit(solution)/shard_map/ppermute | solution.py:546
  831.8 23.0 %collective-permute-start.54 = (bf16[256,2304]{1,0:T(8,128)(2,1)}, bf16[256,2304]{1,0:T(8,128)(2,1)}, u32[]{:S(2)}, u32[]{:S(2)}) collective-permute-start(bf16[256,2304]{1,0:T(8,128)(2,1)} %get-tuple-element.262), channel_id=1, source_target_pairs={{0,2},{2,4},{1,3},{3,5},{8,10},{10,12},{9,11},{11,13},{16,18},{18,... | collective-permute-start | bytes 3538952 | tf_op jit(solution)/shard_map/ppermute | solution.py:602
  876.1 22.8 %collective-permute-start.60 = (bf16[2,288,4352]{2,1,0:T(8,128)(2,1)}, bf16[2,288,4352]{2,1,0:T(8,128)(2,1)}, u32[]{:S(2)}, u32[]{:S(2)}) collective-permute-start(bf16[2,288,4352]{2,1,0:T(8,128)(2,1)} %get-tuple-element.245), channel_id=1, source_target_pairs={{0,1},{1,0},{2,3},{3,2},{4,5},{5,4},{6,7},{7,6},{8,9},{9,8},{10,11... | collective-permute-start | bytes 15040520 | tf_op jit(solution)/shard_map/ppermute | solution.py:697
  886.1 63.6 %collective-permute-start.58 = (bf16[288,2560]{1,0:T(8,128)(2,1)}, bf16[288,2560]{1,0:T(8,128)(2,1)S(1)}, u32[]{:S(2)}, u32[]{:S(2)}) collective-permute-start(bf16[288,2560]{1,0:T(8,128)(2,1)} %concatenate.62), channel_id=1, source_target_pairs={{0,2},{2,4},{4,6},{1,3},{3,5},{5,7},{8,10},{10,12},{12,14},{9,11},... | collective-permute-start | bytes 4423688 | tf_op jit(solution)/shard_map/ppermute | solution.py:545
  887.6 62.1 %collective-permute-start.59 = (bf16[288,2560]{1,0:T(8,128)(2,1)}, bf16[288,2560]{1,0:T(8,128)(2,1)S(1)}, u32[]{:S(2)}, u32[]{:S(2)}) collective-permute-start(bf16[288,2560]{1,0:T(8,128)(2,1)} %concatenate.62), channel_id=1, source_target_pairs={{2,0},{4,2},{6,4},{3,1},{5,3},{7,5},{10,8},{12,10},{14,12},{11,9},... | collective-permute-start | bytes 4423688 | tf_op jit(solution)/shard_map/ppermute | solution.py:546
  892.9 52.6 %collective-permute-start.56 = (bf16[256,2304]{1,0:T(8,128)(2,1)}, bf16[256,2304]{1,0:T(8,128)(2,1)S(1)}, u32[]{:S(2)}, u32[]{:S(2)}) collective-permute-start(bf16[256,2304]{1,0:T(8,128)(2,1)} %get-tuple-element.260), channel_id=1, source_target_pairs={{0,2},{2,4},{4,6},{1,3},{3,5},{5,7},{8,10},{10,12},{12,14},{9,11},... | collective-permute-start | bytes 3538952 | tf_op jit(solution)/shard_map/ppermute | solution.py:602
  897.5 52.1 %collective-permute-start.57 = (bf16[256,2304]{1,0:T(8,128)(2,1)S(1)}, bf16[256,2304]{1,0:T(8,128)(2,1)S(1)}, u32[]{:S(2)}, u32[]{:S(2)}) collective-permute-start(bf16[256,2304]{1,0:T(8,128)(2,1)S(1)} %get-tuple-element.259), channel_id=1, source_target_pairs={{2,0},{4,2},{6,4},{3,1},{5,3},{7,5},{10,8},{12,10},{14,12},{11,9},... | collective-permute-start | bytes 3538952 | tf_op jit(solution)/shard_map/ppermute | solution.py:603
  898.9 92.1 %collective-permute-start.65 = (bf16[256,2304]{1,0:T(8,128)(2,1)S(1)}, bf16[256,2304]{1,0:T(8,128)(2,1)}, u32[]{:S(2)}, u32[]{:S(2)}) collective-permute-start(bf16[256,2304]{1,0:T(8,128)(2,1)S(1)} %copy-done.48), channel_id=1, source_target_pairs={{0,1},{1,0},{2,3},{3,2},{4,5},{5,4},{6,7},{7,6},{8,9},{9,8},{10,11... | collective-permute-start | bytes 3538952 | tf_op jit(solution)/shard_map/ppermute | solution.py:892
  951.7 39.3 %collective-permute-start.62 = (bf16[288,2560]{1,0:T(8,128)(2,1)}, bf16[288,2560]{1,0:T(8,128)(2,1)S(1)}, u32[]{:S(2)}, u32[]{:S(2)}) collective-permute-start(bf16[288,2560]{1,0:T(8,128)(2,1)} %copy-done.60), channel_id=1, source_target_pairs={{2,0},{4,2},{3,1},{5,3},{10,8},{12,10},{11,9},{13,11},{18,16},{20,... | collective-permute-start | bytes 4423688 | tf_op jit(solution)/shard_map/ppermute | solution.py:546
  993.2 36.6 %collective-permute-start.64 = (bf16[288,2560]{1,0:T(8,128)(2,1)S(1)}, bf16[288,2560]{1,0:T(8,128)(2,1)S(1)}, u32[]{:S(2)}, u32[]{:S(2)}) collective-permute-start(bf16[288,2560]{1,0:T(8,128)(2,1)S(1)} %collective-permute-done.62), channel_id=1, source_target_pairs={{2,0},{3,1},{10,8},{11,9},{18,16},{19,17},{26,24},{27,25}} | collective-permute-start | bytes 4423688 | tf_op jit(solution)/shard_map/ppermute | solution.py:546
  (94 other events, 1893.2 us)
Sparse Core Ops, SparseCore 0:
  18.9 59.9 all-gather.5
  86.5 29.5 all-gather.7
  121.5 46.9 all-gather.9
  170.7 76.1 all-gather.11
  450.3 65.3 reduce-scatter.4
  519.1 97.1 reduce-scatter.6
  682.3 43.3 reduce-scatter.8
  794.2 71.9 reduce-scatter.10

commit v5 on v4

--- a/solution.py
+++ b/solution.py
@@ -561,12 +561,11 @@
         return found
 
     def at(self, target):
-        place = lax.axis_index(self.axis)
+        gap = lax.axis_index(self.axis) - target
         found = self.ups[0]
-        for here in range(self.size):
-            if here != target:
-                block = self.ups[here - target] if target < here else self.downs[target - here]
-                found = jnp.where(place == here, block, found)
+        for hops in range(1, self.size):
+            found = jnp.where(gap == hops, self.ups[hops], found)
+            found = jnp.where(gap == -hops, self.downs[hops], found)
         return found
 
 
@@ -690,15 +689,13 @@
         return jnp.concatenate([high, low], axis=1)
 
     def line_pieces(chain):
-        found = [chain.at(q) for q in range(lines)]
-        halves = [jnp.stack(found[h * per_half : (h + 1) * per_half]) for h in range(cores)]
-        own = jnp.where(core == 0, halves[0], halves[1])
-        give = jnp.where(core == 0, halves[1], halves[0])
-        return own, lax.ppermute(give, "tensor", swap_pairs()), found
+        half = lambda c: jnp.stack([chain.at(c * per_half + k) for k in range(per_half)])
+        give = half(1 - core)
+        return half(core), lax.ppermute(give, "tensor", swap_pairs()), give
 
     def gain_total(found, column, gain):
-        marks = sum(piece[:, column : column + 2].astype(jnp.float32) for piece in found)
-        own = jnp.sum(marks, axis=1)
+        marks = [pieces[:, :, column : column + 2].astype(jnp.float32) for pieces in found]
+        own = jnp.sum(marks[0] + marks[1], axis=(0, 2))
         other = lax.ppermute(own, "tensor", swap_pairs())
         total = jnp.concatenate(
             [jnp.where(core == 0, own, other), jnp.where(core == 0, other, own)]
@@ -748,7 +745,9 @@
     out_mine = to_pair(widen(turned_piece(w_out), 1))
     down_mine = to_pair(turned_piece(w_down))
     gate_up_mine = to_pair(column_piece([w_gate, w_up]))
-    gain_a, gain_b, out_mine = stage([tokens_line], gain_a, gain_b, out_mine)
+    gain_a, gain_b, out_mine, own_cot, cos_all, sin_all, order = stage(
+        [tokens_line], gain_a, gain_b, out_mine, own_cot, cos_all, sin_all, order
+    )
     tokens_line.step()
     out_w = gather_pair(out_mine)
     own_cot, down_mine = stage([tokens_line], own_cot, down_mine)
@@ -777,8 +776,9 @@
     (grad_mlp,) = stage([attn_line], grad_mlp)
     attn_line.step()
     half_rows = all_rows // 2
+    cut_rows = [0, half_rows, half_rows + row_count, all_rows]
     grad_hidden = [
-        plain_product(grad_mlp[k * half_rows : (k + 1) * half_rows], down_w) for k in range(2)
+        plain_product(grad_mlp[low:high], down_w) for low, high in zip(cut_rows, cut_rows[1:])
     ]
     grad_hidden = stage([attn_line], *grad_hidden)
     own_x = own_tokens.astype(jnp.float32)
@@ -806,24 +806,29 @@
     second_line.step()
     hidden_near, grad_near = units(near_half, grad_hidden[0])
     hidden_near, grad_near = stage([second_line], hidden_near, grad_near)
+    middle_block = second_line.near(lines // 2)
     second_line.step()
+    hidden_mid, grad_mid = units(middle_block, grad_hidden[1])
     part_near = col_product(grad_near, gate_up_w).astype(jnp.bfloat16)
-    (part_near,) = stage([second_line], part_near)
-    far_half = jnp.concatenate([second_line.near(k) for k in range(lines // 2, lines)], axis=0)
-    hidden_far, grad_far = units(far_half, grad_hidden[1])
-    hidden = jnp.concatenate([hidden_near, hidden_far], axis=0)
+    part_near, hidden_mid, grad_mid = stage([second_line], part_near, hidden_mid, grad_mid)
+    last_block = second_line.near(lines - 1)
+    hidden_last, grad_last = units(last_block, grad_hidden[2])
+    part_last = col_product(grad_last, gate_up_w).astype(jnp.bfloat16)
+    part_last, hidden_last, grad_mid = lax.optimization_barrier((part_last, hidden_last, grad_mid))
+
+    parts = blocks_of(part_near) + [None, part_last]
+    grad_line = add_up(parts)
+    grad_line.step()
+    parts[lines // 2] = col_product(grad_mid, gate_up_w).astype(jnp.bfloat16)
+    hidden = jnp.concatenate([hidden_near, hidden_mid, hidden_last], axis=0)
     down_grad = row_product(grad_mlp, hidden).astype(jnp.bfloat16)
-    down_grad, grad_far = lax.optimization_barrier((down_grad, grad_far))
+    down_grad, grad_mid = lax.optimization_barrier((down_grad, grad_mid))
     down_piece = reduce_pair(down_grad)
-    part_far = col_product(grad_far, gate_up_w).astype(jnp.bfloat16)
-
-    grad_line = add_up(blocks_of(part_near) + blocks_of(part_far))
+    second_in = jnp.concatenate([near_half, middle_block, last_block], axis=0)
+    grad_gate_up = jnp.concatenate([grad_near, grad_mid, grad_last], axis=0)
+    parts[lines // 2], hidden = stage([grad_line], parts[lines // 2], hidden)
     grad_line.step()
-    second_in = jnp.concatenate([near_half, far_half], axis=0)
-    grad_gate_up = jnp.concatenate([grad_near, grad_far], axis=0)
     gate_up_grad = row_product(second_in, grad_gate_up).astype(jnp.bfloat16)
-    (hidden,) = stage([grad_line], hidden)
-    grad_line.step()
     gate_up_grad, down_piece = stage([grad_line], gate_up_grad, down_piece)
     gate_up_piece = reduce_pair(gate_up_grad)
     grad_line.step()
@@ -851,35 +856,34 @@
     unit_line.step()
     grad_attn = jnp.concatenate([attn_grad_line.near(k) for k in range(lines)], axis=0)
     out_grad = row_product(grad_attn, attend).astype(jnp.bfloat16)
-    out_piece = reduce_pair(out_grad)
-    grad_attn, out_grad = stage([unit_line, mlp_line], grad_attn, out_grad)
-    unit_line.step()
     grad_attend = plain_product(grad_attn, out_w).astype(jnp.bfloat16)
     grad_qkv = attend_backward(
         heads, span, order, length.reshape(1), kept, attend, grad_attend, cos_all, sin_all
     )
     qkv_grad = row_product(first_in, grad_qkv).astype(jnp.bfloat16)
-    grad_qkv, qkv_grad, out_piece = stage([unit_line], grad_qkv, qkv_grad, out_piece)
+    out_piece = reduce_pair(out_grad)
+    grad_qkv, qkv_grad, out_piece = stage([unit_line, mlp_line], grad_qkv, qkv_grad, out_piece)
     unit_line.step()
     qkv_piece = reduce_pair(qkv_grad)
     first_part = col_product(grad_qkv, qkv_w).astype(jnp.bfloat16)
+
     first_line = add_up(blocks_of(first_part))
     first_line.step()
     layer_rows = ((middle + BRANCH_SCALE * mlp_line.total()) * live_own).astype(jnp.bfloat16)
-    (layer_rows,) = stage([first_line], layer_rows)
-    first_line.step()
-    stage([unit_line, first_line])
+    (layer_rows,) = stage([unit_line, first_line], layer_rows)
+    unit_line.step()
     first_line.step()
     qkv_marks = gain_marks(qkv_mine, qkv_piece)
-    head_line = walk(
-        jnp.concatenate(
-            [qkv_piece[:, :head_cols], qkv_marks, qkv_piece[:, head_cols + 2 :], out_piece], axis=1
-        )
-    )
+    head_block = jnp.concatenate(
+        [qkv_piece[:, :head_cols], qkv_marks, qkv_piece[:, head_cols + 2 :], out_piece], axis=1
+    )
+    (head_block,) = stage([unit_line, first_line], head_block)
+    head_line = walk(head_block)
     head_line.step()
-    own, other, found = line_pieces(unit_line)
+    first_line.step()
+    own, other, give = line_pieces(unit_line)
     final_gate, final_up, final_down = join_columns(core_index, own, other, 3, unit_cols, unit_cols)
-    final_gain_two = gain_total(found, 3 * unit_cols, mlp_gain)
+    final_gain_two = gain_total((own, give), 3 * unit_cols, mlp_gain)
     final_gate, final_up, final_down = stage([first_line, head_line], final_gate, final_up, final_down)
     head_line.step()
     grad_first = first_line.total()
@@ -897,11 +901,11 @@
     layer_out = both_slots(layer_rows)
     grad_tokens = both_slots(grad_rows.astype(jnp.bfloat16)).astype(jnp.float32)
     layer_out, grad_tokens = stage([head_line], layer_out, grad_tokens)
-    own, other, found = line_pieces(head_line)
+    own, other, give = line_pieces(head_line)
     final_query, final_key, final_value, final_out = join_columns(
         core_index, own, other, 4, pad_cols, head_cols
     )
-    final_gain_one = gain_total(found, head_cols, attn_gain)
+    final_gain_one = gain_total((own, give), head_cols, attn_gain)
     return (
         layer_out,
         grad_tokens,

time: 1060 us -> 1050 us (level)
  waiting for transfers between devices: 443 us -> 411 us
  matrix products: 182 us -> 202 us
    ppermute x12, waiting for transfers between devices: 172 us -> 113 us  [step(): self.up = lax.ppermute(up, self.axis, [(i, i + 1) for i, _ in ups])]
    another operation x0 -> x8, other arithmetic: none -> 20.2 us  [line_pieces(): jnp.stack([chain.at(c * per_half + k) for k in range(per_half)])]
    reduce_scatter x4, waiting for transfers between devices: 1.08 us -> 14.2 us  [reduce_pair(): lax.psum_scatter(grad, ('shard', 'tensor'), scatter_dimension=0, tiled=True)]
    ppermute x18, waiting for transfers between devices: 176 us -> 189 us  [step(): self.downs.append(lax.ppermute(self.downs[-1], self.axis, down_pairs))]
    select_n x4 -> x0, other arithmetic: 12.3 us -> none  [the longest x2 6.77 us: at(): found = jnp.where(place == here, block, found)]
    dot_general x5 -> x6, matrix products: 56.4 us -> 67.1 us  [col_product(): lax.dot_general(left_mat, right_mat, CONTRACT_COLS, preferred_element_typ...]
    dot_general x6 -> x8, matrix products: 73.9 us -> 81.2 us  [plain_product(): return jnp.dot(left_mat, right_mat, preferred_element_type=jnp.float32)]
  transfers between devices with their start and end apart: 78 -> 78, of which waited for: 38 -> 38; matrix products, arithmetic and copies ran while one was open for 27% -> 28% of each run, Pallas kernels for 7% -> 7%
where the time goes in v5:
time: 1050 us; the launch traced here: 1040 us
  waiting for transfers between devices  411 us (39%)
  matrix products  202 us (19%)
  starting transfers between devices  149 us (14%)
  other arithmetic  127 us (12%)
  Pallas kernels  77 us (7%)
  local copies, waits for them, and re-layouts  48 us (5%)
  between operations  16 us (2%)
    ppermute x18, waiting for transfers between devices, step(): self.downs.append(lax.ppermute(self.downs[-1], self.axis, down_pairs))  189 us
    ppermute x12, waiting for transfers between devices, step(): self.up = lax.ppermute(up, self.axis, [(i, i + 1) for i, _ in ups])  113 us
    dot_general x8, matrix products, plain_product(): return jnp.dot(left_mat, right_mat, preferred_element_type=jnp.float32)  81.2 us
    dot_general x6, matrix products, col_product(): lax.dot_general(left_mat, right_mat, CONTRACT_COLS, preferred_element_typ...  67.1 us
    ppermute x18, waiting for transfers between devices, step(): self.ups.append(lax.ppermute(self.ups[-1], self.axis, up_pairs))  66.2 us
    ppermute x12, starting transfers between devices, step(): self.up = lax.ppermute(up, self.axis, [(i, i + 1) for i, _ in ups])  63.5 us
    dot_general x4, matrix products, row_product(): lax.dot_general(left_mat, right_mat, CONTRACT_ROWS, preferred_element_typ...  53.8 us
    ppermute x18, starting transfers between devices, step(): self.ups.append(lax.ppermute(self.ups[-1], self.axis, up_pairs))  44.7 us
  transfers between devices with their start and end apart: 78, of which 38 were waited for; matrix products, arithmetic and copies ran while one was open for 28% of the time, Pallas kernels for 7%

profile of v5, /device:TPU:0, one launch (start us, length us, event | category | flops | bytes accessed | tf_op | source)
XLA Modules:
  0.0 1037.8 jit_solution(7972541594351013808)
XLA Ops:
  18.8 5.7 collective-permute-start
  28.2 21.3 %collective-permute-done = bf16[256,2304]{1,0:T(8,128)(2,1)} collective-permute-done((bf16[256,2304]{1,0:T(8,128)(2,1)S(1)}, bf16[256,2304]{1,0:T(8,128)(2,1)}, u32[]{:S(2)}, u32[]{:S(2)}) %collective-permute-start) | collective-permute-done | bytes 1179680 | tf_op jit(solution)/shard_map/ppermute | solution.py:545
  49.4 5.8 collective-permute-done.1
  63.8 8.6 all-gather
  74.4 12.9 %collective-permute-done.3 = bf16[256,2304]{1,0:T(8,128)(2,1)} collective-permute-done((bf16[256,2304]{1,0:T(8,128)(2,1)}, bf16[256,2304]{1,0:T(8,128)(2,1)}, u32[]{:S(2)}, u32[]{:S(2)}) %collective-permute-start.3) | collective-permute-done | bytes 1179680 | tf_op jit(solution)/shard_map/ppermute | solution.py:546
  95.7 26.6 %collective-permute-done.6 = bf16[256,2304]{1,0:T(8,128)(2,1)} collective-permute-done((bf16[256,2304]{1,0:T(8,128)(2,1)}, bf16[256,2304]{1,0:T(8,128)(2,1)}, u32[]{:S(2)}, u32[]{:S(2)}) %collective-permute-start.6) | collective-permute-done | bytes 1179680 | tf_op jit(solution)/shard_map/ppermute | solution.py:546
  142.2 17.9 %fusion.58.q_in.k_in.v_in = f32[1024,1920]{1,0:T(8,128)} fusion(bf16[2304,1920]{1,0:T(8,128)(2,1)} %all-gather.6.cloned.1.call-done, f32[2304]{0:T(1024)S(1)} %get-tuple-element.148, f32[1024]{0:T(1024)S(1)} %add_rsqrt_fusion, bf16[256,2304]{1,0:T(8,128)(2,1)} %copy-done.42, bf16[256,2304]{1,0:T(8,128)(2,1)} %select_select_fusion.6, ...), kind=kOutput, calls=%fused_computation.155 | convolution fusion | flops 9085648896 | bytes 21443584 | tf_op jit(solution)/shard_map/dot_general | solution.py:30
  161.4 5.8 collective-permute-done.9
  174.1 29.5 %attend.1 = (bf16[1024,640]{1,0:T(8,128)(2,1)S(1)}, bf16[1024,640]{1,0:T(8,128)(2,1)S(1)}, bf16[1024,640]{1,0:T(8,128)(2,1)S(1)}, bf16[1024,640]{1,0:T(8,128)(2,1)S(1)}, f32[5,8,1024]{2,1,0:T(8,128)S(1)}) custom-call(s32[8]{0:T(128)S(1)} %and_select_fusion.order, s32[1]{0:T(128)} %dynamic_slice.60.length, f32[1024,1920]{1,0:T(8,128)S(1)} %copy-done.2, ...), custom_call_target="tpu_custom_call" | custom-call | flops 2415919104 | bytes 15728640 | tf_op jit(solution)/shard_map/attend/pallas_call | solution.py:451
  206.9 7.2 convolution_convert_fusion.4
  214.3 5.2 collective-permute-start.14
  224.6 20.0 %collective-permute-done.14 = bf16[256,2304]{1,0:T(8,128)(2,1)S(1)} collective-permute-done((bf16[256,2304]{1,0:T(8,128)(2,1)S(1)}, bf16[256,2304]{1,0:T(8,128)(2,1)S(1)}, u32[]{:S(2)}, u32[]{:S(2)}) %collective-permute-start.14) | collective-permute-done | bytes 1179680 | tf_op jit(solution)/shard_map/ppermute | solution.py:601
  244.6 6.4 collective-permute-done.17
  256.0 9.1 multiply_convert_fusion
  265.1 12.6 %collective-permute-done.18 = bf16[256,2304]{1,0:T(8,128)(2,1)S(1)} collective-permute-done((bf16[256,2304]{1,0:T(8,128)(2,1)S(1)}, bf16[256,2304]{1,0:T(8,128)(2,1)S(1)}, u32[]{:S(2)}, u32[]{:S(2)}) %collective-permute-start.18) | collective-permute-done | bytes 1179680 | tf_op jit(solution)/shard_map/ppermute | solution.py:601
  279.8 7.5 collective-permute-start.20
  288.8 7.4 fusion.62
  296.2 5.3 fusion.60
  301.5 5.3 fusion.41
  310.1 5.1 collective-permute-done.21
  323.3 21.1 %collective-permute-done.22 = bf16[256,2304]{1,0:T(8,128)(2,1)S(1)} collective-permute-done((bf16[256,2304]{1,0:T(8,128)(2,1)S(1)}, bf16[256,2304]{1,0:T(8,128)(2,1)S(1)}, u32[]{:S(2)}, u32[]{:S(2)}) %collective-permute-start.22) | collective-permute-done | bytes 1179680 | tf_op jit(solution)/shard_map/ppermute | solution.py:545
  354.3 17.9 %fusion.37 = f32[512,2880]{0,1:T(8,128)} fusion(bf16[2304,2880]{1,0:T(8,128)(2,1)} %all-gather.12.cloned.1.call-done, bf16[256,2304]{1,0:T(8,128)(2,1)} %fusion.46, bf16[256,2304]{1,0:T(8,128)(2,1)} %copy-done.49), kind=kOutput, calls=%fused_computation.94 | convolution fusion | flops 6799491072 | bytes 21528576 | tf_op jit(solution)/shard_map/dot_general | solution.py:30
  384.6 9.3 fusion.79
  397.4 13.0 %convolution_convert_fusion.7 = bf16[512,2304]{1,0:T(8,128)(2,1)} fusion(bf16[512,2880]{0,1:T(8,128)(2,1)S(1)} %pad_maximum_fusion.6, bf16[2304,2880]{1,0:T(8,128)(2,1)} %all-gather.12.cloned.1.call-done), kind=kOutput, calls=%fused_computation.38 | convolution fusion | flops 6795952128 | bytes 18579456 | tf_op jit(solution)/shard_map/dot_general | solution.py:26
  413.0 11.9 %fusion.80 = f32[256,2880]{0,1:T(8,128)} fusion(bf16[256,2304]{1,0:T(8,128)(2,1)S(1)} %select_select_fusion.9, bf16[2304,2880]{1,0:T(8,128)(2,1)} %all-gather.12.cloned.1.call-done), kind=kOutput, calls=%fused_computation.234 | convolution fusion | flops 3397386240 | bytes 17399808 | tf_op jit(solution)/shard_map/dot_general | solution.py:30
  428.9 10.3 convolution_convert_fusion.9
  441.0 11.7 %convolution_convert_fusion.2 = bf16[2304,1440]{1,0:T(8,128)(2,1)} fusion(bf16[1024,2304]{1,0:T(8,128)(2,1)S(1)} %bitcast.82, bf16[1024,1440]{0,1:T(8,128)(2,1)} %constant_dynamic-update-slice_fusion), kind=kOutput, calls=%fused_computation.5 | convolution fusion | flops 6798090240 | bytes 14303232 | tf_op jit(solution)/shard_map/dot_general | solution.py:22
  452.8 5.6 collective-permute-start.28
  459.2 10.9 %convolution_convert_fusion.8 = bf16[256,2304]{1,0:T(8,128)(2,1)S(1)} fusion(bf16[256,2880]{0,1:T(8,128)(2,1)} %pad_maximum_fusion.8, bf16[2304,2880]{1,0:T(8,128)(2,1)} %all-gather.12.cloned.1.call-done), kind=kOutput, calls=%fused_computation.45 | convolution fusion | flops 3397976064 | bytes 15925248 | tf_op jit(solution)/shard_map/dot_general | solution.py:26
  470.1 10.0 collective-permute-done.28
  481.9 5.3 collective-permute-start.30
  488.9 22.1 %convolution_convert_fusion = bf16[2304,2880]{1,0:T(8,128)(2,1)} fusion(bf16[256,1440]{0,1:T(8,128)(2,1)} %get-tuple-element.291, bf16[256,1440]{0,1:T(8,128)(2,1)S(1)} %copy-done.61, bf16[256,2880]{0,1:T(8,128)(2,1)} %pad_maximum_fusion.8, bf16[512,2880]{0,1:T(8,128)(2,1)} %copy-done.44, bf16[256,2304]{1,0:T(8,128)(2,1)} %copy-done.51, ...), kind=kOutput, calls=%fused_computation.1 | convolution fusion | flops 13638647808 | bytes 23887872 | tf_op jit(solution)/shard_map/dot_general | solution.py:22
  511.0 10.1 reduce-scatter.5.cloned.1.call-done
  529.4 11.7 %convolution_convert_fusion.5 = bf16[1024,2304]{1,0:T(8,128)(2,1)S(1)} fusion(bf16[1024,1440]{0,1:T(8,128)(2,1)S(1)} %copy-done.62, bf16[2304,1440]{1,0:T(8,128)(2,1)} %all-gather.10.cloned.1.call-done), kind=kOutput, calls=%fused_computation.21 | convolution fusion | flops 6797131776 | bytes 14303232 | tf_op jit(solution)/shard_map/dot_general | solution.py:26
  541.2 11.7 %collective-permute-done.32 = bf16[256,2304]{1,0:T(8,128)(2,1)S(1)} collective-permute-done((bf16[256,2304]{1,0:T(8,128)(2,1)S(1)}, bf16[256,2304]{1,0:T(8,128)(2,1)S(1)}, u32[]{:S(2)}, u32[]{:S(2)}) %collective-permute-start.32) | collective-permute-done | bytes 1179680 | tf_op jit(solution)/shard_map/ppermute | solution.py:601
  565.6 22.5 %collective-permute-done.34 = bf16[256,2304]{1,0:T(8,128)(2,1)S(1)} collective-permute-done((bf16[256,2304]{1,0:T(8,128)(2,1)S(1)}, bf16[256,2304]{1,0:T(8,128)(2,1)S(1)}, u32[]{:S(2)}, u32[]{:S(2)}) %collective-permute-start.34) | collective-permute-done | bytes 1179680 | tf_op jit(solution)/shard_map/ppermute | solution.py:545
  595.4 5.5 collective-permute-start.38
  601.7 20.9 %collective-permute-done.37 = bf16[256,2304]{1,0:T(8,128)(2,1)} collective-permute-done((bf16[256,2304]{1,0:T(8,128)(2,1)S(1)}, bf16[256,2304]{1,0:T(8,128)(2,1)}, u32[]{:S(2)}, u32[]{:S(2)}) %collective-permute-start.37) | collective-permute-done | bytes 1179680 | tf_op jit(solution)/shard_map/ppermute | solution.py:546
  628.6 6.6 collective-permute-start.42
  642.8 5.1 concatenate.60
  660.1 5.3 convolution_convert_fusion.6
  665.5 10.6 %collective-permute-start.44 = (bf16[288,4352]{1,0:T(8,128)(2,1)}, bf16[288,4352]{1,0:T(8,128)(2,1)}, u32[]{:S(2)}, u32[]{:S(2)}) collective-permute-start(bf16[288,4352]{1,0:T(8,128)(2,1)} %concatenate.60), channel_id=1, source_target_pairs={{0,2},{2,4},{4,6},{1,3},{3,5},{5,7},{8,10},{10,12},{12,14},{9,11},... | collective-permute-start | bytes 7520264 | tf_op jit(solution)/shard_map/ppermute | solution.py:545
  677.7 4.8 add_convert_fusion.2
  682.4 5.6 collective-permute-start.46
  689.6 6.1 convolution_convert_fusion.10.do_in
  695.8 29.8 %attend_back.1 = bf16[1024,1920]{1,0:T(8,128)(2,1)} custom-call(s32[8]{0:T(128)S(1)} %and_select_fusion.order, s32[1]{0:T(128)} %dynamic_slice.60.length, bf16[1024,640]{1,0:T(8,128)(2,1)S(1)} %copy-done.6, bf16[1024,640]{1,0:T(8,128)(2,1)S(1)} %copy-done.8, bf16[1024,640]{1,0:T(8,128)(2,1)S(1)} %copy-done.10, f32[5,8,1024]{2,1,0:T(8,128)S(1)} %get-tuple-element.220.log_in, ...), custom_call_target="tpu_custom_call" | custom-call | flops 6039797760 | bytes 10485760 | tf_op jit(solution)/shard_map/attend_back/pallas_call | solution.py:478
  725.7 14.7 %convolution_convert_fusion.1 = bf16[2304,1920]{1,0:T(8,128)(2,1)} fusion(bf16[1024,1920]{1,0:T(8,128)(2,1)} %attend_back.1, f32[2304]{0:T(1024)S(1)} %copy-done.65, f32[1024]{0:T(1024)S(1)} %copy-done.72, bf16[256,2304]{1,0:T(8,128)(2,1)S(1)} %copy-done.43, bf16[256,2304]{1,0:T(8,128)(2,1)S(1)} %copy-done.39, bf16[256,2304]{1,0:T(8,128)(2,1)S(1)} %copy-done.41, ...), kind=kOutput, calls=%fused_computation.4 | convolution fusion | flops 9090072576 | bytes 17511424 | tf_op jit(solution)/shard_map/dot_general | solution.py:22
  740.4 8.6 collective-permute-done.46
  749.0 5.7 collective-permute-done.47
  757.3 14.1 %convolution_convert_fusion.3 = bf16[1024,2304]{1,0:T(8,128)(2,1)S(1)} fusion(bf16[1024,1920]{1,0:T(8,128)(2,1)} %attend_back.1, bf16[2304,1920]{1,0:T(8,128)(2,1)} %all-gather.6.cloned.1.call-done), kind=kOutput, calls=%fused_computation.19 | convolution fusion | flops 9062055936 | bytes 17498112 | tf_op jit(solution)/shard_map/dot_general | solution.py:26
  771.5 4.6 collective-permute-start.50
  780.8 13.9 %collective-permute-done.50 = bf16[256,2304]{1,0:T(8,128)(2,1)S(1)} collective-permute-done((bf16[256,2304]{1,0:T(8,128)(2,1)S(1)}, bf16[256,2304]{1,0:T(8,128)(2,1)S(1)}, u32[]{:S(2)}, u32[]{:S(2)}) %collective-permute-start.50) | collective-permute-done | bytes 1179680 | tf_op jit(solution)/shard_map/ppermute | solution.py:601
  794.7 13.8 %collective-permute-done.49 = bf16[288,4352]{1,0:T(8,128)(2,1)} collective-permute-done((bf16[288,4352]{1,0:T(8,128)(2,1)}, bf16[288,4352]{1,0:T(8,128)(2,1)}, u32[]{:S(2)}, u32[]{:S(2)}) %collective-permute-start.49) | collective-permute-done | bytes 2506784 | tf_op jit(solution)/shard_map/ppermute | solution.py:546
  813.8 7.0 collective-permute-start.54
  838.3 23.9 %collective-permute-done.53 = bf16[288,4352]{1,0:T(8,128)(2,1)} collective-permute-done((bf16[288,4352]{1,0:T(8,128)(2,1)}, bf16[288,4352]{1,0:T(8,128)(2,1)}, u32[]{:S(2)}, u32[]{:S(2)}) %collective-permute-start.53) | collective-permute-done | bytes 2506784 | tf_op jit(solution)/shard_map/ppermute | solution.py:546
  862.2 6.5 select_bitcast_fusion.1
  880.6 5.6 collective-permute-start.56
  887.5 5.3 select_bitcast_fusion.3
  893.4 12.4 %join_columns.2 = (f32[576,2880]{1,0:T(8,128)}, f32[576,2880]{1,0:T(8,128)}, f32[576,2880]{1,0:T(8,128)}) custom-call(s32[1]{0:T(128)} %bitcast.11.core, bf16[2,288,4352]{2,1,0:T(8,128)(2,1)S(1)} %pad_maximum_fusion.own, bf16[2,288,4352]{2,1,0:T(8,128)(2,1)} %collective-permute-done.60.other), custom_call_target="tpu_custom_call" | custom-call | bytes 39960576 | tf_op jit(solution)/shard_map/join_columns/pallas_call | solution.py:515
  905.8 25.7 %collective-permute-done.56 = bf16[256,2304]{1,0:T(8,128)(2,1)} collective-permute-done((bf16[256,2304]{1,0:T(8,128)(2,1)}, bf16[256,2304]{1,0:T(8,128)(2,1)}, u32[]{:S(2)}, u32[]{:S(2)}) %collective-permute-start.56) | collective-permute-done | bytes 1179680 | tf_op jit(solution)/shard_map/ppermute | solution.py:601
  931.5 5.2 collective-permute-done.57
  944.6 28.7 %collective-permute-done.62 = bf16[288,2560]{1,0:T(8,128)(2,1)S(1)} collective-permute-done((bf16[288,2560]{1,0:T(8,128)(2,1)}, bf16[288,2560]{1,0:T(8,128)(2,1)S(1)}, u32[]{:S(2)}, u32[]{:S(2)}) %collective-permute-start.62) | collective-permute-done | bytes 1474592 | tf_op jit(solution)/shard_map/ppermute | solution.py:546
  981.4 31.0 %collective-permute-done.64 = bf16[288,2560]{1,0:T(8,128)(2,1)S(1)} collective-permute-done((bf16[288,2560]{1,0:T(8,128)(2,1)S(1)}, bf16[288,2560]{1,0:T(8,128)(2,1)S(1)}, u32[]{:S(2)}, u32[]{:S(2)}) %collective-permute-start.64) | collective-permute-done | bytes 1474592 | tf_op jit(solution)/shard_map/ppermute | solution.py:546
  1025.5 5.3 join_columns.3
  (404 shorter events, 259.1 us)
Async XLA Ops:
  7.2 135.0 %all-gather.6.cloned.1.call-start = ((), (), s32[]{:S(2)}) async-start(), calls=%async_computation.4 | async-start | bytes 9953280 | tf_op jit(solution)/shard_map/all_gather | solution.py:677
  18.8 188.1 %all-gather.8.cloned.1.call-start = ((), (), s32[]{:S(2)}) async-start(), calls=%async_computation.5 | async-start | bytes 3317760 | tf_op jit(solution)/shard_map/all_gather | solution.py:677
  18.8 30.6 %collective-permute-start = (bf16[256,2304]{1,0:T(8,128)(2,1)S(1)}, bf16[256,2304]{1,0:T(8,128)(2,1)}, u32[]{:S(2)}, u32[]{:S(2)}) collective-permute-start(bf16[256,2304]{1,0:T(8,128)(2,1)S(1)} %dynamic-slice_bitcast_fusion.1), channel_id=1, source_target_pairs={{0,2},{2,4},{4,6},{1,3},{3,5},{5,7},{8,10},{10,12},{12,14},{9,11},... | collective-permute-start | bytes 3538952 | tf_op jit(solution)/shard_map/ppermute | solution.py:545
  24.6 30.7 %collective-permute-start.1 = (bf16[256,2304]{1,0:T(8,128)(2,1)S(1)}, bf16[256,2304]{1,0:T(8,128)(2,1)}, u32[]{:S(2)}, u32[]{:S(2)}) collective-permute-start(bf16[256,2304]{1,0:T(8,128)(2,1)S(1)} %dynamic-slice_bitcast_fusion.1), channel_id=1, source_target_pairs={{2,0},{4,2},{6,4},{3,1},{5,3},{7,5},{10,8},{12,10},{14,12},{11,9},... | collective-permute-start | bytes 3538952 | tf_op jit(solution)/shard_map/ppermute | solution.py:546
  55.2 19.2 %collective-permute-start.2 = (bf16[256,2304]{1,0:T(8,128)(2,1)}, bf16[256,2304]{1,0:T(8,128)(2,1)}, u32[]{:S(2)}, u32[]{:S(2)}) collective-permute-start(bf16[256,2304]{1,0:T(8,128)(2,1)} %collective-permute-done), channel_id=1, source_target_pairs={{2,4},{4,6},{3,5},{5,7},{10,12},{12,14},{11,13},{13,15},{18,20},{2... | collective-permute-start | bytes 3538952 | tf_op jit(solution)/shard_map/ppermute | solution.py:545
  57.0 30.4 %collective-permute-start.3 = (bf16[256,2304]{1,0:T(8,128)(2,1)}, bf16[256,2304]{1,0:T(8,128)(2,1)}, u32[]{:S(2)}, u32[]{:S(2)}) collective-permute-start(bf16[256,2304]{1,0:T(8,128)(2,1)} %collective-permute-done.1), channel_id=1, source_target_pairs={{2,0},{4,2},{3,1},{5,3},{10,8},{12,10},{11,9},{13,11},{18,16},{20,... | collective-permute-start | bytes 3538952 | tf_op jit(solution)/shard_map/ppermute | solution.py:546
  87.3 201.5 %all-gather.10.cloned.1.call-start = ((), (), s32[]{:S(2)}) async-start(), calls=%async_computation.6 | async-start | bytes 7962624 | tf_op jit(solution)/shard_map/all_gather | solution.py:677
  91.7 30.6 %collective-permute-start.6 = (bf16[256,2304]{1,0:T(8,128)(2,1)}, bf16[256,2304]{1,0:T(8,128)(2,1)}, u32[]{:S(2)}, u32[]{:S(2)}) collective-permute-start(bf16[256,2304]{1,0:T(8,128)(2,1)} %collective-permute-done.3), channel_id=1, source_target_pairs={{2,0},{3,1},{10,8},{11,9},{18,16},{19,17},{26,24},{27,25}} | collective-permute-start | bytes 3538952 | tf_op jit(solution)/shard_map/ppermute | solution.py:546
  122.3 232.0 %all-gather.12.cloned.1.call-start = ((), (), s32[]{:S(2)}) async-start(), calls=%async_computation.7 | async-start | bytes 15261696 | tf_op jit(solution)/shard_map/all_gather | solution.py:677
  134.4 27.0 %collective-permute-start.8 = (bf16[256,2304]{1,0:T(8,128)(2,1)S(1)}, bf16[256,2304]{1,0:T(8,128)(2,1)}, u32[]{:S(2)}, u32[]{:S(2)}) collective-permute-start(bf16[256,2304]{1,0:T(8,128)(2,1)S(1)} %dynamic-slice_bitcast_fusion), channel_id=1, source_target_pairs={{0,2},{2,4},{4,6},{1,3},{3,5},{5,7},{8,10},{10,12},{12,14},{9,11},... | collective-permute-start | bytes 3538952 | tf_op jit(solution)/shard_map/ppermute | solution.py:545
  136.9 30.3 %collective-permute-start.9 = (bf16[256,2304]{1,0:T(8,128)(2,1)S(1)}, bf16[256,2304]{1,0:T(8,128)(2,1)}, u32[]{:S(2)}, u32[]{:S(2)}) collective-permute-start(bf16[256,2304]{1,0:T(8,128)(2,1)S(1)} %dynamic-slice_bitcast_fusion), channel_id=1, source_target_pairs={{2,0},{4,2},{6,4},{3,1},{5,3},{7,5},{10,8},{12,10},{14,12},{11,9},... | collective-permute-start | bytes 3538952 | tf_op jit(solution)/shard_map/ppermute | solution.py:546
  167.2 353.9 %reduce-scatter.5.cloned.1.call-start = ((), (), s32[]{:S(2)}) async-start(), calls=%async_computation.8 | async-start | bytes 7962624 | tf_op jit(solution)/shard_map/reduce_scatter | solution.py:680
  167.2 39.7 %collective-permute-start.12 = (bf16[256,2304]{1,0:T(8,128)(2,1)}, bf16[256,2304]{1,0:T(8,128)(2,1)}, u32[]{:S(2)}, u32[]{:S(2)}) collective-permute-start(bf16[256,2304]{1,0:T(8,128)(2,1)} %collective-permute-done.8), channel_id=1, source_target_pairs={{2,4},{4,6},{3,5},{5,7},{10,12},{12,14},{11,13},{13,15},{18,20},{2... | collective-permute-start | bytes 3538952 | tf_op jit(solution)/shard_map/ppermute | solution.py:545
  168.9 38.0 %collective-permute-start.13 = (bf16[256,2304]{1,0:T(8,128)(2,1)}, bf16[256,2304]{1,0:T(8,128)(2,1)}, u32[]{:S(2)}, u32[]{:S(2)}) collective-permute-start(bf16[256,2304]{1,0:T(8,128)(2,1)} %collective-permute-done.9), channel_id=1, source_target_pairs={{2,0},{4,2},{3,1},{5,3},{10,8},{12,10},{11,9},{13,11},{18,16},{20,... | collective-permute-start | bytes 3538952 | tf_op jit(solution)/shard_map/ppermute | solution.py:546
  214.3 30.3 %collective-permute-start.14 = (bf16[256,2304]{1,0:T(8,128)(2,1)S(1)}, bf16[256,2304]{1,0:T(8,128)(2,1)S(1)}, u32[]{:S(2)}, u32[]{:S(2)}) collective-permute-start(bf16[256,2304]{1,0:T(8,128)(2,1)S(1)} %slice.138), channel_id=1, source_target_pairs={{0,2},{1,3},{8,10},{9,11},{16,18},{17,19},{24,26},{25,27}} | collective-permute-start | bytes 3538952 | tf_op jit(solution)/shard_map/ppermute | solution.py:601
  219.4 25.2 %collective-permute-start.15 = (bf16[256,2304]{1,0:T(8,128)(2,1)S(1)}, bf16[256,2304]{1,0:T(8,128)(2,1)S(1)}, u32[]{:S(2)}, u32[]{:S(2)}) collective-permute-start(bf16[256,2304]{1,0:T(8,128)(2,1)S(1)} %slice.138), channel_id=1, source_target_pairs={{6,4},{7,5},{14,12},{15,13},{22,20},{23,21},{30,28},{31,29}} | collective-permute-start | bytes 3538952 | tf_op jit(solution)/shard_map/ppermute | solution.py:602
  220.2 24.4 %collective-permute-start.16 = (bf16[256,2304]{1,0:T(8,128)(2,1)}, bf16[256,2304]{1,0:T(8,128)(2,1)S(1)}, u32[]{:S(2)}, u32[]{:S(2)}) collective-permute-start(bf16[256,2304]{1,0:T(8,128)(2,1)} %collective-permute-done.12), channel_id=1, source_target_pairs={{4,6},{5,7},{12,14},{13,15},{20,22},{21,23},{28,30},{29,31}} | collective-permute-start | bytes 3538952 | tf_op jit(solution)/shard_map/ppermute | solution.py:545
  220.9 30.1 %collective-permute-start.17 = (bf16[256,2304]{1,0:T(8,128)(2,1)}, bf16[256,2304]{1,0:T(8,128)(2,1)S(1)}, u32[]{:S(2)}, u32[]{:S(2)}) collective-permute-start(bf16[256,2304]{1,0:T(8,128)(2,1)} %collective-permute-done.13), channel_id=1, source_target_pairs={{2,0},{3,1},{10,8},{11,9},{18,16},{19,17},{26,24},{27,25}} | collective-permute-start | bytes 3538952 | tf_op jit(solution)/shard_map/ppermute | solution.py:546
  251.5 26.2 %collective-permute-start.18 = (bf16[256,2304]{1,0:T(8,128)(2,1)S(1)}, bf16[256,2304]{1,0:T(8,128)(2,1)S(1)}, u32[]{:S(2)}, u32[]{:S(2)}) collective-permute-start(bf16[256,2304]{1,0:T(8,128)(2,1)S(1)} %get-tuple-element.289), channel_id=1, source_target_pairs={{0,2},{2,4},{1,3},{3,5},{8,10},{10,12},{9,11},{11,13},{16,18},{18,... | collective-permute-start | bytes 3538952 | tf_op jit(solution)/shard_map/ppermute | solution.py:601
  253.2 24.5 %collective-permute-start.19 = (bf16[256,2304]{1,0:T(8,128)(2,1)S(1)}, bf16[256,2304]{1,0:T(8,128)(2,1)S(1)}, u32[]{:S(2)}, u32[]{:S(2)}) collective-permute-start(bf16[256,2304]{1,0:T(8,128)(2,1)S(1)} %get-tuple-element.288), channel_id=1, source_target_pairs={{4,2},{6,4},{5,3},{7,5},{12,10},{14,12},{13,11},{15,13},{20,18},{2... | collective-permute-start | bytes 3538952 | tf_op jit(solution)/shard_map/ppermute | solution.py:602
  279.8 30.3 %collective-permute-start.20 = (bf16[256,2304]{1,0:T(8,128)(2,1)}, bf16[256,2304]{1,0:T(8,128)(2,1)}, u32[]{:S(2)}, u32[]{:S(2)}) collective-permute-start(bf16[256,2304]{1,0:T(8,128)(2,1)} %get-tuple-element.287), channel_id=1, source_target_pairs={{0,2},{2,4},{4,6},{1,3},{3,5},{5,7},{8,10},{10,12},{12,14},{9,11},... | collective-permute-start | bytes 3538952 | tf_op jit(solution)/shard_map/ppermute | solution.py:601
  287.3 27.9 %collective-permute-start.21 = (bf16[256,2304]{1,0:T(8,128)(2,1)}, bf16[256,2304]{1,0:T(8,128)(2,1)}, u32[]{:S(2)}, u32[]{:S(2)}) collective-permute-start(bf16[256,2304]{1,0:T(8,128)(2,1)} %get-tuple-element.286), channel_id=1, source_target_pairs={{2,0},{4,2},{6,4},{3,1},{5,3},{7,5},{10,8},{12,10},{14,12},{11,9},... | collective-permute-start | bytes 3538952 | tf_op jit(solution)/shard_map/ppermute | solution.py:602
  320.5 23.9 %collective-permute-start.22 = (bf16[256,2304]{1,0:T(8,128)(2,1)S(1)}, bf16[256,2304]{1,0:T(8,128)(2,1)S(1)}, u32[]{:S(2)}, u32[]{:S(2)}) collective-permute-start(bf16[256,2304]{1,0:T(8,128)(2,1)S(1)} %multiply_convert_fusion.6), channel_id=1, source_target_pairs={{0,2},{2,4},{4,6},{1,3},{3,5},{5,7},{8,10},{10,12},{12,14},{9,11},... | collective-permute-start | bytes 3538952 | tf_op jit(solution)/shard_map/ppermute | solution.py:545
  322.0 26.7 %collective-permute-start.23 = (bf16[256,2304]{1,0:T(8,128)(2,1)S(1)}, bf16[256,2304]{1,0:T(8,128)(2,1)}, u32[]{:S(2)}, u32[]{:S(2)}) collective-permute-start(bf16[256,2304]{1,0:T(8,128)(2,1)S(1)} %multiply_convert_fusion.6), channel_id=1, source_target_pairs={{2,0},{4,2},{6,4},{3,1},{5,3},{7,5},{10,8},{12,10},{14,12},{11,9},... | collective-permute-start | bytes 3538952 | tf_op jit(solution)/shard_map/ppermute | solution.py:546
  348.7 28.3 %collective-permute-start.24 = (bf16[256,2304]{1,0:T(8,128)(2,1)S(1)}, bf16[256,2304]{1,0:T(8,128)(2,1)}, u32[]{:S(2)}, u32[]{:S(2)}) collective-permute-start(bf16[256,2304]{1,0:T(8,128)(2,1)S(1)} %collective-permute-done.22), channel_id=1, source_target_pairs={{2,4},{4,6},{3,5},{5,7},{10,12},{12,14},{11,13},{13,15},{18,20},{2... | collective-permute-start | bytes 3538952 | tf_op jit(solution)/shard_map/ppermute | solution.py:545
  350.4 26.6 %collective-permute-start.25 = (bf16[256,2304]{1,0:T(8,128)(2,1)}, bf16[256,2304]{1,0:T(8,128)(2,1)}, u32[]{:S(2)}, u32[]{:S(2)}) collective-permute-start(bf16[256,2304]{1,0:T(8,128)(2,1)} %collective-permute-done.23), channel_id=1, source_target_pairs={{2,0},{4,2},{3,1},{5,3},{10,8},{12,10},{11,9},{13,11},{18,16},{20,... | collective-permute-start | bytes 3538952 | tf_op jit(solution)/shard_map/ppermute | solution.py:546
  377.0 33.3 %collective-permute-start.26 = (bf16[256,2304]{1,0:T(8,128)(2,1)}, bf16[256,2304]{1,0:T(8,128)(2,1)}, u32[]{:S(2)}, u32[]{:S(2)}) collective-permute-start(bf16[256,2304]{1,0:T(8,128)(2,1)} %collective-permute-done.24), channel_id=1, source_target_pairs={{4,6},{5,7},{12,14},{13,15},{20,22},{21,23},{28,30},{29,31}} | collective-permute-start | bytes 3538952 | tf_op jit(solution)/shard_map/ppermute | solution.py:545
  378.9 31.4 %collective-permute-start.27 = (bf16[256,2304]{1,0:T(8,128)(2,1)}, bf16[256,2304]{1,0:T(8,128)(2,1)}, u32[]{:S(2)}, u32[]{:S(2)}) collective-permute-start(bf16[256,2304]{1,0:T(8,128)(2,1)} %collective-permute-done.25), channel_id=1, source_target_pairs={{2,0},{3,1},{10,8},{11,9},{18,16},{19,17},{26,24},{27,25}} | collective-permute-start | bytes 3538952 | tf_op jit(solution)/shard_map/ppermute | solution.py:546
  452.7 186.9 %reduce-scatter.7.cloned.1.call-start = ((), (), s32[]{:S(2)}) async-start(), calls=%async_computation.9 | async-start | bytes 15261696 | tf_op jit(solution)/shard_map/reduce_scatter | solution.py:680
  452.8 27.3 %collective-permute-start.28 = (bf16[256,2304]{1,0:T(8,128)(2,1)}, bf16[256,2304]{1,0:T(8,128)(2,1)S(1)}, u32[]{:S(2)}, u32[]{:S(2)}) collective-permute-start(bf16[256,2304]{1,0:T(8,128)(2,1)} %convolution_convert_fusion.9), channel_id=1, source_target_pairs={{0,2},{1,3},{8,10},{9,11},{16,18},{17,19},{24,26},{25,27}} | collective-permute-start | bytes 3538952 | tf_op jit(solution)/shard_map/ppermute | solution.py:601
  458.4 21.6 %collective-permute-start.29 = (bf16[256,2304]{1,0:T(8,128)(2,1)}, bf16[256,2304]{1,0:T(8,128)(2,1)S(1)}, u32[]{:S(2)}, u32[]{:S(2)}) collective-permute-start(bf16[256,2304]{1,0:T(8,128)(2,1)} %convolution_convert_fusion.9), channel_id=1, source_target_pairs={{6,4},{7,5},{14,12},{15,13},{22,20},{23,21},{30,28},{31,29}} | collective-permute-start | bytes 3538952 | tf_op jit(solution)/shard_map/ppermute | solution.py:602
  481.9 29.0 %collective-permute-start.30 = (bf16[256,2304]{1,0:T(8,128)(2,1)}, bf16[256,2304]{1,0:T(8,128)(2,1)}, u32[]{:S(2)}, u32[]{:S(2)}) collective-permute-start(bf16[256,2304]{1,0:T(8,128)(2,1)} %get-tuple-element.310), channel_id=1, source_target_pairs={{0,2},{2,4},{1,3},{3,5},{8,10},{10,12},{9,11},{11,13},{16,18},{18,... | collective-permute-start | bytes 3538952 | tf_op jit(solution)/shard_map/ppermute | solution.py:601
  487.2 23.7 %collective-permute-start.31 = (bf16[256,2304]{1,0:T(8,128)(2,1)}, bf16[256,2304]{1,0:T(8,128)(2,1)}, u32[]{:S(2)}, u32[]{:S(2)}) collective-permute-start(bf16[256,2304]{1,0:T(8,128)(2,1)} %get-tuple-element.309), channel_id=1, source_target_pairs={{4,2},{6,4},{5,3},{7,5},{12,10},{14,12},{13,11},{15,13},{20,18},{2... | collective-permute-start | bytes 3538952 | tf_op jit(solution)/shard_map/ppermute | solution.py:602
  521.1 233.6 %reduce-scatter.9.cloned.1.call-start = ((), (), s32[]{:S(2)}) async-start(), calls=%async_computation.10 | async-start | bytes 3317760 | tf_op jit(solution)/shard_map/reduce_scatter | solution.py:680
  524.4 28.4 %collective-permute-start.32 = (bf16[256,2304]{1,0:T(8,128)(2,1)S(1)}, bf16[256,2304]{1,0:T(8,128)(2,1)S(1)}, u32[]{:S(2)}, u32[]{:S(2)}) collective-permute-start(bf16[256,2304]{1,0:T(8,128)(2,1)S(1)} %get-tuple-element.295), channel_id=1, source_target_pairs={{0,2},{2,4},{4,6},{1,3},{3,5},{5,7},{8,10},{10,12},{12,14},{9,11},... | collective-permute-start | bytes 3538952 | tf_op jit(solution)/shard_map/ppermute | solution.py:601
  527.9 29.4 %collective-permute-start.33 = (bf16[256,2304]{1,0:T(8,128)(2,1)S(1)}, bf16[256,2304]{1,0:T(8,128)(2,1)S(1)}, u32[]{:S(2)}, u32[]{:S(2)}) collective-permute-start(bf16[256,2304]{1,0:T(8,128)(2,1)S(1)} %get-tuple-element.294), channel_id=1, source_target_pairs={{2,0},{4,2},{6,4},{3,1},{5,3},{7,5},{10,8},{12,10},{14,12},{11,9},... | collective-permute-start | bytes 3538952 | tf_op jit(solution)/shard_map/ppermute | solution.py:602
  560.9 27.2 %collective-permute-start.34 = (bf16[256,2304]{1,0:T(8,128)(2,1)S(1)}, bf16[256,2304]{1,0:T(8,128)(2,1)S(1)}, u32[]{:S(2)}, u32[]{:S(2)}) collective-permute-start(bf16[256,2304]{1,0:T(8,128)(2,1)S(1)} %get-tuple-element.263), channel_id=1, source_target_pairs={{0,2},{2,4},{4,6},{1,3},{3,5},{5,7},{8,10},{10,12},{12,14},{9,11},... | collective-permute-start | bytes 3538952 | tf_op jit(solution)/shard_map/ppermute | solution.py:545
  564.3 28.0 %collective-permute-start.35 = (bf16[256,2304]{1,0:T(8,128)(2,1)S(1)}, bf16[256,2304]{1,0:T(8,128)(2,1)S(1)}, u32[]{:S(2)}, u32[]{:S(2)}) collective-permute-start(bf16[256,2304]{1,0:T(8,128)(2,1)S(1)} %get-tuple-element.263), channel_id=1, source_target_pairs={{2,0},{4,2},{6,4},{3,1},{5,3},{7,5},{10,8},{12,10},{14,12},{11,9},... | collective-permute-start | bytes 3538952 | tf_op jit(solution)/shard_map/ppermute | solution.py:546
  594.0 28.5 %collective-permute-start.37 = (bf16[256,2304]{1,0:T(8,128)(2,1)S(1)}, bf16[256,2304]{1,0:T(8,128)(2,1)}, u32[]{:S(2)}, u32[]{:S(2)}) collective-permute-start(bf16[256,2304]{1,0:T(8,128)(2,1)S(1)} %collective-permute-done.35), channel_id=1, source_target_pairs={{2,0},{4,2},{3,1},{5,3},{10,8},{12,10},{11,9},{13,11},{18,16},{20,... | collective-permute-start | bytes 3538952 | tf_op jit(solution)/shard_map/ppermute | solution.py:546
  595.4 28.3 %collective-permute-start.38 = (bf16[256,2304]{1,0:T(8,128)(2,1)S(1)}, bf16[256,2304]{1,0:T(8,128)(2,1)S(1)}, u32[]{:S(2)}, u32[]{:S(2)}) collective-permute-start(bf16[256,2304]{1,0:T(8,128)(2,1)S(1)} %slice.119), channel_id=1, source_target_pairs={{0,2},{1,3},{8,10},{9,11},{16,18},{17,19},{24,26},{25,27}} | collective-permute-start | bytes 3538952 | tf_op jit(solution)/shard_map/ppermute | solution.py:601
  600.9 22.8 %collective-permute-start.39 = (bf16[256,2304]{1,0:T(8,128)(2,1)S(1)}, bf16[256,2304]{1,0:T(8,128)(2,1)S(1)}, u32[]{:S(2)}, u32[]{:S(2)}) collective-permute-start(bf16[256,2304]{1,0:T(8,128)(2,1)S(1)} %slice.119), channel_id=1, source_target_pairs={{6,4},{7,5},{14,12},{15,13},{22,20},{23,21},{30,28},{31,29}} | collective-permute-start | bytes 3538952 | tf_op jit(solution)/shard_map/ppermute | solution.py:602
  623.7 24.2 %collective-permute-start.40 = (bf16[256,2304]{1,0:T(8,128)(2,1)}, bf16[256,2304]{1,0:T(8,128)(2,1)}, u32[]{:S(2)}, u32[]{:S(2)}) collective-permute-start(bf16[256,2304]{1,0:T(8,128)(2,1)} %collective-permute-done.36), channel_id=1, source_target_pairs={{4,6},{5,7},{12,14},{13,15},{20,22},{21,23},{28,30},{29,31}} | collective-permute-start | bytes 3538952 | tf_op jit(solution)/shard_map/ppermute | solution.py:545
  625.4 26.9 %collective-permute-start.41 = (bf16[256,2304]{1,0:T(8,128)(2,1)}, bf16[256,2304]{1,0:T(8,128)(2,1)}, u32[]{:S(2)}, u32[]{:S(2)}) collective-permute-start(bf16[256,2304]{1,0:T(8,128)(2,1)} %collective-permute-done.37), channel_id=1, source_target_pairs={{2,0},{3,1},{10,8},{11,9},{18,16},{19,17},{26,24},{27,25}} | collective-permute-start | bytes 3538952 | tf_op jit(solution)/shard_map/ppermute | solution.py:546
  628.6 27.8 %collective-permute-start.42 = (bf16[256,2304]{1,0:T(8,128)(2,1)}, bf16[256,2304]{1,0:T(8,128)(2,1)}, u32[]{:S(2)}, u32[]{:S(2)}) collective-permute-start(bf16[256,2304]{1,0:T(8,128)(2,1)} %get-tuple-element.285), channel_id=1, source_target_pairs={{0,2},{2,4},{1,3},{3,5},{8,10},{10,12},{9,11},{11,13},{16,18},{18,... | collective-permute-start | bytes 3538952 | tf_op jit(solution)/shard_map/ppermute | solution.py:601
  635.2 21.3 %collective-permute-start.43 = (bf16[256,2304]{1,0:T(8,128)(2,1)}, bf16[256,2304]{1,0:T(8,128)(2,1)}, u32[]{:S(2)}, u32[]{:S(2)}) collective-permute-start(bf16[256,2304]{1,0:T(8,128)(2,1)} %get-tuple-element.284), channel_id=1, source_target_pairs={{4,2},{6,4},{5,3},{7,5},{12,10},{14,12},{13,11},{15,13},{20,18},{2... | collective-permute-start | bytes 3538952 | tf_op jit(solution)/shard_map/ppermute | solution.py:602
  665.4 161.1 %reduce-scatter.11.cloned.1.call-start = ((), (), s32[]{:S(2)}) async-start(), calls=%async_computation.11 | async-start | bytes 9953280 | tf_op jit(solution)/shard_map/reduce_scatter | solution.py:680
  665.5 89.2 %collective-permute-start.44 = (bf16[288,4352]{1,0:T(8,128)(2,1)}, bf16[288,4352]{1,0:T(8,128)(2,1)}, u32[]{:S(2)}, u32[]{:S(2)}) collective-permute-start(bf16[288,4352]{1,0:T(8,128)(2,1)} %concatenate.60), channel_id=1, source_target_pairs={{0,2},{2,4},{4,6},{1,3},{3,5},{5,7},{8,10},{10,12},{12,14},{9,11},... | collective-permute-start | bytes 7520264 | tf_op jit(solution)/shard_map/ppermute | solution.py:545
  676.2 78.6 %collective-permute-start.45 = (bf16[288,4352]{1,0:T(8,128)(2,1)}, bf16[288,4352]{1,0:T(8,128)(2,1)}, u32[]{:S(2)}, u32[]{:S(2)}) collective-permute-start(bf16[288,4352]{1,0:T(8,128)(2,1)} %concatenate.60), channel_id=1, source_target_pairs={{2,0},{4,2},{6,4},{3,1},{5,3},{7,5},{10,8},{12,10},{14,12},{11,9},... | collective-permute-start | bytes 7520264 | tf_op jit(solution)/shard_map/ppermute | solution.py:546
  682.4 66.6 %collective-permute-start.46 = (bf16[256,2304]{1,0:T(8,128)(2,1)}, bf16[256,2304]{1,0:T(8,128)(2,1)}, u32[]{:S(2)}, u32[]{:S(2)}) collective-permute-start(bf16[256,2304]{1,0:T(8,128)(2,1)} %get-tuple-element.283), channel_id=1, source_target_pairs={{0,2},{2,4},{4,6},{1,3},{3,5},{5,7},{8,10},{10,12},{12,14},{9,11},... | collective-permute-start | bytes 3538952 | tf_op jit(solution)/shard_map/ppermute | solution.py:601
  688.0 66.7 %collective-permute-start.47 = (bf16[256,2304]{1,0:T(8,128)(2,1)}, bf16[256,2304]{1,0:T(8,128)(2,1)}, u32[]{:S(2)}, u32[]{:S(2)}) collective-permute-start(bf16[256,2304]{1,0:T(8,128)(2,1)} %get-tuple-element.282), channel_id=1, source_target_pairs={{2,0},{4,2},{6,4},{3,1},{5,3},{7,5},{10,8},{12,10},{14,12},{11,9},... | collective-permute-start | bytes 3538952 | tf_op jit(solution)/shard_map/ppermute | solution.py:602
  754.8 39.9 %collective-permute-start.48 = (bf16[288,4352]{1,0:T(8,128)(2,1)}, bf16[288,4352]{1,0:T(8,128)(2,1)S(1)}, u32[]{:S(2)}, u32[]{:S(2)}) collective-permute-start(bf16[288,4352]{1,0:T(8,128)(2,1)} %collective-permute-done.44), channel_id=1, source_target_pairs={{2,4},{4,6},{3,5},{5,7},{10,12},{12,14},{11,13},{13,15},{18,20},{2... | collective-permute-start | bytes 7520264 | tf_op jit(solution)/shard_map/ppermute | solution.py:545
  756.0 52.4 %collective-permute-start.49 = (bf16[288,4352]{1,0:T(8,128)(2,1)}, bf16[288,4352]{1,0:T(8,128)(2,1)}, u32[]{:S(2)}, u32[]{:S(2)}) collective-permute-start(bf16[288,4352]{1,0:T(8,128)(2,1)} %collective-permute-done.45), channel_id=1, source_target_pairs={{2,0},{4,2},{3,1},{5,3},{10,8},{12,10},{11,9},{13,11},{18,16},{20,... | collective-permute-start | bytes 7520264 | tf_op jit(solution)/shard_map/ppermute | solution.py:546
  771.5 23.2 %collective-permute-start.50 = (bf16[256,2304]{1,0:T(8,128)(2,1)S(1)}, bf16[256,2304]{1,0:T(8,128)(2,1)S(1)}, u32[]{:S(2)}, u32[]{:S(2)}) collective-permute-start(bf16[256,2304]{1,0:T(8,128)(2,1)S(1)} %slice.147), channel_id=1, source_target_pairs={{0,2},{1,3},{8,10},{9,11},{16,18},{17,19},{24,26},{25,27}} | collective-permute-start | bytes 3538952 | tf_op jit(solution)/shard_map/ppermute | solution.py:601
  808.4 29.8 %collective-permute-start.52 = (bf16[288,4352]{1,0:T(8,128)(2,1)S(1)}, bf16[288,4352]{1,0:T(8,128)(2,1)}, u32[]{:S(2)}, u32[]{:S(2)}) collective-permute-start(bf16[288,4352]{1,0:T(8,128)(2,1)S(1)} %collective-permute-done.48), channel_id=1, source_target_pairs={{4,6},{5,7},{12,14},{13,15},{20,22},{21,23},{28,30},{29,31}} | collective-permute-start | bytes 7520264 | tf_op jit(solution)/shard_map/ppermute | solution.py:545
  810.6 51.6 %collective-permute-start.53 = (bf16[288,4352]{1,0:T(8,128)(2,1)}, bf16[288,4352]{1,0:T(8,128)(2,1)}, u32[]{:S(2)}, u32[]{:S(2)}) collective-permute-start(bf16[288,4352]{1,0:T(8,128)(2,1)} %collective-permute-done.49), channel_id=1, source_target_pairs={{2,0},{3,1},{10,8},{11,9},{18,16},{19,17},{26,24},{27,25}} | collective-permute-start | bytes 7520264 | tf_op jit(solution)/shard_map/ppermute | solution.py:546
  813.8 24.5 %collective-permute-start.54 = (bf16[256,2304]{1,0:T(8,128)(2,1)}, bf16[256,2304]{1,0:T(8,128)(2,1)}, u32[]{:S(2)}, u32[]{:S(2)}) collective-permute-start(bf16[256,2304]{1,0:T(8,128)(2,1)} %get-tuple-element.281), channel_id=1, source_target_pairs={{0,2},{2,4},{1,3},{3,5},{8,10},{10,12},{9,11},{11,13},{16,18},{18,... | collective-permute-start | bytes 3538952 | tf_op jit(solution)/shard_map/ppermute | solution.py:601
  871.9 21.4 %collective-permute-start.60 = (bf16[2,288,4352]{2,1,0:T(8,128)(2,1)}, bf16[2,288,4352]{2,1,0:T(8,128)(2,1)}, u32[]{:S(2)}, u32[]{:S(2)}) collective-permute-start(bf16[2,288,4352]{2,1,0:T(8,128)(2,1)} %pad_maximum_fusion.1), channel_id=1, source_target_pairs={{0,1},{1,0},{2,3},{3,2},{4,5},{5,4},{6,7},{7,6},{8,9},{9,8},{10,11... | collective-permute-start | bytes 15040520 | tf_op jit(solution)/shard_map/ppermute | solution.py:694
  871.9 64.9 %collective-permute-start.58 = (bf16[288,2560]{1,0:T(8,128)(2,1)}, bf16[288,2560]{1,0:T(8,128)(2,1)}, u32[]{:S(2)}, u32[]{:S(2)}) collective-permute-start(bf16[288,2560]{1,0:T(8,128)(2,1)} %concatenate.62), channel_id=1, source_target_pairs={{0,2},{2,4},{4,6},{1,3},{3,5},{5,7},{8,10},{10,12},{12,14},{9,11},... | collective-permute-start | bytes 4423688 | tf_op jit(solution)/shard_map/ppermute | solution.py:545
  874.9 61.9 %collective-permute-start.59 = (bf16[288,2560]{1,0:T(8,128)(2,1)}, bf16[288,2560]{1,0:T(8,128)(2,1)}, u32[]{:S(2)}, u32[]{:S(2)}) collective-permute-start(bf16[288,2560]{1,0:T(8,128)(2,1)} %concatenate.62), channel_id=1, source_target_pairs={{2,0},{4,2},{6,4},{3,1},{5,3},{7,5},{10,8},{12,10},{14,12},{11,9},... | collective-permute-start | bytes 4423688 | tf_op jit(solution)/shard_map/ppermute | solution.py:546
  880.6 50.9 %collective-permute-start.56 = (bf16[256,2304]{1,0:T(8,128)(2,1)}, bf16[256,2304]{1,0:T(8,128)(2,1)}, u32[]{:S(2)}, u32[]{:S(2)}) collective-permute-start(bf16[256,2304]{1,0:T(8,128)(2,1)} %get-tuple-element.279), channel_id=1, source_target_pairs={{0,2},{2,4},{4,6},{1,3},{3,5},{5,7},{8,10},{10,12},{12,14},{9,11},... | collective-permute-start | bytes 3538952 | tf_op jit(solution)/shard_map/ppermute | solution.py:601
  886.2 50.5 %collective-permute-start.57 = (bf16[256,2304]{1,0:T(8,128)(2,1)}, bf16[256,2304]{1,0:T(8,128)(2,1)}, u32[]{:S(2)}, u32[]{:S(2)}) collective-permute-start(bf16[256,2304]{1,0:T(8,128)(2,1)} %get-tuple-element.278), channel_id=1, source_target_pairs={{2,0},{4,2},{6,4},{3,1},{5,3},{7,5},{10,8},{12,10},{14,12},{11,9},... | collective-permute-start | bytes 3538952 | tf_op jit(solution)/shard_map/ppermute | solution.py:602
  893.3 80.0 %collective-permute-start.65 = (bf16[256,2304]{1,0:T(8,128)(2,1)}, bf16[256,2304]{1,0:T(8,128)(2,1)}, u32[]{:S(2)}, u32[]{:S(2)}) collective-permute-start(bf16[256,2304]{1,0:T(8,128)(2,1)} %multiply_convert_fusion.4), channel_id=1, source_target_pairs={{0,1},{1,0},{2,3},{3,2},{4,5},{5,4},{6,7},{7,6},{8,9},{9,8},{10,11... | collective-permute-start | bytes 3538952 | tf_op jit(solution)/shard_map/ppermute | solution.py:896
  937.7 35.7 %collective-permute-start.62 = (bf16[288,2560]{1,0:T(8,128)(2,1)}, bf16[288,2560]{1,0:T(8,128)(2,1)S(1)}, u32[]{:S(2)}, u32[]{:S(2)}) collective-permute-start(bf16[288,2560]{1,0:T(8,128)(2,1)} %collective-permute-done.59), channel_id=1, source_target_pairs={{2,0},{4,2},{3,1},{5,3},{10,8},{12,10},{11,9},{13,11},{18,16},{20,... | collective-permute-start | bytes 4423688 | tf_op jit(solution)/shard_map/ppermute | solution.py:546
  975.9 36.6 %collective-permute-start.64 = (bf16[288,2560]{1,0:T(8,128)(2,1)S(1)}, bf16[288,2560]{1,0:T(8,128)(2,1)S(1)}, u32[]{:S(2)}, u32[]{:S(2)}) collective-permute-start(bf16[288,2560]{1,0:T(8,128)(2,1)S(1)} %collective-permute-done.62), channel_id=1, source_target_pairs={{2,0},{3,1},{10,8},{11,9},{18,16},{19,17},{26,24},{27,25}} | collective-permute-start | bytes 4423688 | tf_op jit(solution)/shard_map/ppermute | solution.py:546
  (95 other events, 1719.5 us)
Sparse Core Ops, SparseCore 0:
  18.9 59.9 all-gather.5
  87.5 29.5 all-gather.7
  122.4 46.9 all-gather.9
  171.7 76.1 all-gather.11
  452.8 68.2 reduce-scatter.4
  524.5 97.1 reduce-scatter.6
  665.6 49.0 reduce-scatter.8
  754.9 71.5 reduce-scatter.10

commit v6 on v5

--- a/solution.py
+++ b/solution.py
@@ -735,8 +735,8 @@
     tokens_line.step()
     qkv_mine = to_pair(column_piece([w_query, w_key, w_value], lambda v: widen(v, 1)))
     qkv_w = gather_pair(qkv_mine)
-    w_out, w_gate, w_up, w_down, gain_pair = stage(
-        [tokens_line], w_out, w_gate, w_up, w_down, jnp.stack([attn_gain, mlp_gain])
+    w_out, w_down, gain_pair = stage(
+        [tokens_line], w_out, w_down, jnp.stack([attn_gain, mlp_gain])
     )
     tokens_line.step()
     gains = lax.all_gather(gain_pair, "shard", axis=1, tiled=True)
@@ -744,13 +744,13 @@
     gain_b = gains[1].astype(jnp.float32)
     out_mine = to_pair(widen(turned_piece(w_out), 1))
     down_mine = to_pair(turned_piece(w_down))
-    gate_up_mine = to_pair(column_piece([w_gate, w_up]))
-    gain_a, gain_b, out_mine, own_cot, cos_all, sin_all, order = stage(
-        [tokens_line], gain_a, gain_b, out_mine, own_cot, cos_all, sin_all, order
+    gain_a, gain_b, out_mine, own_cot, cos_all, sin_all, order, w_gate, w_up = stage(
+        [tokens_line], gain_a, gain_b, out_mine, own_cot, cos_all, sin_all, order, w_gate, w_up
     )
     tokens_line.step()
     out_w = gather_pair(out_mine)
-    own_cot, down_mine = stage([tokens_line], own_cot, down_mine)
+    gate_up_mine = to_pair(column_piece([w_gate, w_up]))
+    own_cot, down_mine, gate_up_mine = stage([tokens_line], own_cot, down_mine, gate_up_mine)
     down_w = gather_pair(down_mine)
 
     cot_line = walk(own_cot)
@@ -776,9 +776,8 @@
     (grad_mlp,) = stage([attn_line], grad_mlp)
     attn_line.step()
     half_rows = all_rows // 2
-    cut_rows = [0, half_rows, half_rows + row_count, all_rows]
     grad_hidden = [
-        plain_product(grad_mlp[low:high], down_w) for low, high in zip(cut_rows, cut_rows[1:])
+        plain_product(grad_mlp[k * half_rows : (k + 1) * half_rows], down_w) for k in range(2)
     ]
     grad_hidden = stage([attn_line], *grad_hidden)
     own_x = own_tokens.astype(jnp.float32)
@@ -806,32 +805,27 @@
     second_line.step()
     hidden_near, grad_near = units(near_half, grad_hidden[0])
     hidden_near, grad_near = stage([second_line], hidden_near, grad_near)
-    middle_block = second_line.near(lines // 2)
     second_line.step()
-    hidden_mid, grad_mid = units(middle_block, grad_hidden[1])
     part_near = col_product(grad_near, gate_up_w).astype(jnp.bfloat16)
-    part_near, hidden_mid, grad_mid = stage([second_line], part_near, hidden_mid, grad_mid)
-    last_block = second_line.near(lines - 1)
-    hidden_last, grad_last = units(last_block, grad_hidden[2])
-    part_last = col_product(grad_last, gate_up_w).astype(jnp.bfloat16)
-    part_last, hidden_last, grad_mid = lax.optimization_barrier((part_last, hidden_last, grad_mid))
-
-    parts = blocks_of(part_near) + [None, part_last]
-    grad_line = add_up(parts)
+    (part_near,) = stage([second_line], part_near)
+    far_half = jnp.concatenate([second_line.near(k) for k in range(lines // 2, lines)], axis=0)
+    hidden_far, grad_far = units(far_half, grad_hidden[1])
+    part_far = col_product(grad_far, gate_up_w).astype(jnp.bfloat16)
+    hidden_far, grad_far, part_far = lax.optimization_barrier((hidden_far, grad_far, part_far))
+
+    grad_line = add_up(blocks_of(part_near) + blocks_of(part_far))
     grad_line.step()
-    parts[lines // 2] = col_product(grad_mid, gate_up_w).astype(jnp.bfloat16)
-    hidden = jnp.concatenate([hidden_near, hidden_mid, hidden_last], axis=0)
+    second_in = jnp.concatenate([near_half, far_half], axis=0)
+    grad_gate_up = jnp.concatenate([grad_near, grad_far], axis=0)
+    gate_up_grad = row_product(second_in, grad_gate_up).astype(jnp.bfloat16)
+    hidden = jnp.concatenate([hidden_near, hidden_far], axis=0)
+    gate_up_grad, hidden = stage([grad_line], gate_up_grad, hidden)
+    grad_line.step()
+    gate_up_piece = reduce_pair(gate_up_grad)
     down_grad = row_product(grad_mlp, hidden).astype(jnp.bfloat16)
-    down_grad, grad_mid = lax.optimization_barrier((down_grad, grad_mid))
+    down_grad, hidden = stage([grad_line], down_grad, hidden)
+    grad_line.step()
     down_piece = reduce_pair(down_grad)
-    second_in = jnp.concatenate([near_half, middle_block, last_block], axis=0)
-    grad_gate_up = jnp.concatenate([grad_near, grad_mid, grad_last], axis=0)
-    parts[lines // 2], hidden = stage([grad_line], parts[lines // 2], hidden)
-    grad_line.step()
-    gate_up_grad = row_product(second_in, grad_gate_up).astype(jnp.bfloat16)
-    gate_up_grad, down_piece = stage([grad_line], gate_up_grad, down_piece)
-    gate_up_piece = reduce_pair(gate_up_grad)
-    grad_line.step()
     mlp_part = col_product(hidden, down_w).astype(jnp.bfloat16)
     (mlp_part,) = stage([grad_line], mlp_part)
     grad_second = grad_line.total()
@@ -848,8 +842,8 @@
     attn_grad_line.step()
     mlp_line.step()
     unit_marks = gain_marks(gate_up_mine, gate_up_piece)
-    rest = jnp.zeros((unit_marks.shape[0], -(3 * unit_cols + 2) % LANES), jnp.bfloat16)
-    unit_block = jnp.concatenate([gate_up_piece, down_piece, unit_marks, rest], axis=1)
+    rest = jnp.zeros((unit_marks.shape[0], -(2 * unit_cols + 2) % LANES), jnp.bfloat16)
+    unit_block = jnp.concatenate([gate_up_piece, unit_marks, rest], axis=1)
     (unit_block,) = stage([attn_grad_line, mlp_line], unit_block)
     mlp_line.step()
     unit_line = walk(unit_block)
@@ -862,34 +856,42 @@
     )
     qkv_grad = row_product(first_in, grad_qkv).astype(jnp.bfloat16)
     out_piece = reduce_pair(out_grad)
-    grad_qkv, qkv_grad, out_piece = stage([unit_line, mlp_line], grad_qkv, qkv_grad, out_piece)
+    grad_qkv, qkv_grad, out_piece, down_piece = stage(
+        [unit_line, mlp_line], grad_qkv, qkv_grad, out_piece, down_piece
+    )
     unit_line.step()
+    down_line = walk(down_piece)
+    down_line.step()
     qkv_piece = reduce_pair(qkv_grad)
     first_part = col_product(grad_qkv, qkv_w).astype(jnp.bfloat16)
 
     first_line = add_up(blocks_of(first_part))
     first_line.step()
     layer_rows = ((middle + BRANCH_SCALE * mlp_line.total()) * live_own).astype(jnp.bfloat16)
-    (layer_rows,) = stage([unit_line, first_line], layer_rows)
+    (layer_rows,) = stage([unit_line, first_line, down_line], layer_rows)
     unit_line.step()
     first_line.step()
+    down_line.step()
     qkv_marks = gain_marks(qkv_mine, qkv_piece)
     head_block = jnp.concatenate(
         [qkv_piece[:, :head_cols], qkv_marks, qkv_piece[:, head_cols + 2 :], out_piece], axis=1
     )
-    (head_block,) = stage([unit_line, first_line], head_block)
+    (head_block,) = stage([unit_line, first_line, down_line], head_block)
     head_line = walk(head_block)
     head_line.step()
     first_line.step()
+    down_line.step()
     own, other, give = line_pieces(unit_line)
-    final_gate, final_up, final_down = join_columns(core_index, own, other, 3, unit_cols, unit_cols)
-    final_gain_two = gain_total((own, give), 3 * unit_cols, mlp_gain)
-    final_gate, final_up, final_down = stage([first_line, head_line], final_gate, final_up, final_down)
+    final_gate, final_up = join_columns(core_index, own, other, 2, unit_cols, unit_cols)
+    final_gain_two = gain_total((own, give), 2 * unit_cols, mlp_gain)
+    final_gate, final_up = stage([first_line, head_line, down_line], final_gate, final_up)
     head_line.step()
+    own, other, _ = line_pieces(down_line)
+    (final_down,) = join_columns(core_index, own, other, 1, unit_cols, unit_cols)
     grad_first = first_line.total()
     normed_one, inverse_one = norm_parts(own_x)
     grad_rows = grad_middle + norm_back(grad_first, normed_one, inverse_one, gain_a)
-    (grad_rows,) = stage([head_line], grad_rows)
+    grad_rows, final_down = stage([head_line], grad_rows, final_down)
     head_line.step()
 
     def both_slots(own):

time: 1050 us -> 1030 us (0.981)
  waiting for transfers between devices: 411 us -> 381 us
  starting transfers between devices: 149 us -> 171 us
  matrix products: 202 us -> 189 us
    ppermute x18 -> x21, waiting for transfers between devices: 189 us -> 253 us  [step(): self.downs.append(lax.ppermute(self.downs[-1], self.axis, down_pairs))]
    ppermute x12, waiting for transfers between devices: 113 us -> 52.1 us  [step(): self.up = lax.ppermute(up, self.axis, [(i, i + 1) for i, _ in ups])]
    ppermute x18 -> x21, starting transfers between devices: 44.7 us -> 59.4 us  [step(): self.ups.append(lax.ppermute(self.ups[-1], self.axis, up_pairs))]
    reduce_scatter x4, waiting for transfers between devices: 14.2 us -> 0.04 us  [reduce_pair(): lax.psum_scatter(grad, ('shard', 'tensor'), scatter_dimension=0, tiled=True)]
    dot_general x6 -> x5, matrix products: 67.1 us -> 59 us  [col_product(): lax.dot_general(left_mat, right_mat, CONTRACT_COLS, preferred_element_typ...]
    ppermute x18 -> x21, waiting for transfers between devices: 66.2 us -> 59.2 us  [step(): self.ups.append(lax.ppermute(self.ups[-1], self.axis, up_pairs))]
    dot_general x8 -> x6, matrix products: 81.2 us -> 75.6 us  [plain_product(): return jnp.dot(left_mat, right_mat, preferred_element_type=jnp.float32)]
    ppermute x18 -> x21, starting transfers between devices: 24.4 us -> 28.1 us  [step(): self.downs.append(lax.ppermute(self.downs[-1], self.axis, down_pairs))]
  transfers between devices with their start and end apart: 78 -> 85, of which waited for: 38 -> 30; matrix products, arithmetic and copies ran while one was open for 28% -> 29% of each run, Pallas kernels for 7% -> 7%
where the time goes in v6:
time: 1030 us; the launch traced here: 1020 us
  waiting for transfers between devices  381 us (37%)
  matrix products  189 us (18%)
  starting transfers between devices  171 us (17%)
  other arithmetic  128 us (12%)
  Pallas kernels  75.3 us (7%)
  local copies, waits for them, and re-layouts  53 us (5%)
  between operations  16.4 us (2%)
    ppermute x21, waiting for transfers between devices, step(): self.downs.append(lax.ppermute(self.downs[-1], self.axis, down_pairs))  253 us
    dot_general x6, matrix products, plain_product(): return jnp.dot(left_mat, right_mat, preferred_element_type=jnp.float32)  75.6 us
    ppermute x12, starting transfers between devices, step(): self.up = lax.ppermute(up, self.axis, [(i, i + 1) for i, _ in ups])  65.2 us
    ppermute x21, starting transfers between devices, step(): self.ups.append(lax.ppermute(self.ups[-1], self.axis, up_pairs))  59.4 us
    ppermute x21, waiting for transfers between devices, step(): self.ups.append(lax.ppermute(self.ups[-1], self.axis, up_pairs))  59.2 us
    dot_general x5, matrix products, col_product(): lax.dot_general(left_mat, right_mat, CONTRACT_COLS, preferred_element_typ...  59 us
    dot_general x4, matrix products, row_product(): lax.dot_general(left_mat, right_mat, CONTRACT_ROWS, preferred_element_typ...  54.1 us
    ppermute x12, waiting for transfers between devices, step(): self.up = lax.ppermute(up, self.axis, [(i, i + 1) for i, _ in ups])  52.1 us
  transfers between devices with their start and end apart: 85, of which 30 were waited for; matrix products, arithmetic and copies ran while one was open for 29% of the time, Pallas kernels for 7%

profile of v6, /device:TPU:0, one launch (start us, length us, event | category | flops | bytes accessed | tf_op | source)
XLA Modules:
  0.0 1022.2 jit_solution(10957879941933934390)
XLA Ops:
  18.9 5.7 collective-permute-start
  28.2 21.3 %collective-permute-done = bf16[256,2304]{1,0:T(8,128)(2,1)} collective-permute-done((bf16[256,2304]{1,0:T(8,128)(2,1)S(1)}, bf16[256,2304]{1,0:T(8,128)(2,1)}, u32[]{:S(2)}, u32[]{:S(2)}) %collective-permute-start) | collective-permute-done | bytes 1179680 | tf_op jit(solution)/shard_map/ppermute | solution.py:545
  49.4 5.8 collective-permute-done.1
  63.7 8.6 all-gather
  74.3 12.9 %collective-permute-done.3 = bf16[256,2304]{1,0:T(8,128)(2,1)} collective-permute-done((bf16[256,2304]{1,0:T(8,128)(2,1)}, bf16[256,2304]{1,0:T(8,128)(2,1)}, u32[]{:S(2)}, u32[]{:S(2)}) %collective-permute-start.3) | collective-permute-done | bytes 1179680 | tf_op jit(solution)/shard_map/ppermute | solution.py:546
  106.1 22.8 %collective-permute-done.6 = bf16[256,2304]{1,0:T(8,128)(2,1)} collective-permute-done((bf16[256,2304]{1,0:T(8,128)(2,1)}, bf16[256,2304]{1,0:T(8,128)(2,1)}, u32[]{:S(2)}, u32[]{:S(2)}) %collective-permute-start.6) | collective-permute-done | bytes 1179680 | tf_op jit(solution)/shard_map/ppermute | solution.py:546
  132.0 5.8 collective-permute-start.9
  141.6 17.9 %fusion.56.q_in.k_in.v_in = f32[1024,1920]{1,0:T(8,128)} fusion(bf16[2304,1920]{1,0:T(8,128)(2,1)} %all-gather.6.cloned.1.call-done, f32[2304]{0:T(1024)S(1)} %get-tuple-element.152, f32[1024]{0:T(1024)S(1)} %add_rsqrt_fusion, bf16[256,2304]{1,0:T(8,128)(2,1)} %copy-done.44, bf16[256,2304]{1,0:T(8,128)(2,1)} %copy-done.40, ...), kind=kOutput, calls=%fused_computation.151 | convolution fusion | flops 9085648896 | bytes 21443584 | tf_op jit(solution)/shard_map/dot_general | solution.py:30
  167.8 29.6 %attend.1 = (bf16[1024,640]{1,0:T(8,128)(2,1)S(1)}, bf16[1024,640]{1,0:T(8,128)(2,1)S(1)}, bf16[1024,640]{1,0:T(8,128)(2,1)S(1)}, bf16[1024,640]{1,0:T(8,128)(2,1)S(1)}, f32[5,8,1024]{2,1,0:T(8,128)S(1)}) custom-call(s32[8]{0:T(128)S(1)} %and_select_fusion.order, s32[1]{0:T(128)} %dynamic_slice.64.length, f32[1024,1920]{1,0:T(8,128)S(1)} %copy-done.2, ...), custom_call_target="tpu_custom_call" | custom-call | flops 2415919104 | bytes 15728640 | tf_op jit(solution)/shard_map/attend/pallas_call | solution.py:451
  200.6 6.4 convolution_convert_fusion.4
  207.2 7.0 collective-permute-start.14
  219.4 17.7 %collective-permute-done.14 = bf16[256,2304]{1,0:T(8,128)(2,1)S(1)} collective-permute-done((bf16[256,2304]{1,0:T(8,128)(2,1)S(1)}, bf16[256,2304]{1,0:T(8,128)(2,1)S(1)}, u32[]{:S(2)}, u32[]{:S(2)}) %collective-permute-start.14) | collective-permute-done | bytes 1179680 | tf_op jit(solution)/shard_map/ppermute | solution.py:601
  237.1 6.3 collective-permute-done.17
  248.4 9.1 multiply_convert_fusion
  257.5 10.4 %collective-permute-done.18 = bf16[256,2304]{1,0:T(8,128)(2,1)S(1)} collective-permute-done((bf16[256,2304]{1,0:T(8,128)(2,1)S(1)}, bf16[256,2304]{1,0:T(8,128)(2,1)S(1)}, u32[]{:S(2)}, u32[]{:S(2)}) %collective-permute-start.18) | collective-permute-done | bytes 1179680 | tf_op jit(solution)/shard_map/ppermute | solution.py:601
  270.0 8.7 collective-permute-start.20
  280.2 9.1 fusion.42
  289.4 7.1 fusion.44
  298.8 5.1 collective-permute-done.21
  312.0 18.4 %collective-permute-done.22 = bf16[256,2304]{1,0:T(8,128)(2,1)S(1)} collective-permute-done((bf16[256,2304]{1,0:T(8,128)(2,1)S(1)}, bf16[256,2304]{1,0:T(8,128)(2,1)S(1)}, u32[]{:S(2)}, u32[]{:S(2)}) %collective-permute-start.22) | collective-permute-done | bytes 1179680 | tf_op jit(solution)/shard_map/ppermute | solution.py:545
  330.3 4.3 collective-permute-done.23
  340.3 17.9 %fusion.34 = f32[512,2880]{0,1:T(8,128)} fusion(bf16[2304,2880]{1,0:T(8,128)(2,1)} %all-gather.12.cloned.1.call-done, bf16[256,2304]{1,0:T(8,128)(2,1)} %fusion.49, bf16[256,2304]{1,0:T(8,128)(2,1)} %copy-done.55), kind=kOutput, calls=%fused_computation.92 | convolution fusion | flops 6799491072 | bytes 21528576 | tf_op jit(solution)/shard_map/dot_general | solution.py:30
  358.2 5.4 multiply_convert_fusion.5
  366.3 12.5 %convolution_convert_fusion.8 = bf16[512,2304]{1,0:T(8,128)(2,1)} fusion(bf16[512,2880]{0,1:T(8,128)(2,1)S(1)} %pad_maximum_fusion.6, bf16[2304,2880]{1,0:T(8,128)(2,1)} %all-gather.12.cloned.1.call-done), kind=kOutput, calls=%fused_computation.29 | convolution fusion | flops 6795952128 | bytes 18579456 | tf_op jit(solution)/shard_map/dot_general | solution.py:26
  381.5 6.5 collective-permute-done.27
  389.5 17.9 %fusion.38 = f32[512,2880]{0,1:T(8,128)} fusion(bf16[2304,2880]{1,0:T(8,128)(2,1)} %all-gather.12.cloned.1.call-done, bf16[256,2304]{1,0:T(8,128)(2,1)} %select_select_fusion.9, bf16[256,2304]{1,0:T(8,128)(2,1)} %select_select_fusion.2), kind=kOutput, calls=%fused_computation.96 | convolution fusion | flops 6799491072 | bytes 21528576 | tf_op jit(solution)/shard_map/dot_general | solution.py:30
  407.4 5.4 multiply_convert_fusion.2
  415.7 13.3 %convolution_convert_fusion.7 = bf16[512,2304]{1,0:T(8,128)(2,1)} fusion(bf16[2304,2880]{1,0:T(8,128)(2,1)} %all-gather.12.cloned.1.call-done, bf16[512,1440]{0,1:T(8,128)(2,1)} %copy-done.38, bf16[512,1440]{0,1:T(8,128)(2,1)S(1)} %get-tuple-element.279), kind=kOutput, calls=%fused_computation.28 | convolution fusion | flops 6801850368 | bytes 18579456 | tf_op jit(solution)/shard_map/dot_general | solution.py:26
  431.5 3.8 collective-permute-start.28
  437.0 20.4 %convolution_convert_fusion = bf16[2304,2880]{1,0:T(8,128)(2,1)} fusion(bf16[512,2880]{0,1:T(8,128)(2,1)} %pad_maximum_fusion.7, bf16[512,2880]{0,1:T(8,128)(2,1)} %copy-done.51, bf16[256,2304]{1,0:T(8,128)(2,1)S(1)} %copy-done.57, bf16[256,2304]{1,0:T(8,128)(2,1)} %select_select_fusion.2, bf16[256,2304]{1,0:T(8,128)(2,1)} %fusion.49, ...), kind=kOutput, calls=%fused_computation.1 | convolution fusion | flops 13626851328 | bytes 23887872 | tf_op jit(solution)/shard_map/dot_general | solution.py:22
  468.9 13.7 %convolution_convert_fusion.2 = bf16[2304,1440]{1,0:T(8,128)(2,1)} fusion(bf16[1024,2304]{1,0:T(8,128)(2,1)} %multiply_convert_fusion, bf16[1024,1440]{0,1:T(8,128)(2,1)S(1)} %copy-done.50), kind=kOutput, calls=%fused_computation.5 | convolution fusion | flops 6798090240 | bytes 14303232 | tf_op jit(solution)/shard_map/dot_general | solution.py:22
  484.6 4.4 add_convert_fusion.4
  489.0 6.7 collective-permute-start.32
  497.1 11.9 %convolution_convert_fusion.5 = bf16[1024,2304]{1,0:T(8,128)(2,1)S(1)} fusion(bf16[1024,1440]{0,1:T(8,128)(2,1)} %pad_maximum_fusion.8, bf16[2304,1440]{1,0:T(8,128)(2,1)} %all-gather.10.cloned.1.call-done), kind=kOutput, calls=%fused_computation.17 | convolution fusion | flops 6797131776 | bytes 14303232 | tf_op jit(solution)/shard_map/dot_general | solution.py:26
  509.0 4.0 collective-permute-done.32
  513.0 5.1 collective-permute-done.33
  520.6 4.3 multiply_convert_fusion.8
  528.7 18.4 %collective-permute-done.34 = bf16[256,2304]{1,0:T(8,128)(2,1)S(1)} collective-permute-done((bf16[256,2304]{1,0:T(8,128)(2,1)S(1)}, bf16[256,2304]{1,0:T(8,128)(2,1)S(1)}, u32[]{:S(2)}, u32[]{:S(2)}) %collective-permute-start.34) | collective-permute-done | bytes 1179680 | tf_op jit(solution)/shard_map/ppermute | solution.py:545
  555.4 15.7 %collective-permute-done.38 = bf16[256,2304]{1,0:T(8,128)(2,1)S(1)} collective-permute-done((bf16[256,2304]{1,0:T(8,128)(2,1)S(1)}, bf16[256,2304]{1,0:T(8,128)(2,1)S(1)}, u32[]{:S(2)}, u32[]{:S(2)}) %collective-permute-start.38) | collective-permute-done | bytes 1179680 | tf_op jit(solution)/shard_map/ppermute | solution.py:601
  576.3 7.1 collective-permute-start.42
  597.8 7.4 collective-permute-done.41
  608.8 5.3 convolution_convert_fusion.6
  618.3 4.4 add_convert_fusion.2
  622.7 5.6 collective-permute-start.46
  629.9 5.7 convolution_convert_fusion.9.do_in
  635.7 29.9 %attend_back.1 = bf16[1024,1920]{1,0:T(8,128)(2,1)} custom-call(s32[8]{0:T(128)S(1)} %and_select_fusion.order, s32[1]{0:T(128)} %dynamic_slice.64.length, bf16[1024,640]{1,0:T(8,128)(2,1)S(1)} %copy-done.6, bf16[1024,640]{1,0:T(8,128)(2,1)S(1)} %copy-done.8, bf16[1024,640]{1,0:T(8,128)(2,1)S(1)} %copy-done.10, f32[5,8,1024]{2,1,0:T(8,128)S(1)} %get-tuple-element.217.log_in, ...), custom_call_target="tpu_custom_call" | custom-call | flops 6039797760 | bytes 10485760 | tf_op jit(solution)/shard_map/attend_back/pallas_call | solution.py:478
  665.6 14.7 %convolution_convert_fusion.1 = bf16[2304,1920]{1,0:T(8,128)(2,1)} fusion(bf16[1024,1920]{1,0:T(8,128)(2,1)} %attend_back.1, f32[2304]{0:T(1024)S(1)} %copy-done.68, f32[1024]{0:T(1024)S(1)} %copy-done.75, bf16[256,2304]{1,0:T(8,128)(2,1)S(1)} %copy-done.45, bf16[256,2304]{1,0:T(8,128)(2,1)S(1)} %copy-done.41, bf16[256,2304]{1,0:T(8,128)(2,1)S(1)} %copy-done.43, ...), kind=kOutput, calls=%fused_computation.4 | convolution fusion | flops 9090072576 | bytes 17511424 | tf_op jit(solution)/shard_map/dot_general | solution.py:22
  682.5 6.1 collective-permute-start.52
  688.6 14.9 %convolution_convert_fusion.3 = bf16[1024,2304]{1,0:T(8,128)(2,1)S(1)} fusion(bf16[1024,1920]{1,0:T(8,128)(2,1)} %attend_back.1, bf16[2304,1920]{1,0:T(8,128)(2,1)} %all-gather.6.cloned.1.call-done), kind=kOutput, calls=%fused_computation.15 | convolution fusion | flops 9062055936 | bytes 17498112 | tf_op jit(solution)/shard_map/dot_general | solution.py:26
  703.6 5.3 collective-permute-start.50
  714.7 40.1 %collective-permute-done.53 = bf16[288,1440]{1,0:T(8,128)(2,1)} collective-permute-done((bf16[288,1440]{1,0:T(8,128)(2,1)}, bf16[288,1440]{1,0:T(8,128)(2,1)}, u32[]{:S(2)}, u32[]{:S(2)}) %collective-permute-start.53) | collective-permute-done | bytes 829472 | tf_op jit(solution)/shard_map/ppermute | solution.py:546
  760.7 9.7 collective-permute-start.56
  782.7 4.1 concatenate.62
  786.8 25.7 %collective-permute-done.59 = bf16[288,1440]{1,0:T(8,128)(2,1)} collective-permute-done((bf16[288,1440]{1,0:T(8,128)(2,1)}, bf16[288,1440]{1,0:T(8,128)(2,1)}, u32[]{:S(2)}, u32[]{:S(2)}) %collective-permute-start.59) | collective-permute-done | bytes 829472 | tf_op jit(solution)/shard_map/ppermute | solution.py:546
  812.5 3.9 select_bitcast_fusion.1
  819.3 17.8 %collective-permute-start.62 = (bf16[288,2560]{1,0:T(8,128)(2,1)}, bf16[288,2560]{1,0:T(8,128)(2,1)S(1)}, u32[]{:S(2)}, u32[]{:S(2)}) collective-permute-start(bf16[288,2560]{1,0:T(8,128)(2,1)} %concatenate.62), channel_id=1, source_target_pairs={{0,2},{2,4},{4,6},{1,3},{3,5},{5,7},{8,10},{10,12},{12,14},{9,11},... | collective-permute-start | bytes 4423688 | tf_op jit(solution)/shard_map/ppermute | solution.py:545
  842.2 4.6 collective-permute-start.60
  849.5 3.9 select_bitcast_fusion.3
  853.7 6.3 join_columns.3
  860.0 57.9 %collective-permute-done.65 = bf16[288,1440]{1,0:T(8,128)(2,1)S(1)} collective-permute-done((bf16[288,1440]{1,0:T(8,128)(2,1)}, bf16[288,1440]{1,0:T(8,128)(2,1)S(1)}, u32[]{:S(2)}, u32[]{:S(2)}) %collective-permute-start.65) | collective-permute-done | bytes 829472 | tf_op jit(solution)/shard_map/ppermute | solution.py:546
  929.4 4.3 join_columns.4
  933.7 26.6 %collective-permute-done.68 = bf16[288,2560]{1,0:T(8,128)(2,1)S(1)} collective-permute-done((bf16[288,2560]{1,0:T(8,128)(2,1)S(1)}, bf16[288,2560]{1,0:T(8,128)(2,1)S(1)}, u32[]{:S(2)}, u32[]{:S(2)}) %collective-permute-start.68) | collective-permute-done | bytes 1474592 | tf_op jit(solution)/shard_map/ppermute | solution.py:546
  968.2 30.9 %collective-permute-done.71 = bf16[288,2560]{1,0:T(8,128)(2,1)S(1)} collective-permute-done((bf16[288,2560]{1,0:T(8,128)(2,1)S(1)}, bf16[288,2560]{1,0:T(8,128)(2,1)S(1)}, u32[]{:S(2)}, u32[]{:S(2)}) %collective-permute-start.71) | collective-permute-done | bytes 1474592 | tf_op jit(solution)/shard_map/ppermute | solution.py:546
  1009.6 5.3 join_columns.5
  (418 shorter events, 230.9 us)
Async XLA Ops:
  7.2 134.4 %all-gather.6.cloned.1.call-start = ((), (), s32[]{:S(2)}) async-start(), calls=%async_computation.4 | async-start | bytes 9953280 | tf_op jit(solution)/shard_map/all_gather | solution.py:677
  18.8 181.8 %all-gather.8.cloned.1.call-start = ((), (), s32[]{:S(2)}) async-start(), calls=%async_computation.5 | async-start | bytes 3317760 | tf_op jit(solution)/shard_map/all_gather | solution.py:677
  18.9 30.6 %collective-permute-start = (bf16[256,2304]{1,0:T(8,128)(2,1)S(1)}, bf16[256,2304]{1,0:T(8,128)(2,1)}, u32[]{:S(2)}, u32[]{:S(2)}) collective-permute-start(bf16[256,2304]{1,0:T(8,128)(2,1)S(1)} %dynamic-slice_bitcast_fusion.1), channel_id=1, source_target_pairs={{0,2},{2,4},{4,6},{1,3},{3,5},{5,7},{8,10},{10,12},{12,14},{9,11},... | collective-permute-start | bytes 3538952 | tf_op jit(solution)/shard_map/ppermute | solution.py:545
  24.6 30.7 %collective-permute-start.1 = (bf16[256,2304]{1,0:T(8,128)(2,1)S(1)}, bf16[256,2304]{1,0:T(8,128)(2,1)}, u32[]{:S(2)}, u32[]{:S(2)}) collective-permute-start(bf16[256,2304]{1,0:T(8,128)(2,1)S(1)} %dynamic-slice_bitcast_fusion.1), channel_id=1, source_target_pairs={{2,0},{4,2},{6,4},{3,1},{5,3},{7,5},{10,8},{12,10},{14,12},{11,9},... | collective-permute-start | bytes 3538952 | tf_op jit(solution)/shard_map/ppermute | solution.py:546
  56.9 30.4 %collective-permute-start.3 = (bf16[256,2304]{1,0:T(8,128)(2,1)}, bf16[256,2304]{1,0:T(8,128)(2,1)}, u32[]{:S(2)}, u32[]{:S(2)}) collective-permute-start(bf16[256,2304]{1,0:T(8,128)(2,1)} %collective-permute-done.1), channel_id=1, source_target_pairs={{2,0},{4,2},{3,1},{5,3},{10,8},{12,10},{11,9},{13,11},{18,16},{20,... | collective-permute-start | bytes 3538952 | tf_op jit(solution)/shard_map/ppermute | solution.py:546
  87.3 192.9 %all-gather.10.cloned.1.call-start = ((), (), s32[]{:S(2)}) async-start(), calls=%async_computation.6 | async-start | bytes 7962624 | tf_op jit(solution)/shard_map/all_gather | solution.py:677
  98.8 30.1 %collective-permute-start.6 = (bf16[256,2304]{1,0:T(8,128)(2,1)}, bf16[256,2304]{1,0:T(8,128)(2,1)}, u32[]{:S(2)}, u32[]{:S(2)}) collective-permute-start(bf16[256,2304]{1,0:T(8,128)(2,1)} %collective-permute-done.3), channel_id=1, source_target_pairs={{2,0},{3,1},{10,8},{11,9},{18,16},{19,17},{26,24},{27,25}} | collective-permute-start | bytes 3538952 | tf_op jit(solution)/shard_map/ppermute | solution.py:546
  128.9 211.4 %all-gather.12.cloned.1.call-start = ((), (), s32[]{:S(2)}) async-start(), calls=%async_computation.7 | async-start | bytes 15261696 | tf_op jit(solution)/shard_map/all_gather | solution.py:677
  130.7 29.0 %collective-permute-start.10 = (bf16[256,2304]{1,0:T(8,128)(2,1)S(1)}, bf16[256,2304]{1,0:T(8,128)(2,1)}, u32[]{:S(2)}, u32[]{:S(2)}) collective-permute-start(bf16[256,2304]{1,0:T(8,128)(2,1)S(1)} %dynamic-slice_bitcast_fusion), channel_id=1, source_target_pairs={{2,0},{4,2},{6,4},{3,1},{5,3},{7,5},{10,8},{12,10},{14,12},{11,9},... | collective-permute-start | bytes 3538952 | tf_op jit(solution)/shard_map/ppermute | solution.py:546
  132.0 28.8 %collective-permute-start.9 = (bf16[256,2304]{1,0:T(8,128)(2,1)S(1)}, bf16[256,2304]{1,0:T(8,128)(2,1)}, u32[]{:S(2)}, u32[]{:S(2)}) collective-permute-start(bf16[256,2304]{1,0:T(8,128)(2,1)S(1)} %dynamic-slice_bitcast_fusion), channel_id=1, source_target_pairs={{0,2},{2,4},{4,6},{1,3},{3,5},{5,7},{8,10},{10,12},{12,14},{9,11},... | collective-permute-start | bytes 3538952 | tf_op jit(solution)/shard_map/ppermute | solution.py:545
  160.8 430.1 %reduce-scatter.5.cloned.1.call-start = ((), (), s32[]{:S(2)}) async-start(), calls=%async_computation.8 | async-start | bytes 15261696 | tf_op jit(solution)/shard_map/reduce_scatter | solution.py:680
  160.9 39.7 %collective-permute-start.12 = (bf16[256,2304]{1,0:T(8,128)(2,1)}, bf16[256,2304]{1,0:T(8,128)(2,1)}, u32[]{:S(2)}, u32[]{:S(2)}) collective-permute-start(bf16[256,2304]{1,0:T(8,128)(2,1)} %collective-permute-done.9), channel_id=1, source_target_pairs={{2,4},{4,6},{3,5},{5,7},{10,12},{12,14},{11,13},{13,15},{18,20},{2... | collective-permute-start | bytes 3538952 | tf_op jit(solution)/shard_map/ppermute | solution.py:545
  162.6 38.0 %collective-permute-start.13 = (bf16[256,2304]{1,0:T(8,128)(2,1)}, bf16[256,2304]{1,0:T(8,128)(2,1)}, u32[]{:S(2)}, u32[]{:S(2)}) collective-permute-start(bf16[256,2304]{1,0:T(8,128)(2,1)} %collective-permute-done.10), channel_id=1, source_target_pairs={{2,0},{4,2},{3,1},{5,3},{10,8},{12,10},{11,9},{13,11},{18,16},{20,... | collective-permute-start | bytes 3538952 | tf_op jit(solution)/shard_map/ppermute | solution.py:546
  207.2 30.0 %collective-permute-start.14 = (bf16[256,2304]{1,0:T(8,128)(2,1)S(1)}, bf16[256,2304]{1,0:T(8,128)(2,1)S(1)}, u32[]{:S(2)}, u32[]{:S(2)}) collective-permute-start(bf16[256,2304]{1,0:T(8,128)(2,1)S(1)} %slice.134), channel_id=1, source_target_pairs={{0,2},{1,3},{8,10},{9,11},{16,18},{17,19},{24,26},{25,27}} | collective-permute-start | bytes 3538952 | tf_op jit(solution)/shard_map/ppermute | solution.py:601
  214.2 22.9 %collective-permute-start.15 = (bf16[256,2304]{1,0:T(8,128)(2,1)S(1)}, bf16[256,2304]{1,0:T(8,128)(2,1)S(1)}, u32[]{:S(2)}, u32[]{:S(2)}) collective-permute-start(bf16[256,2304]{1,0:T(8,128)(2,1)S(1)} %slice.134), channel_id=1, source_target_pairs={{6,4},{7,5},{14,12},{15,13},{22,20},{23,21},{30,28},{31,29}} | collective-permute-start | bytes 3538952 | tf_op jit(solution)/shard_map/ppermute | solution.py:602
  214.9 22.2 %collective-permute-start.16 = (bf16[256,2304]{1,0:T(8,128)(2,1)}, bf16[256,2304]{1,0:T(8,128)(2,1)S(1)}, u32[]{:S(2)}, u32[]{:S(2)}) collective-permute-start(bf16[256,2304]{1,0:T(8,128)(2,1)} %collective-permute-done.12), channel_id=1, source_target_pairs={{4,6},{5,7},{12,14},{13,15},{20,22},{21,23},{28,30},{29,31}} | collective-permute-start | bytes 3538952 | tf_op jit(solution)/shard_map/ppermute | solution.py:545
  215.7 27.7 %collective-permute-start.17 = (bf16[256,2304]{1,0:T(8,128)(2,1)}, bf16[256,2304]{1,0:T(8,128)(2,1)S(1)}, u32[]{:S(2)}, u32[]{:S(2)}) collective-permute-start(bf16[256,2304]{1,0:T(8,128)(2,1)} %collective-permute-done.13), channel_id=1, source_target_pairs={{2,0},{3,1},{10,8},{11,9},{18,16},{19,17},{26,24},{27,25}} | collective-permute-start | bytes 3538952 | tf_op jit(solution)/shard_map/ppermute | solution.py:546
  243.9 23.9 %collective-permute-start.18 = (bf16[256,2304]{1,0:T(8,128)(2,1)S(1)}, bf16[256,2304]{1,0:T(8,128)(2,1)S(1)}, u32[]{:S(2)}, u32[]{:S(2)}) collective-permute-start(bf16[256,2304]{1,0:T(8,128)(2,1)S(1)} %get-tuple-element.302), channel_id=1, source_target_pairs={{0,2},{2,4},{1,3},{3,5},{8,10},{10,12},{9,11},{11,13},{16,18},{18,... | collective-permute-start | bytes 3538952 | tf_op jit(solution)/shard_map/ppermute | solution.py:601
  245.6 22.3 %collective-permute-start.19 = (bf16[256,2304]{1,0:T(8,128)(2,1)S(1)}, bf16[256,2304]{1,0:T(8,128)(2,1)S(1)}, u32[]{:S(2)}, u32[]{:S(2)}) collective-permute-start(bf16[256,2304]{1,0:T(8,128)(2,1)S(1)} %get-tuple-element.301), channel_id=1, source_target_pairs={{4,2},{6,4},{5,3},{7,5},{12,10},{14,12},{13,11},{15,13},{20,18},{2... | collective-permute-start | bytes 3538952 | tf_op jit(solution)/shard_map/ppermute | solution.py:602
  270.0 28.8 %collective-permute-start.20 = (bf16[256,2304]{1,0:T(8,128)(2,1)}, bf16[256,2304]{1,0:T(8,128)(2,1)}, u32[]{:S(2)}, u32[]{:S(2)}) collective-permute-start(bf16[256,2304]{1,0:T(8,128)(2,1)} %get-tuple-element.300), channel_id=1, source_target_pairs={{0,2},{2,4},{4,6},{1,3},{3,5},{5,7},{8,10},{10,12},{12,14},{9,11},... | collective-permute-start | bytes 3538952 | tf_op jit(solution)/shard_map/ppermute | solution.py:601
  278.7 25.2 %collective-permute-start.21 = (bf16[256,2304]{1,0:T(8,128)(2,1)}, bf16[256,2304]{1,0:T(8,128)(2,1)}, u32[]{:S(2)}, u32[]{:S(2)}) collective-permute-start(bf16[256,2304]{1,0:T(8,128)(2,1)} %get-tuple-element.299), channel_id=1, source_target_pairs={{2,0},{4,2},{6,4},{3,1},{5,3},{7,5},{10,8},{12,10},{14,12},{11,9},... | collective-permute-start | bytes 3538952 | tf_op jit(solution)/shard_map/ppermute | solution.py:602
  309.1 21.2 %collective-permute-start.22 = (bf16[256,2304]{1,0:T(8,128)(2,1)S(1)}, bf16[256,2304]{1,0:T(8,128)(2,1)S(1)}, u32[]{:S(2)}, u32[]{:S(2)}) collective-permute-start(bf16[256,2304]{1,0:T(8,128)(2,1)S(1)} %multiply_convert_fusion.9), channel_id=1, source_target_pairs={{0,2},{2,4},{4,6},{1,3},{3,5},{5,7},{8,10},{10,12},{12,14},{9,11},... | collective-permute-start | bytes 3538952 | tf_op jit(solution)/shard_map/ppermute | solution.py:545
  310.7 24.0 %collective-permute-start.23 = (bf16[256,2304]{1,0:T(8,128)(2,1)S(1)}, bf16[256,2304]{1,0:T(8,128)(2,1)}, u32[]{:S(2)}, u32[]{:S(2)}) collective-permute-start(bf16[256,2304]{1,0:T(8,128)(2,1)S(1)} %multiply_convert_fusion.9), channel_id=1, source_target_pairs={{2,0},{4,2},{6,4},{3,1},{5,3},{7,5},{10,8},{12,10},{14,12},{11,9},... | collective-permute-start | bytes 3538952 | tf_op jit(solution)/shard_map/ppermute | solution.py:546
  334.6 29.2 %collective-permute-start.24 = (bf16[256,2304]{1,0:T(8,128)(2,1)S(1)}, bf16[256,2304]{1,0:T(8,128)(2,1)}, u32[]{:S(2)}, u32[]{:S(2)}) collective-permute-start(bf16[256,2304]{1,0:T(8,128)(2,1)S(1)} %collective-permute-done.22), channel_id=1, source_target_pairs={{2,4},{4,6},{3,5},{5,7},{10,12},{12,14},{11,13},{13,15},{18,20},{2... | collective-permute-start | bytes 3538952 | tf_op jit(solution)/shard_map/ppermute | solution.py:545
  336.3 27.5 %collective-permute-start.25 = (bf16[256,2304]{1,0:T(8,128)(2,1)}, bf16[256,2304]{1,0:T(8,128)(2,1)}, u32[]{:S(2)}, u32[]{:S(2)}) collective-permute-start(bf16[256,2304]{1,0:T(8,128)(2,1)} %collective-permute-done.23), channel_id=1, source_target_pairs={{2,0},{4,2},{3,1},{5,3},{10,8},{12,10},{11,9},{13,11},{18,16},{20,... | collective-permute-start | bytes 3538952 | tf_op jit(solution)/shard_map/ppermute | solution.py:546
  364.6 23.5 %collective-permute-start.27 = (bf16[256,2304]{1,0:T(8,128)(2,1)}, bf16[256,2304]{1,0:T(8,128)(2,1)S(1)}, u32[]{:S(2)}, u32[]{:S(2)}) collective-permute-start(bf16[256,2304]{1,0:T(8,128)(2,1)} %collective-permute-done.25), channel_id=1, source_target_pairs={{2,0},{3,1},{10,8},{11,9},{18,16},{19,17},{26,24},{27,25}} | collective-permute-start | bytes 3538952 | tf_op jit(solution)/shard_map/ppermute | solution.py:546
  431.5 29.7 %collective-permute-start.28 = (bf16[256,2304]{1,0:T(8,128)(2,1)}, bf16[256,2304]{1,0:T(8,128)(2,1)}, u32[]{:S(2)}, u32[]{:S(2)}) collective-permute-start(bf16[256,2304]{1,0:T(8,128)(2,1)} %slice.112), channel_id=1, source_target_pairs={{0,2},{1,3},{8,10},{9,11},{16,18},{17,19},{24,26},{25,27}} | collective-permute-start | bytes 3538952 | tf_op jit(solution)/shard_map/ppermute | solution.py:601
  435.3 25.9 %collective-permute-start.29 = (bf16[256,2304]{1,0:T(8,128)(2,1)}, bf16[256,2304]{1,0:T(8,128)(2,1)}, u32[]{:S(2)}, u32[]{:S(2)}) collective-permute-start(bf16[256,2304]{1,0:T(8,128)(2,1)} %slice.112), channel_id=1, source_target_pairs={{6,4},{7,5},{14,12},{15,13},{22,20},{23,21},{30,28},{31,29}} | collective-permute-start | bytes 3538952 | tf_op jit(solution)/shard_map/ppermute | solution.py:602
  461.2 219.1 %reduce-scatter.9.cloned.1.call-start = ((), (), s32[]{:S(2)}) async-start(), calls=%async_computation.10 | async-start | bytes 7962624 | tf_op jit(solution)/shard_map/reduce_scatter | solution.py:680
  464.9 19.6 %collective-permute-start.30 = (bf16[256,2304]{1,0:T(8,128)(2,1)}, bf16[256,2304]{1,0:T(8,128)(2,1)}, u32[]{:S(2)}, u32[]{:S(2)}) collective-permute-start(bf16[256,2304]{1,0:T(8,128)(2,1)} %get-tuple-element.310), channel_id=1, source_target_pairs={{0,2},{2,4},{1,3},{3,5},{8,10},{10,12},{9,11},{11,13},{16,18},{18,... | collective-permute-start | bytes 3538952 | tf_op jit(solution)/shard_map/ppermute | solution.py:601
  489.0 24.0 %collective-permute-start.32 = (bf16[256,2304]{1,0:T(8,128)(2,1)}, bf16[256,2304]{1,0:T(8,128)(2,1)}, u32[]{:S(2)}, u32[]{:S(2)}) collective-permute-start(bf16[256,2304]{1,0:T(8,128)(2,1)} %get-tuple-element.298), channel_id=1, source_target_pairs={{0,2},{2,4},{4,6},{1,3},{3,5},{5,7},{8,10},{10,12},{12,14},{9,11},... | collective-permute-start | bytes 3538952 | tf_op jit(solution)/shard_map/ppermute | solution.py:601
  495.7 22.4 %collective-permute-start.33 = (bf16[256,2304]{1,0:T(8,128)(2,1)}, bf16[256,2304]{1,0:T(8,128)(2,1)}, u32[]{:S(2)}, u32[]{:S(2)}) collective-permute-start(bf16[256,2304]{1,0:T(8,128)(2,1)} %get-tuple-element.297), channel_id=1, source_target_pairs={{2,0},{4,2},{6,4},{3,1},{5,3},{7,5},{10,8},{12,10},{14,12},{11,9},... | collective-permute-start | bytes 3538952 | tf_op jit(solution)/shard_map/ppermute | solution.py:602
  497.0 183.4 %reduce-scatter.7.cloned.1.call-start = ((), (), s32[]{:S(2)}) async-start(), calls=%async_computation.9 | async-start | bytes 3317760 | tf_op jit(solution)/shard_map/reduce_scatter | solution.py:680
  524.9 22.2 %collective-permute-start.34 = (bf16[256,2304]{1,0:T(8,128)(2,1)S(1)}, bf16[256,2304]{1,0:T(8,128)(2,1)S(1)}, u32[]{:S(2)}, u32[]{:S(2)}) collective-permute-start(bf16[256,2304]{1,0:T(8,128)(2,1)S(1)} %get-tuple-element.267), channel_id=1, source_target_pairs={{0,2},{2,4},{4,6},{1,3},{3,5},{5,7},{8,10},{10,12},{12,14},{9,11},... | collective-permute-start | bytes 3538952 | tf_op jit(solution)/shard_map/ppermute | solution.py:545
  527.4 21.5 %collective-permute-start.35 = (bf16[256,2304]{1,0:T(8,128)(2,1)S(1)}, bf16[256,2304]{1,0:T(8,128)(2,1)S(1)}, u32[]{:S(2)}, u32[]{:S(2)}) collective-permute-start(bf16[256,2304]{1,0:T(8,128)(2,1)S(1)} %get-tuple-element.267), channel_id=1, source_target_pairs={{2,0},{4,2},{6,4},{3,1},{5,3},{7,5},{10,8},{12,10},{14,12},{11,9},... | collective-permute-start | bytes 3538952 | tf_op jit(solution)/shard_map/ppermute | solution.py:546
  549.0 22.1 %collective-permute-start.38 = (bf16[256,2304]{1,0:T(8,128)(2,1)S(1)}, bf16[256,2304]{1,0:T(8,128)(2,1)S(1)}, u32[]{:S(2)}, u32[]{:S(2)}) collective-permute-start(bf16[256,2304]{1,0:T(8,128)(2,1)S(1)} %slice.115), channel_id=1, source_target_pairs={{0,2},{1,3},{8,10},{9,11},{16,18},{17,19},{24,26},{25,27}} | collective-permute-start | bytes 3538952 | tf_op jit(solution)/shard_map/ppermute | solution.py:601
  551.6 19.4 %collective-permute-start.39 = (bf16[256,2304]{1,0:T(8,128)(2,1)S(1)}, bf16[256,2304]{1,0:T(8,128)(2,1)S(1)}, u32[]{:S(2)}, u32[]{:S(2)}) collective-permute-start(bf16[256,2304]{1,0:T(8,128)(2,1)S(1)} %slice.115), channel_id=1, source_target_pairs={{6,4},{7,5},{14,12},{15,13},{22,20},{23,21},{30,28},{31,29}} | collective-permute-start | bytes 3538952 | tf_op jit(solution)/shard_map/ppermute | solution.py:602
  554.1 20.3 %collective-permute-start.37 = (bf16[256,2304]{1,0:T(8,128)(2,1)S(1)}, bf16[256,2304]{1,0:T(8,128)(2,1)}, u32[]{:S(2)}, u32[]{:S(2)}) collective-permute-start(bf16[256,2304]{1,0:T(8,128)(2,1)S(1)} %collective-permute-done.35), channel_id=1, source_target_pairs={{2,0},{4,2},{3,1},{5,3},{10,8},{12,10},{11,9},{13,11},{18,16},{20,... | collective-permute-start | bytes 3538952 | tf_op jit(solution)/shard_map/ppermute | solution.py:546
  576.3 21.5 %collective-permute-start.42 = (bf16[256,2304]{1,0:T(8,128)(2,1)}, bf16[256,2304]{1,0:T(8,128)(2,1)}, u32[]{:S(2)}, u32[]{:S(2)}) collective-permute-start(bf16[256,2304]{1,0:T(8,128)(2,1)} %get-tuple-element.296), channel_id=1, source_target_pairs={{0,2},{2,4},{1,3},{3,5},{8,10},{10,12},{9,11},{11,13},{16,18},{18,... | collective-permute-start | bytes 3538952 | tf_op jit(solution)/shard_map/ppermute | solution.py:601
  614.1 160.2 %reduce-scatter.11.cloned.1.call-start = ((), (), s32[]{:S(2)}) async-start(), calls=%async_computation.11 | async-start | bytes 9953280 | tf_op jit(solution)/shard_map/reduce_scatter | solution.py:680
  614.2 66.2 %collective-permute-start.44 = (bf16[288,2944]{1,0:T(8,128)(2,1)}, bf16[288,2944]{1,0:T(8,128)(2,1)}, u32[]{:S(2)}, u32[]{:S(2)}) collective-permute-start(bf16[288,2944]{1,0:T(8,128)(2,1)} %concatenate.60), channel_id=1, source_target_pairs={{0,2},{2,4},{4,6},{1,3},{3,5},{5,7},{8,10},{10,12},{12,14},{9,11},... | collective-permute-start | bytes 5087240 | tf_op jit(solution)/shard_map/ppermute | solution.py:545
  617.0 63.4 %collective-permute-start.45 = (bf16[288,2944]{1,0:T(8,128)(2,1)}, bf16[288,2944]{1,0:T(8,128)(2,1)}, u32[]{:S(2)}, u32[]{:S(2)}) collective-permute-start(bf16[288,2944]{1,0:T(8,128)(2,1)} %concatenate.60), channel_id=1, source_target_pairs={{2,0},{4,2},{6,4},{3,1},{5,3},{7,5},{10,8},{12,10},{14,12},{11,9},... | collective-permute-start | bytes 5087240 | tf_op jit(solution)/shard_map/ppermute | solution.py:546
  622.7 57.7 %collective-permute-start.46 = (bf16[256,2304]{1,0:T(8,128)(2,1)}, bf16[256,2304]{1,0:T(8,128)(2,1)}, u32[]{:S(2)}, u32[]{:S(2)}) collective-permute-start(bf16[256,2304]{1,0:T(8,128)(2,1)} %get-tuple-element.294), channel_id=1, source_target_pairs={{0,2},{2,4},{4,6},{1,3},{3,5},{5,7},{8,10},{10,12},{12,14},{9,11},... | collective-permute-start | bytes 3538952 | tf_op jit(solution)/shard_map/ppermute | solution.py:601
  628.3 52.1 %collective-permute-start.47 = (bf16[256,2304]{1,0:T(8,128)(2,1)}, bf16[256,2304]{1,0:T(8,128)(2,1)}, u32[]{:S(2)}, u32[]{:S(2)}) collective-permute-start(bf16[256,2304]{1,0:T(8,128)(2,1)} %get-tuple-element.293), channel_id=1, source_target_pairs={{2,0},{4,2},{6,4},{3,1},{5,3},{7,5},{10,8},{12,10},{14,12},{11,9},... | collective-permute-start | bytes 3538952 | tf_op jit(solution)/shard_map/ppermute | solution.py:602
  680.5 74.4 %collective-permute-start.48 = (bf16[288,2944]{1,0:T(8,128)(2,1)}, bf16[288,2944]{1,0:T(8,128)(2,1)S(1)}, u32[]{:S(2)}, u32[]{:S(2)}) collective-permute-start(bf16[288,2944]{1,0:T(8,128)(2,1)} %collective-permute-done.44), channel_id=1, source_target_pairs={{2,4},{4,6},{3,5},{5,7},{10,12},{12,14},{11,13},{13,15},{18,20},{2... | collective-permute-start | bytes 5087240 | tf_op jit(solution)/shard_map/ppermute | solution.py:545
  681.2 73.7 %collective-permute-start.49 = (bf16[288,2944]{1,0:T(8,128)(2,1)}, bf16[288,2944]{1,0:T(8,128)(2,1)}, u32[]{:S(2)}, u32[]{:S(2)}) collective-permute-start(bf16[288,2944]{1,0:T(8,128)(2,1)} %collective-permute-done.45), channel_id=1, source_target_pairs={{2,0},{4,2},{3,1},{5,3},{10,8},{12,10},{11,9},{13,11},{18,16},{20,... | collective-permute-start | bytes 5087240 | tf_op jit(solution)/shard_map/ppermute | solution.py:546
  682.5 27.2 %collective-permute-start.52 = (bf16[288,1440]{1,0:T(8,128)(2,1)}, bf16[288,1440]{1,0:T(8,128)(2,1)S(1)}, u32[]{:S(2)}, u32[]{:S(2)}) collective-permute-start(bf16[288,1440]{1,0:T(8,128)(2,1)} %reduce-scatter.9.cloned.1.call-done), channel_id=1, source_target_pairs={{0,2},{2,4},{4,6},{1,3},{3,5},{5,7},{8,10},{10,12},{12,14},{9,11},... | collective-permute-start | bytes 2488328 | tf_op jit(solution)/shard_map/ppermute | solution.py:545
  703.6 51.2 %collective-permute-start.50 = (bf16[256,2304]{1,0:T(8,128)(2,1)S(1)}, bf16[256,2304]{1,0:T(8,128)(2,1)S(1)}, u32[]{:S(2)}, u32[]{:S(2)}) collective-permute-start(bf16[256,2304]{1,0:T(8,128)(2,1)S(1)} %slice.141), channel_id=1, source_target_pairs={{0,2},{1,3},{8,10},{9,11},{16,18},{17,19},{24,26},{25,27}} | collective-permute-start | bytes 3538952 | tf_op jit(solution)/shard_map/ppermute | solution.py:601
  708.9 45.9 %collective-permute-start.51 = (bf16[256,2304]{1,0:T(8,128)(2,1)S(1)}, bf16[256,2304]{1,0:T(8,128)(2,1)S(1)}, u32[]{:S(2)}, u32[]{:S(2)}) collective-permute-start(bf16[256,2304]{1,0:T(8,128)(2,1)S(1)} %slice.141), channel_id=1, source_target_pairs={{6,4},{7,5},{14,12},{15,13},{22,20},{23,21},{30,28},{31,29}} | collective-permute-start | bytes 3538952 | tf_op jit(solution)/shard_map/ppermute | solution.py:602
  709.7 45.2 %collective-permute-start.53 = (bf16[288,1440]{1,0:T(8,128)(2,1)}, bf16[288,1440]{1,0:T(8,128)(2,1)}, u32[]{:S(2)}, u32[]{:S(2)}) collective-permute-start(bf16[288,1440]{1,0:T(8,128)(2,1)} %reduce-scatter.9.cloned.1.call-done), channel_id=1, source_target_pairs={{2,0},{4,2},{6,4},{3,1},{5,3},{7,5},{10,8},{12,10},{14,12},{11,9},... | collective-permute-start | bytes 2488328 | tf_op jit(solution)/shard_map/ppermute | solution.py:546
  754.9 57.6 %collective-permute-start.54 = (bf16[288,2944]{1,0:T(8,128)(2,1)S(1)}, bf16[288,2944]{1,0:T(8,128)(2,1)}, u32[]{:S(2)}, u32[]{:S(2)}) collective-permute-start(bf16[288,2944]{1,0:T(8,128)(2,1)S(1)} %collective-permute-done.48), channel_id=1, source_target_pairs={{4,6},{5,7},{12,14},{13,15},{20,22},{21,23},{28,30},{29,31}} | collective-permute-start | bytes 5087240 | tf_op jit(solution)/shard_map/ppermute | solution.py:545
  756.8 55.7 %collective-permute-start.55 = (bf16[288,2944]{1,0:T(8,128)(2,1)}, bf16[288,2944]{1,0:T(8,128)(2,1)}, u32[]{:S(2)}, u32[]{:S(2)}) collective-permute-start(bf16[288,2944]{1,0:T(8,128)(2,1)} %collective-permute-done.49), channel_id=1, source_target_pairs={{2,0},{3,1},{10,8},{11,9},{18,16},{19,17},{26,24},{27,25}} | collective-permute-start | bytes 5087240 | tf_op jit(solution)/shard_map/ppermute | solution.py:546
  760.7 51.8 %collective-permute-start.56 = (bf16[256,2304]{1,0:T(8,128)(2,1)}, bf16[256,2304]{1,0:T(8,128)(2,1)}, u32[]{:S(2)}, u32[]{:S(2)}) collective-permute-start(bf16[256,2304]{1,0:T(8,128)(2,1)} %get-tuple-element.292), channel_id=1, source_target_pairs={{0,2},{2,4},{1,3},{3,5},{8,10},{10,12},{9,11},{11,13},{16,18},{18,... | collective-permute-start | bytes 3538952 | tf_op jit(solution)/shard_map/ppermute | solution.py:601
  770.4 42.0 %collective-permute-start.57 = (bf16[256,2304]{1,0:T(8,128)(2,1)}, bf16[256,2304]{1,0:T(8,128)(2,1)}, u32[]{:S(2)}, u32[]{:S(2)}) collective-permute-start(bf16[256,2304]{1,0:T(8,128)(2,1)} %get-tuple-element.291), channel_id=1, source_target_pairs={{4,2},{6,4},{5,3},{7,5},{12,10},{14,12},{13,11},{15,13},{20,18},{2... | collective-permute-start | bytes 3538952 | tf_op jit(solution)/shard_map/ppermute | solution.py:602
  773.0 39.4 %collective-permute-start.59 = (bf16[288,1440]{1,0:T(8,128)(2,1)}, bf16[288,1440]{1,0:T(8,128)(2,1)}, u32[]{:S(2)}, u32[]{:S(2)}) collective-permute-start(bf16[288,1440]{1,0:T(8,128)(2,1)} %collective-permute-done.53), channel_id=1, source_target_pairs={{2,0},{4,2},{3,1},{5,3},{10,8},{12,10},{11,9},{13,11},{18,16},{20,... | collective-permute-start | bytes 2488328 | tf_op jit(solution)/shard_map/ppermute | solution.py:546
  819.2 28.9 %collective-permute-start.66 = (bf16[2,288,2944]{2,1,0:T(8,128)(2,1)}, bf16[2,288,2944]{2,1,0:T(8,128)(2,1)S(1)}, u32[]{:S(2)}, u32[]{:S(2)}) collective-permute-start(bf16[2,288,2944]{2,1,0:T(8,128)(2,1)} %pad_maximum_fusion.3), channel_id=1, source_target_pairs={{0,1},{1,0},{2,3},{3,2},{4,5},{5,4},{6,7},{7,6},{8,9},{9,8},{10,11... | collective-permute-start | bytes 10174472 | tf_op jit(solution)/shard_map/ppermute | solution.py:694
  819.3 98.6 %collective-permute-start.62 = (bf16[288,2560]{1,0:T(8,128)(2,1)}, bf16[288,2560]{1,0:T(8,128)(2,1)S(1)}, u32[]{:S(2)}, u32[]{:S(2)}) collective-permute-start(bf16[288,2560]{1,0:T(8,128)(2,1)} %concatenate.62), channel_id=1, source_target_pairs={{0,2},{2,4},{4,6},{1,3},{3,5},{5,7},{8,10},{10,12},{12,14},{9,11},... | collective-permute-start | bytes 4423688 | tf_op jit(solution)/shard_map/ppermute | solution.py:545
  837.1 80.8 %collective-permute-start.63 = (bf16[288,2560]{1,0:T(8,128)(2,1)}, bf16[288,2560]{1,0:T(8,128)(2,1)S(1)}, u32[]{:S(2)}, u32[]{:S(2)}) collective-permute-start(bf16[288,2560]{1,0:T(8,128)(2,1)} %concatenate.62), channel_id=1, source_target_pairs={{2,0},{4,2},{6,4},{3,1},{5,3},{7,5},{10,8},{12,10},{14,12},{11,9},... | collective-permute-start | bytes 4423688 | tf_op jit(solution)/shard_map/ppermute | solution.py:546
  842.2 75.7 %collective-permute-start.60 = (bf16[256,2304]{1,0:T(8,128)(2,1)S(1)}, bf16[256,2304]{1,0:T(8,128)(2,1)S(1)}, u32[]{:S(2)}, u32[]{:S(2)}) collective-permute-start(bf16[256,2304]{1,0:T(8,128)(2,1)S(1)} %get-tuple-element.290), channel_id=1, source_target_pairs={{0,2},{2,4},{4,6},{1,3},{3,5},{5,7},{8,10},{10,12},{12,14},{9,11},... | collective-permute-start | bytes 3538952 | tf_op jit(solution)/shard_map/ppermute | solution.py:601
  846.8 71.1 %collective-permute-start.61 = (bf16[256,2304]{1,0:T(8,128)(2,1)S(1)}, bf16[256,2304]{1,0:T(8,128)(2,1)S(1)}, u32[]{:S(2)}, u32[]{:S(2)}) collective-permute-start(bf16[256,2304]{1,0:T(8,128)(2,1)S(1)} %get-tuple-element.289), channel_id=1, source_target_pairs={{2,0},{4,2},{6,4},{3,1},{5,3},{7,5},{10,8},{12,10},{14,12},{11,9},... | collective-permute-start | bytes 3538952 | tf_op jit(solution)/shard_map/ppermute | solution.py:602
  848.1 69.7 %collective-permute-start.65 = (bf16[288,1440]{1,0:T(8,128)(2,1)}, bf16[288,1440]{1,0:T(8,128)(2,1)S(1)}, u32[]{:S(2)}, u32[]{:S(2)}) collective-permute-start(bf16[288,1440]{1,0:T(8,128)(2,1)} %collective-permute-done.59), channel_id=1, source_target_pairs={{2,0},{3,1},{10,8},{11,9},{18,16},{19,17},{26,24},{27,25}} | collective-permute-start | bytes 2488328 | tf_op jit(solution)/shard_map/ppermute | solution.py:546
  917.9 42.4 %collective-permute-start.72 = (bf16[256,2304]{1,0:T(8,128)(2,1)}, bf16[256,2304]{1,0:T(8,128)(2,1)S(1)}, u32[]{:S(2)}, u32[]{:S(2)}) collective-permute-start(bf16[256,2304]{1,0:T(8,128)(2,1)} %multiply_convert_fusion.7), channel_id=1, source_target_pairs={{0,1},{1,0},{2,3},{3,2},{4,5},{5,4},{6,7},{7,6},{8,9},{9,8},{10,11... | collective-permute-start | bytes 3538952 | tf_op jit(solution)/shard_map/ppermute | solution.py:898
  924.0 36.2 %collective-permute-start.68 = (bf16[288,2560]{1,0:T(8,128)(2,1)S(1)}, bf16[288,2560]{1,0:T(8,128)(2,1)S(1)}, u32[]{:S(2)}, u32[]{:S(2)}) collective-permute-start(bf16[288,2560]{1,0:T(8,128)(2,1)S(1)} %collective-permute-done.63), channel_id=1, source_target_pairs={{2,0},{4,2},{3,1},{5,3},{10,8},{12,10},{11,9},{13,11},{18,16},{20,... | collective-permute-start | bytes 4423688 | tf_op jit(solution)/shard_map/ppermute | solution.py:546
  962.5 36.6 %collective-permute-start.71 = (bf16[288,2560]{1,0:T(8,128)(2,1)S(1)}, bf16[288,2560]{1,0:T(8,128)(2,1)S(1)}, u32[]{:S(2)}, u32[]{:S(2)}) collective-permute-start(bf16[288,2560]{1,0:T(8,128)(2,1)S(1)} %collective-permute-done.68), channel_id=1, source_target_pairs={{2,0},{3,1},{10,8},{11,9},{18,16},{19,17},{26,24},{27,25}} | collective-permute-start | bytes 4423688 | tf_op jit(solution)/shard_map/ppermute | solution.py:546
  (102 other events, 1837.6 us)
Sparse Core Ops, SparseCore 0:
  18.9 59.9 all-gather.5
  87.4 29.5 all-gather.7
  129.0 46.9 all-gather.9
  178.3 76.2 all-gather.11
  461.4 97.1 reduce-scatter.4
  561.9 65.4 reduce-scatter.8
  631.5 45.0 reduce-scatter.6
  680.6 74.6 reduce-scatter.10

commit v7 on v6

--- a/solution.py
+++ b/solution.py
@@ -842,56 +842,56 @@
     attn_grad_line.step()
     mlp_line.step()
     unit_marks = gain_marks(gate_up_mine, gate_up_piece)
-    rest = jnp.zeros((unit_marks.shape[0], -(2 * unit_cols + 2) % LANES), jnp.bfloat16)
-    unit_block = jnp.concatenate([gate_up_piece, unit_marks, rest], axis=1)
-    (unit_block,) = stage([attn_grad_line, mlp_line], unit_block)
+    rest = jnp.zeros((unit_marks.shape[0], -(3 * unit_cols + 2) % LANES), jnp.bfloat16)
+    (unit_marks,) = stage([attn_grad_line, mlp_line], unit_marks)
     mlp_line.step()
-    unit_line = walk(unit_block)
-    unit_line.step()
     grad_attn = jnp.concatenate([attn_grad_line.near(k) for k in range(lines)], axis=0)
     out_grad = row_product(grad_attn, attend).astype(jnp.bfloat16)
     grad_attend = plain_product(grad_attn, out_w).astype(jnp.bfloat16)
+    grad_attend, out_grad, gate_up_piece = lax.optimization_barrier(
+        (grad_attend, out_grad, gate_up_piece)
+    )
+    unit_block = jnp.concatenate([gate_up_piece, down_piece, unit_marks, rest], axis=1)
+    out_grad, grad_attend, unit_block = stage([mlp_line], out_grad, grad_attend, unit_block)
+    out_piece = reduce_pair(out_grad)
+    unit_line = walk(unit_block)
+    unit_line.step()
     grad_qkv = attend_backward(
         heads, span, order, length.reshape(1), kept, attend, grad_attend, cos_all, sin_all
     )
     qkv_grad = row_product(first_in, grad_qkv).astype(jnp.bfloat16)
-    out_piece = reduce_pair(out_grad)
-    grad_qkv, qkv_grad, out_piece, down_piece = stage(
-        [unit_line, mlp_line], grad_qkv, qkv_grad, out_piece, down_piece
-    )
+    grad_qkv, qkv_grad, out_piece = stage([unit_line], grad_qkv, qkv_grad, out_piece)
     unit_line.step()
-    down_line = walk(down_piece)
-    down_line.step()
     qkv_piece = reduce_pair(qkv_grad)
     first_part = col_product(grad_qkv, qkv_w).astype(jnp.bfloat16)
 
     first_line = add_up(blocks_of(first_part))
     first_line.step()
     layer_rows = ((middle + BRANCH_SCALE * mlp_line.total()) * live_own).astype(jnp.bfloat16)
-    (layer_rows,) = stage([unit_line, first_line, down_line], layer_rows)
+    (layer_rows,) = stage([unit_line, first_line], layer_rows)
     unit_line.step()
     first_line.step()
-    down_line.step()
     qkv_marks = gain_marks(qkv_mine, qkv_piece)
     head_block = jnp.concatenate(
         [qkv_piece[:, :head_cols], qkv_marks, qkv_piece[:, head_cols + 2 :], out_piece], axis=1
     )
-    (head_block,) = stage([unit_line, first_line, down_line], head_block)
+    (head_block,) = stage([unit_line, first_line], head_block)
     head_line = walk(head_block)
     head_line.step()
     first_line.step()
-    down_line.step()
     own, other, give = line_pieces(unit_line)
-    final_gate, final_up = join_columns(core_index, own, other, 2, unit_cols, unit_cols)
-    final_gain_two = gain_total((own, give), 2 * unit_cols, mlp_gain)
-    final_gate, final_up = stage([first_line, head_line, down_line], final_gate, final_up)
+    final_gate, final_up, final_down = join_columns(
+        core_index, own, other, 3, unit_cols, unit_cols
+    )
+    final_gain_two = gain_total((own, give), 3 * unit_cols, mlp_gain)
+    final_gate, final_up, final_down = stage(
+        [first_line, head_line], final_gate, final_up, final_down
+    )
     head_line.step()
-    own, other, _ = line_pieces(down_line)
-    (final_down,) = join_columns(core_index, own, other, 1, unit_cols, unit_cols)
     grad_first = first_line.total()
     normed_one, inverse_one = norm_parts(own_x)
     grad_rows = grad_middle + norm_back(grad_first, normed_one, inverse_one, gain_a)
-    grad_rows, final_down = stage([head_line], grad_rows, final_down)
+    (grad_rows,) = stage([head_line], grad_rows)
     head_line.step()
 
     def both_slots(own):

time: 1030 us -> 989 us (0.960)
  starting transfers between devices: 171 us -> 144 us
  waiting for transfers between devices: 381 us -> 355 us
    ppermute x21 -> x18, waiting for transfers between devices: 253 us -> 172 us  [step(): self.downs.append(lax.ppermute(self.downs[-1], self.axis, down_pairs))]
    ppermute x12, waiting for transfers between devices: 52.1 us -> 93.9 us  [step(): self.up = lax.ppermute(up, self.axis, [(i, i + 1) for i, _ in ups])]
    ppermute x21 -> x18, starting transfers between devices: 59.4 us -> 40.5 us  [step(): self.ups.append(lax.ppermute(self.ups[-1], self.axis, up_pairs))]
    unnamed x165 -> x153, local copies, waits for them, and re-layouts: 19.3 us -> 23.9 us
    ppermute x21 -> x18, starting transfers between devices: 28.1 us -> 24.6 us  [step(): self.downs.append(lax.ppermute(self.downs[-1], self.axis, down_pairs))]
    ppermute x21 -> x18, waiting for transfers between devices: 59.2 us -> 59.1 us  [step(): self.ups.append(lax.ppermute(self.ups[-1], self.axis, up_pairs))]
  transfers between devices with their start and end apart: 85 -> 78, of which waited for: 30 -> 34; matrix products, arithmetic and copies ran while one was open for 29% -> 30% of each run, Pallas kernels for 7% -> 7%
where the time goes in v7:
time: 989 us; the launch traced here: 979 us
  waiting for transfers between devices  355 us (36%)
  matrix products  189 us (19%)
  starting transfers between devices  144 us (15%)
  other arithmetic  133 us (13%)
  Pallas kernels  77.3 us (8%)
  local copies, waits for them, and re-layouts  55 us (6%)
  between operations  15.9 us (2%)
    ppermute x18, waiting for transfers between devices, step(): self.downs.append(lax.ppermute(self.downs[-1], self.axis, down_pairs))  172 us
    ppermute x12, waiting for transfers between devices, step(): self.up = lax.ppermute(up, self.axis, [(i, i + 1) for i, _ in ups])  93.9 us
    dot_general x6, matrix products, plain_product(): return jnp.dot(left_mat, right_mat, preferred_element_type=jnp.float32)  78.2 us
    ppermute x12, starting transfers between devices, step(): self.up = lax.ppermute(up, self.axis, [(i, i + 1) for i, _ in ups])  62 us
    ppermute x18, waiting for transfers between devices, step(): self.ups.append(lax.ppermute(self.ups[-1], self.axis, up_pairs))  59.1 us
    dot_general x5, matrix products, col_product(): lax.dot_general(left_mat, right_mat, CONTRACT_COLS, preferred_element_typ...  57.5 us
    dot_general x4, matrix products, row_product(): lax.dot_general(left_mat, right_mat, CONTRACT_ROWS, preferred_element_typ...  53.7 us
    ppermute x18, starting transfers between devices, step(): self.ups.append(lax.ppermute(self.ups[-1], self.axis, up_pairs))  40.5 us
  transfers between devices with their start and end apart: 78, of which 34 were waited for; matrix products, arithmetic and copies ran while one was open for 30% of the time, Pallas kernels for 7%

profile of v7, /device:TPU:0, one launch (start us, length us, event | category | flops | bytes accessed | tf_op | source)
XLA Modules:
  0.0 978.8 jit_solution(7148328572196758300)
XLA Ops:
  18.8 5.7 collective-permute-start
  28.1 21.3 %collective-permute-done = bf16[256,2304]{1,0:T(8,128)(2,1)} collective-permute-done((bf16[256,2304]{1,0:T(8,128)(2,1)S(1)}, bf16[256,2304]{1,0:T(8,128)(2,1)}, u32[]{:S(2)}, u32[]{:S(2)}) %collective-permute-start) | collective-permute-done | bytes 1179680 | tf_op jit(solution)/shard_map/ppermute | solution.py:545
  49.4 5.8 collective-permute-done.1
  63.7 8.6 all-gather
  74.3 12.9 %collective-permute-done.3 = bf16[256,2304]{1,0:T(8,128)(2,1)} collective-permute-done((bf16[256,2304]{1,0:T(8,128)(2,1)}, bf16[256,2304]{1,0:T(8,128)(2,1)}, u32[]{:S(2)}, u32[]{:S(2)}) %collective-permute-start.3) | collective-permute-done | bytes 1179680 | tf_op jit(solution)/shard_map/ppermute | solution.py:546
  106.0 22.8 %collective-permute-done.6 = bf16[256,2304]{1,0:T(8,128)(2,1)} collective-permute-done((bf16[256,2304]{1,0:T(8,128)(2,1)}, bf16[256,2304]{1,0:T(8,128)(2,1)}, u32[]{:S(2)}, u32[]{:S(2)}) %collective-permute-start.6) | collective-permute-done | bytes 1179680 | tf_op jit(solution)/shard_map/ppermute | solution.py:546
  132.0 5.8 collective-permute-start.9
  141.5 17.9 %fusion.56.q_in.k_in.v_in = f32[1024,1920]{1,0:T(8,128)} fusion(bf16[2304,1920]{1,0:T(8,128)(2,1)} %all-gather.6.cloned.1.call-done, f32[2304]{0:T(1024)S(1)} %get-tuple-element.152, f32[1024]{0:T(1024)S(1)} %add_rsqrt_fusion, bf16[256,2304]{1,0:T(8,128)(2,1)} %copy-done.44, bf16[256,2304]{1,0:T(8,128)(2,1)} %copy-done.39, ...), kind=kOutput, calls=%fused_computation.149 | convolution fusion | flops 9085648896 | bytes 21443584 | tf_op jit(solution)/shard_map/dot_general | solution.py:30
  167.9 29.6 %attend.1 = (bf16[1024,640]{1,0:T(8,128)(2,1)S(1)}, bf16[1024,640]{1,0:T(8,128)(2,1)S(1)}, bf16[1024,640]{1,0:T(8,128)(2,1)S(1)}, bf16[1024,640]{1,0:T(8,128)(2,1)S(1)}, f32[5,8,1024]{2,1,0:T(8,128)S(1)}) custom-call(s32[8]{0:T(128)S(1)} %and_select_fusion.order, s32[1]{0:T(128)} %dynamic_slice.64.length, f32[1024,1920]{1,0:T(8,128)S(1)} %copy-done.2, ...), custom_call_target="tpu_custom_call" | custom-call | flops 2415919104 | bytes 15728640 | tf_op jit(solution)/shard_map/attend/pallas_call | solution.py:451
  200.8 6.4 convolution_convert_fusion.4
  207.3 7.0 collective-permute-start.14
  219.6 17.7 %collective-permute-done.14 = bf16[256,2304]{1,0:T(8,128)(2,1)S(1)} collective-permute-done((bf16[256,2304]{1,0:T(8,128)(2,1)S(1)}, bf16[256,2304]{1,0:T(8,128)(2,1)S(1)}, u32[]{:S(2)}, u32[]{:S(2)}) %collective-permute-start.14) | collective-permute-done | bytes 1179680 | tf_op jit(solution)/shard_map/ppermute | solution.py:601
  237.3 6.3 collective-permute-done.17
  248.6 9.1 multiply_convert_fusion
  257.7 10.4 %collective-permute-done.18 = bf16[256,2304]{1,0:T(8,128)(2,1)S(1)} collective-permute-done((bf16[256,2304]{1,0:T(8,128)(2,1)S(1)}, bf16[256,2304]{1,0:T(8,128)(2,1)S(1)}, u32[]{:S(2)}, u32[]{:S(2)}) %collective-permute-start.18) | collective-permute-done | bytes 1179680 | tf_op jit(solution)/shard_map/ppermute | solution.py:601
  270.2 8.7 collective-permute-start.20
  280.4 9.1 fusion.42
  289.5 7.1 fusion.44
  298.9 5.1 collective-permute-done.21
  312.1 18.3 %collective-permute-done.22 = bf16[256,2304]{1,0:T(8,128)(2,1)S(1)} collective-permute-done((bf16[256,2304]{1,0:T(8,128)(2,1)S(1)}, bf16[256,2304]{1,0:T(8,128)(2,1)S(1)}, u32[]{:S(2)}, u32[]{:S(2)}) %collective-permute-start.22) | collective-permute-done | bytes 1179680 | tf_op jit(solution)/shard_map/ppermute | solution.py:545
  330.5 4.3 collective-permute-done.23
  340.4 17.9 %fusion.34 = f32[512,2880]{0,1:T(8,128)} fusion(bf16[2304,2880]{1,0:T(8,128)(2,1)} %all-gather.12.cloned.1.call-done, bf16[256,2304]{1,0:T(8,128)(2,1)} %fusion.49, bf16[256,2304]{1,0:T(8,128)(2,1)} %copy-done.50), kind=kOutput, calls=%fused_computation.96 | convolution fusion | flops 6799491072 | bytes 21528576 | tf_op jit(solution)/shard_map/dot_general | solution.py:30
  358.4 5.4 multiply_convert_fusion.5
  366.4 12.5 %convolution_convert_fusion.8 = bf16[512,2304]{1,0:T(8,128)(2,1)} fusion(bf16[512,2880]{0,1:T(8,128)(2,1)S(1)} %pad_maximum_fusion.6, bf16[2304,2880]{1,0:T(8,128)(2,1)} %all-gather.12.cloned.1.call-done), kind=kOutput, calls=%fused_computation.35 | convolution fusion | flops 6795952128 | bytes 18579456 | tf_op jit(solution)/shard_map/dot_general | solution.py:26
  381.7 6.5 collective-permute-done.27
  389.7 17.9 %fusion.38 = f32[512,2880]{0,1:T(8,128)} fusion(bf16[2304,2880]{1,0:T(8,128)(2,1)} %all-gather.12.cloned.1.call-done, bf16[256,2304]{1,0:T(8,128)(2,1)} %select_select_fusion.9, bf16[256,2304]{1,0:T(8,128)(2,1)} %select_select_fusion.2), kind=kOutput, calls=%fused_computation.100 | convolution fusion | flops 6799491072 | bytes 21528576 | tf_op jit(solution)/shard_map/dot_general | solution.py:30
  407.6 5.4 multiply_convert_fusion.2
  415.9 13.2 %convolution_convert_fusion.7 = bf16[512,2304]{1,0:T(8,128)(2,1)} fusion(bf16[2304,2880]{1,0:T(8,128)(2,1)} %all-gather.12.cloned.1.call-done, bf16[512,1440]{0,1:T(8,128)(2,1)} %copy-done.36, bf16[512,1440]{0,1:T(8,128)(2,1)S(1)} %get-tuple-element.279), kind=kOutput, calls=%fused_computation.34 | convolution fusion | flops 6801850368 | bytes 18579456 | tf_op jit(solution)/shard_map/dot_general | solution.py:26
  437.2 20.4 %convolution_convert_fusion = bf16[2304,2880]{1,0:T(8,128)(2,1)} fusion(bf16[512,2880]{0,1:T(8,128)(2,1)} %pad_maximum_fusion.7, bf16[512,2880]{0,1:T(8,128)(2,1)} %copy-done.47, bf16[256,2304]{1,0:T(8,128)(2,1)S(1)} %copy-done.52, bf16[256,2304]{1,0:T(8,128)(2,1)} %select_select_fusion.2, bf16[256,2304]{1,0:T(8,128)(2,1)} %fusion.49, ...), kind=kOutput, calls=%fused_computation.1 | convolution fusion | flops 13626851328 | bytes 23887872 | tf_op jit(solution)/shard_map/dot_general | solution.py:22
  469.1 13.2 %convolution_convert_fusion.2 = bf16[2304,1440]{1,0:T(8,128)(2,1)} fusion(bf16[1024,2304]{1,0:T(8,128)(2,1)} %multiply_convert_fusion, bf16[1024,1440]{0,1:T(8,128)(2,1)S(1)} %copy-done.46), kind=kOutput, calls=%fused_computation.5 | convolution fusion | flops 6798090240 | bytes 14303232 | tf_op jit(solution)/shard_map/dot_general | solution.py:22
  484.8 4.4 add_convert_fusion.4
  489.2 6.8 collective-permute-start.32
  497.3 11.9 %convolution_convert_fusion.5 = bf16[1024,2304]{1,0:T(8,128)(2,1)S(1)} fusion(bf16[1024,1440]{0,1:T(8,128)(2,1)} %pad_maximum_fusion.8, bf16[2304,1440]{1,0:T(8,128)(2,1)} %all-gather.10.cloned.1.call-done), kind=kOutput, calls=%fused_computation.17 | convolution fusion | flops 6797131776 | bytes 14303232 | tf_op jit(solution)/shard_map/dot_general | solution.py:26
  513.2 5.1 collective-permute-done.33
  520.8 4.3 multiply_convert_fusion.8
  528.9 18.3 %collective-permute-done.34 = bf16[256,2304]{1,0:T(8,128)(2,1)S(1)} collective-permute-done((bf16[256,2304]{1,0:T(8,128)(2,1)S(1)}, bf16[256,2304]{1,0:T(8,128)(2,1)S(1)}, u32[]{:S(2)}, u32[]{:S(2)}) %collective-permute-start.34) | collective-permute-done | bytes 1179680 | tf_op jit(solution)/shard_map/ppermute | solution.py:545
  555.5 16.1 %collective-permute-done.38 = bf16[256,2304]{1,0:T(8,128)(2,1)S(1)} collective-permute-done((bf16[256,2304]{1,0:T(8,128)(2,1)S(1)}, bf16[256,2304]{1,0:T(8,128)(2,1)S(1)}, u32[]{:S(2)}, u32[]{:S(2)}) %collective-permute-start.38) | collective-permute-done | bytes 1179680 | tf_op jit(solution)/shard_map/ppermute | solution.py:601
  576.0 7.7 collective-permute-start.42
  596.9 12.1 %collective-permute-done.41 = bf16[256,2304]{1,0:T(8,128)(2,1)} collective-permute-done((bf16[256,2304]{1,0:T(8,128)(2,1)}, bf16[256,2304]{1,0:T(8,128)(2,1)}, u32[]{:S(2)}, u32[]{:S(2)}) %collective-permute-start.41) | collective-permute-done | bytes 1179680 | tf_op jit(solution)/shard_map/ppermute | solution.py:546
  609.0 4.5 add_convert_fusion.2
  620.5 5.3 convolution_convert_fusion.6
  625.8 8.2 convolution_convert_fusion.9.do_in
  634.2 5.3 concatenate.65
  639.6 4.8 collective-permute-start.46
  651.4 29.9 %attend_back.1 = bf16[1024,1920]{1,0:T(8,128)(2,1)} custom-call(s32[8]{0:T(128)S(1)} %and_select_fusion.order, s32[1]{0:T(128)} %dynamic_slice.64.length, bf16[1024,640]{1,0:T(8,128)(2,1)S(1)} %copy-done.6, bf16[1024,640]{1,0:T(8,128)(2,1)S(1)} %copy-done.8, bf16[1024,640]{1,0:T(8,128)(2,1)S(1)} %copy-done.10, f32[5,8,1024]{2,1,0:T(8,128)S(1)} %get-tuple-element.224.log_in, ...), custom_call_target="tpu_custom_call" | custom-call | flops 6039797760 | bytes 10485760 | tf_op jit(solution)/shard_map/attend_back/pallas_call | solution.py:478
  681.4 14.7 %convolution_convert_fusion.1 = bf16[2304,1920]{1,0:T(8,128)(2,1)} fusion(bf16[1024,1920]{1,0:T(8,128)(2,1)} %attend_back.1, f32[2304]{0:T(1024)S(1)} %copy-done.62, f32[1024]{0:T(1024)S(1)} %copy-done.69, bf16[256,2304]{1,0:T(8,128)(2,1)S(1)} %copy-done.45, bf16[256,2304]{1,0:T(8,128)(2,1)S(1)} %copy-done.40, bf16[256,2304]{1,0:T(8,128)(2,1)S(1)} %copy-done.43, ...), kind=kOutput, calls=%fused_computation.4 | convolution fusion | flops 9090072576 | bytes 17511424 | tf_op jit(solution)/shard_map/dot_general | solution.py:22
  699.6 13.4 %convolution_convert_fusion.3 = bf16[1024,2304]{1,0:T(8,128)(2,1)S(1)} fusion(bf16[1024,1920]{1,0:T(8,128)(2,1)} %attend_back.1, bf16[2304,1920]{1,0:T(8,128)(2,1)} %all-gather.6.cloned.1.call-done), kind=kOutput, calls=%fused_computation.15 | convolution fusion | flops 9062055936 | bytes 17498112 | tf_op jit(solution)/shard_map/dot_general | solution.py:26
  713.1 6.4 collective-permute-start.50
  723.9 13.5 %collective-permute-done.50 = bf16[256,2304]{1,0:T(8,128)(2,1)S(1)} collective-permute-done((bf16[256,2304]{1,0:T(8,128)(2,1)S(1)}, bf16[256,2304]{1,0:T(8,128)(2,1)S(1)}, u32[]{:S(2)}, u32[]{:S(2)}) %collective-permute-start.50) | collective-permute-done | bytes 1179680 | tf_op jit(solution)/shard_map/ppermute | solution.py:601
  737.5 14.6 %collective-permute-done.49 = bf16[288,4352]{1,0:T(8,128)(2,1)} collective-permute-done((bf16[288,4352]{1,0:T(8,128)(2,1)}, bf16[288,4352]{1,0:T(8,128)(2,1)}, u32[]{:S(2)}, u32[]{:S(2)}) %collective-permute-start.49) | collective-permute-done | bytes 2506784 | tf_op jit(solution)/shard_map/ppermute | solution.py:546
  757.5 7.0 collective-permute-start.54
  766.2 7.7 reduce-scatter.11.cloned.1.call-done
  778.7 4.0 concatenate.66
  782.6 22.3 %collective-permute-done.53 = bf16[288,4352]{1,0:T(8,128)(2,1)} collective-permute-done((bf16[288,4352]{1,0:T(8,128)(2,1)}, bf16[288,4352]{1,0:T(8,128)(2,1)}, u32[]{:S(2)}, u32[]{:S(2)}) %collective-permute-start.53) | collective-permute-done | bytes 2506784 | tf_op jit(solution)/shard_map/ppermute | solution.py:546
  805.0 5.8 select_bitcast_fusion.1
  818.5 4.4 add_convert_fusion
  822.9 5.5 collective-permute-start.56
  829.7 5.8 select_bitcast_fusion.3
  836.9 12.5 %join_columns.2 = (f32[576,2880]{1,0:T(8,128)}, f32[576,2880]{1,0:T(8,128)}, f32[576,2880]{1,0:T(8,128)}) custom-call(s32[1]{0:T(128)} %bitcast.11.core, bf16[2,288,4352]{2,1,0:T(8,128)(2,1)S(1)} %pad_maximum_fusion.own, bf16[2,288,4352]{2,1,0:T(8,128)(2,1)} %collective-permute-done.60.other), custom_call_target="tpu_custom_call" | custom-call | bytes 39960576 | tf_op jit(solution)/shard_map/join_columns/pallas_call | solution.py:515
  849.3 24.7 %collective-permute-done.56 = bf16[256,2304]{1,0:T(8,128)(2,1)} collective-permute-done((bf16[256,2304]{1,0:T(8,128)(2,1)}, bf16[256,2304]{1,0:T(8,128)(2,1)}, u32[]{:S(2)}, u32[]{:S(2)}) %collective-permute-start.56) | collective-permute-done | bytes 1179680 | tf_op jit(solution)/shard_map/ppermute | solution.py:601
  874.0 5.2 collective-permute-done.57
  886.9 29.0 %collective-permute-done.62 = bf16[288,2560]{1,0:T(8,128)(2,1)S(1)} collective-permute-done((bf16[288,2560]{1,0:T(8,128)(2,1)}, bf16[288,2560]{1,0:T(8,128)(2,1)S(1)}, u32[]{:S(2)}, u32[]{:S(2)}) %collective-permute-start.62) | collective-permute-done | bytes 1474592 | tf_op jit(solution)/shard_map/ppermute | solution.py:546
  922.6 30.8 %collective-permute-done.64 = bf16[288,2560]{1,0:T(8,128)(2,1)S(1)} collective-permute-done((bf16[288,2560]{1,0:T(8,128)(2,1)S(1)}, bf16[288,2560]{1,0:T(8,128)(2,1)S(1)}, u32[]{:S(2)}, u32[]{:S(2)}) %collective-permute-start.64) | collective-permute-done | bytes 1474592 | tf_op jit(solution)/shard_map/ppermute | solution.py:546
  966.4 5.3 join_columns.3
  (386 shorter events, 232.9 us)
Async XLA Ops:
  7.2 134.3 %all-gather.6.cloned.1.call-start = ((), (), s32[]{:S(2)}) async-start(), calls=%async_computation.4 | async-start | bytes 9953280 | tf_op jit(solution)/shard_map/all_gather | solution.py:677
  18.8 182.0 %all-gather.8.cloned.1.call-start = ((), (), s32[]{:S(2)}) async-start(), calls=%async_computation.5 | async-start | bytes 3317760 | tf_op jit(solution)/shard_map/all_gather | solution.py:677
  18.8 30.6 %collective-permute-start = (bf16[256,2304]{1,0:T(8,128)(2,1)S(1)}, bf16[256,2304]{1,0:T(8,128)(2,1)}, u32[]{:S(2)}, u32[]{:S(2)}) collective-permute-start(bf16[256,2304]{1,0:T(8,128)(2,1)S(1)} %dynamic-slice_bitcast_fusion.1), channel_id=1, source_target_pairs={{0,2},{2,4},{4,6},{1,3},{3,5},{5,7},{8,10},{10,12},{12,14},{9,11},... | collective-permute-start | bytes 3538952 | tf_op jit(solution)/shard_map/ppermute | solution.py:545
  24.5 30.7 %collective-permute-start.1 = (bf16[256,2304]{1,0:T(8,128)(2,1)S(1)}, bf16[256,2304]{1,0:T(8,128)(2,1)}, u32[]{:S(2)}, u32[]{:S(2)}) collective-permute-start(bf16[256,2304]{1,0:T(8,128)(2,1)S(1)} %dynamic-slice_bitcast_fusion.1), channel_id=1, source_target_pairs={{2,0},{4,2},{6,4},{3,1},{5,3},{7,5},{10,8},{12,10},{14,12},{11,9},... | collective-permute-start | bytes 3538952 | tf_op jit(solution)/shard_map/ppermute | solution.py:546
  55.2 19.1 %collective-permute-start.2 = (bf16[256,2304]{1,0:T(8,128)(2,1)}, bf16[256,2304]{1,0:T(8,128)(2,1)}, u32[]{:S(2)}, u32[]{:S(2)}) collective-permute-start(bf16[256,2304]{1,0:T(8,128)(2,1)} %collective-permute-done), channel_id=1, source_target_pairs={{2,4},{4,6},{3,5},{5,7},{10,12},{12,14},{11,13},{13,15},{18,20},{2... | collective-permute-start | bytes 3538952 | tf_op jit(solution)/shard_map/ppermute | solution.py:545
  56.9 30.4 %collective-permute-start.3 = (bf16[256,2304]{1,0:T(8,128)(2,1)}, bf16[256,2304]{1,0:T(8,128)(2,1)}, u32[]{:S(2)}, u32[]{:S(2)}) collective-permute-start(bf16[256,2304]{1,0:T(8,128)(2,1)} %collective-permute-done.1), channel_id=1, source_target_pairs={{2,0},{4,2},{3,1},{5,3},{10,8},{12,10},{11,9},{13,11},{18,16},{20,... | collective-permute-start | bytes 3538952 | tf_op jit(solution)/shard_map/ppermute | solution.py:546
  87.3 193.1 %all-gather.10.cloned.1.call-start = ((), (), s32[]{:S(2)}) async-start(), calls=%async_computation.6 | async-start | bytes 7962624 | tf_op jit(solution)/shard_map/all_gather | solution.py:677
  98.8 30.1 %collective-permute-start.6 = (bf16[256,2304]{1,0:T(8,128)(2,1)}, bf16[256,2304]{1,0:T(8,128)(2,1)}, u32[]{:S(2)}, u32[]{:S(2)}) collective-permute-start(bf16[256,2304]{1,0:T(8,128)(2,1)} %collective-permute-done.3), channel_id=1, source_target_pairs={{2,0},{3,1},{10,8},{11,9},{18,16},{19,17},{26,24},{27,25}} | collective-permute-start | bytes 3538952 | tf_op jit(solution)/shard_map/ppermute | solution.py:546
  128.8 211.6 %all-gather.12.cloned.1.call-start = ((), (), s32[]{:S(2)}) async-start(), calls=%async_computation.7 | async-start | bytes 15261696 | tf_op jit(solution)/shard_map/all_gather | solution.py:677
  130.7 29.0 %collective-permute-start.10 = (bf16[256,2304]{1,0:T(8,128)(2,1)S(1)}, bf16[256,2304]{1,0:T(8,128)(2,1)}, u32[]{:S(2)}, u32[]{:S(2)}) collective-permute-start(bf16[256,2304]{1,0:T(8,128)(2,1)S(1)} %dynamic-slice_bitcast_fusion), channel_id=1, source_target_pairs={{2,0},{4,2},{6,4},{3,1},{5,3},{7,5},{10,8},{12,10},{14,12},{11,9},... | collective-permute-start | bytes 3538952 | tf_op jit(solution)/shard_map/ppermute | solution.py:546
  132.0 28.8 %collective-permute-start.9 = (bf16[256,2304]{1,0:T(8,128)(2,1)S(1)}, bf16[256,2304]{1,0:T(8,128)(2,1)}, u32[]{:S(2)}, u32[]{:S(2)}) collective-permute-start(bf16[256,2304]{1,0:T(8,128)(2,1)S(1)} %dynamic-slice_bitcast_fusion), channel_id=1, source_target_pairs={{0,2},{2,4},{4,6},{1,3},{3,5},{5,7},{8,10},{10,12},{12,14},{9,11},... | collective-permute-start | bytes 3538952 | tf_op jit(solution)/shard_map/ppermute | solution.py:545
  160.8 430.7 %reduce-scatter.5.cloned.1.call-start = ((), (), s32[]{:S(2)}) async-start(), calls=%async_computation.8 | async-start | bytes 15261696 | tf_op jit(solution)/shard_map/reduce_scatter | solution.py:680
  160.9 39.9 %collective-permute-start.12 = (bf16[256,2304]{1,0:T(8,128)(2,1)}, bf16[256,2304]{1,0:T(8,128)(2,1)}, u32[]{:S(2)}, u32[]{:S(2)}) collective-permute-start(bf16[256,2304]{1,0:T(8,128)(2,1)} %collective-permute-done.9), channel_id=1, source_target_pairs={{2,4},{4,6},{3,5},{5,7},{10,12},{12,14},{11,13},{13,15},{18,20},{2... | collective-permute-start | bytes 3538952 | tf_op jit(solution)/shard_map/ppermute | solution.py:545
  162.6 38.2 %collective-permute-start.13 = (bf16[256,2304]{1,0:T(8,128)(2,1)}, bf16[256,2304]{1,0:T(8,128)(2,1)}, u32[]{:S(2)}, u32[]{:S(2)}) collective-permute-start(bf16[256,2304]{1,0:T(8,128)(2,1)} %collective-permute-done.10), channel_id=1, source_target_pairs={{2,0},{4,2},{3,1},{5,3},{10,8},{12,10},{11,9},{13,11},{18,16},{20,... | collective-permute-start | bytes 3538952 | tf_op jit(solution)/shard_map/ppermute | solution.py:546
  207.3 30.0 %collective-permute-start.14 = (bf16[256,2304]{1,0:T(8,128)(2,1)S(1)}, bf16[256,2304]{1,0:T(8,128)(2,1)S(1)}, u32[]{:S(2)}, u32[]{:S(2)}) collective-permute-start(bf16[256,2304]{1,0:T(8,128)(2,1)S(1)} %slice.134), channel_id=1, source_target_pairs={{0,2},{1,3},{8,10},{9,11},{16,18},{17,19},{24,26},{25,27}} | collective-permute-start | bytes 3538952 | tf_op jit(solution)/shard_map/ppermute | solution.py:601
  214.4 22.9 %collective-permute-start.15 = (bf16[256,2304]{1,0:T(8,128)(2,1)S(1)}, bf16[256,2304]{1,0:T(8,128)(2,1)S(1)}, u32[]{:S(2)}, u32[]{:S(2)}) collective-permute-start(bf16[256,2304]{1,0:T(8,128)(2,1)S(1)} %slice.134), channel_id=1, source_target_pairs={{6,4},{7,5},{14,12},{15,13},{22,20},{23,21},{30,28},{31,29}} | collective-permute-start | bytes 3538952 | tf_op jit(solution)/shard_map/ppermute | solution.py:602
  215.1 22.2 %collective-permute-start.16 = (bf16[256,2304]{1,0:T(8,128)(2,1)}, bf16[256,2304]{1,0:T(8,128)(2,1)S(1)}, u32[]{:S(2)}, u32[]{:S(2)}) collective-permute-start(bf16[256,2304]{1,0:T(8,128)(2,1)} %collective-permute-done.12), channel_id=1, source_target_pairs={{4,6},{5,7},{12,14},{13,15},{20,22},{21,23},{28,30},{29,31}} | collective-permute-start | bytes 3538952 | tf_op jit(solution)/shard_map/ppermute | solution.py:545
  215.9 27.7 %collective-permute-start.17 = (bf16[256,2304]{1,0:T(8,128)(2,1)}, bf16[256,2304]{1,0:T(8,128)(2,1)S(1)}, u32[]{:S(2)}, u32[]{:S(2)}) collective-permute-start(bf16[256,2304]{1,0:T(8,128)(2,1)} %collective-permute-done.13), channel_id=1, source_target_pairs={{2,0},{3,1},{10,8},{11,9},{18,16},{19,17},{26,24},{27,25}} | collective-permute-start | bytes 3538952 | tf_op jit(solution)/shard_map/ppermute | solution.py:546
  244.1 23.9 %collective-permute-start.18 = (bf16[256,2304]{1,0:T(8,128)(2,1)S(1)}, bf16[256,2304]{1,0:T(8,128)(2,1)S(1)}, u32[]{:S(2)}, u32[]{:S(2)}) collective-permute-start(bf16[256,2304]{1,0:T(8,128)(2,1)S(1)} %get-tuple-element.298), channel_id=1, source_target_pairs={{0,2},{2,4},{1,3},{3,5},{8,10},{10,12},{9,11},{11,13},{16,18},{18,... | collective-permute-start | bytes 3538952 | tf_op jit(solution)/shard_map/ppermute | solution.py:601
  245.8 22.3 %collective-permute-start.19 = (bf16[256,2304]{1,0:T(8,128)(2,1)S(1)}, bf16[256,2304]{1,0:T(8,128)(2,1)S(1)}, u32[]{:S(2)}, u32[]{:S(2)}) collective-permute-start(bf16[256,2304]{1,0:T(8,128)(2,1)S(1)} %get-tuple-element.297), channel_id=1, source_target_pairs={{4,2},{6,4},{5,3},{7,5},{12,10},{14,12},{13,11},{15,13},{20,18},{2... | collective-permute-start | bytes 3538952 | tf_op jit(solution)/shard_map/ppermute | solution.py:602
  270.2 28.7 %collective-permute-start.20 = (bf16[256,2304]{1,0:T(8,128)(2,1)}, bf16[256,2304]{1,0:T(8,128)(2,1)}, u32[]{:S(2)}, u32[]{:S(2)}) collective-permute-start(bf16[256,2304]{1,0:T(8,128)(2,1)} %get-tuple-element.296), channel_id=1, source_target_pairs={{0,2},{2,4},{4,6},{1,3},{3,5},{5,7},{8,10},{10,12},{12,14},{9,11},... | collective-permute-start | bytes 3538952 | tf_op jit(solution)/shard_map/ppermute | solution.py:601
  278.9 25.2 %collective-permute-start.21 = (bf16[256,2304]{1,0:T(8,128)(2,1)}, bf16[256,2304]{1,0:T(8,128)(2,1)}, u32[]{:S(2)}, u32[]{:S(2)}) collective-permute-start(bf16[256,2304]{1,0:T(8,128)(2,1)} %get-tuple-element.295), channel_id=1, source_target_pairs={{2,0},{4,2},{6,4},{3,1},{5,3},{7,5},{10,8},{12,10},{14,12},{11,9},... | collective-permute-start | bytes 3538952 | tf_op jit(solution)/shard_map/ppermute | solution.py:602
  309.3 21.2 %collective-permute-start.22 = (bf16[256,2304]{1,0:T(8,128)(2,1)S(1)}, bf16[256,2304]{1,0:T(8,128)(2,1)S(1)}, u32[]{:S(2)}, u32[]{:S(2)}) collective-permute-start(bf16[256,2304]{1,0:T(8,128)(2,1)S(1)} %multiply_convert_fusion.9), channel_id=1, source_target_pairs={{0,2},{2,4},{4,6},{1,3},{3,5},{5,7},{8,10},{10,12},{12,14},{9,11},... | collective-permute-start | bytes 3538952 | tf_op jit(solution)/shard_map/ppermute | solution.py:545
  310.8 23.9 %collective-permute-start.23 = (bf16[256,2304]{1,0:T(8,128)(2,1)S(1)}, bf16[256,2304]{1,0:T(8,128)(2,1)}, u32[]{:S(2)}, u32[]{:S(2)}) collective-permute-start(bf16[256,2304]{1,0:T(8,128)(2,1)S(1)} %multiply_convert_fusion.9), channel_id=1, source_target_pairs={{2,0},{4,2},{6,4},{3,1},{5,3},{7,5},{10,8},{12,10},{14,12},{11,9},... | collective-permute-start | bytes 3538952 | tf_op jit(solution)/shard_map/ppermute | solution.py:546
  334.7 29.2 %collective-permute-start.24 = (bf16[256,2304]{1,0:T(8,128)(2,1)S(1)}, bf16[256,2304]{1,0:T(8,128)(2,1)}, u32[]{:S(2)}, u32[]{:S(2)}) collective-permute-start(bf16[256,2304]{1,0:T(8,128)(2,1)S(1)} %collective-permute-done.22), channel_id=1, source_target_pairs={{2,4},{4,6},{3,5},{5,7},{10,12},{12,14},{11,13},{13,15},{18,20},{2... | collective-permute-start | bytes 3538952 | tf_op jit(solution)/shard_map/ppermute | solution.py:545
  336.4 27.5 %collective-permute-start.25 = (bf16[256,2304]{1,0:T(8,128)(2,1)}, bf16[256,2304]{1,0:T(8,128)(2,1)}, u32[]{:S(2)}, u32[]{:S(2)}) collective-permute-start(bf16[256,2304]{1,0:T(8,128)(2,1)} %collective-permute-done.23), channel_id=1, source_target_pairs={{2,0},{4,2},{3,1},{5,3},{10,8},{12,10},{11,9},{13,11},{18,16},{20,... | collective-permute-start | bytes 3538952 | tf_op jit(solution)/shard_map/ppermute | solution.py:546
  364.0 17.7 %collective-permute-start.26 = (bf16[256,2304]{1,0:T(8,128)(2,1)}, bf16[256,2304]{1,0:T(8,128)(2,1)S(1)}, u32[]{:S(2)}, u32[]{:S(2)}) collective-permute-start(bf16[256,2304]{1,0:T(8,128)(2,1)} %collective-permute-done.24), channel_id=1, source_target_pairs={{4,6},{5,7},{12,14},{13,15},{20,22},{21,23},{28,30},{29,31}} | collective-permute-start | bytes 3538952 | tf_op jit(solution)/shard_map/ppermute | solution.py:545
  364.7 23.5 %collective-permute-start.27 = (bf16[256,2304]{1,0:T(8,128)(2,1)}, bf16[256,2304]{1,0:T(8,128)(2,1)S(1)}, u32[]{:S(2)}, u32[]{:S(2)}) collective-permute-start(bf16[256,2304]{1,0:T(8,128)(2,1)} %collective-permute-done.25), channel_id=1, source_target_pairs={{2,0},{3,1},{10,8},{11,9},{18,16},{19,17},{26,24},{27,25}} | collective-permute-start | bytes 3538952 | tf_op jit(solution)/shard_map/ppermute | solution.py:546
  431.7 29.7 %collective-permute-start.28 = (bf16[256,2304]{1,0:T(8,128)(2,1)}, bf16[256,2304]{1,0:T(8,128)(2,1)}, u32[]{:S(2)}, u32[]{:S(2)}) collective-permute-start(bf16[256,2304]{1,0:T(8,128)(2,1)} %slice.112), channel_id=1, source_target_pairs={{0,2},{1,3},{8,10},{9,11},{16,18},{17,19},{24,26},{25,27}} | collective-permute-start | bytes 3538952 | tf_op jit(solution)/shard_map/ppermute | solution.py:601
  435.5 25.9 %collective-permute-start.29 = (bf16[256,2304]{1,0:T(8,128)(2,1)}, bf16[256,2304]{1,0:T(8,128)(2,1)}, u32[]{:S(2)}, u32[]{:S(2)}) collective-permute-start(bf16[256,2304]{1,0:T(8,128)(2,1)} %slice.112), channel_id=1, source_target_pairs={{6,4},{7,5},{14,12},{15,13},{22,20},{23,21},{30,28},{31,29}} | collective-permute-start | bytes 3538952 | tf_op jit(solution)/shard_map/ppermute | solution.py:602
  461.4 172.8 %reduce-scatter.7.cloned.1.call-start = ((), (), s32[]{:S(2)}) async-start(), calls=%async_computation.9 | async-start | bytes 7962624 | tf_op jit(solution)/shard_map/reduce_scatter | solution.py:680
  465.1 19.6 %collective-permute-start.30 = (bf16[256,2304]{1,0:T(8,128)(2,1)}, bf16[256,2304]{1,0:T(8,128)(2,1)}, u32[]{:S(2)}, u32[]{:S(2)}) collective-permute-start(bf16[256,2304]{1,0:T(8,128)(2,1)} %get-tuple-element.306), channel_id=1, source_target_pairs={{0,2},{2,4},{1,3},{3,5},{8,10},{10,12},{9,11},{11,13},{16,18},{18,... | collective-permute-start | bytes 3538952 | tf_op jit(solution)/shard_map/ppermute | solution.py:601
  489.2 24.1 %collective-permute-start.32 = (bf16[256,2304]{1,0:T(8,128)(2,1)}, bf16[256,2304]{1,0:T(8,128)(2,1)}, u32[]{:S(2)}, u32[]{:S(2)}) collective-permute-start(bf16[256,2304]{1,0:T(8,128)(2,1)} %get-tuple-element.294), channel_id=1, source_target_pairs={{0,2},{2,4},{4,6},{1,3},{3,5},{5,7},{8,10},{10,12},{12,14},{9,11},... | collective-permute-start | bytes 3538952 | tf_op jit(solution)/shard_map/ppermute | solution.py:601
  496.0 22.4 %collective-permute-start.33 = (bf16[256,2304]{1,0:T(8,128)(2,1)}, bf16[256,2304]{1,0:T(8,128)(2,1)}, u32[]{:S(2)}, u32[]{:S(2)}) collective-permute-start(bf16[256,2304]{1,0:T(8,128)(2,1)} %get-tuple-element.293), channel_id=1, source_target_pairs={{2,0},{4,2},{6,4},{3,1},{5,3},{7,5},{10,8},{12,10},{14,12},{11,9},... | collective-permute-start | bytes 3538952 | tf_op jit(solution)/shard_map/ppermute | solution.py:602
  497.3 198.9 %reduce-scatter.9.cloned.1.call-start = ((), (), s32[]{:S(2)}) async-start(), calls=%async_computation.10 | async-start | bytes 3317760 | tf_op jit(solution)/shard_map/reduce_scatter | solution.py:680
  525.2 22.0 %collective-permute-start.34 = (bf16[256,2304]{1,0:T(8,128)(2,1)S(1)}, bf16[256,2304]{1,0:T(8,128)(2,1)S(1)}, u32[]{:S(2)}, u32[]{:S(2)}) collective-permute-start(bf16[256,2304]{1,0:T(8,128)(2,1)S(1)} %get-tuple-element.267), channel_id=1, source_target_pairs={{0,2},{2,4},{4,6},{1,3},{3,5},{5,7},{8,10},{10,12},{12,14},{9,11},... | collective-permute-start | bytes 3538952 | tf_op jit(solution)/shard_map/ppermute | solution.py:545
  527.6 21.5 %collective-permute-start.35 = (bf16[256,2304]{1,0:T(8,128)(2,1)S(1)}, bf16[256,2304]{1,0:T(8,128)(2,1)S(1)}, u32[]{:S(2)}, u32[]{:S(2)}) collective-permute-start(bf16[256,2304]{1,0:T(8,128)(2,1)S(1)} %get-tuple-element.267), channel_id=1, source_target_pairs={{2,0},{4,2},{6,4},{3,1},{5,3},{7,5},{10,8},{12,10},{14,12},{11,9},... | collective-permute-start | bytes 3538952 | tf_op jit(solution)/shard_map/ppermute | solution.py:546
  549.1 22.4 %collective-permute-start.38 = (bf16[256,2304]{1,0:T(8,128)(2,1)S(1)}, bf16[256,2304]{1,0:T(8,128)(2,1)S(1)}, u32[]{:S(2)}, u32[]{:S(2)}) collective-permute-start(bf16[256,2304]{1,0:T(8,128)(2,1)S(1)} %slice.115), channel_id=1, source_target_pairs={{0,2},{1,3},{8,10},{9,11},{16,18},{17,19},{24,26},{25,27}} | collective-permute-start | bytes 3538952 | tf_op jit(solution)/shard_map/ppermute | solution.py:601
  551.7 19.8 %collective-permute-start.39 = (bf16[256,2304]{1,0:T(8,128)(2,1)S(1)}, bf16[256,2304]{1,0:T(8,128)(2,1)S(1)}, u32[]{:S(2)}, u32[]{:S(2)}) collective-permute-start(bf16[256,2304]{1,0:T(8,128)(2,1)S(1)} %slice.115), channel_id=1, source_target_pairs={{6,4},{7,5},{14,12},{15,13},{22,20},{23,21},{30,28},{31,29}} | collective-permute-start | bytes 3538952 | tf_op jit(solution)/shard_map/ppermute | solution.py:602
  552.5 19.1 %collective-permute-start.36 = (bf16[256,2304]{1,0:T(8,128)(2,1)S(1)}, bf16[256,2304]{1,0:T(8,128)(2,1)}, u32[]{:S(2)}, u32[]{:S(2)}) collective-permute-start(bf16[256,2304]{1,0:T(8,128)(2,1)S(1)} %collective-permute-done.34), channel_id=1, source_target_pairs={{2,4},{4,6},{3,5},{5,7},{10,12},{12,14},{11,13},{13,15},{18,20},{2... | collective-permute-start | bytes 3538952 | tf_op jit(solution)/shard_map/ppermute | solution.py:545
  554.2 20.4 %collective-permute-start.37 = (bf16[256,2304]{1,0:T(8,128)(2,1)S(1)}, bf16[256,2304]{1,0:T(8,128)(2,1)}, u32[]{:S(2)}, u32[]{:S(2)}) collective-permute-start(bf16[256,2304]{1,0:T(8,128)(2,1)S(1)} %collective-permute-done.35), channel_id=1, source_target_pairs={{2,0},{4,2},{3,1},{5,3},{10,8},{12,10},{11,9},{13,11},{18,16},{20,... | collective-permute-start | bytes 3538952 | tf_op jit(solution)/shard_map/ppermute | solution.py:546
  576.0 20.8 %collective-permute-start.42 = (bf16[256,2304]{1,0:T(8,128)(2,1)}, bf16[256,2304]{1,0:T(8,128)(2,1)}, u32[]{:S(2)}, u32[]{:S(2)}) collective-permute-start(bf16[256,2304]{1,0:T(8,128)(2,1)} %get-tuple-element.292), channel_id=1, source_target_pairs={{0,2},{2,4},{1,3},{3,5},{8,10},{10,12},{9,11},{11,13},{16,18},{18,... | collective-permute-start | bytes 3538952 | tf_op jit(solution)/shard_map/ppermute | solution.py:601
  587.0 22.0 %collective-permute-start.41 = (bf16[256,2304]{1,0:T(8,128)(2,1)}, bf16[256,2304]{1,0:T(8,128)(2,1)}, u32[]{:S(2)}, u32[]{:S(2)}) collective-permute-start(bf16[256,2304]{1,0:T(8,128)(2,1)} %collective-permute-done.37), channel_id=1, source_target_pairs={{2,0},{3,1},{10,8},{11,9},{18,16},{19,17},{26,24},{27,25}} | collective-permute-start | bytes 3538952 | tf_op jit(solution)/shard_map/ppermute | solution.py:546
  613.5 26.1 %collective-permute-start.44 = (bf16[256,2304]{1,0:T(8,128)(2,1)}, bf16[256,2304]{1,0:T(8,128)(2,1)}, u32[]{:S(2)}, u32[]{:S(2)}) collective-permute-start(bf16[256,2304]{1,0:T(8,128)(2,1)} %get-tuple-element.290), channel_id=1, source_target_pairs={{0,2},{2,4},{4,6},{1,3},{3,5},{5,7},{8,10},{10,12},{12,14},{9,11},... | collective-permute-start | bytes 3538952 | tf_op jit(solution)/shard_map/ppermute | solution.py:601
  616.0 23.6 %collective-permute-start.45 = (bf16[256,2304]{1,0:T(8,128)(2,1)}, bf16[256,2304]{1,0:T(8,128)(2,1)}, u32[]{:S(2)}, u32[]{:S(2)}) collective-permute-start(bf16[256,2304]{1,0:T(8,128)(2,1)} %get-tuple-element.289), channel_id=1, source_target_pairs={{2,0},{4,2},{6,4},{3,1},{5,3},{7,5},{10,8},{12,10},{14,12},{11,9},... | collective-permute-start | bytes 3538952 | tf_op jit(solution)/shard_map/ppermute | solution.py:602
  639.6 134.4 %reduce-scatter.11.cloned.1.call-start = ((), (), s32[]{:S(2)}) async-start(), calls=%async_computation.11 | async-start | bytes 9953280 | tf_op jit(solution)/shard_map/reduce_scatter | solution.py:680
  639.6 56.5 %collective-permute-start.46 = (bf16[288,4352]{1,0:T(8,128)(2,1)}, bf16[288,4352]{1,0:T(8,128)(2,1)}, u32[]{:S(2)}, u32[]{:S(2)}) collective-permute-start(bf16[288,4352]{1,0:T(8,128)(2,1)} %concatenate.65), channel_id=1, source_target_pairs={{0,2},{2,4},{4,6},{1,3},{3,5},{5,7},{8,10},{10,12},{12,14},{9,11},... | collective-permute-start | bytes 7520264 | tf_op jit(solution)/shard_map/ppermute | solution.py:545
  644.4 51.7 %collective-permute-start.47 = (bf16[288,4352]{1,0:T(8,128)(2,1)}, bf16[288,4352]{1,0:T(8,128)(2,1)}, u32[]{:S(2)}, u32[]{:S(2)}) collective-permute-start(bf16[288,4352]{1,0:T(8,128)(2,1)} %concatenate.65), channel_id=1, source_target_pairs={{2,0},{4,2},{6,4},{3,1},{5,3},{7,5},{10,8},{12,10},{14,12},{11,9},... | collective-permute-start | bytes 7520264 | tf_op jit(solution)/shard_map/ppermute | solution.py:546
  696.2 41.3 %collective-permute-start.48 = (bf16[288,4352]{1,0:T(8,128)(2,1)}, bf16[288,4352]{1,0:T(8,128)(2,1)}, u32[]{:S(2)}, u32[]{:S(2)}) collective-permute-start(bf16[288,4352]{1,0:T(8,128)(2,1)} %collective-permute-done.46), channel_id=1, source_target_pairs={{2,4},{4,6},{3,5},{5,7},{10,12},{12,14},{11,13},{13,15},{18,20},{2... | collective-permute-start | bytes 7520264 | tf_op jit(solution)/shard_map/ppermute | solution.py:545
  698.3 53.8 %collective-permute-start.49 = (bf16[288,4352]{1,0:T(8,128)(2,1)}, bf16[288,4352]{1,0:T(8,128)(2,1)}, u32[]{:S(2)}, u32[]{:S(2)}) collective-permute-start(bf16[288,4352]{1,0:T(8,128)(2,1)} %collective-permute-done.47), channel_id=1, source_target_pairs={{2,0},{4,2},{3,1},{5,3},{10,8},{12,10},{11,9},{13,11},{18,16},{20,... | collective-permute-start | bytes 7520264 | tf_op jit(solution)/shard_map/ppermute | solution.py:546
  713.1 24.4 %collective-permute-start.50 = (bf16[256,2304]{1,0:T(8,128)(2,1)S(1)}, bf16[256,2304]{1,0:T(8,128)(2,1)S(1)}, u32[]{:S(2)}, u32[]{:S(2)}) collective-permute-start(bf16[256,2304]{1,0:T(8,128)(2,1)S(1)} %slice.141), channel_id=1, source_target_pairs={{0,2},{1,3},{8,10},{9,11},{16,18},{17,19},{24,26},{25,27}} | collective-permute-start | bytes 3538952 | tf_op jit(solution)/shard_map/ppermute | solution.py:601
  719.5 18.0 %collective-permute-start.51 = (bf16[256,2304]{1,0:T(8,128)(2,1)S(1)}, bf16[256,2304]{1,0:T(8,128)(2,1)S(1)}, u32[]{:S(2)}, u32[]{:S(2)}) collective-permute-start(bf16[256,2304]{1,0:T(8,128)(2,1)S(1)} %slice.141), channel_id=1, source_target_pairs={{6,4},{7,5},{14,12},{15,13},{22,20},{23,21},{30,28},{31,29}} | collective-permute-start | bytes 3538952 | tf_op jit(solution)/shard_map/ppermute | solution.py:602
  752.1 30.6 %collective-permute-start.52 = (bf16[288,4352]{1,0:T(8,128)(2,1)}, bf16[288,4352]{1,0:T(8,128)(2,1)}, u32[]{:S(2)}, u32[]{:S(2)}) collective-permute-start(bf16[288,4352]{1,0:T(8,128)(2,1)} %collective-permute-done.48), channel_id=1, source_target_pairs={{4,6},{5,7},{12,14},{13,15},{20,22},{21,23},{28,30},{29,31}} | collective-permute-start | bytes 7520264 | tf_op jit(solution)/shard_map/ppermute | solution.py:545
  754.4 50.6 %collective-permute-start.53 = (bf16[288,4352]{1,0:T(8,128)(2,1)}, bf16[288,4352]{1,0:T(8,128)(2,1)}, u32[]{:S(2)}, u32[]{:S(2)}) collective-permute-start(bf16[288,4352]{1,0:T(8,128)(2,1)} %collective-permute-done.49), channel_id=1, source_target_pairs={{2,0},{3,1},{10,8},{11,9},{18,16},{19,17},{26,24},{27,25}} | collective-permute-start | bytes 7520264 | tf_op jit(solution)/shard_map/ppermute | solution.py:546
  757.5 25.1 %collective-permute-start.54 = (bf16[256,2304]{1,0:T(8,128)(2,1)}, bf16[256,2304]{1,0:T(8,128)(2,1)}, u32[]{:S(2)}, u32[]{:S(2)}) collective-permute-start(bf16[256,2304]{1,0:T(8,128)(2,1)} %get-tuple-element.288), channel_id=1, source_target_pairs={{0,2},{2,4},{1,3},{3,5},{8,10},{10,12},{9,11},{11,13},{16,18},{18,... | collective-permute-start | bytes 3538952 | tf_op jit(solution)/shard_map/ppermute | solution.py:601
  764.5 18.1 %collective-permute-start.55 = (bf16[256,2304]{1,0:T(8,128)(2,1)}, bf16[256,2304]{1,0:T(8,128)(2,1)}, u32[]{:S(2)}, u32[]{:S(2)}) collective-permute-start(bf16[256,2304]{1,0:T(8,128)(2,1)} %get-tuple-element.287), channel_id=1, source_target_pairs={{4,2},{6,4},{5,3},{7,5},{12,10},{14,12},{13,11},{15,13},{20,18},{2... | collective-permute-start | bytes 3538952 | tf_op jit(solution)/shard_map/ppermute | solution.py:602
  814.6 21.5 %collective-permute-start.60 = (bf16[2,288,4352]{2,1,0:T(8,128)(2,1)}, bf16[2,288,4352]{2,1,0:T(8,128)(2,1)}, u32[]{:S(2)}, u32[]{:S(2)}) collective-permute-start(bf16[2,288,4352]{2,1,0:T(8,128)(2,1)} %pad_maximum_fusion.1), channel_id=1, source_target_pairs={{0,1},{1,0},{2,3},{3,2},{4,5},{5,4},{6,7},{7,6},{8,9},{9,8},{10,11... | collective-permute-start | bytes 15040520 | tf_op jit(solution)/shard_map/ppermute | solution.py:694
  814.6 64.6 %collective-permute-start.58 = (bf16[288,2560]{1,0:T(8,128)(2,1)}, bf16[288,2560]{1,0:T(8,128)(2,1)}, u32[]{:S(2)}, u32[]{:S(2)}) collective-permute-start(bf16[288,2560]{1,0:T(8,128)(2,1)} %concatenate.66), channel_id=1, source_target_pairs={{0,2},{2,4},{4,6},{1,3},{3,5},{5,7},{8,10},{10,12},{12,14},{9,11},... | collective-permute-start | bytes 4423688 | tf_op jit(solution)/shard_map/ppermute | solution.py:545
  817.2 62.0 %collective-permute-start.59 = (bf16[288,2560]{1,0:T(8,128)(2,1)}, bf16[288,2560]{1,0:T(8,128)(2,1)}, u32[]{:S(2)}, u32[]{:S(2)}) collective-permute-start(bf16[288,2560]{1,0:T(8,128)(2,1)} %concatenate.66), channel_id=1, source_target_pairs={{2,0},{4,2},{6,4},{3,1},{5,3},{7,5},{10,8},{12,10},{14,12},{11,9},... | collective-permute-start | bytes 4423688 | tf_op jit(solution)/shard_map/ppermute | solution.py:546
  822.9 51.1 %collective-permute-start.56 = (bf16[256,2304]{1,0:T(8,128)(2,1)}, bf16[256,2304]{1,0:T(8,128)(2,1)}, u32[]{:S(2)}, u32[]{:S(2)}) collective-permute-start(bf16[256,2304]{1,0:T(8,128)(2,1)} %get-tuple-element.286), channel_id=1, source_target_pairs={{0,2},{2,4},{4,6},{1,3},{3,5},{5,7},{8,10},{10,12},{12,14},{9,11},... | collective-permute-start | bytes 3538952 | tf_op jit(solution)/shard_map/ppermute | solution.py:601
  828.4 50.7 %collective-permute-start.57 = (bf16[256,2304]{1,0:T(8,128)(2,1)}, bf16[256,2304]{1,0:T(8,128)(2,1)}, u32[]{:S(2)}, u32[]{:S(2)}) collective-permute-start(bf16[256,2304]{1,0:T(8,128)(2,1)} %get-tuple-element.285), channel_id=1, source_target_pairs={{2,0},{4,2},{6,4},{3,1},{5,3},{7,5},{10,8},{12,10},{14,12},{11,9},... | collective-permute-start | bytes 3538952 | tf_op jit(solution)/shard_map/ppermute | solution.py:602
  836.9 79.0 %collective-permute-start.65 = (bf16[256,2304]{1,0:T(8,128)(2,1)S(1)}, bf16[256,2304]{1,0:T(8,128)(2,1)S(1)}, u32[]{:S(2)}, u32[]{:S(2)}) collective-permute-start(bf16[256,2304]{1,0:T(8,128)(2,1)S(1)} %copy-done.41), channel_id=1, source_target_pairs={{0,1},{1,0},{2,3},{3,2},{4,5},{5,4},{6,7},{7,6},{8,9},{9,8},{10,11... | collective-permute-start | bytes 3538952 | tf_op jit(solution)/shard_map/ppermute | solution.py:898
  880.1 35.8 %collective-permute-start.62 = (bf16[288,2560]{1,0:T(8,128)(2,1)}, bf16[288,2560]{1,0:T(8,128)(2,1)S(1)}, u32[]{:S(2)}, u32[]{:S(2)}) collective-permute-start(bf16[288,2560]{1,0:T(8,128)(2,1)} %collective-permute-done.59), channel_id=1, source_target_pairs={{2,0},{4,2},{3,1},{5,3},{10,8},{12,10},{11,9},{13,11},{18,16},{20,... | collective-permute-start | bytes 4423688 | tf_op jit(solution)/shard_map/ppermute | solution.py:546
  916.8 36.6 %collective-permute-start.64 = (bf16[288,2560]{1,0:T(8,128)(2,1)S(1)}, bf16[288,2560]{1,0:T(8,128)(2,1)S(1)}, u32[]{:S(2)}, u32[]{:S(2)}) collective-permute-start(bf16[288,2560]{1,0:T(8,128)(2,1)S(1)} %collective-permute-done.62), channel_id=1, source_target_pairs={{2,0},{3,1},{10,8},{11,9},{18,16},{19,17},{26,24},{27,25}} | collective-permute-start | bytes 4423688 | tf_op jit(solution)/shard_map/ppermute | solution.py:546
  (90 other events, 1495.2 us)
Sparse Core Ops, SparseCore 0:
  18.9 59.9 all-gather.5
  87.4 29.5 all-gather.7
  129.0 46.9 all-gather.9
  178.3 76.1 all-gather.11
  461.5 97.2 reduce-scatter.4
  562.2 65.4 reduce-scatter.6
  639.7 47.3 reduce-scatter.8
  696.3 77.5 reduce-scatter.10

commit v8 on v7

--- a/solution.py
+++ b/solution.py
@@ -339,17 +339,20 @@
 
 
 def attend_kernel(
-    heads, span, order, length, q_in, k_in, v_in, cos, sin, out, q_out, k_out, v_out, log_out,
-    q_sort, k_sort, v_sort, turned,
+    heads, span, order, length, q_near, k_near, v_near, q_far, k_far, v_far, cos, sin,
+    out, q_out, k_out, v_out, log_out, q_sort, k_sort, v_sort, turned,
 ):
-    rows = q_in.shape[0]
+    rows = q_out.shape[0]
     pair = pl.program_id(0)
     for block in range(rows // span):
         place = pl.ds(pl.multiple_of(order[block] * span, span), span)
-        stored = slice(block * span, (block + 1) * span)
-        q_sort[place, :] = q_in[stored, :]
-        k_sort[place, :] = k_in[stored, :]
-        v_sort[place, :] = v_in[stored, :]
+        start = block * span
+        near = start < q_near.shape[0]
+        start -= 0 if near else q_near.shape[0]
+        stored = slice(start, start + span)
+        q_sort[place, :] = (q_near if near else q_far)[stored, :]
+        k_sort[place, :] = (k_near if near else k_far)[stored, :]
+        v_sort[place, :] = (v_near if near else v_far)[stored, :]
     queries = q_sort[...]
     keys = k_sort[...]
     q_out[...] = (queries * cos[...] + lane_partner(queries) * sin[...]).astype(jnp.bfloat16)
@@ -442,10 +445,10 @@
         copy.wait()
 
 
-def attend_forward(heads, span, order, length, qkv, cos, sin):
-    rows = qkv.shape[0]
-    pairs = qkv.shape[1] // (3 * LANES)
-    column = lambda offset: pl.BlockSpec((rows, LANES), lambda i, *_: (0, offset + i))
+def attend_forward(heads, span, order, length, near, far, cos, sin):
+    rows = near.shape[0] + far.shape[0]
+    pairs = near.shape[1] // (3 * LANES)
+    column = lambda v, offset: pl.BlockSpec((v.shape[0], LANES), lambda i, *_: (0, offset + i))
     fixed = pl.BlockSpec((rows, LANES), lambda i, *_: (0, 0))
     flat = jax.ShapeDtypeStruct((rows, pairs * LANES), jnp.bfloat16)
     return pl.pallas_call(
@@ -453,8 +456,8 @@
         grid_spec=pltpu.PrefetchScalarGridSpec(
             num_scalar_prefetch=2,
             grid=(pairs,),
-            in_specs=[column(0), column(pairs), column(2 * pairs), fixed, fixed],
-            out_specs=[column(0)] * 4 + [pl.BlockSpec((1, 8, rows), lambda i, *_: (i, 0, 0))],
+            in_specs=[column(v, k * pairs) for v in (near, far) for k in range(3)] + [fixed, fixed],
+            out_specs=[column(cos, 0)] * 4 + [pl.BlockSpec((1, 8, rows), lambda i, *_: (i, 0, 0))],
             scratch_shapes=[pltpu.VMEM((rows, LANES), jnp.float32)] * 3
             + [pltpu.VMEM((LANES, rows), jnp.float32)],
         ),
@@ -466,7 +469,7 @@
             transcendentals=heads * rows * rows,
         ),
         name="attend",
-    )(order, length, qkv, qkv, qkv, cos, sin)
+    )(order, length, near, near, near, far, far, far, cos, sin)
 
 
 def attend_backward(heads, span, order, length, kept, attend, grad_attend, cos, sin):
@@ -750,31 +753,41 @@
     tokens_line.step()
     out_w = gather_pair(out_mine)
     gate_up_mine = to_pair(column_piece([w_gate, w_up]))
-    own_cot, down_mine, gate_up_mine = stage([tokens_line], own_cot, down_mine, gate_up_mine)
+
+    def first_rows(masks):
+        rows = jnp.concatenate([tokens_line.near(k) for k in masks], axis=0)
+        return (norm_parts(rows.astype(jnp.float32))[0] * gain_a).astype(jnp.bfloat16)
+
+    first_near = first_rows(range(lines // 2))
+    qkv_near = plain_product(first_near, qkv_w)
+    own_cot, down_mine, gate_up_mine, qkv_near = stage(
+        [tokens_line], own_cot, down_mine, gate_up_mine, qkv_near
+    )
     down_w = gather_pair(down_mine)
 
     cot_line = walk(own_cot)
     cot_line.step()
-    all_tokens = jnp.concatenate([tokens_line.near(k) for k in range(lines)], axis=0)
-    first_in = (norm_parts(all_tokens.astype(jnp.float32))[0] * gain_a).astype(jnp.bfloat16)
-    qkv = plain_product(first_in, qkv_w)
-    qkv, gate_up_mine = stage([cot_line], qkv, gate_up_mine)
+    first_far = first_rows(range(lines // 2, lines))
+    qkv_far = plain_product(first_far, qkv_w)
+    qkv_far, gate_up_mine = lax.optimization_barrier((qkv_far, gate_up_mine))
     gate_up_w = gather_pair(gate_up_mine)
-
-    cot_line.step()
-    attend, *kept = attend_forward(heads, span, order, length.reshape(1), qkv, cos_all, sin_all)
-    (attend,) = stage([cot_line], attend)
-
-    cot_line.step()
+    first_in = jnp.concatenate([first_near, first_far], axis=0)
+    attend, *kept = attend_forward(
+        heads, span, order, length.reshape(1), qkv_near, qkv_far, cos_all, sin_all
+    )
     attn_part = col_product(attend, out_w).astype(jnp.bfloat16)
+    (attn_part,) = stage([cot_line], attn_part)
+
     attn_line = add_up(blocks_of(attn_part))
     attn_line.step()
+    cot_line.step()
+    stage([attn_line, cot_line])
+    attn_line.step()
+    cot_line.step()
     stage([attn_line, cot_line])
     attn_line.step()
     all_cot = jnp.concatenate([cot_line.near(k) for k in range(lines)], axis=0)
     grad_mlp = (BRANCH_SCALE * (all_cot.astype(jnp.float32) * live_all)).astype(jnp.bfloat16)
-    (grad_mlp,) = stage([attn_line], grad_mlp)
-    attn_line.step()
     half_rows = all_rows // 2
     grad_hidden = [
         plain_product(grad_mlp[k * half_rows : (k + 1) * half_rows], down_w) for k in range(2)

time: 989 us -> 986 us (level)
  starting transfers between devices: 144 us -> 131 us
  waiting for transfers between devices: 355 us -> 366 us
    ppermute x12, waiting for transfers between devices: 93.9 us -> 104 us  [step(): self.up = lax.ppermute(up, self.axis, [(i, i + 1) for i, _ in ups])]
    dot_general x6 -> x7, matrix products: 78.2 us -> 75.8 us  [plain_product(): return jnp.dot(left_mat, right_mat, preferred_element_type=jnp.float32)]
    unnamed x153 -> x147, local copies, waits for them, and re-layouts: 23.9 us -> 24.7 us
  transfers between devices with their start and end apart: 78 -> 78, of which waited for: 34 -> 33; matrix products, arithmetic and copies ran while one was open for 30% -> 30% of each run, Pallas kernels for 7% -> 7%
where the time goes in v8:
time: 986 us; the launch traced here: 976 us
  waiting for transfers between devices  366 us (37%)
  matrix products  187 us (19%)
  starting transfers between devices  131 us (13%)
  other arithmetic  130 us (13%)
  Pallas kernels  77.3 us (8%)
  local copies, waits for them, and re-layouts  58.8 us (6%)
  between operations  15.7 us (2%)
    ppermute x18, waiting for transfers between devices, step(): self.downs.append(lax.ppermute(self.downs[-1], self.axis, down_pairs))  176 us
    ppermute x12, waiting for transfers between devices, step(): self.up = lax.ppermute(up, self.axis, [(i, i + 1) for i, _ in ups])  104 us
    dot_general x7, matrix products, plain_product(): return jnp.dot(left_mat, right_mat, preferred_element_type=jnp.float32)  75.8 us
    ppermute x18, waiting for transfers between devices, step(): self.ups.append(lax.ppermute(self.ups[-1], self.axis, up_pairs))  59.1 us
    dot_general x5, matrix products, col_product(): lax.dot_general(left_mat, right_mat, CONTRACT_COLS, preferred_element_typ...  58 us
    dot_general x4, matrix products, row_product(): lax.dot_general(left_mat, right_mat, CONTRACT_ROWS, preferred_element_typ...  53.7 us
    ppermute x12, starting transfers between devices, step(): self.up = lax.ppermute(up, self.axis, [(i, i + 1) for i, _ in ups])  52.2 us
    ppermute x18, starting transfers between devices, step(): self.ups.append(lax.ppermute(self.ups[-1], self.axis, up_pairs))  37.2 us
  transfers between devices with their start and end apart: 78, of which 33 were waited for; matrix products, arithmetic and copies ran while one was open for 30% of the time, Pallas kernels for 7%

profile of v8, /device:TPU:0, one launch (start us, length us, event | category | flops | bytes accessed | tf_op | source)
XLA Modules:
  0.0 975.7 jit_solution(719019540714507323)
XLA Ops:
  22.2 5.7 collective-permute-start
  32.3 20.5 %collective-permute-done = bf16[256,2304]{1,0:T(8,128)(2,1)} collective-permute-done((bf16[256,2304]{1,0:T(8,128)(2,1)S(1)}, bf16[256,2304]{1,0:T(8,128)(2,1)}, u32[]{:S(2)}, u32[]{:S(2)}) %collective-permute-start) | collective-permute-done | bytes 1179680 | tf_op jit(solution)/shard_map/ppermute | solution.py:548
  52.8 5.8 collective-permute-done.1
  66.5 8.6 all-gather
  79.3 11.3 %collective-permute-done.3 = bf16[256,2304]{1,0:T(8,128)(2,1)} collective-permute-done((bf16[256,2304]{1,0:T(8,128)(2,1)}, bf16[256,2304]{1,0:T(8,128)(2,1)}, u32[]{:S(2)}, u32[]{:S(2)}) %collective-permute-start.3) | collective-permute-done | bytes 1179680 | tf_op jit(solution)/shard_map/ppermute | solution.py:549
  109.2 10.5 %fusion.77.q_near.k_near.v_near = f32[512,1920]{1,0:T(8,128)} fusion(bf16[512,2304]{1,0:T(8,128)(2,1)S(1)} %copy-done.41, bf16[2304,1920]{1,0:T(8,128)(2,1)} %all-gather.6.cloned.1.call-done), kind=kOutput, calls=%fused_computation.231 | convolution fusion | flops 4529848320 | bytes 15138816 | tf_op jit(solution)/shard_map/dot_general | solution.py:30
  119.7 14.8 %collective-permute-done.6 = bf16[256,2304]{1,0:T(8,128)(2,1)} collective-permute-done((bf16[256,2304]{1,0:T(8,128)(2,1)}, bf16[256,2304]{1,0:T(8,128)(2,1)}, u32[]{:S(2)}, u32[]{:S(2)}) %collective-permute-start.6) | collective-permute-done | bytes 1179680 | tf_op jit(solution)/shard_map/ppermute | solution.py:549
  141.1 7.0 fusion.78.q_far.k_far.v_far
  156.9 29.7 %attend.1 = (bf16[1024,640]{1,0:T(8,128)(2,1)S(1)}, bf16[1024,640]{1,0:T(8,128)(2,1)S(1)}, bf16[1024,640]{1,0:T(8,128)(2,1)S(1)}, bf16[1024,640]{1,0:T(8,128)(2,1)S(1)}, f32[5,8,1024]{2,1,0:T(8,128)S(1)}) custom-call(s32[8]{0:T(128)S(1)} %and_select_fusion.order, s32[1]{0:T(128)} %dynamic_slice.69.length, f32[512,1920]{1,0:T(8,128)S(1)} %copy-done.2, ...), custom_call_target="tpu_custom_call" | custom-call | flops 2415919104 | bytes 15728640 | tf_op jit(solution)/shard_map/attend/pallas_call | solution.py:454
  189.9 6.9 convolution_convert_fusion.4
  197.0 4.5 collective-permute-start.12
  204.3 21.8 %collective-permute-done.12 = bf16[256,2304]{1,0:T(8,128)(2,1)S(1)} collective-permute-done((bf16[256,2304]{1,0:T(8,128)(2,1)S(1)}, bf16[256,2304]{1,0:T(8,128)(2,1)S(1)}, u32[]{:S(2)}, u32[]{:S(2)}) %collective-permute-start.12) | collective-permute-done | bytes 1179680 | tf_op jit(solution)/shard_map/ppermute | solution.py:604
  226.1 5.9 collective-permute-done.15
  238.3 20.3 %collective-permute-done.16 = bf16[256,2304]{1,0:T(8,128)(2,1)S(1)} collective-permute-done((bf16[256,2304]{1,0:T(8,128)(2,1)S(1)}, bf16[256,2304]{1,0:T(8,128)(2,1)S(1)}, u32[]{:S(2)}, u32[]{:S(2)}) %collective-permute-start.16) | collective-permute-done | bytes 1179680 | tf_op jit(solution)/shard_map/ppermute | solution.py:604
  258.5 5.7 collective-permute-done.19
  272.3 4.3 multiply_convert_fusion
  276.6 9.1 fusion.40
  285.7 5.2 fusion.42
  291.0 5.1 collective-permute-done.21
  304.6 20.8 %collective-permute-done.22 = bf16[256,2304]{1,0:T(8,128)(2,1)S(1)} collective-permute-done((bf16[256,2304]{1,0:T(8,128)(2,1)S(1)}, bf16[256,2304]{1,0:T(8,128)(2,1)S(1)}, u32[]{:S(2)}, u32[]{:S(2)}) %collective-permute-start.22) | collective-permute-done | bytes 1179680 | tf_op jit(solution)/shard_map/ppermute | solution.py:548
  325.4 4.3 collective-permute-done.23
  335.3 17.9 %fusion.44 = f32[512,2880]{0,1:T(8,128)} fusion(bf16[2304,2880]{1,0:T(8,128)(2,1)} %all-gather.12.cloned.1.call-done, bf16[256,2304]{1,0:T(8,128)(2,1)} %fusion.55, bf16[256,2304]{1,0:T(8,128)(2,1)} %copy-done.47), kind=kOutput, calls=%fused_computation.109 | convolution fusion | flops 6799491072 | bytes 21528576 | tf_op jit(solution)/shard_map/dot_general | solution.py:30
  353.2 5.4 multiply_convert_fusion.5
  361.3 12.5 %convolution_convert_fusion.8 = bf16[512,2304]{1,0:T(8,128)(2,1)} fusion(bf16[512,2880]{0,1:T(8,128)(2,1)S(1)} %pad_maximum_fusion.5, bf16[2304,2880]{1,0:T(8,128)(2,1)} %all-gather.12.cloned.1.call-done), kind=kOutput, calls=%fused_computation.42 | convolution fusion | flops 6795952128 | bytes 18579456 | tf_op jit(solution)/shard_map/dot_general | solution.py:26
  376.6 9.6 collective-permute-done.27
  387.6 17.9 %fusion.48 = f32[512,2880]{0,1:T(8,128)} fusion(bf16[2304,2880]{1,0:T(8,128)(2,1)} %all-gather.12.cloned.1.call-done, bf16[256,2304]{1,0:T(8,128)(2,1)} %select_select_fusion.9, bf16[256,2304]{1,0:T(8,128)(2,1)} %select_select_fusion.2), kind=kOutput, calls=%fused_computation.113 | convolution fusion | flops 6799491072 | bytes 21528576 | tf_op jit(solution)/shard_map/dot_general | solution.py:30
  405.6 5.4 multiply_convert_fusion.2
  413.9 13.2 %convolution_convert_fusion.7 = bf16[512,2304]{1,0:T(8,128)(2,1)} fusion(bf16[2304,2880]{1,0:T(8,128)(2,1)} %all-gather.12.cloned.1.call-done, bf16[512,1440]{0,1:T(8,128)(2,1)} %copy-done.34, bf16[512,1440]{0,1:T(8,128)(2,1)S(1)} %get-tuple-element.279), kind=kOutput, calls=%fused_computation.41 | convolution fusion | flops 6801850368 | bytes 18579456 | tf_op jit(solution)/shard_map/dot_general | solution.py:26
  435.2 20.4 %convolution_convert_fusion = bf16[2304,2880]{1,0:T(8,128)(2,1)} fusion(bf16[512,2880]{0,1:T(8,128)(2,1)} %pad_maximum_fusion.6, bf16[512,2880]{0,1:T(8,128)(2,1)} %copy-done.40, bf16[256,2304]{1,0:T(8,128)(2,1)S(1)} %copy-done.49, bf16[256,2304]{1,0:T(8,128)(2,1)} %select_select_fusion.2, bf16[256,2304]{1,0:T(8,128)(2,1)} %fusion.55, ...), kind=kOutput, calls=%fused_computation.1 | convolution fusion | flops 13626851328 | bytes 23887872 | tf_op jit(solution)/shard_map/dot_general | solution.py:22
  467.1 13.7 %convolution_convert_fusion.2 = bf16[2304,1440]{1,0:T(8,128)(2,1)} fusion(bf16[1024,2304]{1,0:T(8,128)(2,1)} %multiply_convert_fusion, bf16[1024,1440]{0,1:T(8,128)(2,1)S(1)} %copy-done.39), kind=kOutput, calls=%fused_computation.3 | convolution fusion | flops 6798090240 | bytes 14303232 | tf_op jit(solution)/shard_map/dot_general | solution.py:22
  484.9 4.6 add_convert_fusion.4
  489.5 5.3 collective-permute-start.32
  496.2 11.9 %convolution_convert_fusion.5 = bf16[1024,2304]{1,0:T(8,128)(2,1)S(1)} fusion(bf16[1024,1440]{0,1:T(8,128)(2,1)} %pad_maximum_fusion.7, bf16[2304,1440]{1,0:T(8,128)(2,1)} %all-gather.10.cloned.1.call-done), kind=kOutput, calls=%fused_computation.16 | convolution fusion | flops 6797131776 | bytes 14303232 | tf_op jit(solution)/shard_map/dot_general | solution.py:26
  508.1 5.8 collective-permute-done.32
  520.2 4.3 multiply_convert_fusion.8
  529.1 17.7 %collective-permute-done.34 = bf16[256,2304]{1,0:T(8,128)(2,1)S(1)} collective-permute-done((bf16[256,2304]{1,0:T(8,128)(2,1)S(1)}, bf16[256,2304]{1,0:T(8,128)(2,1)S(1)}, u32[]{:S(2)}, u32[]{:S(2)}) %collective-permute-start.34) | collective-permute-done | bytes 1179680 | tf_op jit(solution)/shard_map/ppermute | solution.py:548
  556.6 14.9 %collective-permute-done.38 = bf16[256,2304]{1,0:T(8,128)(2,1)S(1)} collective-permute-done((bf16[256,2304]{1,0:T(8,128)(2,1)S(1)}, bf16[256,2304]{1,0:T(8,128)(2,1)S(1)}, u32[]{:S(2)}, u32[]{:S(2)}) %collective-permute-start.38) | collective-permute-done | bytes 1179680 | tf_op jit(solution)/shard_map/ppermute | solution.py:604
  571.5 5.5 collective-permute-done.37
  578.5 6.4 collective-permute-start.42
  597.9 11.1 %collective-permute-done.41 = bf16[256,2304]{1,0:T(8,128)(2,1)} collective-permute-done((bf16[256,2304]{1,0:T(8,128)(2,1)}, bf16[256,2304]{1,0:T(8,128)(2,1)}, u32[]{:S(2)}, u32[]{:S(2)}) %collective-permute-start.41) | collective-permute-done | bytes 1179680 | tf_op jit(solution)/shard_map/ppermute | solution.py:549
  609.0 4.4 add_convert_fusion.2
  620.4 5.3 convolution_convert_fusion.6
  625.7 8.1 convolution_convert_fusion.9.do_in
  634.1 5.3 concatenate.72
  639.5 4.7 collective-permute-start.46
  651.2 29.9 %attend_back.1 = bf16[1024,1920]{1,0:T(8,128)(2,1)} custom-call(s32[8]{0:T(128)S(1)} %and_select_fusion.order, s32[1]{0:T(128)} %dynamic_slice.69.length, bf16[1024,640]{1,0:T(8,128)(2,1)S(1)} %copy-done.7, bf16[1024,640]{1,0:T(8,128)(2,1)S(1)} %copy-done.9, bf16[1024,640]{1,0:T(8,128)(2,1)S(1)} %copy-done.11, f32[5,8,1024]{2,1,0:T(8,128)S(1)} %get-tuple-element.224.log_in, ...), custom_call_target="tpu_custom_call" | custom-call | flops 6039797760 | bytes 10485760 | tf_op jit(solution)/shard_map/attend_back/pallas_call | solution.py:481
  681.2 14.3 %convolution_convert_fusion.1 = bf16[2304,1920]{1,0:T(8,128)(2,1)} fusion(bf16[1024,1920]{1,0:T(8,128)(2,1)} %attend_back.1, bf16[512,2304]{1,0:T(8,128)(2,1)S(1)} %copy-done.44, bf16[512,2304]{1,0:T(8,128)(2,1)S(1)} %copy-done.42), kind=kOutput, calls=%fused_computation.2 | convolution fusion | flops 9073557504 | bytes 17498112 | tf_op jit(solution)/shard_map/dot_general | solution.py:22
  698.9 13.4 %convolution_convert_fusion.3 = bf16[1024,2304]{1,0:T(8,128)(2,1)S(1)} fusion(bf16[1024,1920]{1,0:T(8,128)(2,1)} %attend_back.1, bf16[2304,1920]{1,0:T(8,128)(2,1)} %all-gather.6.cloned.1.call-done), kind=kOutput, calls=%fused_computation.14 | convolution fusion | flops 9062055936 | bytes 17498112 | tf_op jit(solution)/shard_map/dot_general | solution.py:26
  712.4 7.4 collective-permute-start.50
  724.2 10.1 %collective-permute-done.50 = bf16[256,2304]{1,0:T(8,128)(2,1)S(1)} collective-permute-done((bf16[256,2304]{1,0:T(8,128)(2,1)S(1)}, bf16[256,2304]{1,0:T(8,128)(2,1)S(1)}, u32[]{:S(2)}, u32[]{:S(2)}) %collective-permute-start.50) | collective-permute-done | bytes 1179680 | tf_op jit(solution)/shard_map/ppermute | solution.py:604
  734.4 17.5 %collective-permute-done.49 = bf16[288,4352]{1,0:T(8,128)(2,1)} collective-permute-done((bf16[288,4352]{1,0:T(8,128)(2,1)}, bf16[288,4352]{1,0:T(8,128)(2,1)}, u32[]{:S(2)}, u32[]{:S(2)}) %collective-permute-start.49) | collective-permute-done | bytes 2506784 | tf_op jit(solution)/shard_map/ppermute | solution.py:549
  757.3 7.0 collective-permute-start.54
  766.1 5.6 reduce-scatter.11.cloned.1.call-done
  780.4 21.5 %collective-permute-done.53 = bf16[288,4352]{1,0:T(8,128)(2,1)} collective-permute-done((bf16[288,4352]{1,0:T(8,128)(2,1)}, bf16[288,4352]{1,0:T(8,128)(2,1)}, u32[]{:S(2)}, u32[]{:S(2)}) %collective-permute-start.53) | collective-permute-done | bytes 2506784 | tf_op jit(solution)/shard_map/ppermute | solution.py:549
  801.9 5.8 select_bitcast_fusion.1
  815.4 4.4 add_convert_fusion
  819.8 5.6 collective-permute-start.56
  826.7 5.8 select_bitcast_fusion.3
  833.9 12.5 %join_columns.2 = (f32[576,2880]{1,0:T(8,128)}, f32[576,2880]{1,0:T(8,128)}, f32[576,2880]{1,0:T(8,128)}) custom-call(s32[1]{0:T(128)} %bitcast.11.core, bf16[2,288,4352]{2,1,0:T(8,128)(2,1)S(1)} %pad_maximum_fusion.own, bf16[2,288,4352]{2,1,0:T(8,128)(2,1)} %collective-permute-done.60.other), custom_call_target="tpu_custom_call" | custom-call | bytes 39960576 | tf_op jit(solution)/shard_map/join_columns/pallas_call | solution.py:518
  846.3 24.5 %collective-permute-done.56 = bf16[256,2304]{1,0:T(8,128)(2,1)} collective-permute-done((bf16[256,2304]{1,0:T(8,128)(2,1)}, bf16[256,2304]{1,0:T(8,128)(2,1)}, u32[]{:S(2)}, u32[]{:S(2)}) %collective-permute-start.56) | collective-permute-done | bytes 1179680 | tf_op jit(solution)/shard_map/ppermute | solution.py:604
  870.9 5.3 collective-permute-done.57
  883.9 29.0 %collective-permute-done.62 = bf16[288,2560]{1,0:T(8,128)(2,1)S(1)} collective-permute-done((bf16[288,2560]{1,0:T(8,128)(2,1)}, bf16[288,2560]{1,0:T(8,128)(2,1)S(1)}, u32[]{:S(2)}, u32[]{:S(2)}) %collective-permute-start.62) | collective-permute-done | bytes 1474592 | tf_op jit(solution)/shard_map/ppermute | solution.py:549
  919.6 30.8 %collective-permute-done.64 = bf16[288,2560]{1,0:T(8,128)(2,1)S(1)} collective-permute-done((bf16[288,2560]{1,0:T(8,128)(2,1)S(1)}, bf16[288,2560]{1,0:T(8,128)(2,1)S(1)}, u32[]{:S(2)}, u32[]{:S(2)}) %collective-permute-start.64) | collective-permute-done | bytes 1474592 | tf_op jit(solution)/shard_map/ppermute | solution.py:549
  963.4 5.3 join_columns.3
  (386 shorter events, 245.0 us)
Async XLA Ops:
  7.2 102.0 %all-gather.6.cloned.1.call-start = ((), (), s32[]{:S(2)}) async-start(), calls=%async_computation.4 | async-start | bytes 9953280 | tf_op jit(solution)/shard_map/all_gather | solution.py:680
  22.2 167.7 %all-gather.8.cloned.1.call-start = ((), (), s32[]{:S(2)}) async-start(), calls=%async_computation.5 | async-start | bytes 3317760 | tf_op jit(solution)/shard_map/all_gather | solution.py:680
  22.2 30.6 %collective-permute-start = (bf16[256,2304]{1,0:T(8,128)(2,1)S(1)}, bf16[256,2304]{1,0:T(8,128)(2,1)}, u32[]{:S(2)}, u32[]{:S(2)}) collective-permute-start(bf16[256,2304]{1,0:T(8,128)(2,1)S(1)} %dynamic-slice_bitcast_fusion.1), channel_id=1, source_target_pairs={{0,2},{2,4},{4,6},{1,3},{3,5},{5,7},{8,10},{10,12},{12,14},{9,11},... | collective-permute-start | bytes 3538952 | tf_op jit(solution)/shard_map/ppermute | solution.py:548
  28.0 30.7 %collective-permute-start.1 = (bf16[256,2304]{1,0:T(8,128)(2,1)S(1)}, bf16[256,2304]{1,0:T(8,128)(2,1)}, u32[]{:S(2)}, u32[]{:S(2)}) collective-permute-start(bf16[256,2304]{1,0:T(8,128)(2,1)S(1)} %dynamic-slice_bitcast_fusion.1), channel_id=1, source_target_pairs={{2,0},{4,2},{6,4},{3,1},{5,3},{7,5},{10,8},{12,10},{14,12},{11,9},... | collective-permute-start | bytes 3538952 | tf_op jit(solution)/shard_map/ppermute | solution.py:549
  58.6 20.7 %collective-permute-start.2 = (bf16[256,2304]{1,0:T(8,128)(2,1)}, bf16[256,2304]{1,0:T(8,128)(2,1)}, u32[]{:S(2)}, u32[]{:S(2)}) collective-permute-start(bf16[256,2304]{1,0:T(8,128)(2,1)} %collective-permute-done), channel_id=1, source_target_pairs={{2,4},{4,6},{3,5},{5,7},{10,12},{12,14},{11,13},{13,15},{18,20},{2... | collective-permute-start | bytes 3538952 | tf_op jit(solution)/shard_map/ppermute | solution.py:548
  60.3 30.4 %collective-permute-start.3 = (bf16[256,2304]{1,0:T(8,128)(2,1)}, bf16[256,2304]{1,0:T(8,128)(2,1)}, u32[]{:S(2)}, u32[]{:S(2)}) collective-permute-start(bf16[256,2304]{1,0:T(8,128)(2,1)} %collective-permute-done.1), channel_id=1, source_target_pairs={{2,0},{4,2},{3,1},{5,3},{10,8},{12,10},{11,9},{13,11},{18,16},{20,... | collective-permute-start | bytes 3538952 | tf_op jit(solution)/shard_map/ppermute | solution.py:549
  77.8 21.4 %collective-permute-start.7 = (bf16[288,1440]{1,0:T(8,128)(2,1)}, bf16[288,1440]{1,0:T(8,128)(2,1)}, u32[]{:S(2)}, u32[]{:S(2)}) collective-permute-start(bf16[288,1440]{1,0:T(8,128)(2,1)} %dynamic-slice_bitcast_fusion.2), channel_id=1, source_target_pairs={{0,1},{1,0},{2,3},{3,2},{4,5},{5,4},{6,7},{7,6},{8,9},{9,8},{10,11... | collective-permute-start | bytes 2488328 | tf_op jit(solution)/shard_map/ppermute | solution.py:676
  90.7 185.9 %all-gather.10.cloned.1.call-start = ((), (), s32[]{:S(2)}) async-start(), calls=%async_computation.6 | async-start | bytes 7962624 | tf_op jit(solution)/shard_map/all_gather | solution.py:680
  101.9 17.8 %collective-permute-start.5 = (bf16[256,2304]{1,0:T(8,128)(2,1)}, bf16[256,2304]{1,0:T(8,128)(2,1)}, u32[]{:S(2)}, u32[]{:S(2)}) collective-permute-start(bf16[256,2304]{1,0:T(8,128)(2,1)} %collective-permute-done.2), channel_id=1, source_target_pairs={{4,6},{5,7},{12,14},{13,15},{20,22},{21,23},{28,30},{29,31}} | collective-permute-start | bytes 3538952 | tf_op jit(solution)/shard_map/ppermute | solution.py:548
  103.7 30.8 %collective-permute-start.6 = (bf16[256,2304]{1,0:T(8,128)(2,1)}, bf16[256,2304]{1,0:T(8,128)(2,1)}, u32[]{:S(2)}, u32[]{:S(2)}) collective-permute-start(bf16[256,2304]{1,0:T(8,128)(2,1)} %collective-permute-done.3), channel_id=1, source_target_pairs={{2,0},{3,1},{10,8},{11,9},{18,16},{19,17},{26,24},{27,25}} | collective-permute-start | bytes 3538952 | tf_op jit(solution)/shard_map/ppermute | solution.py:549
  134.5 200.8 %all-gather.12.cloned.1.call-start = ((), (), s32[]{:S(2)}) async-start(), calls=%async_computation.7 | async-start | bytes 15261696 | tf_op jit(solution)/shard_map/all_gather | solution.py:680
  148.1 444.7 %reduce-scatter.5.cloned.1.call-start = ((), (), s32[]{:S(2)}) async-start(), calls=%async_computation.8 | async-start | bytes 15261696 | tf_op jit(solution)/shard_map/reduce_scatter | solution.py:683
  148.1 48.7 %collective-permute-start.10 = (bf16[256,2304]{1,0:T(8,128)(2,1)}, bf16[256,2304]{1,0:T(8,128)(2,1)}, u32[]{:S(2)}, u32[]{:S(2)}) collective-permute-start(bf16[256,2304]{1,0:T(8,128)(2,1)} %dynamic-slice_bitcast_fusion), channel_id=1, source_target_pairs={{0,2},{2,4},{4,6},{1,3},{3,5},{5,7},{8,10},{10,12},{12,14},{9,11},... | collective-permute-start | bytes 3538952 | tf_op jit(solution)/shard_map/ppermute | solution.py:548
  150.4 46.4 %collective-permute-start.11 = (bf16[256,2304]{1,0:T(8,128)(2,1)}, bf16[256,2304]{1,0:T(8,128)(2,1)}, u32[]{:S(2)}, u32[]{:S(2)}) collective-permute-start(bf16[256,2304]{1,0:T(8,128)(2,1)} %dynamic-slice_bitcast_fusion), channel_id=1, source_target_pairs={{2,0},{4,2},{6,4},{3,1},{5,3},{7,5},{10,8},{12,10},{14,12},{11,9},... | collective-permute-start | bytes 3538952 | tf_op jit(solution)/shard_map/ppermute | solution.py:549
  197.0 29.1 %collective-permute-start.12 = (bf16[256,2304]{1,0:T(8,128)(2,1)S(1)}, bf16[256,2304]{1,0:T(8,128)(2,1)S(1)}, u32[]{:S(2)}, u32[]{:S(2)}) collective-permute-start(bf16[256,2304]{1,0:T(8,128)(2,1)S(1)} %slice.102), channel_id=1, source_target_pairs={{0,2},{1,3},{8,10},{9,11},{16,18},{17,19},{24,26},{25,27}} | collective-permute-start | bytes 3538952 | tf_op jit(solution)/shard_map/ppermute | solution.py:604
  201.5 24.6 %collective-permute-start.13 = (bf16[256,2304]{1,0:T(8,128)(2,1)S(1)}, bf16[256,2304]{1,0:T(8,128)(2,1)S(1)}, u32[]{:S(2)}, u32[]{:S(2)}) collective-permute-start(bf16[256,2304]{1,0:T(8,128)(2,1)S(1)} %slice.102), channel_id=1, source_target_pairs={{6,4},{7,5},{14,12},{15,13},{22,20},{23,21},{30,28},{31,29}} | collective-permute-start | bytes 3538952 | tf_op jit(solution)/shard_map/ppermute | solution.py:605
  202.2 23.9 %collective-permute-start.14 = (bf16[256,2304]{1,0:T(8,128)(2,1)}, bf16[256,2304]{1,0:T(8,128)(2,1)S(1)}, u32[]{:S(2)}, u32[]{:S(2)}) collective-permute-start(bf16[256,2304]{1,0:T(8,128)(2,1)} %collective-permute-done.10), channel_id=1, source_target_pairs={{2,4},{4,6},{3,5},{5,7},{10,12},{12,14},{11,13},{13,15},{18,20},{2... | collective-permute-start | bytes 3538952 | tf_op jit(solution)/shard_map/ppermute | solution.py:548
  203.0 29.0 %collective-permute-start.15 = (bf16[256,2304]{1,0:T(8,128)(2,1)}, bf16[256,2304]{1,0:T(8,128)(2,1)S(1)}, u32[]{:S(2)}, u32[]{:S(2)}) collective-permute-start(bf16[256,2304]{1,0:T(8,128)(2,1)} %collective-permute-done.11), channel_id=1, source_target_pairs={{2,0},{4,2},{3,1},{5,3},{10,8},{12,10},{11,9},{13,11},{18,16},{20,... | collective-permute-start | bytes 3538952 | tf_op jit(solution)/shard_map/ppermute | solution.py:549
  232.5 26.1 %collective-permute-start.16 = (bf16[256,2304]{1,0:T(8,128)(2,1)S(1)}, bf16[256,2304]{1,0:T(8,128)(2,1)S(1)}, u32[]{:S(2)}, u32[]{:S(2)}) collective-permute-start(bf16[256,2304]{1,0:T(8,128)(2,1)S(1)} %get-tuple-element.298), channel_id=1, source_target_pairs={{0,2},{2,4},{1,3},{3,5},{8,10},{10,12},{9,11},{11,13},{16,18},{18,... | collective-permute-start | bytes 3538952 | tf_op jit(solution)/shard_map/ppermute | solution.py:604
  234.7 23.8 %collective-permute-start.17 = (bf16[256,2304]{1,0:T(8,128)(2,1)S(1)}, bf16[256,2304]{1,0:T(8,128)(2,1)S(1)}, u32[]{:S(2)}, u32[]{:S(2)}) collective-permute-start(bf16[256,2304]{1,0:T(8,128)(2,1)S(1)} %get-tuple-element.297), channel_id=1, source_target_pairs={{4,2},{6,4},{5,3},{7,5},{12,10},{14,12},{13,11},{15,13},{20,18},{2... | collective-permute-start | bytes 3538952 | tf_op jit(solution)/shard_map/ppermute | solution.py:605
  235.4 23.1 %collective-permute-start.18 = (bf16[256,2304]{1,0:T(8,128)(2,1)S(1)}, bf16[256,2304]{1,0:T(8,128)(2,1)S(1)}, u32[]{:S(2)}, u32[]{:S(2)}) collective-permute-start(bf16[256,2304]{1,0:T(8,128)(2,1)S(1)} %collective-permute-done.14), channel_id=1, source_target_pairs={{4,6},{5,7},{12,14},{13,15},{20,22},{21,23},{28,30},{29,31}} | collective-permute-start | bytes 3538952 | tf_op jit(solution)/shard_map/ppermute | solution.py:548
  236.2 28.0 %collective-permute-start.19 = (bf16[256,2304]{1,0:T(8,128)(2,1)S(1)}, bf16[256,2304]{1,0:T(8,128)(2,1)S(1)}, u32[]{:S(2)}, u32[]{:S(2)}) collective-permute-start(bf16[256,2304]{1,0:T(8,128)(2,1)S(1)} %collective-permute-done.15), channel_id=1, source_target_pairs={{2,0},{3,1},{10,8},{11,9},{18,16},{19,17},{26,24},{27,25}} | collective-permute-start | bytes 3538952 | tf_op jit(solution)/shard_map/ppermute | solution.py:549
  266.3 24.7 %collective-permute-start.20 = (bf16[256,2304]{1,0:T(8,128)(2,1)}, bf16[256,2304]{1,0:T(8,128)(2,1)}, u32[]{:S(2)}, u32[]{:S(2)}) collective-permute-start(bf16[256,2304]{1,0:T(8,128)(2,1)} %get-tuple-element.296), channel_id=1, source_target_pairs={{0,2},{2,4},{4,6},{1,3},{3,5},{5,7},{8,10},{10,12},{12,14},{9,11},... | collective-permute-start | bytes 3538952 | tf_op jit(solution)/shard_map/ppermute | solution.py:604
  268.8 27.3 %collective-permute-start.21 = (bf16[256,2304]{1,0:T(8,128)(2,1)}, bf16[256,2304]{1,0:T(8,128)(2,1)}, u32[]{:S(2)}, u32[]{:S(2)}) collective-permute-start(bf16[256,2304]{1,0:T(8,128)(2,1)} %get-tuple-element.295), channel_id=1, source_target_pairs={{2,0},{4,2},{6,4},{3,1},{5,3},{7,5},{10,8},{12,10},{14,12},{11,9},... | collective-permute-start | bytes 3538952 | tf_op jit(solution)/shard_map/ppermute | solution.py:605
  301.3 24.1 %collective-permute-start.22 = (bf16[256,2304]{1,0:T(8,128)(2,1)S(1)}, bf16[256,2304]{1,0:T(8,128)(2,1)S(1)}, u32[]{:S(2)}, u32[]{:S(2)}) collective-permute-start(bf16[256,2304]{1,0:T(8,128)(2,1)S(1)} %multiply_convert_fusion.9), channel_id=1, source_target_pairs={{0,2},{2,4},{4,6},{1,3},{3,5},{5,7},{8,10},{10,12},{12,14},{9,11},... | collective-permute-start | bytes 3538952 | tf_op jit(solution)/shard_map/ppermute | solution.py:548
  303.3 26.4 %collective-permute-start.23 = (bf16[256,2304]{1,0:T(8,128)(2,1)S(1)}, bf16[256,2304]{1,0:T(8,128)(2,1)}, u32[]{:S(2)}, u32[]{:S(2)}) collective-permute-start(bf16[256,2304]{1,0:T(8,128)(2,1)S(1)} %multiply_convert_fusion.9), channel_id=1, source_target_pairs={{2,0},{4,2},{6,4},{3,1},{5,3},{7,5},{10,8},{12,10},{14,12},{11,9},... | collective-permute-start | bytes 3538952 | tf_op jit(solution)/shard_map/ppermute | solution.py:549
  329.7 29.1 %collective-permute-start.24 = (bf16[256,2304]{1,0:T(8,128)(2,1)S(1)}, bf16[256,2304]{1,0:T(8,128)(2,1)}, u32[]{:S(2)}, u32[]{:S(2)}) collective-permute-start(bf16[256,2304]{1,0:T(8,128)(2,1)S(1)} %collective-permute-done.22), channel_id=1, source_target_pairs={{2,4},{4,6},{3,5},{5,7},{10,12},{12,14},{11,13},{13,15},{18,20},{2... | collective-permute-start | bytes 3538952 | tf_op jit(solution)/shard_map/ppermute | solution.py:548
  331.4 27.5 %collective-permute-start.25 = (bf16[256,2304]{1,0:T(8,128)(2,1)}, bf16[256,2304]{1,0:T(8,128)(2,1)}, u32[]{:S(2)}, u32[]{:S(2)}) collective-permute-start(bf16[256,2304]{1,0:T(8,128)(2,1)} %collective-permute-done.23), channel_id=1, source_target_pairs={{2,0},{4,2},{3,1},{5,3},{10,8},{12,10},{11,9},{13,11},{18,16},{20,... | collective-permute-start | bytes 3538952 | tf_op jit(solution)/shard_map/ppermute | solution.py:549
  359.6 26.6 %collective-permute-start.27 = (bf16[256,2304]{1,0:T(8,128)(2,1)}, bf16[256,2304]{1,0:T(8,128)(2,1)S(1)}, u32[]{:S(2)}, u32[]{:S(2)}) collective-permute-start(bf16[256,2304]{1,0:T(8,128)(2,1)} %collective-permute-done.25), channel_id=1, source_target_pairs={{2,0},{3,1},{10,8},{11,9},{18,16},{19,17},{26,24},{27,25}} | collective-permute-start | bytes 3538952 | tf_op jit(solution)/shard_map/ppermute | solution.py:549
  429.6 29.8 %collective-permute-start.28 = (bf16[256,2304]{1,0:T(8,128)(2,1)}, bf16[256,2304]{1,0:T(8,128)(2,1)}, u32[]{:S(2)}, u32[]{:S(2)}) collective-permute-start(bf16[256,2304]{1,0:T(8,128)(2,1)} %slice.112), channel_id=1, source_target_pairs={{0,2},{1,3},{8,10},{9,11},{16,18},{17,19},{24,26},{25,27}} | collective-permute-start | bytes 3538952 | tf_op jit(solution)/shard_map/ppermute | solution.py:604
  433.5 25.9 %collective-permute-start.29 = (bf16[256,2304]{1,0:T(8,128)(2,1)}, bf16[256,2304]{1,0:T(8,128)(2,1)}, u32[]{:S(2)}, u32[]{:S(2)}) collective-permute-start(bf16[256,2304]{1,0:T(8,128)(2,1)} %slice.112), channel_id=1, source_target_pairs={{6,4},{7,5},{14,12},{15,13},{22,20},{23,21},{30,28},{31,29}} | collective-permute-start | bytes 3538952 | tf_op jit(solution)/shard_map/ppermute | solution.py:605
  459.4 174.6 %reduce-scatter.7.cloned.1.call-start = ((), (), s32[]{:S(2)}) async-start(), calls=%async_computation.9 | async-start | bytes 7962624 | tf_op jit(solution)/shard_map/reduce_scatter | solution.py:683
  463.1 21.8 %collective-permute-start.30 = (bf16[256,2304]{1,0:T(8,128)(2,1)}, bf16[256,2304]{1,0:T(8,128)(2,1)}, u32[]{:S(2)}, u32[]{:S(2)}) collective-permute-start(bf16[256,2304]{1,0:T(8,128)(2,1)} %get-tuple-element.306), channel_id=1, source_target_pairs={{0,2},{2,4},{1,3},{3,5},{8,10},{10,12},{9,11},{11,13},{16,18},{18,... | collective-permute-start | bytes 3538952 | tf_op jit(solution)/shard_map/ppermute | solution.py:604
  465.4 19.5 %collective-permute-start.31 = (bf16[256,2304]{1,0:T(8,128)(2,1)S(1)}, bf16[256,2304]{1,0:T(8,128)(2,1)}, u32[]{:S(2)}, u32[]{:S(2)}) collective-permute-start(bf16[256,2304]{1,0:T(8,128)(2,1)S(1)} %get-tuple-element.305), channel_id=1, source_target_pairs={{4,2},{6,4},{5,3},{7,5},{12,10},{14,12},{13,11},{15,13},{20,18},{2... | collective-permute-start | bytes 3538952 | tf_op jit(solution)/shard_map/ppermute | solution.py:605
  489.5 24.4 %collective-permute-start.32 = (bf16[256,2304]{1,0:T(8,128)(2,1)}, bf16[256,2304]{1,0:T(8,128)(2,1)S(1)}, u32[]{:S(2)}, u32[]{:S(2)}) collective-permute-start(bf16[256,2304]{1,0:T(8,128)(2,1)} %get-tuple-element.294), channel_id=1, source_target_pairs={{0,2},{2,4},{4,6},{1,3},{3,5},{5,7},{8,10},{10,12},{12,14},{9,11},... | collective-permute-start | bytes 3538952 | tf_op jit(solution)/shard_map/ppermute | solution.py:604
  494.8 23.3 %collective-permute-start.33 = (bf16[256,2304]{1,0:T(8,128)(2,1)}, bf16[256,2304]{1,0:T(8,128)(2,1)}, u32[]{:S(2)}, u32[]{:S(2)}) collective-permute-start(bf16[256,2304]{1,0:T(8,128)(2,1)} %get-tuple-element.293), channel_id=1, source_target_pairs={{2,0},{4,2},{6,4},{3,1},{5,3},{7,5},{10,8},{12,10},{14,12},{11,9},... | collective-permute-start | bytes 3538952 | tf_op jit(solution)/shard_map/ppermute | solution.py:605
  496.1 199.3 %reduce-scatter.9.cloned.1.call-start = ((), (), s32[]{:S(2)}) async-start(), calls=%async_computation.10 | async-start | bytes 3317760 | tf_op jit(solution)/shard_map/reduce_scatter | solution.py:683
  524.5 22.2 %collective-permute-start.34 = (bf16[256,2304]{1,0:T(8,128)(2,1)S(1)}, bf16[256,2304]{1,0:T(8,128)(2,1)S(1)}, u32[]{:S(2)}, u32[]{:S(2)}) collective-permute-start(bf16[256,2304]{1,0:T(8,128)(2,1)S(1)} %get-tuple-element.267), channel_id=1, source_target_pairs={{0,2},{2,4},{4,6},{1,3},{3,5},{5,7},{8,10},{10,12},{12,14},{9,11},... | collective-permute-start | bytes 3538952 | tf_op jit(solution)/shard_map/ppermute | solution.py:548
  527.8 22.3 %collective-permute-start.35 = (bf16[256,2304]{1,0:T(8,128)(2,1)S(1)}, bf16[256,2304]{1,0:T(8,128)(2,1)S(1)}, u32[]{:S(2)}, u32[]{:S(2)}) collective-permute-start(bf16[256,2304]{1,0:T(8,128)(2,1)S(1)} %get-tuple-element.267), channel_id=1, source_target_pairs={{2,0},{4,2},{6,4},{3,1},{5,3},{7,5},{10,8},{12,10},{14,12},{11,9},... | collective-permute-start | bytes 3538952 | tf_op jit(solution)/shard_map/ppermute | solution.py:549
  550.2 21.3 %collective-permute-start.38 = (bf16[256,2304]{1,0:T(8,128)(2,1)S(1)}, bf16[256,2304]{1,0:T(8,128)(2,1)S(1)}, u32[]{:S(2)}, u32[]{:S(2)}) collective-permute-start(bf16[256,2304]{1,0:T(8,128)(2,1)S(1)} %slice.115), channel_id=1, source_target_pairs={{0,2},{1,3},{8,10},{9,11},{16,18},{17,19},{24,26},{25,27}} | collective-permute-start | bytes 3538952 | tf_op jit(solution)/shard_map/ppermute | solution.py:604
  552.9 18.6 %collective-permute-start.39 = (bf16[256,2304]{1,0:T(8,128)(2,1)S(1)}, bf16[256,2304]{1,0:T(8,128)(2,1)S(1)}, u32[]{:S(2)}, u32[]{:S(2)}) collective-permute-start(bf16[256,2304]{1,0:T(8,128)(2,1)S(1)} %slice.115), channel_id=1, source_target_pairs={{6,4},{7,5},{14,12},{15,13},{22,20},{23,21},{30,28},{31,29}} | collective-permute-start | bytes 3538952 | tf_op jit(solution)/shard_map/ppermute | solution.py:605
  553.6 17.9 %collective-permute-start.36 = (bf16[256,2304]{1,0:T(8,128)(2,1)S(1)}, bf16[256,2304]{1,0:T(8,128)(2,1)}, u32[]{:S(2)}, u32[]{:S(2)}) collective-permute-start(bf16[256,2304]{1,0:T(8,128)(2,1)S(1)} %collective-permute-done.34), channel_id=1, source_target_pairs={{2,4},{4,6},{3,5},{5,7},{10,12},{12,14},{11,13},{13,15},{18,20},{2... | collective-permute-start | bytes 3538952 | tf_op jit(solution)/shard_map/ppermute | solution.py:548
  555.3 21.7 %collective-permute-start.37 = (bf16[256,2304]{1,0:T(8,128)(2,1)S(1)}, bf16[256,2304]{1,0:T(8,128)(2,1)}, u32[]{:S(2)}, u32[]{:S(2)}) collective-permute-start(bf16[256,2304]{1,0:T(8,128)(2,1)S(1)} %collective-permute-done.35), channel_id=1, source_target_pairs={{2,0},{4,2},{3,1},{5,3},{10,8},{12,10},{11,9},{13,11},{18,16},{20,... | collective-permute-start | bytes 3538952 | tf_op jit(solution)/shard_map/ppermute | solution.py:549
  578.5 19.4 %collective-permute-start.42 = (bf16[256,2304]{1,0:T(8,128)(2,1)}, bf16[256,2304]{1,0:T(8,128)(2,1)}, u32[]{:S(2)}, u32[]{:S(2)}) collective-permute-start(bf16[256,2304]{1,0:T(8,128)(2,1)} %get-tuple-element.292), channel_id=1, source_target_pairs={{0,2},{2,4},{1,3},{3,5},{8,10},{10,12},{9,11},{11,13},{16,18},{18,... | collective-permute-start | bytes 3538952 | tf_op jit(solution)/shard_map/ppermute | solution.py:604
  588.3 20.7 %collective-permute-start.41 = (bf16[256,2304]{1,0:T(8,128)(2,1)}, bf16[256,2304]{1,0:T(8,128)(2,1)}, u32[]{:S(2)}, u32[]{:S(2)}) collective-permute-start(bf16[256,2304]{1,0:T(8,128)(2,1)} %collective-permute-done.37), channel_id=1, source_target_pairs={{2,0},{3,1},{10,8},{11,9},{18,16},{19,17},{26,24},{27,25}} | collective-permute-start | bytes 3538952 | tf_op jit(solution)/shard_map/ppermute | solution.py:549
  613.4 26.0 %collective-permute-start.44 = (bf16[256,2304]{1,0:T(8,128)(2,1)}, bf16[256,2304]{1,0:T(8,128)(2,1)}, u32[]{:S(2)}, u32[]{:S(2)}) collective-permute-start(bf16[256,2304]{1,0:T(8,128)(2,1)} %get-tuple-element.290), channel_id=1, source_target_pairs={{0,2},{2,4},{4,6},{1,3},{3,5},{5,7},{8,10},{10,12},{12,14},{9,11},... | collective-permute-start | bytes 3538952 | tf_op jit(solution)/shard_map/ppermute | solution.py:604
  615.9 23.5 %collective-permute-start.45 = (bf16[256,2304]{1,0:T(8,128)(2,1)}, bf16[256,2304]{1,0:T(8,128)(2,1)}, u32[]{:S(2)}, u32[]{:S(2)}) collective-permute-start(bf16[256,2304]{1,0:T(8,128)(2,1)} %get-tuple-element.289), channel_id=1, source_target_pairs={{2,0},{4,2},{6,4},{3,1},{5,3},{7,5},{10,8},{12,10},{14,12},{11,9},... | collective-permute-start | bytes 3538952 | tf_op jit(solution)/shard_map/ppermute | solution.py:605
  639.4 132.2 %reduce-scatter.11.cloned.1.call-start = ((), (), s32[]{:S(2)}) async-start(), calls=%async_computation.11 | async-start | bytes 9953280 | tf_op jit(solution)/shard_map/reduce_scatter | solution.py:683
  639.5 56.0 %collective-permute-start.46 = (bf16[288,4352]{1,0:T(8,128)(2,1)}, bf16[288,4352]{1,0:T(8,128)(2,1)}, u32[]{:S(2)}, u32[]{:S(2)}) collective-permute-start(bf16[288,4352]{1,0:T(8,128)(2,1)} %concatenate.72), channel_id=1, source_target_pairs={{0,2},{2,4},{4,6},{1,3},{3,5},{5,7},{8,10},{10,12},{12,14},{9,11},... | collective-permute-start | bytes 7520264 | tf_op jit(solution)/shard_map/ppermute | solution.py:548
  644.2 51.2 %collective-permute-start.47 = (bf16[288,4352]{1,0:T(8,128)(2,1)}, bf16[288,4352]{1,0:T(8,128)(2,1)}, u32[]{:S(2)}, u32[]{:S(2)}) collective-permute-start(bf16[288,4352]{1,0:T(8,128)(2,1)} %concatenate.72), channel_id=1, source_target_pairs={{2,0},{4,2},{6,4},{3,1},{5,3},{7,5},{10,8},{12,10},{14,12},{11,9},... | collective-permute-start | bytes 7520264 | tf_op jit(solution)/shard_map/ppermute | solution.py:549
  695.5 38.9 %collective-permute-start.48 = (bf16[288,4352]{1,0:T(8,128)(2,1)}, bf16[288,4352]{1,0:T(8,128)(2,1)}, u32[]{:S(2)}, u32[]{:S(2)}) collective-permute-start(bf16[288,4352]{1,0:T(8,128)(2,1)} %collective-permute-done.46), channel_id=1, source_target_pairs={{2,4},{4,6},{3,5},{5,7},{10,12},{12,14},{11,13},{13,15},{18,20},{2... | collective-permute-start | bytes 7520264 | tf_op jit(solution)/shard_map/ppermute | solution.py:548
  697.6 54.3 %collective-permute-start.49 = (bf16[288,4352]{1,0:T(8,128)(2,1)}, bf16[288,4352]{1,0:T(8,128)(2,1)}, u32[]{:S(2)}, u32[]{:S(2)}) collective-permute-start(bf16[288,4352]{1,0:T(8,128)(2,1)} %collective-permute-done.47), channel_id=1, source_target_pairs={{2,0},{4,2},{3,1},{5,3},{10,8},{12,10},{11,9},{13,11},{18,16},{20,... | collective-permute-start | bytes 7520264 | tf_op jit(solution)/shard_map/ppermute | solution.py:549
  712.4 21.9 %collective-permute-start.50 = (bf16[256,2304]{1,0:T(8,128)(2,1)S(1)}, bf16[256,2304]{1,0:T(8,128)(2,1)S(1)}, u32[]{:S(2)}, u32[]{:S(2)}) collective-permute-start(bf16[256,2304]{1,0:T(8,128)(2,1)S(1)} %slice.139), channel_id=1, source_target_pairs={{0,2},{1,3},{8,10},{9,11},{16,18},{17,19},{24,26},{25,27}} | collective-permute-start | bytes 3538952 | tf_op jit(solution)/shard_map/ppermute | solution.py:604
  751.9 28.5 %collective-permute-start.52 = (bf16[288,4352]{1,0:T(8,128)(2,1)}, bf16[288,4352]{1,0:T(8,128)(2,1)}, u32[]{:S(2)}, u32[]{:S(2)}) collective-permute-start(bf16[288,4352]{1,0:T(8,128)(2,1)} %collective-permute-done.48), channel_id=1, source_target_pairs={{4,6},{5,7},{12,14},{13,15},{20,22},{21,23},{28,30},{29,31}} | collective-permute-start | bytes 7520264 | tf_op jit(solution)/shard_map/ppermute | solution.py:548
  754.0 47.9 %collective-permute-start.53 = (bf16[288,4352]{1,0:T(8,128)(2,1)}, bf16[288,4352]{1,0:T(8,128)(2,1)}, u32[]{:S(2)}, u32[]{:S(2)}) collective-permute-start(bf16[288,4352]{1,0:T(8,128)(2,1)} %collective-permute-done.49), channel_id=1, source_target_pairs={{2,0},{3,1},{10,8},{11,9},{18,16},{19,17},{26,24},{27,25}} | collective-permute-start | bytes 7520264 | tf_op jit(solution)/shard_map/ppermute | solution.py:549
  757.3 23.0 %collective-permute-start.54 = (bf16[256,2304]{1,0:T(8,128)(2,1)}, bf16[256,2304]{1,0:T(8,128)(2,1)}, u32[]{:S(2)}, u32[]{:S(2)}) collective-permute-start(bf16[256,2304]{1,0:T(8,128)(2,1)} %get-tuple-element.288), channel_id=1, source_target_pairs={{0,2},{2,4},{1,3},{3,5},{8,10},{10,12},{9,11},{11,13},{16,18},{18,... | collective-permute-start | bytes 3538952 | tf_op jit(solution)/shard_map/ppermute | solution.py:604
  811.5 21.6 %collective-permute-start.60 = (bf16[2,288,4352]{2,1,0:T(8,128)(2,1)}, bf16[2,288,4352]{2,1,0:T(8,128)(2,1)}, u32[]{:S(2)}, u32[]{:S(2)}) collective-permute-start(bf16[2,288,4352]{2,1,0:T(8,128)(2,1)} %pad_maximum_fusion.1), channel_id=1, source_target_pairs={{0,1},{1,0},{2,3},{3,2},{4,5},{5,4},{6,7},{7,6},{8,9},{9,8},{10,11... | collective-permute-start | bytes 15040520 | tf_op jit(solution)/shard_map/ppermute | solution.py:697
  811.5 64.6 %collective-permute-start.58 = (bf16[288,2560]{1,0:T(8,128)(2,1)}, bf16[288,2560]{1,0:T(8,128)(2,1)}, u32[]{:S(2)}, u32[]{:S(2)}) collective-permute-start(bf16[288,2560]{1,0:T(8,128)(2,1)} %concatenate.74), channel_id=1, source_target_pairs={{0,2},{2,4},{4,6},{1,3},{3,5},{5,7},{8,10},{10,12},{12,14},{9,11},... | collective-permute-start | bytes 4423688 | tf_op jit(solution)/shard_map/ppermute | solution.py:548
  814.1 62.0 %collective-permute-start.59 = (bf16[288,2560]{1,0:T(8,128)(2,1)}, bf16[288,2560]{1,0:T(8,128)(2,1)}, u32[]{:S(2)}, u32[]{:S(2)}) collective-permute-start(bf16[288,2560]{1,0:T(8,128)(2,1)} %concatenate.74), channel_id=1, source_target_pairs={{2,0},{4,2},{6,4},{3,1},{5,3},{7,5},{10,8},{12,10},{14,12},{11,9},... | collective-permute-start | bytes 4423688 | tf_op jit(solution)/shard_map/ppermute | solution.py:549
  819.8 51.0 %collective-permute-start.56 = (bf16[256,2304]{1,0:T(8,128)(2,1)}, bf16[256,2304]{1,0:T(8,128)(2,1)}, u32[]{:S(2)}, u32[]{:S(2)}) collective-permute-start(bf16[256,2304]{1,0:T(8,128)(2,1)} %get-tuple-element.286), channel_id=1, source_target_pairs={{0,2},{2,4},{4,6},{1,3},{3,5},{5,7},{8,10},{10,12},{12,14},{9,11},... | collective-permute-start | bytes 3538952 | tf_op jit(solution)/shard_map/ppermute | solution.py:604
  825.4 50.7 %collective-permute-start.57 = (bf16[256,2304]{1,0:T(8,128)(2,1)}, bf16[256,2304]{1,0:T(8,128)(2,1)}, u32[]{:S(2)}, u32[]{:S(2)}) collective-permute-start(bf16[256,2304]{1,0:T(8,128)(2,1)} %get-tuple-element.285), channel_id=1, source_target_pairs={{2,0},{4,2},{6,4},{3,1},{5,3},{7,5},{10,8},{12,10},{14,12},{11,9},... | collective-permute-start | bytes 3538952 | tf_op jit(solution)/shard_map/ppermute | solution.py:605
  833.9 79.0 %collective-permute-start.65 = (bf16[256,2304]{1,0:T(8,128)(2,1)S(1)}, bf16[256,2304]{1,0:T(8,128)(2,1)S(1)}, u32[]{:S(2)}, u32[]{:S(2)}) collective-permute-start(bf16[256,2304]{1,0:T(8,128)(2,1)S(1)} %copy-done.38), channel_id=1, source_target_pairs={{0,1},{1,0},{2,3},{3,2},{4,5},{5,4},{6,7},{7,6},{8,9},{9,8},{10,11... | collective-permute-start | bytes 3538952 | tf_op jit(solution)/shard_map/ppermute | solution.py:911
  877.0 35.8 %collective-permute-start.62 = (bf16[288,2560]{1,0:T(8,128)(2,1)}, bf16[288,2560]{1,0:T(8,128)(2,1)S(1)}, u32[]{:S(2)}, u32[]{:S(2)}) collective-permute-start(bf16[288,2560]{1,0:T(8,128)(2,1)} %collective-permute-done.59), channel_id=1, source_target_pairs={{2,0},{4,2},{3,1},{5,3},{10,8},{12,10},{11,9},{13,11},{18,16},{20,... | collective-permute-start | bytes 4423688 | tf_op jit(solution)/shard_map/ppermute | solution.py:549
  913.8 36.6 %collective-permute-start.64 = (bf16[288,2560]{1,0:T(8,128)(2,1)S(1)}, bf16[288,2560]{1,0:T(8,128)(2,1)S(1)}, u32[]{:S(2)}, u32[]{:S(2)}) collective-permute-start(bf16[288,2560]{1,0:T(8,128)(2,1)S(1)} %collective-permute-done.62), channel_id=1, source_target_pairs={{2,0},{3,1},{10,8},{11,9},{18,16},{19,17},{26,24},{27,25}} | collective-permute-start | bytes 4423688 | tf_op jit(solution)/shard_map/ppermute | solution.py:549
  (87 other events, 1286.0 us)
Sparse Core Ops, SparseCore 0:
  22.3 59.9 all-gather.5
  90.8 29.5 all-gather.7
  134.7 46.9 all-gather.9
  183.4 76.1 all-gather.11
  459.5 96.7 reduce-scatter.4
  559.7 65.4 reduce-scatter.6
  639.6 45.8 reduce-scatter.8
  695.6 76.0 reduce-scatter.10

commit v9 on v8

--- a/solution.py
+++ b/solution.py
@@ -747,12 +747,11 @@
     gain_b = gains[1].astype(jnp.float32)
     out_mine = to_pair(widen(turned_piece(w_out), 1))
     down_mine = to_pair(turned_piece(w_down))
-    gain_a, gain_b, out_mine, own_cot, cos_all, sin_all, order, w_gate, w_up = stage(
-        [tokens_line], gain_a, gain_b, out_mine, own_cot, cos_all, sin_all, order, w_gate, w_up
+    gain_a, gain_b, out_mine, own_cot, cos_all, sin_all, order = stage(
+        [tokens_line], gain_a, gain_b, out_mine, own_cot, cos_all, sin_all, order
     )
     tokens_line.step()
     out_w = gather_pair(out_mine)
-    gate_up_mine = to_pair(column_piece([w_gate, w_up]))
 
     def first_rows(masks):
         rows = jnp.concatenate([tokens_line.near(k) for k in masks], axis=0)
@@ -760,23 +759,21 @@
 
     first_near = first_rows(range(lines // 2))
     qkv_near = plain_product(first_near, qkv_w)
-    own_cot, down_mine, gate_up_mine, qkv_near = stage(
-        [tokens_line], own_cot, down_mine, gate_up_mine, qkv_near
-    )
+    own_cot, down_mine, qkv_near = stage([tokens_line], own_cot, down_mine, qkv_near)
     down_w = gather_pair(down_mine)
 
     cot_line = walk(own_cot)
     cot_line.step()
     first_far = first_rows(range(lines // 2, lines))
     qkv_far = plain_product(first_far, qkv_w)
-    qkv_far, gate_up_mine = lax.optimization_barrier((qkv_far, gate_up_mine))
-    gate_up_w = gather_pair(gate_up_mine)
     first_in = jnp.concatenate([first_near, first_far], axis=0)
     attend, *kept = attend_forward(
         heads, span, order, length.reshape(1), qkv_near, qkv_far, cos_all, sin_all
     )
     attn_part = col_product(attend, out_w).astype(jnp.bfloat16)
-    (attn_part,) = stage([cot_line], attn_part)
+    attn_part, w_gate, w_up = stage([cot_line], attn_part, w_gate, w_up)
+    gate_up_mine = to_pair(column_piece([w_gate, w_up]))
+    gate_up_w = gather_pair(gate_up_mine)
 
     attn_line = add_up(blocks_of(attn_part))
     attn_line.step()

time: 986 us -> 998 us (1.012)
  waiting for transfers between devices: 366 us -> 378 us
    unnamed x147 -> x161, local copies, waits for them, and re-layouts: 24.7 us -> 24.1 us
  transfers between devices with their start and end apart: 78 -> 78, of which waited for: 33 -> 36; matrix products, arithmetic and copies ran while one was open for 30% -> 29% of each run, Pallas kernels for 7% -> 7%
where the time goes in v9:
time: 998 us; the launch traced here: 984 us
  waiting for transfers between devices  378 us (38%)
  matrix products  185 us (19%)
  other arithmetic  136 us (14%)
  starting transfers between devices  129 us (13%)
  Pallas kernels  74.6 us (7%)
  local copies, waits for them, and re-layouts  56.7 us (6%)
  between operations  15.8 us (2%)
    ppermute x18, waiting for transfers between devices, step(): self.downs.append(lax.ppermute(self.downs[-1], self.axis, down_pairs))  178 us
    ppermute x12, waiting for transfers between devices, step(): self.up = lax.ppermute(up, self.axis, [(i, i + 1) for i, _ in ups])  114 us
    dot_general x7, matrix products, plain_product(): return jnp.dot(left_mat, right_mat, preferred_element_type=jnp.float32)  73.7 us
    dot_general x5, matrix products, col_product(): lax.dot_general(left_mat, right_mat, CONTRACT_COLS, preferred_element_typ...  60.4 us
    ppermute x18, waiting for transfers between devices, step(): self.ups.append(lax.ppermute(self.ups[-1], self.axis, up_pairs))  58.3 us
    dot_general x4, matrix products, row_product(): lax.dot_general(left_mat, right_mat, CONTRACT_ROWS, preferred_element_typ...  50.9 us
    ppermute x12, starting transfers between devices, step(): self.up = lax.ppermute(up, self.axis, [(i, i + 1) for i, _ in ups])  48.7 us
    ppermute x18, starting transfers between devices, step(): self.ups.append(lax.ppermute(self.ups[-1], self.axis, up_pairs))  38.7 us
  transfers between devices with their start and end apart: 78, of which 36 were waited for; matrix products, arithmetic and copies ran while one was open for 29% of the time, Pallas kernels for 7%

profile of v9, /device:TPU:0, one launch (start us, length us, event | category | flops | bytes accessed | tf_op | source)
XLA Modules:
  0.0 983.6 jit_solution(7283730695042210219)
XLA Ops:
  25.3 5.7 collective-permute-start
  35.7 20.4 %collective-permute-done = bf16[256,2304]{1,0:T(8,128)(2,1)} collective-permute-done((bf16[256,2304]{1,0:T(8,128)(2,1)}, bf16[256,2304]{1,0:T(8,128)(2,1)}, u32[]{:S(2)}, u32[]{:S(2)}) %collective-permute-start) | collective-permute-done | bytes 1179680 | tf_op jit(solution)/shard_map/ppermute | solution.py:548
  56.1 5.1 collective-permute-done.1
  69.2 8.6 all-gather
  79.8 12.9 %collective-permute-done.3 = bf16[256,2304]{1,0:T(8,128)(2,1)} collective-permute-done((bf16[256,2304]{1,0:T(8,128)(2,1)}, bf16[256,2304]{1,0:T(8,128)(2,1)}, u32[]{:S(2)}, u32[]{:S(2)}) %collective-permute-start.3) | collective-permute-done | bytes 1179680 | tf_op jit(solution)/shard_map/ppermute | solution.py:549
  106.8 10.4 %fusion.77.q_near.k_near.v_near = f32[512,1920]{1,0:T(8,128)} fusion(bf16[512,2304]{1,0:T(8,128)(2,1)} %fusion.5, bf16[2304,1920]{1,0:T(8,128)(2,1)} %all-gather.6.cloned.1.call-done), kind=kOutput, calls=%fused_computation.231 | convolution fusion | flops 4529848320 | bytes 15138816 | tf_op jit(solution)/shard_map/dot_general | solution.py:30
  117.2 15.3 %collective-permute-done.6 = bf16[256,2304]{1,0:T(8,128)(2,1)} collective-permute-done((bf16[256,2304]{1,0:T(8,128)(2,1)}, bf16[256,2304]{1,0:T(8,128)(2,1)}, u32[]{:S(2)}, u32[]{:S(2)}) %collective-permute-start.6) | collective-permute-done | bytes 1179680 | tf_op jit(solution)/shard_map/ppermute | solution.py:549
  136.1 5.8 collective-permute-start.9
  146.2 5.0 fusion.78.q_far.k_far.v_far
  151.2 30.2 %attend.1 = (bf16[1024,640]{1,0:T(8,128)(2,1)S(1)}, bf16[1024,640]{1,0:T(8,128)(2,1)S(1)}, bf16[1024,640]{1,0:T(8,128)(2,1)S(1)}, bf16[1024,640]{1,0:T(8,128)(2,1)S(1)}, f32[5,8,1024]{2,1,0:T(8,128)S(1)}) custom-call(s32[8]{0:T(128)S(1)} %and_select_fusion.order, s32[1]{0:T(128)} %dynamic_slice.65.length, f32[512,1920]{1,0:T(8,128)S(1)} %copy-done.2, ...), custom_call_target="tpu_custom_call" | custom-call | flops 2415919104 | bytes 15728640 | tf_op jit(solution)/shard_map/attend/pallas_call | solution.py:454
  186.5 8.3 convolution_convert_fusion.4
  209.5 22.9 %collective-permute-done.11 = bf16[256,2304]{1,0:T(8,128)(2,1)S(1)} collective-permute-done((bf16[256,2304]{1,0:T(8,128)(2,1)S(1)}, bf16[256,2304]{1,0:T(8,128)(2,1)S(1)}, u32[]{:S(2)}, u32[]{:S(2)}) %collective-permute-start.11) | collective-permute-done | bytes 1179680 | tf_op jit(solution)/shard_map/ppermute | solution.py:604
  232.4 5.9 collective-permute-done.14
  247.4 19.9 %collective-permute-done.15 = bf16[256,2304]{1,0:T(8,128)(2,1)S(1)} collective-permute-done((bf16[256,2304]{1,0:T(8,128)(2,1)S(1)}, bf16[256,2304]{1,0:T(8,128)(2,1)S(1)}, u32[]{:S(2)}, u32[]{:S(2)}) %collective-permute-start.15) | collective-permute-done | bytes 1179680 | tf_op jit(solution)/shard_map/ppermute | solution.py:604
  267.3 5.7 collective-permute-done.18
  281.0 4.3 multiply_convert_fusion
  285.3 9.1 fusion.40
  294.4 5.4 fusion.42
  300.0 5.2 collective-permute-done.20
  313.1 20.1 %collective-permute-done.21 = bf16[256,2304]{1,0:T(8,128)(2,1)} collective-permute-done((bf16[256,2304]{1,0:T(8,128)(2,1)S(1)}, bf16[256,2304]{1,0:T(8,128)(2,1)}, u32[]{:S(2)}, u32[]{:S(2)}) %collective-permute-start.21) | collective-permute-done | bytes 1179680 | tf_op jit(solution)/shard_map/ppermute | solution.py:548
  333.2 5.3 collective-permute-done.22
  344.3 17.9 %fusion.44 = f32[512,2880]{0,1:T(8,128)} fusion(bf16[2304,2880]{1,0:T(8,128)(2,1)} %all-gather.12.cloned.1.call-done, bf16[256,2304]{1,0:T(8,128)(2,1)} %fusion.55, bf16[256,2304]{1,0:T(8,128)(2,1)} %copy-done.52), kind=kOutput, calls=%fused_computation.109 | convolution fusion | flops 6799491072 | bytes 21528576 | tf_op jit(solution)/shard_map/dot_general | solution.py:30
  362.3 5.4 multiply_convert_fusion.5
  370.1 12.8 %convolution_convert_fusion.8 = bf16[512,2304]{1,0:T(8,128)(2,1)} fusion(bf16[512,2880]{0,1:T(8,128)(2,1)S(1)} %pad_maximum_fusion.5, bf16[2304,2880]{1,0:T(8,128)(2,1)} %all-gather.12.cloned.1.call-done), kind=kOutput, calls=%fused_computation.42 | convolution fusion | flops 6795952128 | bytes 18579456 | tf_op jit(solution)/shard_map/dot_general | solution.py:26
  385.7 8.8 collective-permute-done.27
  395.8 17.9 %fusion.48 = f32[512,2880]{0,1:T(8,128)} fusion(bf16[2304,2880]{1,0:T(8,128)(2,1)} %all-gather.12.cloned.1.call-done, bf16[256,2304]{1,0:T(8,128)(2,1)} %select_select_fusion.9, bf16[256,2304]{1,0:T(8,128)(2,1)} %select_select_fusion.2), kind=kOutput, calls=%fused_computation.113 | convolution fusion | flops 6799491072 | bytes 21528576 | tf_op jit(solution)/shard_map/dot_general | solution.py:30
  413.7 5.4 multiply_convert_fusion.2
  422.0 13.3 %convolution_convert_fusion.7 = bf16[512,2304]{1,0:T(8,128)(2,1)} fusion(bf16[2304,2880]{1,0:T(8,128)(2,1)} %all-gather.12.cloned.1.call-done, bf16[512,1440]{0,1:T(8,128)(2,1)} %copy-done.40, bf16[512,1440]{0,1:T(8,128)(2,1)S(1)} %get-tuple-element.273), kind=kOutput, calls=%fused_computation.41 | convolution fusion | flops 6801850368 | bytes 18579456 | tf_op jit(solution)/shard_map/dot_general | solution.py:26
  443.2 20.4 %convolution_convert_fusion = bf16[2304,2880]{1,0:T(8,128)(2,1)} fusion(bf16[512,2880]{0,1:T(8,128)(2,1)} %pad_maximum_fusion.6, bf16[512,2880]{0,1:T(8,128)(2,1)} %copy-done.46, bf16[256,2304]{1,0:T(8,128)(2,1)S(1)} %copy-done.54, bf16[256,2304]{1,0:T(8,128)(2,1)} %select_select_fusion.2, bf16[256,2304]{1,0:T(8,128)(2,1)} %fusion.55, ...), kind=kOutput, calls=%fused_computation.1 | convolution fusion | flops 13626851328 | bytes 23887872 | tf_op jit(solution)/shard_map/dot_general | solution.py:22
  475.5 13.0 %convolution_convert_fusion.2 = bf16[2304,1440]{1,0:T(8,128)(2,1)} fusion(bf16[1024,2304]{1,0:T(8,128)(2,1)} %multiply_convert_fusion, bf16[1024,1440]{0,1:T(8,128)(2,1)S(1)} %copy-done.45), kind=kOutput, calls=%fused_computation.3 | convolution fusion | flops 6798090240 | bytes 14303232 | tf_op jit(solution)/shard_map/dot_general | solution.py:22
  488.6 5.0 collective-permute-done.30
  493.6 4.5 add_convert_fusion.4
  498.0 8.9 collective-permute-start.32
  508.3 11.9 %convolution_convert_fusion.5 = bf16[1024,2304]{1,0:T(8,128)(2,1)S(1)} fusion(bf16[1024,1440]{0,1:T(8,128)(2,1)} %pad_maximum_fusion.7, bf16[2304,1440]{1,0:T(8,128)(2,1)} %all-gather.10.cloned.1.call-done), kind=kOutput, calls=%fused_computation.16 | convolution fusion | flops 6797131776 | bytes 14303232 | tf_op jit(solution)/shard_map/dot_general | solution.py:26
  524.1 5.1 collective-permute-done.33
  531.6 4.6 multiply_convert_fusion.8
  539.8 17.8 %collective-permute-done.34 = bf16[256,2304]{1,0:T(8,128)(2,1)S(1)} collective-permute-done((bf16[256,2304]{1,0:T(8,128)(2,1)S(1)}, bf16[256,2304]{1,0:T(8,128)(2,1)S(1)}, u32[]{:S(2)}, u32[]{:S(2)}) %collective-permute-start.34) | collective-permute-done | bytes 1179680 | tf_op jit(solution)/shard_map/ppermute | solution.py:548
  565.4 16.3 %collective-permute-done.38 = bf16[256,2304]{1,0:T(8,128)(2,1)S(1)} collective-permute-done((bf16[256,2304]{1,0:T(8,128)(2,1)S(1)}, bf16[256,2304]{1,0:T(8,128)(2,1)S(1)}, u32[]{:S(2)}, u32[]{:S(2)}) %collective-permute-start.38) | collective-permute-done | bytes 1179680 | tf_op jit(solution)/shard_map/ppermute | solution.py:604
  587.4 4.5 collective-permute-start.42
  601.4 5.2 collective-permute-done.42
  606.5 7.9 collective-permute-done.41
  614.5 4.6 add_convert_fusion.2
  626.0 5.3 convolution_convert_fusion.6
  631.3 8.0 convolution_convert_fusion.9.do_in
  639.5 5.0 concatenate.72
  644.6 4.9 collective-permute-start.46
  656.8 26.6 %attend_back.1 = bf16[1024,1920]{1,0:T(8,128)(2,1)S(1)} custom-call(s32[8]{0:T(128)S(1)} %and_select_fusion.order, s32[1]{0:T(128)} %dynamic_slice.65.length, bf16[1024,640]{1,0:T(8,128)(2,1)S(1)} %copy-done.11, bf16[1024,640]{1,0:T(8,128)(2,1)S(1)} %copy-done.13, bf16[1024,640]{1,0:T(8,128)(2,1)S(1)} %copy-done.15, f32[5,8,1024]{2,1,0:T(8,128)S(1)} %copy-done.17, ...), custom_call_target="tpu_custom_call" | custom-call | flops 6039797760 | bytes 10485760 | tf_op jit(solution)/shard_map/attend_back/pallas_call | solution.py:481
  685.3 12.2 %convolution_convert_fusion.1 = bf16[2304,1920]{1,0:T(8,128)(2,1)} fusion(bf16[1024,1920]{1,0:T(8,128)(2,1)S(1)} %attend_back.1, bf16[512,2304]{1,0:T(8,128)(2,1)S(1)} %copy-done.49, bf16[512,2304]{1,0:T(8,128)(2,1)S(1)} %copy-done.47), kind=kOutput, calls=%fused_computation.2 | convolution fusion | flops 9073557504 | bytes 17498112 | tf_op jit(solution)/shard_map/dot_general | solution.py:22
  697.5 4.8 collective-permute-done.47
  705.7 14.1 %convolution_convert_fusion.3 = bf16[1024,2304]{1,0:T(8,128)(2,1)S(1)} fusion(bf16[1024,1920]{1,0:T(8,128)(2,1)} %copy-done.18, bf16[2304,1920]{1,0:T(8,128)(2,1)} %all-gather.6.cloned.1.call-done), kind=kOutput, calls=%fused_computation.14 | convolution fusion | flops 9062055936 | bytes 17498112 | tf_op jit(solution)/shard_map/dot_general | solution.py:26
  720.0 5.2 collective-permute-start.50
  730.0 12.5 %collective-permute-done.50 = bf16[256,2304]{1,0:T(8,128)(2,1)S(1)} collective-permute-done((bf16[256,2304]{1,0:T(8,128)(2,1)S(1)}, bf16[256,2304]{1,0:T(8,128)(2,1)S(1)}, u32[]{:S(2)}, u32[]{:S(2)}) %collective-permute-start.50) | collective-permute-done | bytes 1179680 | tf_op jit(solution)/shard_map/ppermute | solution.py:604
  742.6 15.0 %collective-permute-done.49 = bf16[288,4352]{1,0:T(8,128)(2,1)} collective-permute-done((bf16[288,4352]{1,0:T(8,128)(2,1)}, bf16[288,4352]{1,0:T(8,128)(2,1)}, u32[]{:S(2)}, u32[]{:S(2)}) %collective-permute-start.49) | collective-permute-done | bytes 2506784 | tf_op jit(solution)/shard_map/ppermute | solution.py:549
  763.1 7.0 collective-permute-start.54
  785.1 25.0 %collective-permute-done.53 = bf16[288,4352]{1,0:T(8,128)(2,1)} collective-permute-done((bf16[288,4352]{1,0:T(8,128)(2,1)}, bf16[288,4352]{1,0:T(8,128)(2,1)}, u32[]{:S(2)}, u32[]{:S(2)}) %collective-permute-start.53) | collective-permute-done | bytes 2506784 | tf_op jit(solution)/shard_map/ppermute | solution.py:549
  810.1 5.8 select_bitcast_fusion.1
  822.6 4.4 add_convert_fusion
  827.0 5.6 collective-permute-start.56
  833.8 5.8 select_bitcast_fusion.3
  841.0 12.5 %join_columns.2 = (f32[576,2880]{1,0:T(8,128)}, f32[576,2880]{1,0:T(8,128)}, f32[576,2880]{1,0:T(8,128)}) custom-call(s32[1]{0:T(128)} %bitcast.11.core, bf16[2,288,4352]{2,1,0:T(8,128)(2,1)S(1)} %pad_maximum_fusion.own, bf16[2,288,4352]{2,1,0:T(8,128)(2,1)} %collective-permute-done.60.other), custom_call_target="tpu_custom_call" | custom-call | bytes 39960576 | tf_op jit(solution)/shard_map/join_columns/pallas_call | solution.py:518
  853.4 25.6 %collective-permute-done.56 = bf16[256,2304]{1,0:T(8,128)(2,1)} collective-permute-done((bf16[256,2304]{1,0:T(8,128)(2,1)}, bf16[256,2304]{1,0:T(8,128)(2,1)}, u32[]{:S(2)}, u32[]{:S(2)}) %collective-permute-start.56) | collective-permute-done | bytes 1179680 | tf_op jit(solution)/shard_map/ppermute | solution.py:604
  890.8 29.1 %collective-permute-done.62 = bf16[288,2560]{1,0:T(8,128)(2,1)S(1)} collective-permute-done((bf16[288,2560]{1,0:T(8,128)(2,1)}, bf16[288,2560]{1,0:T(8,128)(2,1)S(1)}, u32[]{:S(2)}, u32[]{:S(2)}) %collective-permute-start.62) | collective-permute-done | bytes 1474592 | tf_op jit(solution)/shard_map/ppermute | solution.py:549
  928.0 30.8 %collective-permute-done.64 = bf16[288,2560]{1,0:T(8,128)(2,1)S(1)} collective-permute-done((bf16[288,2560]{1,0:T(8,128)(2,1)S(1)}, bf16[288,2560]{1,0:T(8,128)(2,1)S(1)}, u32[]{:S(2)}, u32[]{:S(2)}) %collective-permute-start.64) | collective-permute-done | bytes 1474592 | tf_op jit(solution)/shard_map/ppermute | solution.py:549
  971.2 5.3 join_columns.3
  (402 shorter events, 254.7 us)
Async XLA Ops:
  7.2 99.6 %all-gather.6.cloned.1.call-start = ((), (), s32[]{:S(2)}) async-start(), calls=%async_computation.4 | async-start | bytes 9953280 | tf_op jit(solution)/shard_map/all_gather | solution.py:680
  25.2 161.2 %all-gather.8.cloned.1.call-start = ((), (), s32[]{:S(2)}) async-start(), calls=%async_computation.5 | async-start | bytes 3317760 | tf_op jit(solution)/shard_map/all_gather | solution.py:680
  25.3 30.9 %collective-permute-start = (bf16[256,2304]{1,0:T(8,128)(2,1)}, bf16[256,2304]{1,0:T(8,128)(2,1)}, u32[]{:S(2)}, u32[]{:S(2)}) collective-permute-start(bf16[256,2304]{1,0:T(8,128)(2,1)} %dynamic-slice_bitcast_fusion.1), channel_id=1, source_target_pairs={{0,2},{2,4},{4,6},{1,3},{3,5},{5,7},{8,10},{10,12},{12,14},{9,11},... | collective-permute-start | bytes 3538952 | tf_op jit(solution)/shard_map/ppermute | solution.py:548
  31.0 30.3 %collective-permute-start.1 = (bf16[256,2304]{1,0:T(8,128)(2,1)}, bf16[256,2304]{1,0:T(8,128)(2,1)}, u32[]{:S(2)}, u32[]{:S(2)}) collective-permute-start(bf16[256,2304]{1,0:T(8,128)(2,1)} %dynamic-slice_bitcast_fusion.1), channel_id=1, source_target_pairs={{2,0},{4,2},{6,4},{3,1},{5,3},{7,5},{10,8},{12,10},{14,12},{11,9},... | collective-permute-start | bytes 3538952 | tf_op jit(solution)/shard_map/ppermute | solution.py:549
  61.2 18.5 %collective-permute-start.2 = (bf16[256,2304]{1,0:T(8,128)(2,1)}, bf16[256,2304]{1,0:T(8,128)(2,1)}, u32[]{:S(2)}, u32[]{:S(2)}) collective-permute-start(bf16[256,2304]{1,0:T(8,128)(2,1)} %collective-permute-done), channel_id=1, source_target_pairs={{2,4},{4,6},{3,5},{5,7},{10,12},{12,14},{11,13},{13,15},{18,20},{2... | collective-permute-start | bytes 3538952 | tf_op jit(solution)/shard_map/ppermute | solution.py:548
  63.0 29.8 %collective-permute-start.3 = (bf16[256,2304]{1,0:T(8,128)(2,1)}, bf16[256,2304]{1,0:T(8,128)(2,1)}, u32[]{:S(2)}, u32[]{:S(2)}) collective-permute-start(bf16[256,2304]{1,0:T(8,128)(2,1)} %collective-permute-done.1), channel_id=1, source_target_pairs={{2,0},{4,2},{3,1},{5,3},{10,8},{12,10},{11,9},{13,11},{18,16},{20,... | collective-permute-start | bytes 3538952 | tf_op jit(solution)/shard_map/ppermute | solution.py:549
  92.8 192.5 %all-gather.10.cloned.1.call-start = ((), (), s32[]{:S(2)}) async-start(), calls=%async_computation.6 | async-start | bytes 7962624 | tf_op jit(solution)/shard_map/all_gather | solution.py:680
  101.8 30.6 %collective-permute-start.6 = (bf16[256,2304]{1,0:T(8,128)(2,1)}, bf16[256,2304]{1,0:T(8,128)(2,1)}, u32[]{:S(2)}, u32[]{:S(2)}) collective-permute-start(bf16[256,2304]{1,0:T(8,128)(2,1)} %collective-permute-done.3), channel_id=1, source_target_pairs={{2,0},{3,1},{10,8},{11,9},{18,16},{19,17},{26,24},{27,25}} | collective-permute-start | bytes 3538952 | tf_op jit(solution)/shard_map/ppermute | solution.py:549
  132.4 211.9 %all-gather.12.cloned.1.call-start = ((), (), s32[]{:S(2)}) async-start(), calls=%async_computation.7 | async-start | bytes 15261696 | tf_op jit(solution)/shard_map/all_gather | solution.py:680
  134.8 59.9 %collective-permute-start.10 = (bf16[256,2304]{1,0:T(8,128)(2,1)}, bf16[256,2304]{1,0:T(8,128)(2,1)}, u32[]{:S(2)}, u32[]{:S(2)}) collective-permute-start(bf16[256,2304]{1,0:T(8,128)(2,1)} %dynamic-slice_bitcast_fusion), channel_id=1, source_target_pairs={{2,0},{4,2},{6,4},{3,1},{5,3},{7,5},{10,8},{12,10},{14,12},{11,9},... | collective-permute-start | bytes 3538952 | tf_op jit(solution)/shard_map/ppermute | solution.py:549
  136.1 58.6 %collective-permute-start.9 = (bf16[256,2304]{1,0:T(8,128)(2,1)}, bf16[256,2304]{1,0:T(8,128)(2,1)}, u32[]{:S(2)}, u32[]{:S(2)}) collective-permute-start(bf16[256,2304]{1,0:T(8,128)(2,1)} %dynamic-slice_bitcast_fusion), channel_id=1, source_target_pairs={{0,2},{2,4},{4,6},{1,3},{3,5},{5,7},{8,10},{10,12},{12,14},{9,11},... | collective-permute-start | bytes 3538952 | tf_op jit(solution)/shard_map/ppermute | solution.py:548
  203.6 395.7 %reduce-scatter.5.cloned.1.call-start = ((), (), s32[]{:S(2)}) async-start(), calls=%async_computation.8 | async-start | bytes 15261696 | tf_op jit(solution)/shard_map/reduce_scatter | solution.py:683
  205.2 27.2 %collective-permute-start.11 = (bf16[256,2304]{1,0:T(8,128)(2,1)S(1)}, bf16[256,2304]{1,0:T(8,128)(2,1)S(1)}, u32[]{:S(2)}, u32[]{:S(2)}) collective-permute-start(bf16[256,2304]{1,0:T(8,128)(2,1)S(1)} %slice.102), channel_id=1, source_target_pairs={{0,2},{1,3},{8,10},{9,11},{16,18},{17,19},{24,26},{25,27}} | collective-permute-start | bytes 3538952 | tf_op jit(solution)/shard_map/ppermute | solution.py:604
  206.7 25.7 %collective-permute-start.12 = (bf16[256,2304]{1,0:T(8,128)(2,1)S(1)}, bf16[256,2304]{1,0:T(8,128)(2,1)S(1)}, u32[]{:S(2)}, u32[]{:S(2)}) collective-permute-start(bf16[256,2304]{1,0:T(8,128)(2,1)S(1)} %slice.102), channel_id=1, source_target_pairs={{6,4},{7,5},{14,12},{15,13},{22,20},{23,21},{30,28},{31,29}} | collective-permute-start | bytes 3538952 | tf_op jit(solution)/shard_map/ppermute | solution.py:605
  207.4 25.0 %collective-permute-start.13 = (bf16[256,2304]{1,0:T(8,128)(2,1)}, bf16[256,2304]{1,0:T(8,128)(2,1)S(1)}, u32[]{:S(2)}, u32[]{:S(2)}) collective-permute-start(bf16[256,2304]{1,0:T(8,128)(2,1)} %collective-permute-done.9), channel_id=1, source_target_pairs={{2,4},{4,6},{3,5},{5,7},{10,12},{12,14},{11,13},{13,15},{18,20},{2... | collective-permute-start | bytes 3538952 | tf_op jit(solution)/shard_map/ppermute | solution.py:548
  208.2 30.1 %collective-permute-start.14 = (bf16[256,2304]{1,0:T(8,128)(2,1)}, bf16[256,2304]{1,0:T(8,128)(2,1)S(1)}, u32[]{:S(2)}, u32[]{:S(2)}) collective-permute-start(bf16[256,2304]{1,0:T(8,128)(2,1)} %collective-permute-done.10), channel_id=1, source_target_pairs={{2,0},{4,2},{3,1},{5,3},{10,8},{12,10},{11,9},{13,11},{18,16},{20,... | collective-permute-start | bytes 3538952 | tf_op jit(solution)/shard_map/ppermute | solution.py:549
  240.4 26.9 %collective-permute-start.15 = (bf16[256,2304]{1,0:T(8,128)(2,1)S(1)}, bf16[256,2304]{1,0:T(8,128)(2,1)S(1)}, u32[]{:S(2)}, u32[]{:S(2)}) collective-permute-start(bf16[256,2304]{1,0:T(8,128)(2,1)S(1)} %get-tuple-element.292), channel_id=1, source_target_pairs={{0,2},{2,4},{1,3},{3,5},{8,10},{10,12},{9,11},{11,13},{16,18},{18,... | collective-permute-start | bytes 3538952 | tf_op jit(solution)/shard_map/ppermute | solution.py:604
  243.4 23.9 %collective-permute-start.16 = (bf16[256,2304]{1,0:T(8,128)(2,1)S(1)}, bf16[256,2304]{1,0:T(8,128)(2,1)S(1)}, u32[]{:S(2)}, u32[]{:S(2)}) collective-permute-start(bf16[256,2304]{1,0:T(8,128)(2,1)S(1)} %get-tuple-element.291), channel_id=1, source_target_pairs={{4,2},{6,4},{5,3},{7,5},{12,10},{14,12},{13,11},{15,13},{20,18},{2... | collective-permute-start | bytes 3538952 | tf_op jit(solution)/shard_map/ppermute | solution.py:605
  244.1 23.2 %collective-permute-start.17 = (bf16[256,2304]{1,0:T(8,128)(2,1)S(1)}, bf16[256,2304]{1,0:T(8,128)(2,1)S(1)}, u32[]{:S(2)}, u32[]{:S(2)}) collective-permute-start(bf16[256,2304]{1,0:T(8,128)(2,1)S(1)} %collective-permute-done.13), channel_id=1, source_target_pairs={{4,6},{5,7},{12,14},{13,15},{20,22},{21,23},{28,30},{29,31}} | collective-permute-start | bytes 3538952 | tf_op jit(solution)/shard_map/ppermute | solution.py:548
  244.9 28.1 %collective-permute-start.18 = (bf16[256,2304]{1,0:T(8,128)(2,1)S(1)}, bf16[256,2304]{1,0:T(8,128)(2,1)S(1)}, u32[]{:S(2)}, u32[]{:S(2)}) collective-permute-start(bf16[256,2304]{1,0:T(8,128)(2,1)S(1)} %collective-permute-done.14), channel_id=1, source_target_pairs={{2,0},{3,1},{10,8},{11,9},{18,16},{19,17},{26,24},{27,25}} | collective-permute-start | bytes 3538952 | tf_op jit(solution)/shard_map/ppermute | solution.py:549
  275.1 24.9 %collective-permute-start.19 = (bf16[256,2304]{1,0:T(8,128)(2,1)}, bf16[256,2304]{1,0:T(8,128)(2,1)}, u32[]{:S(2)}, u32[]{:S(2)}) collective-permute-start(bf16[256,2304]{1,0:T(8,128)(2,1)} %get-tuple-element.290), channel_id=1, source_target_pairs={{0,2},{2,4},{4,6},{1,3},{3,5},{5,7},{8,10},{10,12},{12,14},{9,11},... | collective-permute-start | bytes 3538952 | tf_op jit(solution)/shard_map/ppermute | solution.py:604
  277.6 27.5 %collective-permute-start.20 = (bf16[256,2304]{1,0:T(8,128)(2,1)}, bf16[256,2304]{1,0:T(8,128)(2,1)}, u32[]{:S(2)}, u32[]{:S(2)}) collective-permute-start(bf16[256,2304]{1,0:T(8,128)(2,1)} %get-tuple-element.289), channel_id=1, source_target_pairs={{2,0},{4,2},{6,4},{3,1},{5,3},{7,5},{10,8},{12,10},{14,12},{11,9},... | collective-permute-start | bytes 3538952 | tf_op jit(solution)/shard_map/ppermute | solution.py:605
  309.0 24.2 %collective-permute-start.21 = (bf16[256,2304]{1,0:T(8,128)(2,1)S(1)}, bf16[256,2304]{1,0:T(8,128)(2,1)}, u32[]{:S(2)}, u32[]{:S(2)}) collective-permute-start(bf16[256,2304]{1,0:T(8,128)(2,1)S(1)} %multiply_convert_fusion.9), channel_id=1, source_target_pairs={{0,2},{2,4},{4,6},{1,3},{3,5},{5,7},{8,10},{10,12},{12,14},{9,11},... | collective-permute-start | bytes 3538952 | tf_op jit(solution)/shard_map/ppermute | solution.py:548
  311.8 26.6 %collective-permute-start.22 = (bf16[256,2304]{1,0:T(8,128)(2,1)S(1)}, bf16[256,2304]{1,0:T(8,128)(2,1)}, u32[]{:S(2)}, u32[]{:S(2)}) collective-permute-start(bf16[256,2304]{1,0:T(8,128)(2,1)S(1)} %multiply_convert_fusion.9), channel_id=1, source_target_pairs={{2,0},{4,2},{6,4},{3,1},{5,3},{7,5},{10,8},{12,10},{14,12},{11,9},... | collective-permute-start | bytes 3538952 | tf_op jit(solution)/shard_map/ppermute | solution.py:549
  338.4 29.4 %collective-permute-start.23 = (bf16[256,2304]{1,0:T(8,128)(2,1)}, bf16[256,2304]{1,0:T(8,128)(2,1)}, u32[]{:S(2)}, u32[]{:S(2)}) collective-permute-start(bf16[256,2304]{1,0:T(8,128)(2,1)} %collective-permute-done.21), channel_id=1, source_target_pairs={{2,4},{4,6},{3,5},{5,7},{10,12},{12,14},{11,13},{13,15},{18,20},{2... | collective-permute-start | bytes 3538952 | tf_op jit(solution)/shard_map/ppermute | solution.py:548
  340.1 27.8 %collective-permute-start.24 = (bf16[256,2304]{1,0:T(8,128)(2,1)}, bf16[256,2304]{1,0:T(8,128)(2,1)}, u32[]{:S(2)}, u32[]{:S(2)}) collective-permute-start(bf16[256,2304]{1,0:T(8,128)(2,1)} %collective-permute-done.22), channel_id=1, source_target_pairs={{2,0},{4,2},{3,1},{5,3},{10,8},{12,10},{11,9},{13,11},{18,16},{20,... | collective-permute-start | bytes 3538952 | tf_op jit(solution)/shard_map/ppermute | solution.py:549
  367.9 17.9 %collective-permute-start.26 = (bf16[256,2304]{1,0:T(8,128)(2,1)}, bf16[256,2304]{1,0:T(8,128)(2,1)S(1)}, u32[]{:S(2)}, u32[]{:S(2)}) collective-permute-start(bf16[256,2304]{1,0:T(8,128)(2,1)} %collective-permute-done.23), channel_id=1, source_target_pairs={{4,6},{5,7},{12,14},{13,15},{20,22},{21,23},{28,30},{29,31}} | collective-permute-start | bytes 3538952 | tf_op jit(solution)/shard_map/ppermute | solution.py:548
  368.6 25.9 %collective-permute-start.27 = (bf16[256,2304]{1,0:T(8,128)(2,1)}, bf16[256,2304]{1,0:T(8,128)(2,1)S(1)}, u32[]{:S(2)}, u32[]{:S(2)}) collective-permute-start(bf16[256,2304]{1,0:T(8,128)(2,1)} %collective-permute-done.24), channel_id=1, source_target_pairs={{2,0},{3,1},{10,8},{11,9},{18,16},{19,17},{26,24},{27,25}} | collective-permute-start | bytes 3538952 | tf_op jit(solution)/shard_map/ppermute | solution.py:549
  437.8 29.7 %collective-permute-start.28 = (bf16[256,2304]{1,0:T(8,128)(2,1)}, bf16[256,2304]{1,0:T(8,128)(2,1)}, u32[]{:S(2)}, u32[]{:S(2)}) collective-permute-start(bf16[256,2304]{1,0:T(8,128)(2,1)} %slice.112), channel_id=1, source_target_pairs={{0,2},{1,3},{8,10},{9,11},{16,18},{17,19},{24,26},{25,27}} | collective-permute-start | bytes 3538952 | tf_op jit(solution)/shard_map/ppermute | solution.py:604
  441.6 25.9 %collective-permute-start.29 = (bf16[256,2304]{1,0:T(8,128)(2,1)}, bf16[256,2304]{1,0:T(8,128)(2,1)}, u32[]{:S(2)}, u32[]{:S(2)}) collective-permute-start(bf16[256,2304]{1,0:T(8,128)(2,1)} %slice.112), channel_id=1, source_target_pairs={{6,4},{7,5},{14,12},{15,13},{22,20},{23,21},{30,28},{31,29}} | collective-permute-start | bytes 3538952 | tf_op jit(solution)/shard_map/ppermute | solution.py:605
  467.5 172.0 %reduce-scatter.7.cloned.1.call-start = ((), (), s32[]{:S(2)}) async-start(), calls=%async_computation.9 | async-start | bytes 7962624 | tf_op jit(solution)/shard_map/reduce_scatter | solution.py:683
  471.6 22.0 %collective-permute-start.30 = (bf16[256,2304]{1,0:T(8,128)(2,1)}, bf16[256,2304]{1,0:T(8,128)(2,1)}, u32[]{:S(2)}, u32[]{:S(2)}) collective-permute-start(bf16[256,2304]{1,0:T(8,128)(2,1)} %get-tuple-element.300), channel_id=1, source_target_pairs={{0,2},{2,4},{1,3},{3,5},{8,10},{10,12},{9,11},{11,13},{16,18},{18,... | collective-permute-start | bytes 3538952 | tf_op jit(solution)/shard_map/ppermute | solution.py:604
  473.8 19.7 %collective-permute-start.31 = (bf16[256,2304]{1,0:T(8,128)(2,1)}, bf16[256,2304]{1,0:T(8,128)(2,1)}, u32[]{:S(2)}, u32[]{:S(2)}) collective-permute-start(bf16[256,2304]{1,0:T(8,128)(2,1)} %get-tuple-element.299), channel_id=1, source_target_pairs={{4,2},{6,4},{5,3},{7,5},{12,10},{14,12},{13,11},{15,13},{20,18},{2... | collective-permute-start | bytes 3538952 | tf_op jit(solution)/shard_map/ppermute | solution.py:605
  498.0 26.1 %collective-permute-start.32 = (bf16[256,2304]{1,0:T(8,128)(2,1)}, bf16[256,2304]{1,0:T(8,128)(2,1)}, u32[]{:S(2)}, u32[]{:S(2)}) collective-permute-start(bf16[256,2304]{1,0:T(8,128)(2,1)} %get-tuple-element.288), channel_id=1, source_target_pairs={{0,2},{2,4},{4,6},{1,3},{3,5},{5,7},{8,10},{10,12},{12,14},{9,11},... | collective-permute-start | bytes 3538952 | tf_op jit(solution)/shard_map/ppermute | solution.py:604
  506.9 22.3 %collective-permute-start.33 = (bf16[256,2304]{1,0:T(8,128)(2,1)}, bf16[256,2304]{1,0:T(8,128)(2,1)}, u32[]{:S(2)}, u32[]{:S(2)}) collective-permute-start(bf16[256,2304]{1,0:T(8,128)(2,1)} %get-tuple-element.287), channel_id=1, source_target_pairs={{2,0},{4,2},{6,4},{3,1},{5,3},{7,5},{10,8},{12,10},{14,12},{11,9},... | collective-permute-start | bytes 3538952 | tf_op jit(solution)/shard_map/ppermute | solution.py:605
  508.2 194.1 %reduce-scatter.9.cloned.1.call-start = ((), (), s32[]{:S(2)}) async-start(), calls=%async_computation.10 | async-start | bytes 3317760 | tf_op jit(solution)/shard_map/reduce_scatter | solution.py:683
  536.2 21.5 %collective-permute-start.34 = (bf16[256,2304]{1,0:T(8,128)(2,1)S(1)}, bf16[256,2304]{1,0:T(8,128)(2,1)S(1)}, u32[]{:S(2)}, u32[]{:S(2)}) collective-permute-start(bf16[256,2304]{1,0:T(8,128)(2,1)S(1)} %get-tuple-element.261), channel_id=1, source_target_pairs={{0,2},{2,4},{4,6},{1,3},{3,5},{5,7},{8,10},{10,12},{12,14},{9,11},... | collective-permute-start | bytes 3538952 | tf_op jit(solution)/shard_map/ppermute | solution.py:548
  538.5 21.8 %collective-permute-start.35 = (bf16[256,2304]{1,0:T(8,128)(2,1)S(1)}, bf16[256,2304]{1,0:T(8,128)(2,1)S(1)}, u32[]{:S(2)}, u32[]{:S(2)}) collective-permute-start(bf16[256,2304]{1,0:T(8,128)(2,1)S(1)} %get-tuple-element.261), channel_id=1, source_target_pairs={{2,0},{4,2},{6,4},{3,1},{5,3},{7,5},{10,8},{12,10},{14,12},{11,9},... | collective-permute-start | bytes 3538952 | tf_op jit(solution)/shard_map/ppermute | solution.py:549
  560.4 21.3 %collective-permute-start.38 = (bf16[256,2304]{1,0:T(8,128)(2,1)S(1)}, bf16[256,2304]{1,0:T(8,128)(2,1)S(1)}, u32[]{:S(2)}, u32[]{:S(2)}) collective-permute-start(bf16[256,2304]{1,0:T(8,128)(2,1)S(1)} %slice.115), channel_id=1, source_target_pairs={{0,2},{1,3},{8,10},{9,11},{16,18},{17,19},{24,26},{25,27}} | collective-permute-start | bytes 3538952 | tf_op jit(solution)/shard_map/ppermute | solution.py:604
  562.6 19.1 %collective-permute-start.39 = (bf16[256,2304]{1,0:T(8,128)(2,1)S(1)}, bf16[256,2304]{1,0:T(8,128)(2,1)S(1)}, u32[]{:S(2)}, u32[]{:S(2)}) collective-permute-start(bf16[256,2304]{1,0:T(8,128)(2,1)S(1)} %slice.115), channel_id=1, source_target_pairs={{6,4},{7,5},{14,12},{15,13},{22,20},{23,21},{30,28},{31,29}} | collective-permute-start | bytes 3538952 | tf_op jit(solution)/shard_map/ppermute | solution.py:605
  563.4 18.4 %collective-permute-start.36 = (bf16[256,2304]{1,0:T(8,128)(2,1)S(1)}, bf16[256,2304]{1,0:T(8,128)(2,1)S(1)}, u32[]{:S(2)}, u32[]{:S(2)}) collective-permute-start(bf16[256,2304]{1,0:T(8,128)(2,1)S(1)} %collective-permute-done.34), channel_id=1, source_target_pairs={{2,4},{4,6},{3,5},{5,7},{10,12},{12,14},{11,13},{13,15},{18,20},{2... | collective-permute-start | bytes 3538952 | tf_op jit(solution)/shard_map/ppermute | solution.py:548
  564.1 21.3 %collective-permute-start.37 = (bf16[256,2304]{1,0:T(8,128)(2,1)S(1)}, bf16[256,2304]{1,0:T(8,128)(2,1)}, u32[]{:S(2)}, u32[]{:S(2)}) collective-permute-start(bf16[256,2304]{1,0:T(8,128)(2,1)S(1)} %collective-permute-done.35), channel_id=1, source_target_pairs={{2,0},{4,2},{3,1},{5,3},{10,8},{12,10},{11,9},{13,11},{18,16},{20,... | collective-permute-start | bytes 3538952 | tf_op jit(solution)/shard_map/ppermute | solution.py:549
  587.4 19.1 %collective-permute-start.42 = (bf16[256,2304]{1,0:T(8,128)(2,1)}, bf16[256,2304]{1,0:T(8,128)(2,1)}, u32[]{:S(2)}, u32[]{:S(2)}) collective-permute-start(bf16[256,2304]{1,0:T(8,128)(2,1)} %get-tuple-element.286), channel_id=1, source_target_pairs={{0,2},{2,4},{1,3},{3,5},{8,10},{10,12},{9,11},{11,13},{16,18},{18,... | collective-permute-start | bytes 3538952 | tf_op jit(solution)/shard_map/ppermute | solution.py:604
  595.3 19.1 %collective-permute-start.41 = (bf16[256,2304]{1,0:T(8,128)(2,1)}, bf16[256,2304]{1,0:T(8,128)(2,1)}, u32[]{:S(2)}, u32[]{:S(2)}) collective-permute-start(bf16[256,2304]{1,0:T(8,128)(2,1)} %collective-permute-done.37), channel_id=1, source_target_pairs={{2,0},{3,1},{10,8},{11,9},{18,16},{19,17},{26,24},{27,25}} | collective-permute-start | bytes 3538952 | tf_op jit(solution)/shard_map/ppermute | solution.py:549
  619.0 25.4 %collective-permute-start.44 = (bf16[256,2304]{1,0:T(8,128)(2,1)}, bf16[256,2304]{1,0:T(8,128)(2,1)}, u32[]{:S(2)}, u32[]{:S(2)}) collective-permute-start(bf16[256,2304]{1,0:T(8,128)(2,1)} %get-tuple-element.284), channel_id=1, source_target_pairs={{0,2},{2,4},{4,6},{1,3},{3,5},{5,7},{8,10},{10,12},{12,14},{9,11},... | collective-permute-start | bytes 3538952 | tf_op jit(solution)/shard_map/ppermute | solution.py:604
  621.4 23.1 %collective-permute-start.45 = (bf16[256,2304]{1,0:T(8,128)(2,1)}, bf16[256,2304]{1,0:T(8,128)(2,1)}, u32[]{:S(2)}, u32[]{:S(2)}) collective-permute-start(bf16[256,2304]{1,0:T(8,128)(2,1)} %get-tuple-element.283), channel_id=1, source_target_pairs={{2,0},{4,2},{6,4},{3,1},{5,3},{7,5},{10,8},{12,10},{14,12},{11,9},... | collective-permute-start | bytes 3538952 | tf_op jit(solution)/shard_map/ppermute | solution.py:605
  644.5 131.0 %reduce-scatter.11.cloned.1.call-start = ((), (), s32[]{:S(2)}) async-start(), calls=%async_computation.11 | async-start | bytes 9953280 | tf_op jit(solution)/shard_map/reduce_scatter | solution.py:683
  644.6 52.9 %collective-permute-start.46 = (bf16[288,4352]{1,0:T(8,128)(2,1)}, bf16[288,4352]{1,0:T(8,128)(2,1)}, u32[]{:S(2)}, u32[]{:S(2)}) collective-permute-start(bf16[288,4352]{1,0:T(8,128)(2,1)} %concatenate.72), channel_id=1, source_target_pairs={{0,2},{2,4},{4,6},{1,3},{3,5},{5,7},{8,10},{10,12},{12,14},{9,11},... | collective-permute-start | bytes 7520264 | tf_op jit(solution)/shard_map/ppermute | solution.py:548
  649.5 52.8 %collective-permute-start.47 = (bf16[288,4352]{1,0:T(8,128)(2,1)}, bf16[288,4352]{1,0:T(8,128)(2,1)}, u32[]{:S(2)}, u32[]{:S(2)}) collective-permute-start(bf16[288,4352]{1,0:T(8,128)(2,1)} %concatenate.72), channel_id=1, source_target_pairs={{2,0},{4,2},{6,4},{3,1},{5,3},{7,5},{10,8},{12,10},{14,12},{11,9},... | collective-permute-start | bytes 7520264 | tf_op jit(solution)/shard_map/ppermute | solution.py:549
  702.3 40.2 %collective-permute-start.48 = (bf16[288,4352]{1,0:T(8,128)(2,1)}, bf16[288,4352]{1,0:T(8,128)(2,1)}, u32[]{:S(2)}, u32[]{:S(2)}) collective-permute-start(bf16[288,4352]{1,0:T(8,128)(2,1)} %collective-permute-done.46), channel_id=1, source_target_pairs={{2,4},{4,6},{3,5},{5,7},{10,12},{12,14},{11,13},{13,15},{18,20},{2... | collective-permute-start | bytes 7520264 | tf_op jit(solution)/shard_map/ppermute | solution.py:548
  704.4 53.2 %collective-permute-start.49 = (bf16[288,4352]{1,0:T(8,128)(2,1)}, bf16[288,4352]{1,0:T(8,128)(2,1)}, u32[]{:S(2)}, u32[]{:S(2)}) collective-permute-start(bf16[288,4352]{1,0:T(8,128)(2,1)} %collective-permute-done.47), channel_id=1, source_target_pairs={{2,0},{4,2},{3,1},{5,3},{10,8},{12,10},{11,9},{13,11},{18,16},{20,... | collective-permute-start | bytes 7520264 | tf_op jit(solution)/shard_map/ppermute | solution.py:549
  720.0 22.6 %collective-permute-start.50 = (bf16[256,2304]{1,0:T(8,128)(2,1)S(1)}, bf16[256,2304]{1,0:T(8,128)(2,1)S(1)}, u32[]{:S(2)}, u32[]{:S(2)}) collective-permute-start(bf16[256,2304]{1,0:T(8,128)(2,1)S(1)} %slice.139), channel_id=1, source_target_pairs={{0,2},{1,3},{8,10},{9,11},{16,18},{17,19},{24,26},{25,27}} | collective-permute-start | bytes 3538952 | tf_op jit(solution)/shard_map/ppermute | solution.py:604
  725.2 17.4 %collective-permute-start.51 = (bf16[256,2304]{1,0:T(8,128)(2,1)S(1)}, bf16[256,2304]{1,0:T(8,128)(2,1)S(1)}, u32[]{:S(2)}, u32[]{:S(2)}) collective-permute-start(bf16[256,2304]{1,0:T(8,128)(2,1)S(1)} %slice.139), channel_id=1, source_target_pairs={{6,4},{7,5},{14,12},{15,13},{22,20},{23,21},{30,28},{31,29}} | collective-permute-start | bytes 3538952 | tf_op jit(solution)/shard_map/ppermute | solution.py:605
  757.6 27.5 %collective-permute-start.52 = (bf16[288,4352]{1,0:T(8,128)(2,1)}, bf16[288,4352]{1,0:T(8,128)(2,1)}, u32[]{:S(2)}, u32[]{:S(2)}) collective-permute-start(bf16[288,4352]{1,0:T(8,128)(2,1)} %collective-permute-done.48), channel_id=1, source_target_pairs={{4,6},{5,7},{12,14},{13,15},{20,22},{21,23},{28,30},{29,31}} | collective-permute-start | bytes 7520264 | tf_op jit(solution)/shard_map/ppermute | solution.py:548
  759.7 50.4 %collective-permute-start.53 = (bf16[288,4352]{1,0:T(8,128)(2,1)}, bf16[288,4352]{1,0:T(8,128)(2,1)}, u32[]{:S(2)}, u32[]{:S(2)}) collective-permute-start(bf16[288,4352]{1,0:T(8,128)(2,1)} %collective-permute-done.49), channel_id=1, source_target_pairs={{2,0},{3,1},{10,8},{11,9},{18,16},{19,17},{26,24},{27,25}} | collective-permute-start | bytes 7520264 | tf_op jit(solution)/shard_map/ppermute | solution.py:549
  763.1 22.0 %collective-permute-start.54 = (bf16[256,2304]{1,0:T(8,128)(2,1)}, bf16[256,2304]{1,0:T(8,128)(2,1)}, u32[]{:S(2)}, u32[]{:S(2)}) collective-permute-start(bf16[256,2304]{1,0:T(8,128)(2,1)} %get-tuple-element.282), channel_id=1, source_target_pairs={{0,2},{2,4},{1,3},{3,5},{8,10},{10,12},{9,11},{11,13},{16,18},{18,... | collective-permute-start | bytes 3538952 | tf_op jit(solution)/shard_map/ppermute | solution.py:604
  819.7 20.5 %collective-permute-start.60 = (bf16[2,288,4352]{2,1,0:T(8,128)(2,1)}, bf16[2,288,4352]{2,1,0:T(8,128)(2,1)}, u32[]{:S(2)}, u32[]{:S(2)}) collective-permute-start(bf16[2,288,4352]{2,1,0:T(8,128)(2,1)} %pad_maximum_fusion.1), channel_id=1, source_target_pairs={{0,1},{1,0},{2,3},{3,2},{4,5},{5,4},{6,7},{7,6},{8,9},{9,8},{10,11... | collective-permute-start | bytes 15040520 | tf_op jit(solution)/shard_map/ppermute | solution.py:697
  819.7 63.6 %collective-permute-start.58 = (bf16[288,2560]{1,0:T(8,128)(2,1)}, bf16[288,2560]{1,0:T(8,128)(2,1)S(1)}, u32[]{:S(2)}, u32[]{:S(2)}) collective-permute-start(bf16[288,2560]{1,0:T(8,128)(2,1)} %concatenate.74), channel_id=1, source_target_pairs={{0,2},{2,4},{4,6},{1,3},{3,5},{5,7},{8,10},{10,12},{12,14},{9,11},... | collective-permute-start | bytes 4423688 | tf_op jit(solution)/shard_map/ppermute | solution.py:548
  821.3 62.0 %collective-permute-start.59 = (bf16[288,2560]{1,0:T(8,128)(2,1)}, bf16[288,2560]{1,0:T(8,128)(2,1)}, u32[]{:S(2)}, u32[]{:S(2)}) collective-permute-start(bf16[288,2560]{1,0:T(8,128)(2,1)} %concatenate.74), channel_id=1, source_target_pairs={{2,0},{4,2},{6,4},{3,1},{5,3},{7,5},{10,8},{12,10},{14,12},{11,9},... | collective-permute-start | bytes 4423688 | tf_op jit(solution)/shard_map/ppermute | solution.py:549
  827.0 52.1 %collective-permute-start.56 = (bf16[256,2304]{1,0:T(8,128)(2,1)}, bf16[256,2304]{1,0:T(8,128)(2,1)}, u32[]{:S(2)}, u32[]{:S(2)}) collective-permute-start(bf16[256,2304]{1,0:T(8,128)(2,1)} %get-tuple-element.280), channel_id=1, source_target_pairs={{0,2},{2,4},{4,6},{1,3},{3,5},{5,7},{8,10},{10,12},{12,14},{9,11},... | collective-permute-start | bytes 3538952 | tf_op jit(solution)/shard_map/ppermute | solution.py:604
  832.6 50.7 %collective-permute-start.57 = (bf16[256,2304]{1,0:T(8,128)(2,1)}, bf16[256,2304]{1,0:T(8,128)(2,1)}, u32[]{:S(2)}, u32[]{:S(2)}) collective-permute-start(bf16[256,2304]{1,0:T(8,128)(2,1)} %get-tuple-element.279), channel_id=1, source_target_pairs={{2,0},{4,2},{6,4},{3,1},{5,3},{7,5},{10,8},{12,10},{14,12},{11,9},... | collective-permute-start | bytes 3538952 | tf_op jit(solution)/shard_map/ppermute | solution.py:605
  841.0 79.0 %collective-permute-start.65 = (bf16[256,2304]{1,0:T(8,128)(2,1)S(1)}, bf16[256,2304]{1,0:T(8,128)(2,1)}, u32[]{:S(2)}, u32[]{:S(2)}) collective-permute-start(bf16[256,2304]{1,0:T(8,128)(2,1)S(1)} %copy-done.44), channel_id=1, source_target_pairs={{0,1},{1,0},{2,3},{3,2},{4,5},{5,4},{6,7},{7,6},{8,9},{9,8},{10,11... | collective-permute-start | bytes 3538952 | tf_op jit(solution)/shard_map/ppermute | solution.py:908
  884.2 35.8 %collective-permute-start.62 = (bf16[288,2560]{1,0:T(8,128)(2,1)}, bf16[288,2560]{1,0:T(8,128)(2,1)S(1)}, u32[]{:S(2)}, u32[]{:S(2)}) collective-permute-start(bf16[288,2560]{1,0:T(8,128)(2,1)} %collective-permute-done.59), channel_id=1, source_target_pairs={{2,0},{4,2},{3,1},{5,3},{10,8},{12,10},{11,9},{13,11},{18,16},{20,... | collective-permute-start | bytes 4423688 | tf_op jit(solution)/shard_map/ppermute | solution.py:549
  922.2 36.6 %collective-permute-start.64 = (bf16[288,2560]{1,0:T(8,128)(2,1)S(1)}, bf16[288,2560]{1,0:T(8,128)(2,1)S(1)}, u32[]{:S(2)}, u32[]{:S(2)}) collective-permute-start(bf16[288,2560]{1,0:T(8,128)(2,1)S(1)} %collective-permute-done.62), channel_id=1, source_target_pairs={{2,0},{3,1},{10,8},{11,9},{18,16},{19,17},{26,24},{27,25}} | collective-permute-start | bytes 4423688 | tf_op jit(solution)/shard_map/ppermute | solution.py:549
  (94 other events, 1672.2 us)
Sparse Core Ops, SparseCore 0:
  25.3 59.0 all-gather.5
  92.9 30.7 all-gather.7
  132.6 46.8 all-gather.9
  203.7 74.3 all-gather.11
  467.6 97.6 reduce-scatter.4
  568.7 65.4 reduce-scatter.6
  644.6 47.6 reduce-scatter.8
  702.4 73.0 reduce-scatter.10
